TPU v7x, 256 devices: a whole 4x4x8 slice. The times are simulated.
256 devices in a mesh: energy: 64 (over z_hi, y, x), slab: 4 (over z_lo, core).
Axes of the slice: x: 4, y: 4, z: 8 (z_hi: 4, z_lo: 2; z = z_hi * 2 + z_lo), core: 2. Of those that a mesh axis runs over, the one named last changes fastest.
Arguments:
- g_less: bfloat16 [1024, 4, 5, 64, 128], P('energy', 'slab'), may hold values from -6 to 6
- g_greater: bfloat16 [1024, 4, 5, 64, 128], P('energy', 'slab'), may hold values from -6 to 6
- coulomb: bfloat16 [4, 64, 192], P('slab'), may hold values from -0.4375 to 0.4375
- pattern: int32 [4, 5], replicated, may hold values from 0 to 9, as said below
Outputs:
- screened: bfloat16 [1024, 4, 5, 64, 128], P('energy', 'slab')
Inputs may be any that keep to these rules, and one draw needn't show every extreme that they name: `pattern`: row r holds 5 distinct columns: r, r + 3, r + 6 and two of r + 1, r + 2, r + 4, r + 5, in any order of slots.
All inputs are finite; a program needn't handle non-finite values.
Results may differ from a plain program's by a relative error of at most 0.007.
Values may be sent and summed in bfloat16 or wider, within the bound.
No kernel may reach another device: no remote copies, remote signals or barrier semaphores. Data moves between devices by JAX's collectives and lax.ppermute only.
A program may use at most 64 MiB of HBM per device.

v0:
```python
import math

import jax
import jax.numpy as jnp
from jax import lax
from jax.sharding import PartitionSpec as P

NE = 1024


def with_halo(cells, sides, width):
    for axis, dim in sides:
        count = lax.axis_size(axis)
        ends = count - 1
        head = lax.slice_in_dim(cells, 0, width, axis=dim)
        tail = lax.slice_in_dim(cells, cells.shape[dim] - width, cells.shape[dim], axis=dim)
        cells = jnp.concatenate(
            [
                lax.ppermute(tail, axis, [(i, (i + 1) % count) for i in range(ends)]),
                cells,
                lax.ppermute(head, axis, [((i + 1) % count, i) for i in range(ends)]),
            ],
            axis=dim,
        )
    return cells


def make_tables():
    energy_index = jnp.arange(NE, dtype=jnp.int32)
    phases = energy_index[:, None] * energy_index[None, :] % NE
    angles = phases.astype(jnp.float32) * (2.0 * math.pi / NE)
    norm_scale = 1.0 / math.sqrt(NE)
    table_real = (jnp.cos(angles) * norm_scale).astype(jnp.bfloat16)
    table_imag = (-jnp.sin(angles) * norm_scale).astype(jnp.bfloat16)
    return (table_real, table_imag)


def two_products(values, table_real, table_imag):
    flat = values.reshape(NE, -1)
    direct = jnp.dot(table_real, flat, preferred_element_type=jnp.float32).reshape(values.shape)
    swapped = jnp.dot(table_imag, flat, preferred_element_type=jnp.float32).reshape(values.shape)
    return (direct, swapped)


def shards(g_less, g_greater, coulomb, pattern):
    e_local, rows_local, slots_count, orbitals, wide_cols = g_less.shape
    half_cols = wide_cols // 2
    lesser = lax.all_to_all(g_less, "energy", split_axis=3, concat_axis=0, tiled=True)
    greater = lax.all_to_all(g_greater, "energy", split_axis=3, concat_axis=0, tiled=True)
    table_real, table_imag = make_tables()
    direct, swapped = two_products(lesser, table_real, table_imag)
    less_real = direct[..., :half_cols] - swapped[..., half_cols:]
    less_imag = direct[..., half_cols:] + swapped[..., :half_cols]
    direct, swapped = two_products(greater, table_real, table_imag)
    great_real = direct[..., :half_cols] - swapped[..., half_cols:]
    great_imag = direct[..., half_cols:] + swapped[..., :half_cols]
    prod_real = less_real * great_real + less_imag * great_imag
    prod_imag = less_imag * great_real - less_real * great_imag
    product = jnp.concatenate([prod_real, prod_imag], -1).astype(jnp.bfloat16)
    direct, swapped = two_products(product, table_real, table_imag)
    back_real = direct[..., :half_cols] + swapped[..., half_cols:]
    back_imag = direct[..., half_cols:] - swapped[..., :half_cols]
    polar = jnp.concatenate([back_real, back_imag], -1).astype(jnp.bfloat16)
    returned = lax.all_to_all(polar, "energy", split_axis=0, concat_axis=3, tiled=True)
    padded = with_halo(returned, (("slab", 1),), 1)
    start_row = lax.axis_index("slab") * rows_local
    filler = jnp.full((1, slots_count), -1, jnp.int32)
    extended = jnp.concatenate([filler, pattern, filler], 0)
    local_pattern = lax.dynamic_slice_in_dim(extended, start_row, rows_local + 2, 0)
    neigh_cols = jnp.stack([local_pattern[offset : offset + rows_local] for offset in range(3)], 1)
    center_cols = local_pattern[1 : rows_local + 1]
    selector = (neigh_cols[:, :, None, :] == center_cols[:, None, :, None]).astype(jnp.bfloat16)
    neighbours = jnp.stack([padded[:, offset : offset + rows_local] for offset in range(3)], 2)
    picked = jnp.einsum(
        "rdst,erdtin->erdsin", selector, neighbours, preferred_element_type=jnp.float32
    ).astype(jnp.bfloat16)
    weights = coulomb.reshape(rows_local, orbitals, 3, orbitals)
    screened = jnp.einsum("radi,erdsin->ersan", weights, picked, preferred_element_type=jnp.float32)
    return screened.astype(jnp.bfloat16)


def solution(mesh):
    placed = (
        P("energy", "slab", None, None, None),
        P("energy", "slab", None, None, None),
        P("slab", None, None),
        P(),
    )
    return jax.shard_map(
        shards,
        mesh=mesh,
        in_specs=placed,
        out_specs=P("energy", "slab", None, None, None),
        check_vma=False,
    )
```

profile of v0, /device:TPU:1, one launch (start us, length us, event | category | flops | bytes accessed | tf_op | source)
XLA Modules:
  0.0 264.9 jit_solution(11489579964996317793)
XLA Ops:
  0.0 0.0 copy-start.2
  0.0 3.3 %copy.34 = bf16[16,1,5,64,128]{4,0,2,1,3:T(8,128)(2,1)} copy(bf16[16,1,5,64,128]{4,3,2,1,0:T(8,128)(2,1)} %param.4) | data formatting | bytes 2621440 | tf_op args[0]
  3.3 15.1 %all-to-all-start = ((bf16[16,1,5,64,128]{4,0,2,1,3:T(8,128)(2,1)}), bf16[16,1,5,64,128]{4,0,2,1,3:T(8,128)(2,1)S(1)}, u32[]{:S(2)}, u32[]{:S(2)}) async-start(bf16[16,1,5,64,128]{4,0,2,1,3:T(8,128)(2,1)} %copy.34), calls=%async_computation | async-start | bytes 2621440 | tf_op jit(solution)/shard_map/all_to_all | solution.py:48
  18.4 0.0 copy-done.2
  18.5 2.0 copy.37
  20.4 29.5 %all-to-all-done = bf16[16,1,5,64,128]{4,0,2,1,3:T(8,128)(2,1)S(1)} async-done(((bf16[16,1,5,64,128]{4,0,2,1,3:T(8,128)(2,1)}), bf16[16,1,5,64,128]{4,0,2,1,3:T(8,128)(2,1)S(1)}, u32[]{:S(2)}, u32[]{:S(2)}) %all-to-all-start) | async-done | bytes 1310752 | tf_op jit(solution)/shard_map/all_to_all | solution.py:48
  49.9 10.1 %all-to-all-start.1 = ((bf16[16,1,5,64,128]{4,0,2,1,3:T(8,128)(2,1)}), bf16[16,1,5,64,128]{4,0,2,1,3:T(8,128)(2,1)S(1)}, u32[]{:S(2)}, u32[]{:S(2)}) async-start(bf16[16,1,5,64,128]{4,0,2,1,3:T(8,128)(2,1)} %copy.37), calls=%async_computation.1 | async-start | bytes 2621440 | tf_op jit(solution)/shard_map/all_to_all | solution.py:49
  60.0 0.5 copy.35
  60.6 0.3 copy.75
  60.8 1.5 copy.36
  62.3 0.0 copy-start.3
  62.3 19.0 %fusion.29 = f32[1024,1,5,1,128]{0,4,2,3,1:T(8,128)} fusion(bf16[5,128,1024]{2,1,0:T(8,128)(2,1)} %bitcast.139), kind=kOutput, calls=%fused_computation.33 | convolution fusion | flops 1358954496 | bytes 3932160 | tf_op jit(solution)/shard_map/dot_general | solution.py:40
  81.3 0.0 copy-done.3
  81.3 17.7 %fusion.38 = f32[1024,1,5,1,128]{0,4,2,3,1:T(8,128)} fusion(bf16[5,128,1024]{2,1,0:T(8,128)(2,1)S(1)} %bitcast.140), kind=kOutput, calls=%fused_computation.36 | convolution fusion | flops 1360003072 | bytes 3932160 | tf_op jit(solution)/shard_map/dot_general | solution.py:41
  98.9 0.0 all-to-all-done.1
  98.9 0.5 copy.38
  99.5 0.3 copy.74
  99.7 0.7 copy.39
  100.4 17.1 %fusion.32 = f32[1024,1,5,1,128]{0,4,2,3,1:T(8,128)S(1)} fusion(bf16[5,128,1024]{2,1,0:T(8,128)(2,1)S(1)} %bitcast.141), kind=kOutput, calls=%fused_computation.34 | convolution fusion | flops 1358954496 | bytes 3932160 | tf_op jit(solution)/shard_map/dot_general | solution.py:40
  117.5 0.0 copy-start
  117.5 0.0 copy-start.1
  117.5 17.4 %fusion.41 = f32[1024,1,5,1,128]{0,4,2,3,1:T(8,128)S(1)} fusion(bf16[5,128,1024]{2,1,0:T(8,128)(2,1)S(1)} %bitcast.142), kind=kOutput, calls=%fused_computation.37 | convolution fusion | flops 1360003072 | bytes 3932160 | tf_op jit(solution)/shard_map/dot_general | solution.py:41
  135.0 0.0 copy-done
  135.0 0.0 copy-done.1
  135.0 1.4 add_convert_fusion
  136.4 16.5 %fusion.35 = f32[1024,1,5,1,128]{0,4,2,3,1:T(8,128)S(1)} fusion(bf16[1024,1,5,1,64]{0,4,2,3,1:T(8,128)(2,1)S(1)} %get-tuple-element.6, bf16[1024,1,5,1,64]{0,4,2,3,1:T(8,128)(2,1)S(1)} %get-tuple-element.5), kind=kOutput, calls=%fused_computation.35 | convolution fusion | flops 1361575936 | bytes 3932160 | tf_op jit(solution)/shard_map/dot_general | solution.py:40
  152.9 16.6 %fusion.44 = f32[1024,1,5,1,128]{0,4,2,3,1:T(8,128)S(1)} fusion(bf16[1024,1,5,1,64]{0,4,2,3,1:T(8,128)(2,1)S(1)} %get-tuple-element.6, bf16[1024,1,5,1,64]{0,4,2,3,1:T(8,128)(2,1)S(1)} %get-tuple-element.5), kind=kOutput, calls=%fused_computation.38 | convolution fusion | flops 1362624512 | bytes 3932160 | tf_op jit(solution)/shard_map/dot_general | solution.py:41
  169.5 0.7 fusion.51
  170.2 0.1 pad_maximum_fusion
  170.3 2.4 copy.40
  172.7 63.0 %all_to_all.48 = bf16[1024,1,5,1,128]{4,2,3,1,0:T(8,128)(2,1)S(1)} all-to-all(bf16[1024,1,5,1,128]{4,2,3,1,0:T(8,128)(2,1)S(1)} %copy.40), channel_id=1, replica_groups=mesh['energy'=64,'slab'=4] {'energy'}, dimensions={0} | all-to-all | bytes 2621440 | tf_op jit(solution)/shard_map/all_to_all | solution.py:64
  235.7 0.0 copy-start.4
  235.7 0.0 copy-start.5
  235.7 0.5 copy.73
  236.2 0.3 copy.43
  236.6 4.9 %collective-permute-start.1 = (bf16[16,1,5,64,128]{4,3,2,1,0:T(8,128)(2,1)S(1)}, bf16[16,1,5,64,128]{4,3,2,1,0:T(8,128)(2,1)}, u32[]{:S(2)}, u32[]{:S(2)}) collective-permute-start(bf16[16,1,5,64,128]{4,3,2,1,0:T(8,128)(2,1)S(1)} %copy.43), channel_id=1, source_target_pairs={{1,0},{2,1},{3,2},{5,4},{6,5},{7,6},{9,8},{10,9},{11,10},{13,12},{... | collective-permute-start | bytes 3932168 | tf_op jit(solution)/shard_map/ppermute | solution.py:21
  241.5 1.9 collective-permute-start
  243.4 0.0 copy-done.4
  243.4 0.1 copy.47
  243.5 0.0 copy-done.5
  243.6 12.0 %collective-permute-done.1 = bf16[16,1,5,64,128]{4,3,2,1,0:T(8,128)(2,1)} collective-permute-done((bf16[16,1,5,64,128]{4,3,2,1,0:T(8,128)(2,1)S(1)}, bf16[16,1,5,64,128]{4,3,2,1,0:T(8,128)(2,1)}, u32[]{:S(2)}, u32[]{:S(2)}) %collective-permute-start.1) | collective-permute-done | bytes 1310752 | tf_op jit(solution)/shard_map/ppermute | solution.py:21
  255.6 2.4 copy.71
  258.0 0.0 collective-permute-done
  258.0 2.4 copy.72
  260.4 2.3 convert_bitcast_fusion
  262.7 1.9 fusion.47
  (5 shorter events, 0.0 us)
Async XLA Ops:
  0.0 18.5 %copy-start.2 = (bf16[16,1,5,64,128]{4,3,2,1,0:T(8,128)(2,1)S(1)}, bf16[16,1,5,64,128]{4,3,2,1,0:T(8,128)(2,1)}, u32[]{:S(2)}) copy-start(bf16[16,1,5,64,128]{4,3,2,1,0:T(8,128)(2,1)} %param.5) | copy-start | bytes 3932164
  3.3 46.6 %all-to-all-start = ((bf16[16,1,5,64,128]{4,0,2,1,3:T(8,128)(2,1)}), bf16[16,1,5,64,128]{4,0,2,1,3:T(8,128)(2,1)S(1)}, u32[]{:S(2)}, u32[]{:S(2)}) async-start(bf16[16,1,5,64,128]{4,0,2,1,3:T(8,128)(2,1)} %copy.34), calls=%async_computation | async-start | bytes 2621440 | tf_op jit(solution)/shard_map/all_to_all | solution.py:48
  49.9 49.1 %all-to-all-start.1 = ((bf16[16,1,5,64,128]{4,0,2,1,3:T(8,128)(2,1)}), bf16[16,1,5,64,128]{4,0,2,1,3:T(8,128)(2,1)S(1)}, u32[]{:S(2)}, u32[]{:S(2)}) async-start(bf16[16,1,5,64,128]{4,0,2,1,3:T(8,128)(2,1)} %copy.37), calls=%async_computation.1 | async-start | bytes 2621440 | tf_op jit(solution)/shard_map/all_to_all | solution.py:49
  62.3 19.0 %copy-start.3 = (bf16[640,1024]{1,0:T(8,128)(2,1)S(1)}, bf16[640,1024]{1,0:T(8,128)(2,1)}, u32[]{:S(2)}) copy-start(bf16[640,1024]{1,0:T(8,128)(2,1)} %copy.36) | copy-start | bytes 3932164
  117.5 17.5 %copy-start = (f32[1024,1,5,1,128]{0,4,2,3,1:T(8,128)S(1)}, f32[1024,1,5,1,128]{0,4,2,3,1:T(8,128)}, u32[]{:S(2)}) copy-start(f32[1024,1,5,1,128]{0,4,2,3,1:T(8,128)} %fusion.29) | copy-start | bytes 7864324
  117.5 17.5 %copy-start.1 = (f32[1024,1,5,1,128]{0,4,2,3,1:T(8,128)S(1)}, f32[1024,1,5,1,128]{0,4,2,3,1:T(8,128)}, u32[]{:S(2)}) copy-start(f32[1024,1,5,1,128]{0,4,2,3,1:T(8,128)} %fusion.38) | copy-start | bytes 7864324
  235.7 7.7 %copy-start.4 = (bf16[1,64,192]{2,1,0:T(8,128)(2,1)S(1)}, bf16[1,64,192]{2,1,0:T(8,128)(2,1)}, u32[]{:S(2)}) copy-start(bf16[1,64,192]{2,1,0:T(8,128)(2,1)} %param.6) | copy-start | bytes 73732
  235.7 7.9 %copy-start.5 = (s32[4,5]{1,0:T(4,128)S(1)}, s32[4,5]{1,0:T(4,128)}, u32[]{:S(2)}) copy-start(s32[4,5]{1,0:T(4,128)} %param.7) | copy-start | bytes 244
  236.6 19.0 %collective-permute-start.1 = (bf16[16,1,5,64,128]{4,3,2,1,0:T(8,128)(2,1)S(1)}, bf16[16,1,5,64,128]{4,3,2,1,0:T(8,128)(2,1)}, u32[]{:S(2)}, u32[]{:S(2)}) collective-permute-start(bf16[16,1,5,64,128]{4,3,2,1,0:T(8,128)(2,1)S(1)} %copy.43), channel_id=1, source_target_pairs={{1,0},{2,1},{3,2},{5,4},{6,5},{7,6},{9,8},{10,9},{11,10},{13,12},{... | collective-permute-start | bytes 3932168 | tf_op jit(solution)/shard_map/ppermute | solution.py:21
  241.5 16.5 %collective-permute-start = (bf16[16,1,5,64,128]{4,3,2,1,0:T(8,128)(2,1)S(1)}, bf16[16,1,5,64,128]{4,3,2,1,0:T(8,128)(2,1)}, u32[]{:S(2)}, u32[]{:S(2)}) collective-permute-start(bf16[16,1,5,64,128]{4,3,2,1,0:T(8,128)(2,1)S(1)} %copy.43), channel_id=1, source_target_pairs={{0,1},{1,2},{2,3},{4,5},{5,6},{6,7},{8,9},{9,10},{10,11},{12,13},{... | collective-permute-start | bytes 3932168 | tf_op jit(solution)/shard_map/ppermute | solution.py:19
where the time goes:
time: 269 us; the launch traced here: 265 us
  matrix products  109 us (41%)
  blocking collectives  63 us (23%)
  waiting for transfers between devices  41.5 us (15%)
  starting transfers between devices  32.1 us (12%)
  local copies, waits for them, and re-layouts  17.2 us (6%)
    all_to_all x1, blocking collectives, shards(): lax.all_to_all(polar, 'energy', split_axis=0, concat_axis=3, tiled=True)  63 us
    dot_general x3, matrix products, two_products(): jnp.dot(table_real, flat, preferred_element_type=jnp.float32)  52.5 us
    dot_general x3, matrix products, two_products(): jnp.dot(table_imag, flat, preferred_element_type=jnp.float32)  51.7 us
    all_to_all x1, waiting for transfers between devices, shards(): lax.all_to_all(g_less, 'energy', split_axis=3, concat_axis=0, tiled=True)  29.5 us
    all_to_all x1, starting transfers between devices, shards(): lax.all_to_all(g_less, 'energy', split_axis=3, concat_axis=0, tiled=True)  15.1 us
    ppermute x1, waiting for transfers between devices, with_halo(): lax.ppermute(head, axis, [((i + 1) % count, i) for i in range(ends)])  12 us
    all_to_all x1, starting transfers between devices, shards(): lax.all_to_all(g_greater, 'energy', split_axis=3, concat_axis=0, tiled=True)  10.1 us
    unnamed x17, local copies, waits for them, and re-layouts  5.91 us
  transfers between devices with their start and end apart: 4, of which 2 were waited for; matrix products, arithmetic and copies ran while one was open for 16% of the time, Pallas kernels for 0%

commit v1 on v0

v1 whole, which is shorter than its diff:
```python
import functools
import math

import jax
import jax.numpy as jnp
import ml_dtypes
import numpy as np
from jax import lax
from jax.experimental import pallas as pl
from jax.experimental.pallas import tpu as pltpu
from jax.sharding import Mesh, PartitionSpec as P

NE = 1024
QUART = NE // 4
NZ = 4
NP = 16
NL = 16
ALL = ("z", "y", "x", "s")
PLANE = ("y", "x")
STEPS = (3, 1, -1, -3)


def tables():
    e = np.arange(QUART)
    out = []
    for first in range(4):
        t = 4 * np.arange(QUART) + first
        angle = 2.0 * math.pi * ((e[:, None] * t[None, :]) % NE) / NE
        scale = 1.0 / math.sqrt(NE)
        real = (np.cos(angle) * scale).astype(np.float32).astype(ml_dtypes.bfloat16)
        imag = (-np.sin(angle) * scale).astype(np.float32).astype(ml_dtypes.bfloat16)
        out.append((real, imag))
    forward = np.stack([np.concatenate([r.T, i.T], 0) for r, i in out])
    inverse = np.stack([np.concatenate([r, i], 0) for r, i in out])
    return forward, inverse


def hop(piece, step):
    perm = []
    for z in range(4):
        for yx in range(16):
            for s in range(4):
                to = (2 * z + s // 2 + step) % 8
                perm.append(((z * 16 + yx) * 4 + s, ((to // 2) * 16 + yx) * 4 + (to % 2) * 2 + s % 2))
    return lax.ppermute(piece, ALL, perm)


def times_i(v):
    lane = lax.broadcasted_iota(jnp.int32, v.shape, 1)
    return jnp.where(lane < 64, -1.0, 1.0) * pltpu.roll(v, 64, 1)


def correlate_kernel(slots, split, rot_ref, *refs):
    less_refs, great_ref, fwd_ref, inv_ref = refs[:4], refs[4], refs[5], refs[6]
    n_out = 4 if split else 1
    outs = refs[7 : 7 + n_out]
    xl_ref, xg_ref, z_ref = refs[7 + n_out :]
    f32, bf16 = jnp.float32, jnp.bfloat16

    def butterflies(get, x_ref):
        for s in range(slots):
            x0, x1, x2, x3 = (get(j, s).reshape(QUART, 128).astype(f32) for j in range(4))
            a, b, c, d = x0 + x2, x0 - x2, x1 + x3, x1 - x3
            d = times_i(d)
            for t1, v in enumerate((a + c, b - d, a - c, b + d)):
                hi = v.astype(bf16)
                x_ref[t1, 0, :, s * 128 : (s + 1) * 128] = hi
                x_ref[t1, 1, :, s * 128 : (s + 1) * 128] = (v - hi.astype(f32)).astype(bf16)

    butterflies(lambda j, s: less_refs[j][:, s], xl_ref)
    butterflies(lambda j, s: great_ref[:, j, s], xg_ref)

    @pl.loop(0, 4)
    def _(t1):
        table, back = fwd_ref[t1], inv_ref[t1]
        for s in range(0, slots, 2):
            n = min(2, slots - s)
            cols = slice(s * 128, (s + n) * 128)

            def transform(x_ref):
                y = jnp.dot(table, x_ref[t1, 0, :, cols], preferred_element_type=f32)
                y = y + jnp.dot(table, x_ref[t1, 1, :, cols], preferred_element_type=f32)
                return y

            yl, yg = transform(xl_ref), transform(xg_ref)
            prods = []
            for k in range(n):
                own = slice(k * 128, (k + 1) * 128)
                le = yl[:QUART, own] + times_i(yl[QUART:, own])
                gr = yg[:QUART, own] + times_i(yg[QUART:, own])
                m1 = le * gr
                m2 = le * pltpu.roll(gr, 64, 1)
                lane = lax.broadcasted_iota(jnp.int32, m1.shape, 1)
                prod = jnp.where(lane < 64, m1 + pltpu.roll(m1, 64, 1), m2 - pltpu.roll(m2, 64, 1))
                prods.append(prod.astype(bf16))
            prod = prods[0] if n == 1 else jnp.concatenate(prods, 1)
            zz = jnp.dot(back, prod, preferred_element_type=f32)
            for k in range(n):
                own = slice(k * 128, (k + 1) * 128)
                z_ref[t1, :, (s + k) * 128 : (s + k + 1) * 128] = zz[:QUART, own] - times_i(zz[QUART:, own])

    ca, cb, cc = rot_ref[0], rot_ref[1], rot_ref[2]
    for s in range(slots):
        z0, z1, z2, z3 = (z_ref[t, :, s * 128 : (s + 1) * 128] for t in range(4))
        u1 = ca * z1 + cb * times_i(z1)
        u3 = ca * z3 - cb * times_i(z3)
        u2 = cc * z2
        a, b, c = z0 + u2, z0 - u2, u1 + u3
        d = times_i(u1 - u3)
        for j, v in enumerate((a + c, b - d, a - c, b + d)):
            v = v.astype(bf16).reshape(NP, NL, 128)
            if split:
                outs[j][:, s] = v
            else:
                outs[0][:, j, s] = v


def correlate(rot, less, great, fwd, inv, split):
    slots = great.shape[2]
    n = slots * 128
    vmem = pl.BlockSpec(memory_space=pltpu.VMEM)
    piece = jax.ShapeDtypeStruct((NP, slots, NL, 128), jnp.bfloat16)
    whole = jax.ShapeDtypeStruct((NP, NZ, slots, NL, 128), jnp.bfloat16)
    out = pl.pallas_call(
        functools.partial(correlate_kernel, slots, split),
        out_shape=[piece] * 4 if split else [whole],
        in_specs=[pl.BlockSpec(memory_space=pltpu.SMEM)] + [vmem] * 7,
        out_specs=[vmem] * (4 if split else 1),
        scratch_shapes=[
            pltpu.VMEM((4, 2, QUART, n), jnp.bfloat16),
            pltpu.VMEM((4, 2, QUART, n), jnp.bfloat16),
            pltpu.VMEM((4, QUART, n), jnp.float32),
        ],
        compiler_params=pltpu.CompilerParams(vmem_limit_bytes=40 << 20),
        cost_estimate=pl.CostEstimate(
            flops=2 * 4 * 512 * 256 * n * 5, bytes_accessed=3 * NE * n * 2 + (2 << 20), transcendentals=0
        ),
        name="correlate",
    )(rot, *less, great, fwd, inv)
    return out if split else out[0]


def screen_kernel(at_ref, ok_ref, w_ref, up_ref, own_ref, down_ref, out_ref):
    slots = own_ref.shape[1]
    w = w_ref[...]
    for l in range(own_ref.shape[0]):
        cols = []
        for s in range(slots):
            blocks = []
            for d, ref in enumerate((up_ref, own_ref, down_ref)):
                if d == 1:
                    blocks.append(ref[l, s])
                else:
                    got = ref[l, at_ref[d, s]]
                    blocks.append(jnp.where(ok_ref[d, s] > 0, got, jnp.zeros_like(got)))
            cols.append(jnp.concatenate(blocks, 0))
        res = jnp.dot(w, jnp.concatenate(cols, 1), preferred_element_type=jnp.float32)
        for s in range(slots):
            out_ref[l, s] = res[:, s * 128 : (s + 1) * 128].astype(jnp.bfloat16)


def screen(at, ok, weights, up, own, down):
    el, slots, bi, wide = own.shape
    step = 4
    block = pl.BlockSpec((step, slots, bi, wide), lambda i: (i, 0, 0, 0))
    smem = pl.BlockSpec(memory_space=pltpu.SMEM)
    return pl.pallas_call(
        screen_kernel,
        grid=(el // step,),
        out_shape=jax.ShapeDtypeStruct(own.shape, jnp.bfloat16),
        in_specs=[smem, smem, pl.BlockSpec(weights.shape, lambda i: (0, 0)), block, block, block],
        out_specs=block,
        cost_estimate=pl.CostEstimate(
            flops=2 * el * slots * bi * 3 * bi * wide, bytes_accessed=4 * own.size * 2, transcendentals=0
        ),
        name="screen",
    )(at, ok, weights, up, own, down)


def shards(g_less, g_greater, coulomb, pattern):
    el, rows, slots, bi, wide = g_less.shape
    iz, s_row = lax.axis_index("z"), lax.axis_index("s")
    z_lo = s_row // 2
    turn = iz + z_lo + 1
    fwd, inv = (jnp.asarray(t) for t in tables())

    def piece_of(arr, j, axis, size):
        q = (turn + 4 - j) % 4
        return lax.dynamic_slice_in_dim(arr, q * size, size, axis)

    great = g_greater.reshape(el, slots, bi, wide)
    great = [hop(piece_of(great, j, 2, NP), STEPS[j]) for j in range(4)]
    less = g_less.reshape(el, slots, NZ, NP, wide).transpose(3, 2, 1, 0, 4)
    less = lax.all_to_all(less, PLANE, split_axis=0, concat_axis=0, tiled=True)
    less = [hop(piece_of(less, j, 1, 1)[:, 0], STEPS[j]) for j in range(4)]
    great = jnp.stack(great).transpose(3, 0, 2, 1, 4)
    great = lax.all_to_all(great, PLANE, split_axis=0, concat_axis=0, tiled=True)

    c = turn % 4
    rot = jnp.stack([
        jnp.where(c == 0, 1.0, jnp.where(c == 2, -1.0, 0.0)),
        jnp.where(c == 1, 1.0, jnp.where(c == 3, -1.0, 0.0)),
        jnp.where(c % 2 == 0, 1.0, -1.0),
    ]).astype(jnp.float32)

    first = 3
    lo = correlate(rot, [p[:, :first] for p in less], great[:, :, :first], fwd, inv, True)
    hi = correlate(rot, [p[:, first:] for p in less], great[:, :, first:], fwd, inv, False)
    lo = [hop(p, STEPS[j]) for j, p in enumerate(lo)]
    hi = lax.all_to_all(hi, PLANE, split_axis=0, concat_axis=0, tiled=True)
    hi = [hop(hi[:, j], STEPS[j]) for j in range(4)]
    lo = lax.all_to_all(jnp.stack(lo, 1), PLANE, split_axis=0, concat_axis=0, tiled=True)
    lo = lo.transpose(3, 2, 1, 0, 4).reshape(el, first, bi, wide)
    hi = jnp.stack(hi).transpose(3, 2, 0, 1, 4).reshape(el, slots - first, bi, wide)
    own = jnp.concatenate([lo, hi], 1)
    up = lax.ppermute(own, "s", [(0, 1), (1, 2), (2, 3)])
    down = lax.ppermute(own, "s", [(1, 0), (2, 1), (3, 2)])

    filler = jnp.full((1, slots), -1, jnp.int32)
    extended = jnp.concatenate([filler, pattern, filler], 0)
    cols = lax.dynamic_slice_in_dim(extended, s_row, 3, 0)
    same = cols[:, None, :] == cols[1][None, :, None]
    at = jnp.argmax(same, 2).astype(jnp.int32)
    ok = jnp.any(same, 2).astype(jnp.int32)

    near = (s_row + jnp.arange(3) - 1 + 4) % 4 // 2
    order = (iz + near[:, None] + 2 + jnp.arange(4)[None, :]) % 4
    pick = (order[:, :, None] == jnp.arange(4)[None, None, :]).astype(jnp.bfloat16)
    weights = jnp.einsum(
        "djq,adqp->adjp", pick, coulomb.reshape(bi, 3, NZ, NP), preferred_element_type=jnp.float32
    ).astype(jnp.bfloat16).reshape(bi, 3 * bi)
    return screen(at, ok, weights, up, own, down)[:, None]


def solution(mesh):
    fine = Mesh(mesh.devices.reshape(4, 4, 4, 4), ALL)
    energy = ("z", "y", "x")
    return jax.shard_map(
        shards,
        mesh=fine,
        in_specs=(P(energy, "s"), P(energy, "s"), P("s"), P()),
        out_specs=P(energy, "s"),
        check_vma=False,
    )
```

time: 269 us -> 187 us (0.70); the launches traced: 265 us -> 186 us
  matrix products: 109 us -> 0.22 us
  blocking collectives: 63 us -> 0 us
  starting transfers between devices: 32.1 us -> 73.5 us
  waiting for transfers between devices: 41.5 us -> 70.7 us
  Pallas kernels: 0 us -> 20.5 us
    dot_general x8 -> x1, matrix products: 109 us -> 0.22 us  [shards(): jnp.einsum('djq,adqp->adjp', pick, coulomb.reshape(bi, 3, NZ, NP), prefer...]
    all_to_all x1 -> x0, blocking collectives: 63 us -> none  [shards(): lax.all_to_all(polar, 'energy', split_axis=0, concat_axis=3, tiled=True)]
    ppermute x2 -> x18, waiting for transfers between devices: 12 us -> 60.8 us  [the longest x16 50.1 us: hop(): return lax.ppermute(piece, ALL, perm)]
    ppermute x2 -> x18, starting transfers between devices: 6.82 us -> 46.3 us  [the longest x16 32.7 us: hop(): return lax.ppermute(piece, ALL, perm)]
    pallas_call x0 -> x3, Pallas kernels: none -> 20.5 us  [the longest x2 16 us: correlate(): pl.pallas_call(functools.partial(correlate_kernel, slots, split), out_sha...]
    all_to_all x2 -> x4, waiting for transfers between devices: 29.5 us -> 9.84 us  [the longest x1 9.84 us: shards(): lax.all_to_all(great, PLANE, split_axis=0, concat_axis=0, tiled=True)]
    slice x0 -> x10, local copies, waits for them, and re-layouts: none -> 7.59 us  [the longest x4 3.79 us: shards(): p[:, :first]]
    unnamed x17 -> x15, local copies, waits for them, and re-layouts: 5.91 us -> 0.14 us
  transfers between devices with their start and end apart: 4 -> 22, of which waited for: 2 -> 13; matrix products, arithmetic and copies ran while one was open for 16% -> 9% of each run, Pallas kernels for 0% -> 5%
where the time goes in v1:
time: 187 us; the launch traced here: 186 us
  starting transfers between devices  73.5 us (39%)
  waiting for transfers between devices  70.7 us (38%)
  Pallas kernels  20.5 us (11%)
  local copies, waits for them, and re-layouts  17.2 us (9%)
  other arithmetic  3.41 us (2%)
    ppermute x16, waiting for transfers between devices, hop(): return lax.ppermute(piece, ALL, perm)  50.1 us
    ppermute x16, starting transfers between devices, hop(): return lax.ppermute(piece, ALL, perm)  32.7 us
    pallas_call x2, Pallas kernels, correlate(): pl.pallas_call(functools.partial(correlate_kernel, slots, split), out_sha...  16 us
    ppermute x1, starting transfers between devices, shards(): down = lax.ppermute(own, 's', [(1, 0), (2, 1), (3, 2)])  10.4 us
    all_to_all x1, waiting for transfers between devices, shards(): lax.all_to_all(great, PLANE, split_axis=0, concat_axis=0, tiled=True)  9.84 us
    ppermute x1, waiting for transfers between devices, shards(): down = lax.ppermute(own, 's', [(1, 0), (2, 1), (3, 2)])  9.62 us
    all_to_all x1, starting transfers between devices, shards(): less = lax.all_to_all(less, PLANE, split_axis=0, concat_axis=0, tiled=True)  7.72 us
    all_to_all x1, starting transfers between devices, shards(): lax.all_to_all(jnp.stack(lo, 1), PLANE, split_axis=0, concat_axis=0, tile...  6.69 us
  transfers between devices with their start and end apart: 22, of which 13 were waited for; matrix products, arithmetic and copies ran while one was open for 9% of the time, Pallas kernels for 5%

profile of v1, /device:TPU:1, one launch (start us, length us, event | category | flops | bytes accessed | tf_op | source)
XLA Modules:
  0.0 186.0 jit_solution(15955362636416297357)
XLA Ops:
  0.0 3.2 %copy.70 = bf16[16,4,5,16,128]{4,3,2,1,0:T(8,128)(2,1)} copy(bf16[16,4,5,16,128]{4,0,1,2,3:T(8,128)(2,1)} %bitcast.76) | data formatting | bytes 2621440 | tf_op jit(solution)/shard_map/transpose | solution.py:193
  3.2 7.7 %all-to-all-start = ((bf16[16,4,5,16,128]{4,3,2,1,0:T(8,128)(2,1)}), bf16[16,4,5,16,128]{4,3,2,1,0:T(8,128)(2,1)S(1)}, u32[]{:S(2)}, u32[]{:S(2)}) async-start(bf16[16,4,5,16,128]{4,3,2,1,0:T(8,128)(2,1)} %copy.70), calls=%async_computation | async-start | bytes 2621440 | tf_op jit(solution)/shard_map/all_to_all | solution.py:194
  11.1 0.3 constant_dynamic-slice_fusion.3
  11.4 0.1 copy.95
  11.5 5.7 %collective-permute-start.6 = (bf16[16,5,16,128]{3,0,1,2:T(8,128)(2,1)S(1)}, bf16[16,5,16,128]{3,0,1,2:T(8,128)(2,1)S(1)}, u32[]{:S(2)}, u32[]{:S(2)}) collective-permute-start(bf16[16,5,16,128]{3,0,1,2:T(8,128)(2,1)S(1)} %bitcast.81), channel_id=1, source_target_pairs={{0,194},{1,195},{2,0},{3,1},{4,198},{5,199},{6,4},{7,5},{8,202},{9... | collective-permute-start | bytes 983048 | tf_op jit(solution)/shard_map/ppermute | solution.py:45
  17.2 1.7 collective-permute-start.7
  19.0 0.8 collective-permute-start.5
  19.9 1.0 collective-permute-start.4
  20.9 6.0 %collective-permute-done.6 = bf16[16,5,16,128]{3,0,1,2:T(8,128)(2,1)S(1)} collective-permute-done((bf16[16,5,16,128]{3,0,1,2:T(8,128)(2,1)S(1)}, bf16[16,5,16,128]{3,0,1,2:T(8,128)(2,1)S(1)}, u32[]{:S(2)}, u32[]{:S(2)}) %collective-permute-start.6) | collective-permute-done | bytes 327712 | tf_op jit(solution)/shard_map/ppermute | solution.py:45
  27.0 17.3 %collective-permute-done.7 = bf16[16,5,16,128]{3,0,1,2:T(8,128)(2,1)S(1)} collective-permute-done((bf16[16,5,16,128]{3,0,1,2:T(8,128)(2,1)S(1)}, bf16[16,5,16,128]{3,0,1,2:T(8,128)(2,1)S(1)}, u32[]{:S(2)}, u32[]{:S(2)}) %collective-permute-start.7) | collective-permute-done | bytes 327712 | tf_op jit(solution)/shard_map/ppermute | solution.py:45
  44.3 2.6 %collective-permute-done.4 = bf16[16,5,16,128]{3,0,1,2:T(8,128)(2,1)S(1)} collective-permute-done((bf16[16,5,16,128]{3,0,1,2:T(8,128)(2,1)S(1)}, bf16[16,5,16,128]{3,0,1,2:T(8,128)(2,1)S(1)}, u32[]{:S(2)}, u32[]{:S(2)}) %collective-permute-start.4) | collective-permute-done | bytes 327712 | tf_op jit(solution)/shard_map/ppermute | solution.py:45
  46.9 1.2 maximum_bitcast_fusion
  48.1 6.2 %all-to-all-start.1 = ((bf16[16,4,5,16,128]{4,3,2,1,0:T(8,128)(2,1)}), bf16[16,4,5,16,128]{4,3,2,1,0:T(8,128)(2,1)S(1)}, u32[]{:S(2)}, u32[]{:S(2)}) async-start(bf16[16,4,5,16,128]{4,3,2,1,0:T(8,128)(2,1)} %maximum_bitcast_fusion), calls=%async_computation.1 | async-start | bytes 2621440 | tf_op jit(solution)/shard_map/all_to_all | solution.py:197
  54.3 1.2 dynamic-slice_bitcast_fusion
  55.5 2.7 %collective-permute-start.3 = (bf16[16,5,16,128]{3,2,1,0:T(8,128)(2,1)}, bf16[16,5,16,128]{3,2,1,0:T(8,128)(2,1)}, u32[]{:S(2)}, u32[]{:S(2)}) collective-permute-start(bf16[16,5,16,128]{3,2,1,0:T(8,128)(2,1)} %get-tuple-element.19), channel_id=1, source_target_pairs={{0,130},{1,131},{2,192},{3,193},{4,134},{5,135},{6,196},{7,197},{8... | collective-permute-start | bytes 983048 | tf_op jit(solution)/shard_map/ppermute | solution.py:45
  58.2 1.5 collective-permute-start.1
  59.7 1.8 collective-permute-start
  61.5 9.8 %all-to-all-done.1 = bf16[16,4,5,16,128]{4,3,2,1,0:T(8,128)(2,1)S(1)} async-done(((bf16[16,4,5,16,128]{4,3,2,1,0:T(8,128)(2,1)}), bf16[16,4,5,16,128]{4,3,2,1,0:T(8,128)(2,1)S(1)}, u32[]{:S(2)}, u32[]{:S(2)}) %all-to-all-start.1) | async-done | bytes 1310752 | tf_op jit(solution)/shard_map/all_to_all | solution.py:197
  71.4 2.6 %collective-permute-done.3 = bf16[16,5,16,128]{3,2,1,0:T(8,128)(2,1)} collective-permute-done((bf16[16,5,16,128]{3,2,1,0:T(8,128)(2,1)}, bf16[16,5,16,128]{3,2,1,0:T(8,128)(2,1)}, u32[]{:S(2)}, u32[]{:S(2)}) %collective-permute-start.3) | collective-permute-done | bytes 327712 | tf_op jit(solution)/shard_map/ppermute | solution.py:45
  74.0 0.9 slice.68.refs_3_
  74.9 3.6 %collective-permute-done.2 = bf16[16,5,16,128]{3,2,1,0:T(8,128)(2,1)} collective-permute-done((bf16[16,5,16,128]{3,2,1,0:T(8,128)(2,1)}, bf16[16,5,16,128]{3,2,1,0:T(8,128)(2,1)}, u32[]{:S(2)}, u32[]{:S(2)}) %collective-permute-start.2) | collective-permute-done | bytes 327712 | tf_op jit(solution)/shard_map/ppermute | solution.py:45
  78.6 0.9 slice.67.refs_2_
  79.5 0.9 slice.66.refs_1_
  80.4 0.9 slice.65.refs_0_
  81.4 6.7 %correlate.3 = bf16[16,4,2,16,128]{4,3,2,1,0:T(8,128)(2,1)} custom-call(f32[3]{0:T(128)S(1)} %pad_maximum_fusion.2.rot_ref, bf16[16,2,16,128]{3,2,1,0:T(8,128)(2,1)S(1)} %slice.65.refs_0_, bf16[16,2,16,128]{3,2,1,0:T(8,128)(2,1)S(1)} %slice.66.refs_1_, bf16[16,2,16,128]{3,2,1,0:T(8,128)(2,1)S(1)} %slice.67.refs_2_, ...), custom_call_target="tpu_custom_call" | custom-call | flops 1342177280 | bytes 3670016 | tf_op jit(solution)/shard_map/correlate/pallas_call | solution.py:124
  88.1 6.6 %all-to-all-start.3 = ((bf16[16,4,2,16,128]{4,3,2,1,0:T(8,128)(2,1)}), bf16[16,4,2,16,128]{4,3,2,1,0:T(8,128)(2,1)}, u32[]{:S(2)}, u32[]{:S(2)}) async-start(bf16[16,4,2,16,128]{4,3,2,1,0:T(8,128)(2,1)} %correlate.3), calls=%async_computation.3 | async-start | bytes 1048576 | tf_op jit(solution)/shard_map/all_to_all | solution.py:210
  94.7 0.1 slice.64.refs_4_
  94.8 0.9 slice.63.refs_3_
  95.7 0.9 slice.62.refs_2_
  96.7 0.9 slice.61.refs_1_
  97.6 0.9 slice.60.refs_0_
  98.6 9.3 %correlate.2 = (bf16[16,3,16,128]{3,2,1,0:T(8,128)(2,1)S(1)}, bf16[16,3,16,128]{3,2,1,0:T(8,128)(2,1)S(1)}, bf16[16,3,16,128]{3,2,1,0:T(8,128)(2,1)S(1)}, bf16[16,3,16,128]{3,2,1,0:T(8,128)(2,1)S(1)}) custom-call(f32[3]{0:T(128)S(1)} %pad_maximum_fusion.2.rot_ref, bf16[16,3,16,128]{3,2,1,0:T(8,128)(2,1)S(1)} %slice.60.refs_0_, ...), custom_call_target="tpu_custom_call" | custom-call | flops 2013265920 | bytes 4456448 | tf_op jit(solution)/shard_map/correlate/pallas_call | solution.py:124
  107.8 6.0 %collective-permute-start.8 = (bf16[16,3,16,128]{3,2,1,0:T(8,128)(2,1)S(1)}, bf16[16,3,16,128]{3,2,1,0:T(8,128)(2,1)S(1)}, u32[]{:S(2)}, u32[]{:S(2)}) collective-permute-start(bf16[16,3,16,128]{3,2,1,0:T(8,128)(2,1)S(1)} %get-tuple-element.11), channel_id=1, source_target_pairs={{0,66},{1,67},{2,128},{3,129},{4,70},{5,71},{6,132},{7,133},{8,74}... | collective-permute-start | bytes 589832 | tf_op jit(solution)/shard_map/ppermute | solution.py:45
  113.8 0.3 collective-permute-start.9
  114.1 3.1 %collective-permute-start.10 = (bf16[16,3,16,128]{3,2,1,0:T(8,128)(2,1)S(1)}, bf16[16,3,16,128]{3,2,1,0:T(8,128)(2,1)S(1)}, u32[]{:S(2)}, u32[]{:S(2)}) collective-permute-start(bf16[16,3,16,128]{3,2,1,0:T(8,128)(2,1)S(1)} %get-tuple-element.13), channel_id=1, source_target_pairs={{0,194},{1,195},{2,0},{3,1},{4,198},{5,199},{6,4},{7,5},{8,202},{9... | collective-permute-start | bytes 589832 | tf_op jit(solution)/shard_map/ppermute | solution.py:45
  117.2 1.3 collective-permute-start.11
  118.5 11.2 %collective-permute-done.9 = bf16[16,3,16,128]{3,2,1,0:T(8,128)(2,1)S(1)} collective-permute-done((bf16[16,3,16,128]{3,2,1,0:T(8,128)(2,1)S(1)}, bf16[16,3,16,128]{3,2,1,0:T(8,128)(2,1)S(1)}, u32[]{:S(2)}, u32[]{:S(2)}) %collective-permute-start.9) | collective-permute-done | bytes 196640 | tf_op jit(solution)/shard_map/ppermute | solution.py:45
  129.7 0.1 pad_maximum_fusion.1
  129.8 1.0 copy.75
  130.8 6.7 %all-to-all-start.2 = ((bf16[16,4,3,16,128]{4,3,2,1,0:T(8,128)(2,1)}), bf16[16,4,3,16,128]{4,3,2,1,0:T(8,128)(2,1)S(1)}, u32[]{:S(2)}, u32[]{:S(2)}) async-start(bf16[16,4,3,16,128]{4,3,2,1,0:T(8,128)(2,1)} %copy.75), calls=%async_computation.2 | async-start | bytes 1572864 | tf_op jit(solution)/shard_map/all_to_all | solution.py:212
  137.5 1.1 slice_bitcast_fusion.3
  138.7 3.3 %collective-permute-start.12 = (bf16[16,2,16,128]{3,2,1,0:T(8,128)(2,1)S(1)}, bf16[16,2,16,128]{3,2,1,0:T(8,128)(2,1)S(1)}, u32[]{:S(2)}, u32[]{:S(2)}) collective-permute-start(bf16[16,2,16,128]{3,2,1,0:T(8,128)(2,1)S(1)} %get-tuple-element.23), channel_id=1, source_target_pairs={{0,66},{1,67},{2,128},{3,129},{4,70},{5,71},{6,132},{7,133},{8,74}... | collective-permute-start | bytes 393224 | tf_op jit(solution)/shard_map/ppermute | solution.py:45
  142.0 3.4 %collective-permute-start.13 = (bf16[16,2,16,128]{3,2,1,0:T(8,128)(2,1)S(1)}, bf16[16,2,16,128]{3,2,1,0:T(8,128)(2,1)S(1)}, u32[]{:S(2)}, u32[]{:S(2)}) collective-permute-start(bf16[16,2,16,128]{3,2,1,0:T(8,128)(2,1)S(1)} %get-tuple-element.24), channel_id=1, source_target_pairs={{0,2},{1,3},{2,64},{3,65},{4,6},{5,7},{6,68},{7,69},{8,10},{9,11},... | collective-permute-start | bytes 393224 | tf_op jit(solution)/shard_map/ppermute | solution.py:45
  145.4 0.2 collective-permute-start.14
  145.6 0.2 collective-permute-done.12
  145.8 3.6 %collective-permute-done.13 = bf16[16,2,16,128]{3,2,1,0:T(8,128)(2,1)S(1)} collective-permute-done((bf16[16,2,16,128]{3,2,1,0:T(8,128)(2,1)S(1)}, bf16[16,2,16,128]{3,2,1,0:T(8,128)(2,1)S(1)}, u32[]{:S(2)}, u32[]{:S(2)}) %collective-permute-start.13) | collective-permute-done | bytes 131104 | tf_op jit(solution)/shard_map/ppermute | solution.py:45
  149.4 2.3 %collective-permute-done.15 = bf16[16,2,16,128]{3,2,1,0:T(8,128)(2,1)S(1)} collective-permute-done((bf16[16,2,16,128]{3,2,1,0:T(8,128)(2,1)S(1)}, bf16[16,2,16,128]{3,2,1,0:T(8,128)(2,1)S(1)}, u32[]{:S(2)}, u32[]{:S(2)}) %collective-permute-start.15) | collective-permute-done | bytes 131104 | tf_op jit(solution)/shard_map/ppermute | solution.py:45
  151.7 0.6 collective-permute-done.14
  152.3 0.2 copy.80
  152.6 0.5 copy.76
  153.1 0.1 pad_maximum_fusion.own_ref
  153.2 10.4 %collective-permute-start.17 = (bf16[16,5,64,128]{3,2,1,0:T(8,128)(2,1)S(1)}, bf16[16,5,64,128]{3,2,1,0:T(8,128)(2,1)S(1)}, u32[]{:S(2)}, u32[]{:S(2)}) collective-permute-start(bf16[16,5,64,128]{3,2,1,0:T(8,128)(2,1)S(1)} %pad_maximum_fusion.own_ref), channel_id=1, source_target_pairs={{1,0},{2,1},{3,2},{5,4},{6,5},{7,6},{9,8},{10,9},{11,10},{13,12},{... | collective-permute-start | bytes 3932168 | tf_op jit(solution)/shard_map/ppermute | solution.py:217
  163.6 3.2 %collective-permute-start.16 = (bf16[16,5,64,128]{3,2,1,0:T(8,128)(2,1)S(1)}, bf16[16,5,64,128]{3,2,1,0:T(8,128)(2,1)}, u32[]{:S(2)}, u32[]{:S(2)}) collective-permute-start(bf16[16,5,64,128]{3,2,1,0:T(8,128)(2,1)S(1)} %pad_maximum_fusion.own_ref), channel_id=1, source_target_pairs={{0,1},{1,2},{2,3},{4,5},{5,6},{6,7},{8,9},{9,10},{10,11},{12,13},{... | collective-permute-start | bytes 3932168 | tf_op jit(solution)/shard_map/ppermute | solution.py:216
  167.0 0.3 compare_reduce_fusion
  167.2 0.1 copy.66
  167.3 0.6 convert_element_type.10.ok_ref
  167.9 0.9 compare_reduce_fusion.1
  168.8 0.7 copy.81.at_ref
  169.5 0.1 copy.67
  169.7 0.2 fusion
  169.9 0.7 copy.82.w_ref
  170.6 9.6 %collective-permute-done.17.down_ref = bf16[16,5,64,128]{3,2,1,0:T(8,128)(2,1)S(1)} collective-permute-done((bf16[16,5,64,128]{3,2,1,0:T(8,128)(2,1)S(1)}, bf16[16,5,64,128]{3,2,1,0:T(8,128)(2,1)S(1)}, u32[]{:S(2)}, u32[]{:S(2)}) %collective-permute-start.17) | collective-permute-done | bytes 1310752 | tf_op jit(solution)/shard_map/ppermute | solution.py:217
  180.2 1.2 collective-permute-done.16.up_ref
  181.4 4.6 %screen.1 = bf16[16,5,64,128]{3,2,1,0:T(8,128)(2,1)} custom-call(s32[3,5]{1,0:T(4,128)} %copy.81.at_ref, s32[3,5]{1,0:T(4,128)} %convert_element_type.10.ok_ref, bf16[64,192]{1,0:T(8,128)(2,1)} %copy.82.w_ref, bf16[16,5,64,128]{3,2,1,0:T(8,128)(2,1)} %collective-permute-done.16.up_ref, bf16[16,5,64,128]{3,2,1,0:T(8,128)(2,1)} %copy-done.2, ...), custom_call_target="tpu_custom_call" | custom-call | flops 251658240 | bytes 5242880 | tf_op jit(solution)/shard_map/screen/pallas_call | solution.py:167
  (38 shorter events, 0.6 us)
Async XLA Ops:
  3.2 7.8 %copy-start.3 = (bf16[16,1,5,64,128]{4,3,2,1,0:T(8,128)(2,1)S(1)}, bf16[16,1,5,64,128]{4,3,2,1,0:T(8,128)(2,1)}, u32[]{:S(2)}) copy-start(bf16[16,1,5,64,128]{4,3,2,1,0:T(8,128)(2,1)} %param.7) | copy-start | bytes 3932164
  3.2 44.9 %all-to-all-start = ((bf16[16,4,5,16,128]{4,3,2,1,0:T(8,128)(2,1)}), bf16[16,4,5,16,128]{4,3,2,1,0:T(8,128)(2,1)S(1)}, u32[]{:S(2)}, u32[]{:S(2)}) async-start(bf16[16,4,5,16,128]{4,3,2,1,0:T(8,128)(2,1)} %copy.70), calls=%async_computation | async-start | bytes 2621440 | tf_op jit(solution)/shard_map/all_to_all | solution.py:194
  11.5 15.5 %collective-permute-start.6 = (bf16[16,5,16,128]{3,0,1,2:T(8,128)(2,1)S(1)}, bf16[16,5,16,128]{3,0,1,2:T(8,128)(2,1)S(1)}, u32[]{:S(2)}, u32[]{:S(2)}) collective-permute-start(bf16[16,5,16,128]{3,0,1,2:T(8,128)(2,1)S(1)} %bitcast.81), channel_id=1, source_target_pairs={{0,194},{1,195},{2,0},{3,1},{4,198},{5,199},{6,4},{7,5},{8,202},{9... | collective-permute-start | bytes 983048 | tf_op jit(solution)/shard_map/ppermute | solution.py:45
  17.2 27.0 %collective-permute-start.7 = (bf16[16,5,16,128]{3,0,1,2:T(8,128)(2,1)S(1)}, bf16[16,5,16,128]{3,0,1,2:T(8,128)(2,1)S(1)}, u32[]{:S(2)}, u32[]{:S(2)}) collective-permute-start(bf16[16,5,16,128]{3,0,1,2:T(8,128)(2,1)S(1)} %bitcast.82), channel_id=1, source_target_pairs={{0,130},{1,131},{2,192},{3,193},{4,134},{5,135},{6,196},{7,197},{8... | collective-permute-start | bytes 983048 | tf_op jit(solution)/shard_map/ppermute | solution.py:45
  19.0 25.3 %collective-permute-start.5 = (bf16[16,5,16,128]{3,0,1,2:T(8,128)(2,1)S(1)}, bf16[16,5,16,128]{3,0,1,2:T(8,128)(2,1)S(1)}, u32[]{:S(2)}, u32[]{:S(2)}) collective-permute-start(bf16[16,5,16,128]{3,0,1,2:T(8,128)(2,1)S(1)} %bitcast.83), channel_id=1, source_target_pairs={{0,2},{1,3},{2,64},{3,65},{4,6},{5,7},{6,68},{7,69},{8,10},{9,11},... | collective-permute-start | bytes 983048 | tf_op jit(solution)/shard_map/ppermute | solution.py:45
  19.9 26.9 %collective-permute-start.4 = (bf16[16,5,16,128]{3,0,1,2:T(8,128)(2,1)S(1)}, bf16[16,5,16,128]{3,0,1,2:T(8,128)(2,1)S(1)}, u32[]{:S(2)}, u32[]{:S(2)}) collective-permute-start(bf16[16,5,16,128]{3,0,1,2:T(8,128)(2,1)S(1)} %bitcast.84), channel_id=1, source_target_pairs={{0,66},{1,67},{2,128},{3,129},{4,70},{5,71},{6,132},{7,133},{8,74}... | collective-permute-start | bytes 983048 | tf_op jit(solution)/shard_map/ppermute | solution.py:45
  48.1 23.3 %all-to-all-start.1 = ((bf16[16,4,5,16,128]{4,3,2,1,0:T(8,128)(2,1)}), bf16[16,4,5,16,128]{4,3,2,1,0:T(8,128)(2,1)S(1)}, u32[]{:S(2)}, u32[]{:S(2)}) async-start(bf16[16,4,5,16,128]{4,3,2,1,0:T(8,128)(2,1)} %maximum_bitcast_fusion), calls=%async_computation.1 | async-start | bytes 2621440 | tf_op jit(solution)/shard_map/all_to_all | solution.py:197
  55.5 25.9 %copy-start = (bf16[4,512,256]{2,1,0:T(8,128)(2,1)S(1)}, bf16[4,512,256]{2,1,0:T(8,128)(2,1)}, u32[]{:S(2)}) copy-start(bf16[4,512,256]{2,1,0:T(8,128)(2,1)} %constant.135.clone.refs_6_) | copy-start | bytes 3145732
  55.5 25.9 %copy-start.1 = (bf16[4,512,256]{2,1,0:T(8,128)(2,1)S(1)}, bf16[4,512,256]{2,1,0:T(8,128)(2,1)}, u32[]{:S(2)}) copy-start(bf16[4,512,256]{2,1,0:T(8,128)(2,1)} %constant.134.clone.refs_5_) | copy-start | bytes 3145732
  55.5 18.5 %collective-permute-start.3 = (bf16[16,5,16,128]{3,2,1,0:T(8,128)(2,1)}, bf16[16,5,16,128]{3,2,1,0:T(8,128)(2,1)}, u32[]{:S(2)}, u32[]{:S(2)}) collective-permute-start(bf16[16,5,16,128]{3,2,1,0:T(8,128)(2,1)} %get-tuple-element.19), channel_id=1, source_target_pairs={{0,130},{1,131},{2,192},{3,193},{4,134},{5,135},{6,196},{7,197},{8... | collective-permute-start | bytes 983048 | tf_op jit(solution)/shard_map/ppermute | solution.py:45
  58.2 20.4 %collective-permute-start.2 = (bf16[16,5,16,128]{3,2,1,0:T(8,128)(2,1)}, bf16[16,5,16,128]{3,2,1,0:T(8,128)(2,1)}, u32[]{:S(2)}, u32[]{:S(2)}) collective-permute-start(bf16[16,5,16,128]{3,2,1,0:T(8,128)(2,1)} %get-tuple-element.20), channel_id=1, source_target_pairs={{0,194},{1,195},{2,0},{3,1},{4,198},{5,199},{6,4},{7,5},{8,202},{9... | collective-permute-start | bytes 983048 | tf_op jit(solution)/shard_map/ppermute | solution.py:45
  58.2 21.3 %collective-permute-start.1 = (bf16[16,5,16,128]{3,2,1,0:T(8,128)(2,1)}, bf16[16,5,16,128]{3,2,1,0:T(8,128)(2,1)}, u32[]{:S(2)}, u32[]{:S(2)}) collective-permute-start(bf16[16,5,16,128]{3,2,1,0:T(8,128)(2,1)} %get-tuple-element.21), channel_id=1, source_target_pairs={{0,2},{1,3},{2,64},{3,65},{4,6},{5,7},{6,68},{7,69},{8,10},{9,11},... | collective-permute-start | bytes 983048 | tf_op jit(solution)/shard_map/ppermute | solution.py:45
  59.7 20.8 %collective-permute-start = (bf16[16,5,16,128]{3,2,1,0:T(8,128)(2,1)}, bf16[16,5,16,128]{3,2,1,0:T(8,128)(2,1)}, u32[]{:S(2)}, u32[]{:S(2)}) collective-permute-start(bf16[16,5,16,128]{3,2,1,0:T(8,128)(2,1)} %get-tuple-element.22), channel_id=1, source_target_pairs={{0,66},{1,67},{2,128},{3,129},{4,70},{5,71},{6,132},{7,133},{8,74}... | collective-permute-start | bytes 983048 | tf_op jit(solution)/shard_map/ppermute | solution.py:45
  88.1 42.7 %all-to-all-start.3 = ((bf16[16,4,2,16,128]{4,3,2,1,0:T(8,128)(2,1)}), bf16[16,4,2,16,128]{4,3,2,1,0:T(8,128)(2,1)}, u32[]{:S(2)}, u32[]{:S(2)}) async-start(bf16[16,4,2,16,128]{4,3,2,1,0:T(8,128)(2,1)} %correlate.3), calls=%async_computation.3 | async-start | bytes 1048576 | tf_op jit(solution)/shard_map/all_to_all | solution.py:210
  107.8 10.7 %collective-permute-start.8 = (bf16[16,3,16,128]{3,2,1,0:T(8,128)(2,1)S(1)}, bf16[16,3,16,128]{3,2,1,0:T(8,128)(2,1)S(1)}, u32[]{:S(2)}, u32[]{:S(2)}) collective-permute-start(bf16[16,3,16,128]{3,2,1,0:T(8,128)(2,1)S(1)} %get-tuple-element.11), channel_id=1, source_target_pairs={{0,66},{1,67},{2,128},{3,129},{4,70},{5,71},{6,132},{7,133},{8,74}... | collective-permute-start | bytes 589832 | tf_op jit(solution)/shard_map/ppermute | solution.py:45
  113.8 15.9 %collective-permute-start.9 = (bf16[16,3,16,128]{3,2,1,0:T(8,128)(2,1)S(1)}, bf16[16,3,16,128]{3,2,1,0:T(8,128)(2,1)S(1)}, u32[]{:S(2)}, u32[]{:S(2)}) collective-permute-start(bf16[16,3,16,128]{3,2,1,0:T(8,128)(2,1)S(1)} %get-tuple-element.12), channel_id=1, source_target_pairs={{0,2},{1,3},{2,64},{3,65},{4,6},{5,7},{6,68},{7,69},{8,10},{9,11},... | collective-permute-start | bytes 589832 | tf_op jit(solution)/shard_map/ppermute | solution.py:45
  114.1 15.6 %collective-permute-start.10 = (bf16[16,3,16,128]{3,2,1,0:T(8,128)(2,1)S(1)}, bf16[16,3,16,128]{3,2,1,0:T(8,128)(2,1)S(1)}, u32[]{:S(2)}, u32[]{:S(2)}) collective-permute-start(bf16[16,3,16,128]{3,2,1,0:T(8,128)(2,1)S(1)} %get-tuple-element.13), channel_id=1, source_target_pairs={{0,194},{1,195},{2,0},{3,1},{4,198},{5,199},{6,4},{7,5},{8,202},{9... | collective-permute-start | bytes 589832 | tf_op jit(solution)/shard_map/ppermute | solution.py:45
  117.2 12.5 %collective-permute-start.11 = (bf16[16,3,16,128]{3,2,1,0:T(8,128)(2,1)S(1)}, bf16[16,3,16,128]{3,2,1,0:T(8,128)(2,1)S(1)}, u32[]{:S(2)}, u32[]{:S(2)}) collective-permute-start(bf16[16,3,16,128]{3,2,1,0:T(8,128)(2,1)S(1)} %get-tuple-element.14), channel_id=1, source_target_pairs={{0,130},{1,131},{2,192},{3,193},{4,134},{5,135},{6,196},{7,197},{8... | collective-permute-start | bytes 589832 | tf_op jit(solution)/shard_map/ppermute | solution.py:45
  130.8 21.7 %all-to-all-start.2 = ((bf16[16,4,3,16,128]{4,3,2,1,0:T(8,128)(2,1)}), bf16[16,4,3,16,128]{4,3,2,1,0:T(8,128)(2,1)S(1)}, u32[]{:S(2)}, u32[]{:S(2)}) async-start(bf16[16,4,3,16,128]{4,3,2,1,0:T(8,128)(2,1)} %copy.75), calls=%async_computation.2 | async-start | bytes 1572864 | tf_op jit(solution)/shard_map/all_to_all | solution.py:212
  138.7 7.1 %collective-permute-start.12 = (bf16[16,2,16,128]{3,2,1,0:T(8,128)(2,1)S(1)}, bf16[16,2,16,128]{3,2,1,0:T(8,128)(2,1)S(1)}, u32[]{:S(2)}, u32[]{:S(2)}) collective-permute-start(bf16[16,2,16,128]{3,2,1,0:T(8,128)(2,1)S(1)} %get-tuple-element.23), channel_id=1, source_target_pairs={{0,66},{1,67},{2,128},{3,129},{4,70},{5,71},{6,132},{7,133},{8,74}... | collective-permute-start | bytes 393224 | tf_op jit(solution)/shard_map/ppermute | solution.py:45
  142.0 7.4 %collective-permute-start.13 = (bf16[16,2,16,128]{3,2,1,0:T(8,128)(2,1)S(1)}, bf16[16,2,16,128]{3,2,1,0:T(8,128)(2,1)S(1)}, u32[]{:S(2)}, u32[]{:S(2)}) collective-permute-start(bf16[16,2,16,128]{3,2,1,0:T(8,128)(2,1)S(1)} %get-tuple-element.24), channel_id=1, source_target_pairs={{0,2},{1,3},{2,64},{3,65},{4,6},{5,7},{6,68},{7,69},{8,10},{9,11},... | collective-permute-start | bytes 393224 | tf_op jit(solution)/shard_map/ppermute | solution.py:45
  145.4 6.3 %collective-permute-start.15 = (bf16[16,2,16,128]{3,2,1,0:T(8,128)(2,1)S(1)}, bf16[16,2,16,128]{3,2,1,0:T(8,128)(2,1)S(1)}, u32[]{:S(2)}, u32[]{:S(2)}) collective-permute-start(bf16[16,2,16,128]{3,2,1,0:T(8,128)(2,1)S(1)} %get-tuple-element.25), channel_id=1, source_target_pairs={{0,130},{1,131},{2,192},{3,193},{4,134},{5,135},{6,196},{7,197},{8... | collective-permute-start | bytes 393224 | tf_op jit(solution)/shard_map/ppermute | solution.py:45
  145.4 6.9 %collective-permute-start.14 = (bf16[16,2,16,128]{3,2,1,0:T(8,128)(2,1)S(1)}, bf16[16,2,16,128]{3,2,1,0:T(8,128)(2,1)S(1)}, u32[]{:S(2)}, u32[]{:S(2)}) collective-permute-start(bf16[16,2,16,128]{3,2,1,0:T(8,128)(2,1)S(1)} %get-tuple-element.26), channel_id=1, source_target_pairs={{0,194},{1,195},{2,0},{3,1},{4,198},{5,199},{6,4},{7,5},{8,202},{9... | collective-permute-start | bytes 393224 | tf_op jit(solution)/shard_map/ppermute | solution.py:45
  153.1 13.8 %copy-start.6 = (s32[4,5]{1,0:T(4,128)S(1)}, s32[4,5]{1,0:T(4,128)}, u32[]{:S(2)}) copy-start(s32[4,5]{1,0:T(4,128)} %param.9) | copy-start | bytes 244
  153.1 16.4 %copy-start.5 = (bf16[1,64,192]{2,1,0:T(8,128)(2,1)S(1)}, bf16[1,64,192]{2,1,0:T(8,128)(2,1)}, u32[]{:S(2)}) copy-start(bf16[1,64,192]{2,1,0:T(8,128)(2,1)} %param.8) | copy-start | bytes 73732
  153.2 28.2 %copy-start.2 = (bf16[16,5,64,128]{3,2,1,0:T(8,128)(2,1)}, bf16[16,5,64,128]{3,2,1,0:T(8,128)(2,1)S(1)}, u32[]{:S(2)}) copy-start(bf16[16,5,64,128]{3,2,1,0:T(8,128)(2,1)S(1)} %pad_maximum_fusion.own_ref) | copy-start | bytes 3932164
  153.2 27.0 %collective-permute-start.17 = (bf16[16,5,64,128]{3,2,1,0:T(8,128)(2,1)S(1)}, bf16[16,5,64,128]{3,2,1,0:T(8,128)(2,1)S(1)}, u32[]{:S(2)}, u32[]{:S(2)}) collective-permute-start(bf16[16,5,64,128]{3,2,1,0:T(8,128)(2,1)S(1)} %pad_maximum_fusion.own_ref), channel_id=1, source_target_pairs={{1,0},{2,1},{3,2},{5,4},{6,5},{7,6},{9,8},{10,9},{11,10},{13,12},{... | collective-permute-start | bytes 3932168 | tf_op jit(solution)/shard_map/ppermute | solution.py:217
  163.6 17.8 %collective-permute-start.16 = (bf16[16,5,64,128]{3,2,1,0:T(8,128)(2,1)S(1)}, bf16[16,5,64,128]{3,2,1,0:T(8,128)(2,1)}, u32[]{:S(2)}, u32[]{:S(2)}) collective-permute-start(bf16[16,5,64,128]{3,2,1,0:T(8,128)(2,1)S(1)} %pad_maximum_fusion.own_ref), channel_id=1, source_target_pairs={{0,1},{1,2},{2,3},{4,5},{5,6},{6,7},{8,9},{9,10},{10,11},{12,13},{... | collective-permute-start | bytes 3932168 | tf_op jit(solution)/shard_map/ppermute | solution.py:216
  180.2 1.2 copy-start.4

commit v2 on v1

v2 whole, which is shorter than its diff:
```python
import functools
import math

import jax
import jax.numpy as jnp
import ml_dtypes
import numpy as np
from jax import lax
from jax.experimental import pallas as pl
from jax.experimental.pallas import tpu as pltpu
from jax.sharding import Mesh, PartitionSpec as P

NE = 1024
QUART = NE // 4
NZ = 4
NP = 16
NL = 16
ALL = ("z", "y", "x", "s")
PLANE = ("y", "x")
CUT = 3
HEAVY = 100 * 10**9
STEPS = (3, 1, -1, -3)


def tables():
    e = np.arange(QUART)
    out = []
    for first in range(4):
        t = 4 * np.arange(QUART) + first
        angle = 2.0 * math.pi * ((e[:, None] * t[None, :]) % NE) / NE
        scale = 1.0 / math.sqrt(NE)
        real = (np.cos(angle) * scale).astype(np.float32).astype(ml_dtypes.bfloat16)
        imag = (-np.sin(angle) * scale).astype(np.float32).astype(ml_dtypes.bfloat16)
        out.append((real, imag))
    forward = np.stack([np.concatenate([r.T, i.T]) for r, i in out])
    inverse = np.stack([np.concatenate([r, i]) for r, i in out])
    return forward, inverse


def hop(piece, step):
    perm = []
    for z in range(4):
        for yx in range(16):
            for s in range(4):
                to = (2 * z + s // 2 + step) % 8
                perm.append(((z * 16 + yx) * 4 + s, ((to // 2) * 16 + yx) * 4 + (to % 2) * 2 + s % 2))
    return lax.ppermute(piece, ALL, perm)


def times_i(v):
    lane = lax.broadcasted_iota(jnp.int32, v.shape, 1)
    return jnp.where(lane < 64, -1.0, 1.0) * pltpu.roll(v, 64, 1)


def correlate_kernel(slots, pieces, split, rot_ref, *refs):
    in_refs, fwd_ref, inv_ref = refs[:pieces], refs[pieces], refs[pieces + 1]
    n_out = 4 if split else 1
    outs = refs[pieces + 2 : pieces + 2 + n_out]
    xl_ref, xg_ref, p_ref, y_ref, z_ref, f_ref, b_ref, sem = refs[pieces + 2 + n_out :]
    loads = [pltpu.make_async_copy(fwd_ref, f_ref, sem.at[0]), pltpu.make_async_copy(inv_ref, b_ref, sem.at[1])]
    for load in loads:
        load.start()
    f32, bf16 = jnp.float32, jnp.bfloat16
    left = lax.broadcasted_iota(jnp.int32, (32, 128), 1) < 64

    def fetch(j, which, s, p):
        ref = in_refs[j][p : p + 2, which, s] if pieces == 4 else in_refs[0][p : p + 2, j, which, s]
        return ref.reshape(2 * NL, 128).astype(f32)

    for s in range(slots):
        cols = slice(s * 128, (s + 1) * 128)
        for which, x_ref in enumerate((xl_ref, xg_ref)):
            for p in range(0, NP, 2):
                rows = slice(p * NL, (p + 2) * NL)
                x0, x1, x2, x3 = (fetch(j, which, s, p) for j in range(4))
                a, b, c, d = x0 + x2, x0 - x2, x1 + x3, times_i(x1 - x3)
                for t1, v in enumerate((a + c, b - d, a - c, b + d)):
                    hi = v.astype(bf16)
                    x_ref[t1, 0, rows, cols] = hi
                    x_ref[t1, 1, rows, cols] = (v - hi.astype(f32)).astype(bf16)

    for load in loads:
        load.wait()

    @pl.loop(0, 4)
    def _(t1):
        table, back = f_ref[t1], b_ref[t1]
        for s in range(0, slots, 2):
            n = min(2, slots - s)
            cols = slice(s * 128, (s + n) * 128)
            width = slice(0, n * 128)
            for k, x_ref in enumerate((xl_ref, xg_ref)):
                y_ref[k, :, width] = jnp.dot(table, x_ref[t1, 0, :, cols], preferred_element_type=f32) + jnp.dot(
                    table, x_ref[t1, 1, :, cols], preferred_element_type=f32
                )
            for k in range(n):
                own = slice(k * 128, (k + 1) * 128)
                for r in range(0, QUART, 32):
                    one, two = slice(r, r + 32), slice(QUART + r, QUART + r + 32)
                    le = y_ref[0, one, own] + times_i(y_ref[0, two, own])
                    gr = y_ref[1, one, own] + times_i(y_ref[1, two, own])
                    m1, m2 = le * gr, le * pltpu.roll(gr, 64, 1)
                    p_ref[one, own] = (
                        jnp.where(left, m1, m2) + pltpu.roll(jnp.where(left, -m2, m1), 64, 1)
                    ).astype(bf16)
            z_ref[t1, :, cols] = jnp.dot(back, p_ref[:, width], preferred_element_type=f32)

    ca, cb, cc = rot_ref[0], rot_ref[1], rot_ref[2]
    for s in range(slots):
        cols = slice(s * 128, (s + 1) * 128)
        for p in range(0, NP, 2):
            one = slice(p * NL, (p + 2) * NL)
            two = slice(QUART + p * NL, QUART + (p + 2) * NL)
            z0, z1, z2, z3 = (z_ref[t, one, cols] - times_i(z_ref[t, two, cols]) for t in range(4))
            u2 = cc * z2
            a, b = z0 + u2, z0 - u2
            plus, minus = z1 + z3, times_i(z1 - z3)
            c = ca * plus + cb * minus
            d = ca * minus - cb * plus
            for j, v in enumerate((a + c, b - d, a - c, b + d)):
                v = v.astype(bf16).reshape(2, NL, 128)
                if split:
                    outs[j][p : p + 2, s] = v
                else:
                    outs[0][p : p + 2, j, s] = v


def correlate(rot, inputs, fwd, inv, split):
    slots = inputs[0].shape[-3]
    n = slots * 128
    vmem = pl.BlockSpec(memory_space=pltpu.VMEM)
    hbm = pl.BlockSpec(memory_space=pltpu.HBM)
    piece = jax.ShapeDtypeStruct((NP, slots, NL, 128), jnp.bfloat16)
    whole = jax.ShapeDtypeStruct((NP, NZ, slots, NL, 128), jnp.bfloat16)
    out = pl.pallas_call(
        functools.partial(correlate_kernel, slots, len(inputs), split),
        out_shape=[piece] * 4 if split else [whole],
        in_specs=[pl.BlockSpec(memory_space=pltpu.SMEM)] + [vmem] * len(inputs) + [hbm] * 2,
        out_specs=[vmem] * (4 if split else 1),
        scratch_shapes=[
            pltpu.VMEM((4, 2, QUART, n), jnp.bfloat16),
            pltpu.VMEM((4, 2, QUART, n), jnp.bfloat16),
            pltpu.VMEM((QUART, 256), jnp.bfloat16),
            pltpu.VMEM((2, 2 * QUART, 256), jnp.float32),
            pltpu.VMEM((4, 2 * QUART, n), jnp.float32),
            pltpu.VMEM((4, 2 * QUART, QUART), jnp.bfloat16),
            pltpu.VMEM((4, 2 * QUART, QUART), jnp.bfloat16),
            pltpu.SemaphoreType.DMA((2,)),
        ],
        compiler_params=pltpu.CompilerParams(vmem_limit_bytes=40 << 20),
        cost_estimate=pl.CostEstimate(
            flops=HEAVY, bytes_accessed=3 * NE * n * 2 + (2 << 20), transcendentals=0
        ),
        name="correlate",
    )(rot, *inputs, fwd, inv)
    return out if split else out[0]


def turning():
    row = lax.broadcasted_iota(jnp.int32, (256, 256), 0)
    col = lax.broadcasted_iota(jnp.int32, (256, 256), 1)
    return jnp.where((row % 16) * 16 + row // 16 == col, 1.0, 0.0).astype(jnp.bfloat16)


def prepare_kernel(cut, turn_ref, less_ref, great_ref, *refs):
    early_ref, late_refs, turn, held, sem = refs[0], refs[1:5], refs[5], refs[6], refs[7]
    slots = less_ref.shape[1]
    loads = [
        [pltpu.make_async_copy(ref.at[:, s], held.at[s, k], sem.at[s, k]) for k, ref in enumerate((less_ref, great_ref))]
        for s in range(slots)
    ]
    order = [*range(cut, slots), *range(cut)]
    for s in order:
        for load in loads[s]:
            load.start()
    turn[...] = turning()
    for s in order:
        for load in loads[s]:
            load.wait()
        for j in range(4):
            q = lax.rem(turn_ref[0] + 4 - j, 4)
            at = pl.ds(pl.multiple_of(q * NP, NP), NP)
            x = jnp.concatenate([held[s, k, :, at, :].reshape(256, 128) for k in range(2)], 1)
            x = jnp.dot(turn[...], x, preferred_element_type=jnp.float32).astype(jnp.bfloat16)
            for k in range(2):
                v = x[:, k * 128 : (k + 1) * 128].reshape(NP, NL, 128)
                if s < cut:
                    early_ref[:, j, k, s] = v
                else:
                    late_refs[j][:, k, s - cut] = v


def prepare(turn, less, great, cut):
    el, slots, bi, wide = less.shape
    vmem = pl.BlockSpec(memory_space=pltpu.VMEM)
    hbm = pl.BlockSpec(memory_space=pltpu.HBM)
    piece = jax.ShapeDtypeStruct((NP, 2, slots - cut, el, wide), jnp.bfloat16)
    early, *late = pl.pallas_call(
        functools.partial(prepare_kernel, cut),
        out_shape=[jax.ShapeDtypeStruct((NP, NZ, 2, cut, el, wide), jnp.bfloat16)] + [piece] * 4,
        in_specs=[pl.BlockSpec(memory_space=pltpu.SMEM), hbm, hbm],
        out_specs=[vmem] * 5,
        scratch_shapes=[
            pltpu.VMEM((256, 256), jnp.bfloat16),
            pltpu.VMEM((slots, 2, el, bi, wide), jnp.bfloat16),
            pltpu.SemaphoreType.DMA((slots, 2)),
        ],
        compiler_params=pltpu.CompilerParams(vmem_limit_bytes=20 << 20),
        cost_estimate=pl.CostEstimate(flops=0, bytes_accessed=4 * el * slots * bi * wide * 2, transcendentals=0),
        name="prepare",
    )(turn, less, great)
    return early, late


def settle_kernel(slots, *refs):
    in_refs, out_ref, turn = refs[:-2], refs[-2], refs[-1]
    turn[...] = turning()
    for j in range(4):
        for s in range(slots):
            x = (in_refs[j][:, s] if len(in_refs) == 4 else in_refs[0][:, j, s]).reshape(256, 128)
            x = jnp.dot(turn[...], x, preferred_element_type=jnp.float32).astype(jnp.bfloat16)
            out_ref[:, s, j * NP : (j + 1) * NP] = x.reshape(NL, NP, 128)


def settle(inputs, flops):
    slots = inputs[0].shape[-3]
    vmem = pl.BlockSpec(memory_space=pltpu.VMEM)
    return pl.pallas_call(
        functools.partial(settle_kernel, slots),
        out_shape=jax.ShapeDtypeStruct((NL, slots, 64, 128), jnp.bfloat16),
        in_specs=[vmem] * len(inputs),
        out_specs=vmem,
        scratch_shapes=[pltpu.VMEM((256, 256), jnp.bfloat16)],
        cost_estimate=pl.CostEstimate(flops=flops, bytes_accessed=NL * slots * 64 * 128 * 4, transcendentals=0),
        name="settle",
    )(*inputs)


def gather_kernel(*refs):
    sem = refs[5]
    copies = [pltpu.make_async_copy(refs[j], refs[4].at[:, j], sem.at[j]) for j in range(4)]
    for copy in copies:
        copy.start()
    for copy in copies:
        copy.wait()


def gather(pieces, flops):
    shape = pieces[0].shape
    hbm = pl.BlockSpec(memory_space=pltpu.HBM)
    return pl.pallas_call(
        gather_kernel,
        out_shape=jax.ShapeDtypeStruct((shape[0], 4, *shape[1:]), jnp.bfloat16),
        in_specs=[hbm] * 4,
        out_specs=hbm,
        scratch_shapes=[pltpu.SemaphoreType.DMA((4,))],
        cost_estimate=pl.CostEstimate(flops=flops, bytes_accessed=8 * pieces[0].size * 2, transcendentals=0),
        name="gather",
    )(*pieces)


def screen_kernel(row_ref, pattern_ref, w_ref, up_ref, own_ref, down_ref, out_ref):
    slots = own_ref.shape[1]
    rows = pattern_ref.shape[0]
    row = row_ref[0]
    found = {}
    for d, step in ((0, -1), (2, 1)):
        k = row + step
        inside = jnp.logical_and(k >= 0, k < rows)
        k = jnp.clip(k, 0, rows - 1)
        for s in range(slots):
            want = pattern_ref[row, s]
            at, hit = jnp.int32(0), jnp.int32(0)
            for t in range(slots):
                same = jnp.logical_and(inside, pattern_ref[k, t] == want)
                at = jnp.where(same, t, at)
                hit = jnp.where(same, 1, hit)
            found[d, s] = at, hit
    w = w_ref[...]
    for l in range(own_ref.shape[0]):
        cols = []
        for s in range(slots):
            blocks = []
            for d, ref in enumerate((up_ref, own_ref, down_ref)):
                if d == 1:
                    blocks.append(ref[l, s])
                else:
                    at, hit = found[d, s]
                    got = ref[l, at]
                    blocks.append(jnp.where(hit > 0, got, jnp.zeros_like(got)))
            cols.append(jnp.concatenate(blocks, 0))
        res = jnp.dot(w, jnp.concatenate(cols, 1), preferred_element_type=jnp.float32)
        for s in range(slots):
            out_ref[l, s] = res[:, s * 128 : (s + 1) * 128].astype(jnp.bfloat16)


def screen(row, pattern, weights, up, own, down):
    el, slots, bi, wide = own.shape
    step = 4
    block = pl.BlockSpec((step, slots, bi, wide), lambda i: (i, 0, 0, 0))
    smem = pl.BlockSpec(memory_space=pltpu.SMEM)
    return pl.pallas_call(
        screen_kernel,
        grid=(el // step,),
        out_shape=jax.ShapeDtypeStruct(own.shape, jnp.bfloat16),
        in_specs=[smem, smem, pl.BlockSpec(weights.shape, lambda i: (0, 0)), block, block, block],
        out_specs=block,
        cost_estimate=pl.CostEstimate(
            flops=2 * el * slots * bi * 3 * bi * wide, bytes_accessed=4 * own.size * 2, transcendentals=0
        ),
        name="screen",
    )(row, pattern, weights, up, own, down)


def shards(g_less, g_greater, coulomb, pattern):
    el, rows, slots, bi, wide = g_less.shape
    iz, s_row = lax.axis_index("z"), lax.axis_index("s")
    z_lo = s_row // 2
    turn = iz + z_lo + 1
    fwd, inv = (jnp.asarray(t) for t in tables())

    def piece_of(arr, j, axis, size):
        q = (turn + 4 - j) % 4
        return lax.dynamic_slice_in_dim(arr, q * size, size, axis)

    c = turn % 4
    rot = jnp.stack([
        jnp.where(c == 0, 1.0, jnp.where(c == 2, -1.0, 0.0)),
        jnp.where(c == 1, 1.0, jnp.where(c == 3, -1.0, 0.0)),
        jnp.where(c % 2 == 0, 1.0, -1.0),
    ]).astype(jnp.float32)
    near = (s_row + jnp.arange(3) - 1 + 4) % 4 // 2
    order = (iz + near[:, None] + 2 + jnp.arange(4)[None, :]) % 4
    pick = (order[:, :, None] == jnp.arange(4)[None, None, :]).astype(jnp.bfloat16)
    weights = jnp.einsum(
        "djq,adqp->adjp", pick, coulomb.reshape(bi, 3, NZ, NP), preferred_element_type=jnp.float32
    ).astype(jnp.bfloat16).reshape(bi, 3 * bi)

    cut = CUT
    both = (g_less.reshape(el, slots, bi, wide), g_greater.reshape(el, slots, bi, wide))
    early, late = prepare((turn % 4).reshape(1), *both, cut)
    late = gather([hop(late[j], STEPS[j]) for j in range(4)], HEAVY)
    early = lax.all_to_all(early, PLANE, split_axis=0, concat_axis=0, tiled=True)
    early = lax.optimization_barrier([early, late])[0]
    early = [hop(early[:, j], STEPS[j]) for j in range(4)]
    late = lax.all_to_all(late, PLANE, split_axis=0, concat_axis=0, tiled=True)

    lo = correlate(rot, early, fwd, inv, True)
    late = lax.optimization_barrier([late] + list(lo))[0]
    hi = correlate(rot, [late], fwd, inv, False)

    lo = gather([hop(p, STEPS[j]) for j, p in enumerate(lo)], HEAVY)
    hi = lax.all_to_all(hi, PLANE, split_axis=0, concat_axis=0, tiled=True)
    hi = lax.optimization_barrier([hi, lo])[0]
    hi = settle([hop(hi[:, j], STEPS[j]) for j in range(4)], HEAVY)
    lo = lax.all_to_all(lo, PLANE, split_axis=0, concat_axis=0, tiled=True)
    lo = settle([lax.optimization_barrier([lo, hi])[0]], 0)
    own = jnp.concatenate([lo, hi], 1)
    up = lax.ppermute(own, "s", [(0, 1), (1, 2), (2, 3)])
    down = lax.ppermute(own, "s", [(1, 0), (2, 1), (3, 2)])
    return screen(s_row.reshape(1), pattern, weights, up, own, down)[:, None]


def solution(mesh):
    fine = Mesh(mesh.devices.reshape(4, 4, 4, 4), ALL)
    energy = ("z", "y", "x")
    return jax.shard_map(
        shards,
        mesh=fine,
        in_specs=(P(energy, "s"), P(energy, "s"), P("s"), P()),
        out_specs=P(energy, "s"),
        check_vma=False,
    )
```

time: 187 us -> 232 us (1.24)
  Pallas kernels: 20.5 us -> 88.1 us
  waiting for transfers between devices: 70.7 us -> 58.6 us
  starting transfers between devices: 73.5 us -> 69.4 us
  local copies, waits for them, and re-layouts: 17.2 us -> 13.3 us
    pallas_call x2 -> x7, Pallas kernels: 16 us -> 83.3 us  [the longest x2 57.9 us: gather(): pl.pallas_call(gather_kernel, out_shape=jax.ShapeDtypeStruct((shape[0], 4...]
    unnamed x15 -> x45, local copies, waits for them, and re-layouts: 0.14 us -> 11.4 us
    ppermute x16, waiting for transfers between devices: 50.1 us -> 39.6 us  [hop(): return lax.ppermute(piece, ALL, perm)]
    slice x10 -> x0, local copies, waits for them, and re-layouts: 7.59 us -> none  [the longest x4 3.79 us: shards(): p[:, :first]]
    ppermute x16, starting transfers between devices: 32.7 us -> 27.9 us  [hop(): return lax.ppermute(piece, ALL, perm)]
    all_to_all x3, waiting for transfers between devices: 9.84 us -> 5.65 us  [the longest x1 5.65 us: shards(): lo = lax.all_to_all(lo, PLANE, split_axis=0, concat_axis=0, tiled=True)]
    transpose x3 -> x0, local copies, waits for them, and re-layouts: 3.94 us -> none  [the longest x1 3.22 us: shards(): less = g_less.reshape(el, slots, NZ, NP, wide).transpose(3, 2, 1, 0, 4)]
    ppermute x1, waiting for transfers between devices: 9.62 us -> 12.2 us  [shards(): down = lax.ppermute(own, 's', [(1, 0), (2, 1), (3, 2)])]
  transfers between devices with their start and end apart: 22 -> 22, of which waited for: 13 -> 8; matrix products, arithmetic and copies ran while one was open for 9% -> 1% of each run, Pallas kernels for 5% -> 34%
where the time goes in v2:
time: 232 us; the launch traced here: 231 us
  Pallas kernels  88.1 us (38%)
  starting transfers between devices  69.4 us (30%)
  waiting for transfers between devices  58.6 us (25%)
  local copies, waits for them, and re-layouts  13.3 us (6%)
    pallas_call x2, Pallas kernels, gather(): pl.pallas_call(gather_kernel, out_shape=jax.ShapeDtypeStruct((shape[0], 4...  57.9 us
    ppermute x16, waiting for transfers between devices, hop(): return lax.ppermute(piece, ALL, perm)  39.6 us
    ppermute x16, starting transfers between devices, hop(): return lax.ppermute(piece, ALL, perm)  27.9 us
    pallas_call x2, Pallas kernels, correlate(): pl.pallas_call(functools.partial(correlate_kernel, slots, len(inputs), sp...  17.5 us
    ppermute x1, waiting for transfers between devices, shards(): down = lax.ppermute(own, 's', [(1, 0), (2, 1), (3, 2)])  12.2 us
    unnamed x45, local copies, waits for them, and re-layouts  11.4 us
    ppermute x1, starting transfers between devices, shards(): down = lax.ppermute(own, 's', [(1, 0), (2, 1), (3, 2)])  11 us
    all_to_all x1, starting transfers between devices, shards(): late = lax.all_to_all(late, PLANE, split_axis=0, concat_axis=0, tiled=True)  6.76 us
  transfers between devices with their start and end apart: 22, of which 8 were waited for; matrix products, arithmetic and copies ran while one was open for 1% of the time, Pallas kernels for 34%

profile of v2, /device:TPU:1, one launch (start us, length us, event | category | flops | bytes accessed | tf_op | source)
XLA Modules:
  0.0 231.3 jit_solution(4075728919316100830)
XLA Ops:
  0.0 1.3 copy-done
  1.3 1.3 copy-done.1
  2.6 3.0 %prepare.1 = (bf16[16,4,2,3,16,128]{5,4,3,2,1,0:T(8,128)(2,1)}, bf16[16,2,2,16,128]{4,3,2,1,0:T(8,128)(2,1)S(1)}, bf16[16,2,2,16,128]{4,3,2,1,0:T(8,128)(2,1)S(1...) custom-call(s32[1]{0:T(128)} %bitcast.9.turn_ref, bf16[16,5,64,128]{3,2,1,0:T(8,128)(2,1)S(1)} %bitcast.35, ...), custom_call_target="tpu_custom_call" | custom-call | bytes 5242880 | tf_op jit(solution)/shard_map/prepare/pallas_call | solution.py:198
  5.7 5.2 %collective-permute-start = (bf16[16,2,2,16,128]{4,3,2,1,0:T(8,128)(2,1)S(1)}, bf16[16,2,2,16,128]{4,3,2,1,0:T(8,128)(2,1)S(1)}, u32[]{:S(2)}, u32[]{:S(2)}) collective-permute-start(bf16[16,2,2,16,128]{4,3,2,1,0:T(8,128)(2,1)S(1)} %get-tuple-element.19), channel_id=1, source_target_pairs={{0,66},{1,67},{2,128},{3,129},{4,70},{5,71},{6,132},{7,133},{8,74}... | collective-permute-start | bytes 786440 | tf_op jit(solution)/shard_map/ppermute | solution.py:47
  10.9 2.9 %collective-permute-start.1 = (bf16[16,2,2,16,128]{4,3,2,1,0:T(8,128)(2,1)S(1)}, bf16[16,2,2,16,128]{4,3,2,1,0:T(8,128)(2,1)S(1)}, u32[]{:S(2)}, u32[]{:S(2)}) collective-permute-start(bf16[16,2,2,16,128]{4,3,2,1,0:T(8,128)(2,1)S(1)} %get-tuple-element.20), channel_id=1, source_target_pairs={{0,2},{1,3},{2,64},{3,65},{4,6},{5,7},{6,68},{7,69},{8,10},{9,11},... | collective-permute-start | bytes 786440 | tf_op jit(solution)/shard_map/ppermute | solution.py:47
  13.8 0.0 collective-permute-start.2
  13.8 1.6 collective-permute-start.3
  15.4 6.8 %all-to-all-start = ((bf16[16,4,2,3,16,128]{5,4,3,2,1,0:T(8,128)(2,1)}), bf16[16,4,2,3,16,128]{5,4,3,2,1,0:T(8,128)(2,1)S(1)}, u32[]{:S(2)}, u32[]{:S(2)}) async-start(bf16[16,4,2,3,16,128]{5,4,3,2,1,0:T(8,128)(2,1)} %get-tuple-element.18), calls=%async_computation | async-start | bytes 3145728 | tf_op jit(solution)/shard_map/all_to_all | solution.py:343
  22.2 4.8 %collective-permute-done.refs_0_ = bf16[16,2,2,16,128]{4,3,2,1,0:T(8,128)(2,1)S(1)} collective-permute-done((bf16[16,2,2,16,128]{4,3,2,1,0:T(8,128)(2,1)S(1)}, bf16[16,2,2,16,128]{4,3,2,1,0:T(8,128)(2,1)S(1)}, u32[]{:S(2)}, u32[]{:S(2)}) %collective-permute-start) | collective-permute-done | bytes 262176 | tf_op jit(solution)/shard_map/ppermute | solution.py:47
  27.0 8.6 %collective-permute-done.1.refs_1_ = bf16[16,2,2,16,128]{4,3,2,1,0:T(8,128)(2,1)S(1)} collective-permute-done((bf16[16,2,2,16,128]{4,3,2,1,0:T(8,128)(2,1)S(1)}, bf16[16,2,2,16,128]{4,3,2,1,0:T(8,128)(2,1)S(1)}, u32[]{:S(2)}, u32[]{:S(2)}) %collective-permute-start.1) | collective-permute-done | bytes 262176 | tf_op jit(solution)/shard_map/ppermute | solution.py:47
  35.6 0.0 collective-permute-done.2.refs_2_
  35.6 0.7 copy-done.12
  36.3 0.1 copy-done.13
  36.4 32.9 %gather.2 = bf16[16,4,2,2,16,128]{5,4,3,2,1,0:T(8,128)(2,1)} custom-call(bf16[16,2,2,16,128]{4,3,2,1,0:T(8,128)(2,1)} %copy-done.11, bf16[16,2,2,16,128]{4,3,2,1,0:T(8,128)(2,1)} %copy-done.12, bf16[16,2,2,16,128]{4,3,2,1,0:T(8,128)(2,1)} %copy-done.13, bf16[16,2,2,16,128]{4,3,2,1,0:T(8,128)(2,1)} %collective-permute-done.3.refs_3_), custom_call_target="tpu_custom_call" | custom-call | flops 99999997952 | bytes 2097152 | tf_op jit(solution)/shard_map/gather/pallas_call | solution.py:251
  69.3 0.0 all-to-all-done
  69.3 1.1 slice_bitcast_fusion
  70.4 2.6 %collective-permute-start.7 = (bf16[16,2,3,16,128]{4,3,2,1,0:T(8,128)(2,1)}, bf16[16,2,3,16,128]{4,3,2,1,0:T(8,128)(2,1)S(1)}, u32[]{:S(2)}, u32[]{:S(2)}) collective-permute-start(bf16[16,2,3,16,128]{4,3,2,1,0:T(8,128)(2,1)} %get-tuple-element.31), channel_id=1, source_target_pairs={{0,130},{1,131},{2,192},{3,193},{4,134},{5,135},{6,196},{7,197},{8... | collective-permute-start | bytes 1179656 | tf_op jit(solution)/shard_map/ppermute | solution.py:47
  73.0 2.3 %collective-permute-start.6 = (bf16[16,2,3,16,128]{4,3,2,1,0:T(8,128)(2,1)}, bf16[16,2,3,16,128]{4,3,2,1,0:T(8,128)(2,1)S(1)}, u32[]{:S(2)}, u32[]{:S(2)}) collective-permute-start(bf16[16,2,3,16,128]{4,3,2,1,0:T(8,128)(2,1)} %get-tuple-element.32), channel_id=1, source_target_pairs={{0,194},{1,195},{2,0},{3,1},{4,198},{5,199},{6,4},{7,5},{8,202},{9... | collective-permute-start | bytes 1179656 | tf_op jit(solution)/shard_map/ppermute | solution.py:47
  75.4 0.0 collective-permute-start.5
  75.4 1.0 collective-permute-start.4
  76.4 0.1 pad_maximum_fusion.1.rot_ref
  76.5 6.8 %all-to-all-start.2 = ((bf16[16,4,2,2,16,128]{5,4,3,2,1,0:T(8,128)(2,1)}), bf16[16,4,2,2,16,128]{5,4,3,2,1,0:T(8,128)(2,1)S(1)}, u32[]{:S(2)}, u32[]{:S(2)}) async-start(bf16[16,4,2,2,16,128]{5,4,3,2,1,0:T(8,128)(2,1)} %gather.2), calls=%async_computation.2 | async-start | bytes 2097152 | tf_op jit(solution)/shard_map/all_to_all | solution.py:346
  83.2 11.8 %collective-permute-done.7.refs_3_ = bf16[16,2,3,16,128]{4,3,2,1,0:T(8,128)(2,1)S(1)} collective-permute-done((bf16[16,2,3,16,128]{4,3,2,1,0:T(8,128)(2,1)}, bf16[16,2,3,16,128]{4,3,2,1,0:T(8,128)(2,1)S(1)}, u32[]{:S(2)}, u32[]{:S(2)}) %collective-permute-start.7) | collective-permute-done | bytes 393248 | tf_op jit(solution)/shard_map/ppermute | solution.py:47
  95.0 12.6 %collective-permute-done.6.refs_2_ = bf16[16,2,3,16,128]{4,3,2,1,0:T(8,128)(2,1)S(1)} collective-permute-done((bf16[16,2,3,16,128]{4,3,2,1,0:T(8,128)(2,1)}, bf16[16,2,3,16,128]{4,3,2,1,0:T(8,128)(2,1)S(1)}, u32[]{:S(2)}, u32[]{:S(2)}) %collective-permute-start.6) | collective-permute-done | bytes 393248 | tf_op jit(solution)/shard_map/ppermute | solution.py:47
  107.6 0.0 collective-permute-done.5.refs_1_
  107.6 1.2 copy-done.2
  108.9 1.2 copy-done.4
  110.1 10.4 %correlate.2 = (bf16[16,3,16,128]{3,2,1,0:T(8,128)(2,1)S(1)}, bf16[16,3,16,128]{3,2,1,0:T(8,128)(2,1)S(1)}, bf16[16,3,16,128]{3,2,1,0:T(8,128)(2,1)S(1)}, bf16[16,3,16,128]{3,2,1,0:T(8,128)(2,1)S(1)}) custom-call(f32[3]{0:T(128)S(1)} %pad_maximum_fusion.1.rot_ref, bf16[16,2,3,16,128]{4,3,2,1,0:T(8,128)(2,1)S(1)} %collective-permute-done.4.refs_0_, ...), custom_call_target="tpu_custom_call" | custom-call | flops 99999997952 | bytes 4456448 | tf_op jit(solution)/shard_map/correlate/pallas_call | solution.py:135
  120.5 1.8 collective-permute-start.8
  122.3 0.5 collective-permute-start.9
  122.8 2.2 collective-permute-start.10
  125.0 1.7 collective-permute-start.11
  126.7 1.2 copy-done.3
  127.9 1.2 copy-done.5
  129.1 7.1 %correlate.3 = bf16[16,4,2,16,128]{4,3,2,1,0:T(8,128)(2,1)} custom-call(f32[3]{0:T(128)S(1)} %pad_maximum_fusion.1.rot_ref, bf16[16,4,2,2,16,128]{5,4,3,2,1,0:T(8,128)(2,1)S(1)} %all-to-all-done.2.refs_0_, bf16[4,512,256]{2,1,0:T(8,128)(2,1)S(1)} %copy-done.5, bf16[4,512,256]{2,1,0:T(8,128)(2,1)S(1)} %copy-done.3), custom_call_target="tpu_custom_call" | custom-call | flops 99999997952 | bytes 3670016 | tf_op jit(solution)/shard_map/correlate/pallas_call | solution.py:135
  136.3 6.7 %all-to-all-start.3 = ((bf16[16,4,2,16,128]{4,3,2,1,0:T(8,128)(2,1)}), bf16[16,4,2,16,128]{4,3,2,1,0:T(8,128)(2,1)S(1)}, u32[]{:S(2)}, u32[]{:S(2)}) async-start(bf16[16,4,2,16,128]{4,3,2,1,0:T(8,128)(2,1)} %correlate.3), calls=%async_computation.3 | async-start | bytes 1048576 | tf_op jit(solution)/shard_map/all_to_all | solution.py:353
  143.0 0.0 collective-permute-done.8.refs_0_
  143.1 0.0 collective-permute-done.9.refs_1_
  143.1 0.0 collective-permute-done.11.refs_3_
  143.1 0.6 copy-done.14
  143.7 0.1 copy-done.15
  143.8 0.1 copy-done.16
  143.9 0.7 copy-done.17
  144.6 25.0 %gather.3 = bf16[16,4,3,16,128]{4,3,2,1,0:T(8,128)(2,1)} custom-call(bf16[16,3,16,128]{3,2,1,0:T(8,128)(2,1)} %copy-done.14, bf16[16,3,16,128]{3,2,1,0:T(8,128)(2,1)} %copy-done.15, bf16[16,3,16,128]{3,2,1,0:T(8,128)(2,1)} %copy-done.16, bf16[16,3,16,128]{3,2,1,0:T(8,128)(2,1)} %copy-done.17), custom_call_target="tpu_custom_call" | custom-call | flops 99999997952 | bytes 1572864 | tf_op jit(solution)/shard_map/gather/pallas_call | solution.py:251
  169.6 3.7 %collective-permute-start.15 = (bf16[16,2,16,128]{3,2,1,0:T(8,128)(2,1)S(1)}, bf16[16,2,16,128]{3,2,1,0:T(8,128)(2,1)S(1)}, u32[]{:S(2)}, u32[]{:S(2)}) collective-permute-start(bf16[16,2,16,128]{3,2,1,0:T(8,128)(2,1)S(1)} %get-tuple-element.35), channel_id=1, source_target_pairs={{0,130},{1,131},{2,192},{3,193},{4,134},{5,135},{6,196},{7,197},{8... | collective-permute-start | bytes 393224 | tf_op jit(solution)/shard_map/ppermute | solution.py:47
  173.3 1.5 collective-permute-start.13
  174.7 0.9 collective-permute-start.12
  175.6 6.7 %all-to-all-start.1 = ((bf16[16,4,3,16,128]{4,3,2,1,0:T(8,128)(2,1)}), bf16[16,4,3,16,128]{4,3,2,1,0:T(8,128)(2,1)S(1)}, u32[]{:S(2)}, u32[]{:S(2)}) async-start(bf16[16,4,3,16,128]{4,3,2,1,0:T(8,128)(2,1)} %gather.3), calls=%async_computation.1 | async-start | bytes 1572864 | tf_op jit(solution)/shard_map/all_to_all | solution.py:356
  182.3 1.8 collective-permute-done.12.refs_0_
  184.1 0.6 copy-done.21
  184.8 2.3 settle.2
  187.1 5.6 %all-to-all-done.1.refs_0_ = bf16[16,4,3,16,128]{4,3,2,1,0:T(8,128)(2,1)S(1)} async-done(((bf16[16,4,3,16,128]{4,3,2,1,0:T(8,128)(2,1)}), bf16[16,4,3,16,128]{4,3,2,1,0:T(8,128)(2,1)S(1)}, u32[]{:S(2)}, u32[]{:S(2)}) %all-to-all-start.1) | async-done | bytes 786464 | tf_op jit(solution)/shard_map/all_to_all | solution.py:356
  192.7 0.9 copy-done.7
  193.6 2.6 %settle.3 = bf16[16,3,64,128]{3,2,1,0:T(8,128)(2,1)} custom-call(bf16[16,4,3,16,128]{4,3,2,1,0:T(8,128)(2,1)} %copy-done.7), custom_call_target="tpu_custom_call" | custom-call | bytes 1572864 | tf_op jit(solution)/shard_map/settle/pallas_call | solution.py:228
  196.2 1.3 pad_maximum_fusion.own_ref
  197.4 11.0 %collective-permute-start.17 = (bf16[16,5,64,128]{3,2,1,0:T(8,128)(2,1)S(1)}, bf16[16,5,64,128]{3,2,1,0:T(8,128)(2,1)S(1)}, u32[]{:S(2)}, u32[]{:S(2)}) collective-permute-start(bf16[16,5,64,128]{3,2,1,0:T(8,128)(2,1)S(1)} %pad_maximum_fusion.own_ref), channel_id=1, source_target_pairs={{1,0},{2,1},{3,2},{5,4},{6,5},{7,6},{9,8},{10,9},{11,10},{13,12},{... | collective-permute-start | bytes 3932168 | tf_op jit(solution)/shard_map/ppermute | solution.py:360
  208.5 3.6 %collective-permute-start.16 = (bf16[16,5,64,128]{3,2,1,0:T(8,128)(2,1)S(1)}, bf16[16,5,64,128]{3,2,1,0:T(8,128)(2,1)}, u32[]{:S(2)}, u32[]{:S(2)}) collective-permute-start(bf16[16,5,64,128]{3,2,1,0:T(8,128)(2,1)S(1)} %pad_maximum_fusion.own_ref), channel_id=1, source_target_pairs={{0,1},{1,2},{2,3},{4,5},{5,6},{6,7},{8,9},{9,10},{10,11},{12,13},{... | collective-permute-start | bytes 3932168 | tf_op jit(solution)/shard_map/ppermute | solution.py:359
  212.0 0.1 copy.19
  212.2 0.1 add_select_fusion
  212.2 0.2 fusion
  212.5 0.7 copy.30.w_ref
  213.2 12.2 %collective-permute-done.17.down_ref = bf16[16,5,64,128]{3,2,1,0:T(8,128)(2,1)S(1)} collective-permute-done((bf16[16,5,64,128]{3,2,1,0:T(8,128)(2,1)S(1)}, bf16[16,5,64,128]{3,2,1,0:T(8,128)(2,1)S(1)}, u32[]{:S(2)}, u32[]{:S(2)}) %collective-permute-start.17) | collective-permute-done | bytes 1310752 | tf_op jit(solution)/shard_map/ppermute | solution.py:360
  225.4 1.2 collective-permute-done.16.up_ref
  226.6 4.7 %screen.1 = bf16[16,5,64,128]{3,2,1,0:T(8,128)(2,1)} custom-call(s32[1]{0:T(128)} %bitcast.row_ref, s32[4,5]{1,0:T(4,128)} %pattern_ref.1, bf16[64,192]{1,0:T(8,128)(2,1)} %copy.30.w_ref, bf16[16,5,64,128]{3,2,1,0:T(8,128)(2,1)} %collective-permute-done.16.up_ref, bf16[16,5,64,128]{3,2,1,0:T(8,128)(2,1)} %copy-done.6, bf16[16,5,64,128]{3,2,1,0:T(8,128)(2,1)} %copy-done.8), custom_call_target="tpu_custom_call" | custom-call | flops 251658240 | bytes 5242880 | tf_op jit(solution)/shard_map/screen/pallas_call | solution.py:302
  (42 shorter events, 0.1 us)
Async XLA Ops:
  0.0 1.3 copy-start
  1.3 1.3 copy-start.1
  5.7 21.3 %collective-permute-start = (bf16[16,2,2,16,128]{4,3,2,1,0:T(8,128)(2,1)S(1)}, bf16[16,2,2,16,128]{4,3,2,1,0:T(8,128)(2,1)S(1)}, u32[]{:S(2)}, u32[]{:S(2)}) collective-permute-start(bf16[16,2,2,16,128]{4,3,2,1,0:T(8,128)(2,1)S(1)} %get-tuple-element.19), channel_id=1, source_target_pairs={{0,66},{1,67},{2,128},{3,129},{4,70},{5,71},{6,132},{7,133},{8,74}... | collective-permute-start | bytes 786440 | tf_op jit(solution)/shard_map/ppermute | solution.py:47
  10.9 24.6 %collective-permute-start.1 = (bf16[16,2,2,16,128]{4,3,2,1,0:T(8,128)(2,1)S(1)}, bf16[16,2,2,16,128]{4,3,2,1,0:T(8,128)(2,1)S(1)}, u32[]{:S(2)}, u32[]{:S(2)}) collective-permute-start(bf16[16,2,2,16,128]{4,3,2,1,0:T(8,128)(2,1)S(1)} %get-tuple-element.20), channel_id=1, source_target_pairs={{0,2},{1,3},{2,64},{3,65},{4,6},{5,7},{6,68},{7,69},{8,10},{9,11},... | collective-permute-start | bytes 786440 | tf_op jit(solution)/shard_map/ppermute | solution.py:47
  13.8 21.8 %collective-permute-start.2 = (bf16[16,2,2,16,128]{4,3,2,1,0:T(8,128)(2,1)S(1)}, bf16[16,2,2,16,128]{4,3,2,1,0:T(8,128)(2,1)S(1)}, u32[]{:S(2)}, u32[]{:S(2)}) collective-permute-start(bf16[16,2,2,16,128]{4,3,2,1,0:T(8,128)(2,1)S(1)} %get-tuple-element.21), channel_id=1, source_target_pairs={{0,194},{1,195},{2,0},{3,1},{4,198},{5,199},{6,4},{7,5},{8,202},{9... | collective-permute-start | bytes 786440 | tf_op jit(solution)/shard_map/ppermute | solution.py:47
  13.8 21.8 %collective-permute-start.3 = (bf16[16,2,2,16,128]{4,3,2,1,0:T(8,128)(2,1)S(1)}, bf16[16,2,2,16,128]{4,3,2,1,0:T(8,128)(2,1)}, u32[]{:S(2)}, u32[]{:S(2)}) collective-permute-start(bf16[16,2,2,16,128]{4,3,2,1,0:T(8,128)(2,1)S(1)} %get-tuple-element.22), channel_id=1, source_target_pairs={{0,130},{1,131},{2,192},{3,193},{4,134},{5,135},{6,196},{7,197},{8... | collective-permute-start | bytes 786440 | tf_op jit(solution)/shard_map/ppermute | solution.py:47
  15.4 53.9 %all-to-all-start = ((bf16[16,4,2,3,16,128]{5,4,3,2,1,0:T(8,128)(2,1)}), bf16[16,4,2,3,16,128]{5,4,3,2,1,0:T(8,128)(2,1)S(1)}, u32[]{:S(2)}, u32[]{:S(2)}) async-start(bf16[16,4,2,3,16,128]{5,4,3,2,1,0:T(8,128)(2,1)} %get-tuple-element.18), calls=%async_computation | async-start | bytes 3145728 | tf_op jit(solution)/shard_map/all_to_all | solution.py:343
  27.0 8.6 %copy-start.11 = (bf16[16,2,2,16,128]{4,3,2,1,0:T(8,128)(2,1)}, bf16[16,2,2,16,128]{4,3,2,1,0:T(8,128)(2,1)S(1)}, u32[]{:S(2)}) copy-start(bf16[16,2,2,16,128]{4,3,2,1,0:T(8,128)(2,1)S(1)} %collective-permute-done.refs_0_) | copy-start | bytes 786436
  35.6 0.7 copy-start.12
  35.6 0.8 copy-start.13
  70.4 24.6 %collective-permute-start.7 = (bf16[16,2,3,16,128]{4,3,2,1,0:T(8,128)(2,1)}, bf16[16,2,3,16,128]{4,3,2,1,0:T(8,128)(2,1)S(1)}, u32[]{:S(2)}, u32[]{:S(2)}) collective-permute-start(bf16[16,2,3,16,128]{4,3,2,1,0:T(8,128)(2,1)} %get-tuple-element.31), channel_id=1, source_target_pairs={{0,130},{1,131},{2,192},{3,193},{4,134},{5,135},{6,196},{7,197},{8... | collective-permute-start | bytes 1179656 | tf_op jit(solution)/shard_map/ppermute | solution.py:47
  73.0 34.6 %collective-permute-start.6 = (bf16[16,2,3,16,128]{4,3,2,1,0:T(8,128)(2,1)}, bf16[16,2,3,16,128]{4,3,2,1,0:T(8,128)(2,1)S(1)}, u32[]{:S(2)}, u32[]{:S(2)}) collective-permute-start(bf16[16,2,3,16,128]{4,3,2,1,0:T(8,128)(2,1)} %get-tuple-element.32), channel_id=1, source_target_pairs={{0,194},{1,195},{2,0},{3,1},{4,198},{5,199},{6,4},{7,5},{8,202},{9... | collective-permute-start | bytes 1179656 | tf_op jit(solution)/shard_map/ppermute | solution.py:47
  75.4 32.2 %collective-permute-start.5 = (bf16[16,2,3,16,128]{4,3,2,1,0:T(8,128)(2,1)}, bf16[16,2,3,16,128]{4,3,2,1,0:T(8,128)(2,1)S(1)}, u32[]{:S(2)}, u32[]{:S(2)}) collective-permute-start(bf16[16,2,3,16,128]{4,3,2,1,0:T(8,128)(2,1)} %get-tuple-element.33), channel_id=1, source_target_pairs={{0,2},{1,3},{2,64},{3,65},{4,6},{5,7},{6,68},{7,69},{8,10},{9,11},... | collective-permute-start | bytes 1179656 | tf_op jit(solution)/shard_map/ppermute | solution.py:47
  75.4 32.2 %collective-permute-start.4 = (bf16[16,2,3,16,128]{4,3,2,1,0:T(8,128)(2,1)S(1)}, bf16[16,2,3,16,128]{4,3,2,1,0:T(8,128)(2,1)S(1)}, u32[]{:S(2)}, u32[]{:S(2)}) collective-permute-start(bf16[16,2,3,16,128]{4,3,2,1,0:T(8,128)(2,1)S(1)} %get-tuple-element.34), channel_id=1, source_target_pairs={{0,66},{1,67},{2,128},{3,129},{4,70},{5,71},{6,132},{7,133},{8,74}... | collective-permute-start | bytes 1179656 | tf_op jit(solution)/shard_map/ppermute | solution.py:47
  76.5 50.2 %all-to-all-start.2 = ((bf16[16,4,2,2,16,128]{5,4,3,2,1,0:T(8,128)(2,1)}), bf16[16,4,2,2,16,128]{5,4,3,2,1,0:T(8,128)(2,1)S(1)}, u32[]{:S(2)}, u32[]{:S(2)}) async-start(bf16[16,4,2,2,16,128]{5,4,3,2,1,0:T(8,128)(2,1)} %gather.2), calls=%async_computation.2 | async-start | bytes 2097152 | tf_op jit(solution)/shard_map/all_to_all | solution.py:346
  107.6 1.2 copy-start.2
  108.9 1.2 copy-start.4
  120.5 22.5 %collective-permute-start.8 = (bf16[16,3,16,128]{3,2,1,0:T(8,128)(2,1)S(1)}, bf16[16,3,16,128]{3,2,1,0:T(8,128)(2,1)S(1)}, u32[]{:S(2)}, u32[]{:S(2)}) collective-permute-start(bf16[16,3,16,128]{3,2,1,0:T(8,128)(2,1)S(1)} %get-tuple-element.24), channel_id=1, source_target_pairs={{0,66},{1,67},{2,128},{3,129},{4,70},{5,71},{6,132},{7,133},{8,74}... | collective-permute-start | bytes 589832 | tf_op jit(solution)/shard_map/ppermute | solution.py:47
  122.3 20.8 %collective-permute-start.9 = (bf16[16,3,16,128]{3,2,1,0:T(8,128)(2,1)S(1)}, bf16[16,3,16,128]{3,2,1,0:T(8,128)(2,1)S(1)}, u32[]{:S(2)}, u32[]{:S(2)}) collective-permute-start(bf16[16,3,16,128]{3,2,1,0:T(8,128)(2,1)S(1)} %get-tuple-element.25), channel_id=1, source_target_pairs={{0,2},{1,3},{2,64},{3,65},{4,6},{5,7},{6,68},{7,69},{8,10},{9,11},... | collective-permute-start | bytes 589832 | tf_op jit(solution)/shard_map/ppermute | solution.py:47
  122.8 20.3 %collective-permute-start.10 = (bf16[16,3,16,128]{3,2,1,0:T(8,128)(2,1)S(1)}, bf16[16,3,16,128]{3,2,1,0:T(8,128)(2,1)S(1)}, u32[]{:S(2)}, u32[]{:S(2)}) collective-permute-start(bf16[16,3,16,128]{3,2,1,0:T(8,128)(2,1)S(1)} %get-tuple-element.26), channel_id=1, source_target_pairs={{0,194},{1,195},{2,0},{3,1},{4,198},{5,199},{6,4},{7,5},{8,202},{9... | collective-permute-start | bytes 589832 | tf_op jit(solution)/shard_map/ppermute | solution.py:47
  125.0 18.1 %collective-permute-start.11 = (bf16[16,3,16,128]{3,2,1,0:T(8,128)(2,1)S(1)}, bf16[16,3,16,128]{3,2,1,0:T(8,128)(2,1)S(1)}, u32[]{:S(2)}, u32[]{:S(2)}) collective-permute-start(bf16[16,3,16,128]{3,2,1,0:T(8,128)(2,1)S(1)} %get-tuple-element.27), channel_id=1, source_target_pairs={{0,130},{1,131},{2,192},{3,193},{4,134},{5,135},{6,196},{7,197},{8... | collective-permute-start | bytes 589832 | tf_op jit(solution)/shard_map/ppermute | solution.py:47
  126.7 1.2 copy-start.3
  127.9 1.2 copy-start.5
  136.3 33.2 %all-to-all-start.3 = ((bf16[16,4,2,16,128]{4,3,2,1,0:T(8,128)(2,1)}), bf16[16,4,2,16,128]{4,3,2,1,0:T(8,128)(2,1)S(1)}, u32[]{:S(2)}, u32[]{:S(2)}) async-start(bf16[16,4,2,16,128]{4,3,2,1,0:T(8,128)(2,1)} %correlate.3), calls=%async_computation.3 | async-start | bytes 1048576 | tf_op jit(solution)/shard_map/all_to_all | solution.py:353
  143.0 0.7 copy-start.14
  143.1 0.7 copy-start.15
  143.1 0.8 copy-start.16
  143.9 0.7 copy-start.17
  169.6 12.7 %collective-permute-start.15 = (bf16[16,2,16,128]{3,2,1,0:T(8,128)(2,1)S(1)}, bf16[16,2,16,128]{3,2,1,0:T(8,128)(2,1)S(1)}, u32[]{:S(2)}, u32[]{:S(2)}) collective-permute-start(bf16[16,2,16,128]{3,2,1,0:T(8,128)(2,1)S(1)} %get-tuple-element.35), channel_id=1, source_target_pairs={{0,130},{1,131},{2,192},{3,193},{4,134},{5,135},{6,196},{7,197},{8... | collective-permute-start | bytes 393224 | tf_op jit(solution)/shard_map/ppermute | solution.py:47
  173.2 9.1 %collective-permute-start.14 = (bf16[16,2,16,128]{3,2,1,0:T(8,128)(2,1)S(1)}, bf16[16,2,16,128]{3,2,1,0:T(8,128)(2,1)S(1)}, u32[]{:S(2)}, u32[]{:S(2)}) collective-permute-start(bf16[16,2,16,128]{3,2,1,0:T(8,128)(2,1)S(1)} %get-tuple-element.36), channel_id=1, source_target_pairs={{0,194},{1,195},{2,0},{3,1},{4,198},{5,199},{6,4},{7,5},{8,202},{9... | collective-permute-start | bytes 393224 | tf_op jit(solution)/shard_map/ppermute | solution.py:47
  173.3 9.1 %collective-permute-start.13 = (bf16[16,2,16,128]{3,2,1,0:T(8,128)(2,1)S(1)}, bf16[16,2,16,128]{3,2,1,0:T(8,128)(2,1)S(1)}, u32[]{:S(2)}, u32[]{:S(2)}) collective-permute-start(bf16[16,2,16,128]{3,2,1,0:T(8,128)(2,1)S(1)} %get-tuple-element.37), channel_id=1, source_target_pairs={{0,2},{1,3},{2,64},{3,65},{4,6},{5,7},{6,68},{7,69},{8,10},{9,11},... | collective-permute-start | bytes 393224 | tf_op jit(solution)/shard_map/ppermute | solution.py:47
  174.7 9.4 %collective-permute-start.12 = (bf16[16,2,16,128]{3,2,1,0:T(8,128)(2,1)S(1)}, bf16[16,2,16,128]{3,2,1,0:T(8,128)(2,1)S(1)}, u32[]{:S(2)}, u32[]{:S(2)}) collective-permute-start(bf16[16,2,16,128]{3,2,1,0:T(8,128)(2,1)S(1)} %get-tuple-element.38), channel_id=1, source_target_pairs={{0,66},{1,67},{2,128},{3,129},{4,70},{5,71},{6,132},{7,133},{8,74}... | collective-permute-start | bytes 393224 | tf_op jit(solution)/shard_map/ppermute | solution.py:47
  175.6 17.1 %all-to-all-start.1 = ((bf16[16,4,3,16,128]{4,3,2,1,0:T(8,128)(2,1)}), bf16[16,4,3,16,128]{4,3,2,1,0:T(8,128)(2,1)S(1)}, u32[]{:S(2)}, u32[]{:S(2)}) async-start(bf16[16,4,3,16,128]{4,3,2,1,0:T(8,128)(2,1)} %gather.3), calls=%async_computation.1 | async-start | bytes 1572864 | tf_op jit(solution)/shard_map/all_to_all | solution.py:356
  182.3 1.8 copy-start.18
  182.3 1.8 copy-start.19
  182.3 1.8 copy-start.20
  184.1 0.6 copy-start.21
  187.1 9.1 %copy-start.9 = (bf16[16,2,64,128]{3,2,1,0:T(8,128)(2,1)S(1)}, bf16[16,2,64,128]{3,2,1,0:T(8,128)(2,1)}, u32[]{:S(2)}) copy-start(bf16[16,2,64,128]{3,2,1,0:T(8,128)(2,1)} %settle.2) | copy-start | bytes 1572868
  192.7 0.9 copy-start.7
  196.2 15.8 %copy-start.10 = (bf16[1,64,192]{2,1,0:T(8,128)(2,1)S(1)}, bf16[1,64,192]{2,1,0:T(8,128)(2,1)}, u32[]{:S(2)}) copy-start(bf16[1,64,192]{2,1,0:T(8,128)(2,1)} %param.8) | copy-start | bytes 73732
  197.4 29.1 %copy-start.6 = (bf16[16,5,64,128]{3,2,1,0:T(8,128)(2,1)}, bf16[16,5,64,128]{3,2,1,0:T(8,128)(2,1)S(1)}, u32[]{:S(2)}) copy-start(bf16[16,5,64,128]{3,2,1,0:T(8,128)(2,1)S(1)} %pad_maximum_fusion.own_ref) | copy-start | bytes 3932164
  197.4 27.9 %collective-permute-start.17 = (bf16[16,5,64,128]{3,2,1,0:T(8,128)(2,1)S(1)}, bf16[16,5,64,128]{3,2,1,0:T(8,128)(2,1)S(1)}, u32[]{:S(2)}, u32[]{:S(2)}) collective-permute-start(bf16[16,5,64,128]{3,2,1,0:T(8,128)(2,1)S(1)} %pad_maximum_fusion.own_ref), channel_id=1, source_target_pairs={{1,0},{2,1},{3,2},{5,4},{6,5},{7,6},{9,8},{10,9},{11,10},{13,12},{... | collective-permute-start | bytes 3932168 | tf_op jit(solution)/shard_map/ppermute | solution.py:360
  208.5 18.1 %collective-permute-start.16 = (bf16[16,5,64,128]{3,2,1,0:T(8,128)(2,1)S(1)}, bf16[16,5,64,128]{3,2,1,0:T(8,128)(2,1)}, u32[]{:S(2)}, u32[]{:S(2)}) collective-permute-start(bf16[16,5,64,128]{3,2,1,0:T(8,128)(2,1)S(1)} %pad_maximum_fusion.own_ref), channel_id=1, source_target_pairs={{0,1},{1,2},{2,3},{4,5},{5,6},{6,7},{8,9},{9,10},{10,11},{12,13},{... | collective-permute-start | bytes 3932168 | tf_op jit(solution)/shard_map/ppermute | solution.py:359
  225.4 1.2 copy-start.8

commit v3 on v2

--- a/solution.py
+++ b/solution.py
@@ -18,6 +18,7 @@
 ALL = ("z", "y", "x", "s")
 PLANE = ("y", "x")
 CUT = 3
+BUF = 2
 HEAVY = 100 * 10**9
 STEPS = (3, 1, -1, -3)
 
@@ -56,10 +57,14 @@
     in_refs, fwd_ref, inv_ref = refs[:pieces], refs[pieces], refs[pieces + 1]
     n_out = 4 if split else 1
     outs = refs[pieces + 2 : pieces + 2 + n_out]
-    xl_ref, xg_ref, p_ref, y_ref, z_ref, f_ref, b_ref, sem = refs[pieces + 2 + n_out :]
-    loads = [pltpu.make_async_copy(fwd_ref, f_ref, sem.at[0]), pltpu.make_async_copy(inv_ref, b_ref, sem.at[1])]
-    for load in loads:
-        load.start()
+    x_ref, p_ref, y_ref, z_ref, f_ref, b_ref, sem = refs[pieces + 2 + n_out :]
+    loads = [
+        [pltpu.make_async_copy(ref.at[t1], held.at[t1], sem.at[k, t1]) for t1 in range(4)]
+        for k, (ref, held) in enumerate(((fwd_ref, f_ref), (inv_ref, b_ref)))
+    ]
+    for t1 in range(4):
+        for k in range(2):
+            loads[k][t1].start()
     f32, bf16 = jnp.float32, jnp.bfloat16
     left = lax.broadcasted_iota(jnp.int32, (32, 128), 1) < 64
 
@@ -68,8 +73,8 @@
         return ref.reshape(2 * NL, 128).astype(f32)
 
     for s in range(slots):
-        cols = slice(s * 128, (s + 1) * 128)
-        for which, x_ref in enumerate((xl_ref, xg_ref)):
+        for which in range(2):
+            cols = slice((which * slots + s) * 128, (which * slots + s + 1) * 128)
             for p in range(0, NP, 2):
                 rows = slice(p * NL, (p + 2) * NL)
                 x0, x1, x2, x3 = (fetch(j, which, s, p) for j in range(4))
@@ -79,31 +84,25 @@
                     x_ref[t1, 0, rows, cols] = hi
                     x_ref[t1, 1, rows, cols] = (v - hi.astype(f32)).astype(bf16)
 
-    for load in loads:
-        load.wait()
-
-    @pl.loop(0, 4)
-    def _(t1):
-        table, back = f_ref[t1], b_ref[t1]
-        for s in range(0, slots, 2):
-            n = min(2, slots - s)
-            cols = slice(s * 128, (s + n) * 128)
-            width = slice(0, n * 128)
-            for k, x_ref in enumerate((xl_ref, xg_ref)):
-                y_ref[k, :, width] = jnp.dot(table, x_ref[t1, 0, :, cols], preferred_element_type=f32) + jnp.dot(
-                    table, x_ref[t1, 1, :, cols], preferred_element_type=f32
-                )
-            for k in range(n):
-                own = slice(k * 128, (k + 1) * 128)
-                for r in range(0, QUART, 32):
-                    one, two = slice(r, r + 32), slice(QUART + r, QUART + r + 32)
-                    le = y_ref[0, one, own] + times_i(y_ref[0, two, own])
-                    gr = y_ref[1, one, own] + times_i(y_ref[1, two, own])
-                    m1, m2 = le * gr, le * pltpu.roll(gr, 64, 1)
-                    p_ref[one, own] = (
-                        jnp.where(left, m1, m2) + pltpu.roll(jnp.where(left, -m2, m1), 64, 1)
-                    ).astype(bf16)
-            z_ref[t1, :, cols] = jnp.dot(back, p_ref[:, width], preferred_element_type=f32)
+    n = slots * 128
+    for t1 in range(4):
+        loads[0][t1].wait()
+        loads[1][t1].wait()
+        table, at = f_ref[t1], t1 % BUF
+        y_ref[at] = jnp.dot(table, x_ref[t1, 0], preferred_element_type=f32) + jnp.dot(
+            table, x_ref[t1, 1], preferred_element_type=f32
+        )
+        for s in range(slots):
+            own, other = slice(s * 128, (s + 1) * 128), slice(n + s * 128, n + (s + 1) * 128)
+            for r in range(0, QUART, 32):
+                one, two = slice(r, r + 32), slice(QUART + r, QUART + r + 32)
+                le = y_ref[at, one, own] + times_i(y_ref[at, two, own])
+                gr = y_ref[at, one, other] + times_i(y_ref[at, two, other])
+                m1, m2 = le * gr, le * pltpu.roll(gr, 64, 1)
+                p_ref[at, one, own] = (
+                    jnp.where(left, m1, m2) + pltpu.roll(jnp.where(left, -m2, m1), 64, 1)
+                ).astype(bf16)
+        z_ref[t1] = jnp.dot(b_ref[t1], p_ref[at], preferred_element_type=f32)
 
     ca, cb, cc = rot_ref[0], rot_ref[1], rot_ref[2]
     for s in range(slots):
@@ -138,16 +137,15 @@
         in_specs=[pl.BlockSpec(memory_space=pltpu.SMEM)] + [vmem] * len(inputs) + [hbm] * 2,
         out_specs=[vmem] * (4 if split else 1),
         scratch_shapes=[
-            pltpu.VMEM((4, 2, QUART, n), jnp.bfloat16),
-            pltpu.VMEM((4, 2, QUART, n), jnp.bfloat16),
-            pltpu.VMEM((QUART, 256), jnp.bfloat16),
-            pltpu.VMEM((2, 2 * QUART, 256), jnp.float32),
+            pltpu.VMEM((4, 2, QUART, 2 * n), jnp.bfloat16),
+            pltpu.VMEM((BUF, QUART, n), jnp.bfloat16),
+            pltpu.VMEM((BUF, 2 * QUART, 2 * n), jnp.float32),
             pltpu.VMEM((4, 2 * QUART, n), jnp.float32),
             pltpu.VMEM((4, 2 * QUART, QUART), jnp.bfloat16),
             pltpu.VMEM((4, 2 * QUART, QUART), jnp.bfloat16),
-            pltpu.SemaphoreType.DMA((2,)),
+            pltpu.SemaphoreType.DMA((2, 4)),
         ],
-        compiler_params=pltpu.CompilerParams(vmem_limit_bytes=40 << 20),
+        compiler_params=pltpu.CompilerParams(vmem_limit_bytes=53 << 20),
         cost_estimate=pl.CostEstimate(
             flops=HEAVY, bytes_accessed=3 * NE * n * 2 + (2 << 20), transcendentals=0
         ),
@@ -205,56 +203,56 @@
             pltpu.VMEM((slots, 2, el, bi, wide), jnp.bfloat16),
             pltpu.SemaphoreType.DMA((slots, 2)),
         ],
-        compiler_params=pltpu.CompilerParams(vmem_limit_bytes=20 << 20),
+        compiler_params=pltpu.CompilerParams(vmem_limit_bytes=60 << 20),
         cost_estimate=pl.CostEstimate(flops=0, bytes_accessed=4 * el * slots * bi * wide * 2, transcendentals=0),
         name="prepare",
     )(turn, less, great)
     return early, late
 
 
-def settle_kernel(slots, *refs):
-    in_refs, out_ref, turn = refs[:-2], refs[-2], refs[-1]
+def settle_kernel(slots, pieces, *refs):
+    in_refs, more, out_ref, turn = refs[:pieces], refs[pieces:-2], refs[-2], refs[-1]
     turn[...] = turning()
     for j in range(4):
-        for s in range(slots):
-            x = (in_refs[j][:, s] if len(in_refs) == 4 else in_refs[0][:, j, s]).reshape(256, 128)
-            x = jnp.dot(turn[...], x, preferred_element_type=jnp.float32).astype(jnp.bfloat16)
-            out_ref[:, s, j * NP : (j + 1) * NP] = x.reshape(NL, NP, 128)
-
-
-def settle(inputs, flops):
+        x = [(in_refs[j][:, s] if pieces == 4 else in_refs[0][:, j, s]).reshape(256, 128) for s in range(slots)]
+        x = jnp.dot(turn[...], jnp.concatenate(x, 1), preferred_element_type=jnp.float32).astype(jnp.bfloat16)
+        for s in range(slots):
+            out_ref[:, s, j * NP : (j + 1) * NP] = x[:, s * 128 : (s + 1) * 128].reshape(NL, NP, 128)
+    for ref in more:
+        out_ref[:, slots:] = ref[...]
+
+
+def settle(inputs, more, flops):
     slots = inputs[0].shape[-3]
+    total = slots + sum(m.shape[1] for m in more)
     vmem = pl.BlockSpec(memory_space=pltpu.VMEM)
     return pl.pallas_call(
-        functools.partial(settle_kernel, slots),
-        out_shape=jax.ShapeDtypeStruct((NL, slots, 64, 128), jnp.bfloat16),
-        in_specs=[vmem] * len(inputs),
+        functools.partial(settle_kernel, slots, len(inputs)),
+        out_shape=jax.ShapeDtypeStruct((NL, total, 64, 128), jnp.bfloat16),
+        in_specs=[vmem] * (len(inputs) + len(more)),
         out_specs=vmem,
         scratch_shapes=[pltpu.VMEM((256, 256), jnp.bfloat16)],
-        cost_estimate=pl.CostEstimate(flops=flops, bytes_accessed=NL * slots * 64 * 128 * 4, transcendentals=0),
+        cost_estimate=pl.CostEstimate(flops=flops, bytes_accessed=NL * total * 64 * 128 * 4, transcendentals=0),
+        compiler_params=pltpu.CompilerParams(vmem_limit_bytes=12 << 20),
         name="settle",
-    )(*inputs)
+    )(*inputs, *more)
 
 
 def gather_kernel(*refs):
-    sem = refs[5]
-    copies = [pltpu.make_async_copy(refs[j], refs[4].at[:, j], sem.at[j]) for j in range(4)]
-    for copy in copies:
-        copy.start()
-    for copy in copies:
-        copy.wait()
+    for j in range(4):
+        refs[4][:, j] = refs[j][...]
 
 
 def gather(pieces, flops):
     shape = pieces[0].shape
-    hbm = pl.BlockSpec(memory_space=pltpu.HBM)
+    vmem = pl.BlockSpec(memory_space=pltpu.VMEM)
     return pl.pallas_call(
         gather_kernel,
         out_shape=jax.ShapeDtypeStruct((shape[0], 4, *shape[1:]), jnp.bfloat16),
-        in_specs=[hbm] * 4,
-        out_specs=hbm,
-        scratch_shapes=[pltpu.SemaphoreType.DMA((4,))],
+        in_specs=[vmem] * 4,
+        out_specs=vmem,
         cost_estimate=pl.CostEstimate(flops=flops, bytes_accessed=8 * pieces[0].size * 2, transcendentals=0),
+        compiler_params=pltpu.CompilerParams(vmem_limit_bytes=12 << 20),
         name="gather",
     )(*pieces)
 
@@ -308,6 +306,7 @@
         cost_estimate=pl.CostEstimate(
             flops=2 * el * slots * bi * 3 * bi * wide, bytes_accessed=4 * own.size * 2, transcendentals=0
         ),
+        compiler_params=pltpu.CompilerParams(vmem_limit_bytes=12 << 20),
         name="screen",
     )(row, pattern, weights, up, own, down)
 
@@ -352,10 +351,9 @@
     lo = gather([hop(p, STEPS[j]) for j, p in enumerate(lo)], HEAVY)
     hi = lax.all_to_all(hi, PLANE, split_axis=0, concat_axis=0, tiled=True)
     hi = lax.optimization_barrier([hi, lo])[0]
-    hi = settle([hop(hi[:, j], STEPS[j]) for j in range(4)], HEAVY)
+    hi = settle([hop(hi[:, j], STEPS[j]) for j in range(4)], [], HEAVY)
     lo = lax.all_to_all(lo, PLANE, split_axis=0, concat_axis=0, tiled=True)
-    lo = settle([lax.optimization_barrier([lo, hi])[0]], 0)
-    own = jnp.concatenate([lo, hi], 1)
+    own = settle([lo], [hi], 0)
     up = lax.ppermute(own, "s", [(0, 1), (1, 2), (2, 3)])
     down = lax.ppermute(own, "s", [(1, 0), (2, 1), (3, 2)])
     return screen(s_row.reshape(1), pattern, weights, up, own, down)[:, None]

time: 232 us -> 170 us (0.73)
  Pallas kernels: 88.1 us -> 26.4 us
  waiting for transfers between devices: 58.6 us -> 76.5 us
  local copies, waits for them, and re-layouts: 13.3 us -> 2.3 us
  starting transfers between devices: 69.4 us -> 63.6 us
    pallas_call x2, Pallas kernels: 57.9 us -> 1.97 us  [gather(): pl.pallas_call(gather_kernel, out_shape=jax.ShapeDtypeStruct((shape[0], 4...]
    unnamed x45 -> x11, local copies, waits for them, and re-layouts: 11.4 us -> 1.87 us
    all_to_all x1, waiting for transfers between devices: 0.01 us -> 8.01 us  [shards(): hi = lax.all_to_all(hi, PLANE, split_axis=0, concat_axis=0, tiled=True)]
    all_to_all x1, waiting for transfers between devices: 0.01 us -> 6.24 us  [shards(): lax.all_to_all(early, PLANE, split_axis=0, concat_axis=0, tiled=True)]
    pallas_call x2, Pallas kernels: 4.88 us -> 0.72 us  [settle(): pl.pallas_call(functools.partial(settle_kernel, slots, len(inputs)), out_...]
    all_to_all x1, starting transfers between devices: 6.65 us -> 3.61 us  [shards(): lo = lax.all_to_all(lo, PLANE, split_axis=0, concat_axis=0, tiled=True)]
    all_to_all x1, waiting for transfers between devices: 5.65 us -> 8.22 us  [shards(): lo = lax.all_to_all(lo, PLANE, split_axis=0, concat_axis=0, tiled=True)]
    ppermute x1, starting transfers between devices: 11 us -> 8.5 us  [shards(): down = lax.ppermute(own, 's', [(1, 0), (2, 1), (3, 2)])]
  transfers between devices with their start and end apart: 22 -> 22, of which waited for: 8 -> 11; matrix products, arithmetic and copies ran while one was open for 1% -> 0% of each run, Pallas kernels for 34% -> 11%
where the time goes in v3:
time: 170 us; the launch traced here: 169 us
  waiting for transfers between devices  76.5 us (45%)
  starting transfers between devices  63.6 us (37%)
  Pallas kernels  26.4 us (16%)
  local copies, waits for them, and re-layouts  2.3 us (1%)
    ppermute x16, waiting for transfers between devices, hop(): return lax.ppermute(piece, ALL, perm)  40.1 us
    ppermute x16, starting transfers between devices, hop(): return lax.ppermute(piece, ALL, perm)  27.8 us
    pallas_call x2, Pallas kernels, correlate(): pl.pallas_call(functools.partial(correlate_kernel, slots, len(inputs), sp...  15.5 us
    ppermute x1, waiting for transfers between devices, shards(): down = lax.ppermute(own, 's', [(1, 0), (2, 1), (3, 2)])  12.8 us
    ppermute x1, starting transfers between devices, shards(): down = lax.ppermute(own, 's', [(1, 0), (2, 1), (3, 2)])  8.5 us
    all_to_all x1, waiting for transfers between devices, shards(): lo = lax.all_to_all(lo, PLANE, split_axis=0, concat_axis=0, tiled=True)  8.22 us
    all_to_all x1, waiting for transfers between devices, shards(): hi = lax.all_to_all(hi, PLANE, split_axis=0, concat_axis=0, tiled=True)  8.01 us
    all_to_all x1, starting transfers between devices, shards(): hi = lax.all_to_all(hi, PLANE, split_axis=0, concat_axis=0, tiled=True)  7.34 us
  transfers between devices with their start and end apart: 22, of which 11 were waited for; matrix products, arithmetic and copies ran while one was open for 0% of the time, Pallas kernels for 11%

profile of v3, /device:TPU:1, one launch (start us, length us, event | category | flops | bytes accessed | tf_op | source)
XLA Modules:
  0.0 169.5 jit_solution(11250581840329374663)
XLA Ops:
  0.0 4.0 %prepare.1 = (bf16[16,4,2,3,16,128]{5,4,3,2,1,0:T(8,128)(2,1)}, bf16[16,2,2,16,128]{4,3,2,1,0:T(8,128)(2,1)}, bf16[16,2,2,16,128]{4,3,2,1,0:T(8,128)(2,1)}, bf16...) custom-call(s32[1]{0:T(128)} %bitcast.9.turn_ref, bf16[16,5,64,128]{3,2,1,0:T(8,128)(2,1)} %bitcast.35, ...), custom_call_target="tpu_custom_call" | custom-call | bytes 5242880 | tf_op jit(solution)/shard_map/prepare/pallas_call | solution.py:196
  4.0 5.2 %collective-permute-start = (bf16[16,2,2,16,128]{4,3,2,1,0:T(8,128)(2,1)}, bf16[16,2,2,16,128]{4,3,2,1,0:T(8,128)(2,1)S(1)}, u32[]{:S(2)}, u32[]{:S(2)}) collective-permute-start(bf16[16,2,2,16,128]{4,3,2,1,0:T(8,128)(2,1)} %get-tuple-element.18), channel_id=1, source_target_pairs={{0,66},{1,67},{2,128},{3,129},{4,70},{5,71},{6,132},{7,133},{8,74}... | collective-permute-start | bytes 786440 | tf_op jit(solution)/shard_map/ppermute | solution.py:48
  9.2 2.8 %collective-permute-start.1 = (bf16[16,2,2,16,128]{4,3,2,1,0:T(8,128)(2,1)}, bf16[16,2,2,16,128]{4,3,2,1,0:T(8,128)(2,1)S(1)}, u32[]{:S(2)}, u32[]{:S(2)}) collective-permute-start(bf16[16,2,2,16,128]{4,3,2,1,0:T(8,128)(2,1)} %get-tuple-element.19), channel_id=1, source_target_pairs={{0,2},{1,3},{2,64},{3,65},{4,6},{5,7},{6,68},{7,69},{8,10},{9,11},... | collective-permute-start | bytes 786440 | tf_op jit(solution)/shard_map/ppermute | solution.py:48
  12.1 0.0 collective-permute-start.2
  12.1 1.6 collective-permute-start.3
  13.7 6.8 %all-to-all-start = ((bf16[16,4,2,3,16,128]{5,4,3,2,1,0:T(8,128)(2,1)}), bf16[16,4,2,3,16,128]{5,4,3,2,1,0:T(8,128)(2,1)S(1)}, u32[]{:S(2)}, u32[]{:S(2)}) async-start(bf16[16,4,2,3,16,128]{5,4,3,2,1,0:T(8,128)(2,1)} %get-tuple-element.17), calls=%async_computation | async-start | bytes 3145728 | tf_op jit(solution)/shard_map/all_to_all | solution.py:342
  20.5 5.0 %collective-permute-done.refs_0_ = bf16[16,2,2,16,128]{4,3,2,1,0:T(8,128)(2,1)S(1)} collective-permute-done((bf16[16,2,2,16,128]{4,3,2,1,0:T(8,128)(2,1)}, bf16[16,2,2,16,128]{4,3,2,1,0:T(8,128)(2,1)S(1)}, u32[]{:S(2)}, u32[]{:S(2)}) %collective-permute-start) | collective-permute-done | bytes 262176 | tf_op jit(solution)/shard_map/ppermute | solution.py:48
  25.5 8.5 %collective-permute-done.1.refs_1_ = bf16[16,2,2,16,128]{4,3,2,1,0:T(8,128)(2,1)S(1)} collective-permute-done((bf16[16,2,2,16,128]{4,3,2,1,0:T(8,128)(2,1)}, bf16[16,2,2,16,128]{4,3,2,1,0:T(8,128)(2,1)S(1)}, u32[]{:S(2)}, u32[]{:S(2)}) %collective-permute-start.1) | collective-permute-done | bytes 262176 | tf_op jit(solution)/shard_map/ppermute | solution.py:48
  34.0 0.0 collective-permute-done.2.refs_2_
  34.0 0.0 collective-permute-done.3.refs_3_
  34.0 1.0 gather.2
  35.0 6.2 %all-to-all-done = bf16[16,4,2,3,16,128]{5,4,3,2,1,0:T(8,128)(2,1)S(1)} async-done(((bf16[16,4,2,3,16,128]{5,4,3,2,1,0:T(8,128)(2,1)}), bf16[16,4,2,3,16,128]{5,4,3,2,1,0:T(8,128)(2,1)S(1)}, u32[]{:S(2)}, u32[]{:S(2)}) %all-to-all-start) | async-done | bytes 1572896 | tf_op jit(solution)/shard_map/all_to_all | solution.py:342
  41.3 0.3 slice_bitcast_fusion
  41.6 3.4 %collective-permute-start.7 = (bf16[16,2,3,16,128]{4,3,2,1,0:T(8,128)(2,1)S(1)}, bf16[16,2,3,16,128]{4,3,2,1,0:T(8,128)(2,1)S(1)}, u32[]{:S(2)}, u32[]{:S(2)}) collective-permute-start(bf16[16,2,3,16,128]{4,3,2,1,0:T(8,128)(2,1)S(1)} %get-tuple-element.29), channel_id=1, source_target_pairs={{0,130},{1,131},{2,192},{3,193},{4,134},{5,135},{6,196},{7,197},{8... | collective-permute-start | bytes 1179656 | tf_op jit(solution)/shard_map/ppermute | solution.py:48
  44.9 0.7 collective-permute-start.6
  45.6 0.7 collective-permute-start.5
  46.4 1.2 collective-permute-start.4
  47.6 0.1 pad_maximum_fusion.rot_ref
  47.7 6.0 %all-to-all-start.2 = ((bf16[16,4,2,2,16,128]{5,4,3,2,1,0:T(8,128)(2,1)}), bf16[16,4,2,2,16,128]{5,4,3,2,1,0:T(8,128)(2,1)S(1)}, u32[]{:S(2)}, u32[]{:S(2)}) async-start(bf16[16,4,2,2,16,128]{5,4,3,2,1,0:T(8,128)(2,1)} %gather.2), calls=%async_computation.2 | async-start | bytes 2097152 | tf_op jit(solution)/shard_map/all_to_all | solution.py:345
  53.7 11.9 %collective-permute-done.7.refs_3_ = bf16[16,2,3,16,128]{4,3,2,1,0:T(8,128)(2,1)S(1)} collective-permute-done((bf16[16,2,3,16,128]{4,3,2,1,0:T(8,128)(2,1)S(1)}, bf16[16,2,3,16,128]{4,3,2,1,0:T(8,128)(2,1)S(1)}, u32[]{:S(2)}, u32[]{:S(2)}) %collective-permute-start.7) | collective-permute-done | bytes 393248 | tf_op jit(solution)/shard_map/ppermute | solution.py:48
  65.6 12.8 %collective-permute-done.6.refs_2_ = bf16[16,2,3,16,128]{4,3,2,1,0:T(8,128)(2,1)S(1)} collective-permute-done((bf16[16,2,3,16,128]{4,3,2,1,0:T(8,128)(2,1)S(1)}, bf16[16,2,3,16,128]{4,3,2,1,0:T(8,128)(2,1)S(1)}, u32[]{:S(2)}, u32[]{:S(2)}) %collective-permute-start.6) | collective-permute-done | bytes 393248 | tf_op jit(solution)/shard_map/ppermute | solution.py:48
  78.3 0.0 collective-permute-done.5.refs_1_
  78.3 0.8 copy-done.4
  79.1 0.0 collective-permute-done.4.refs_0_
  79.1 0.0 copy-done.3
  79.1 8.2 %correlate.2 = (bf16[16,3,16,128]{3,2,1,0:T(8,128)(2,1)S(1)}, bf16[16,3,16,128]{3,2,1,0:T(8,128)(2,1)S(1)}, bf16[16,3,16,128]{3,2,1,0:T(8,128)(2,1)S(1)}, bf16[16,3,16,128]{3,2,1,0:T(8,128)(2,1)S(1)}) custom-call(f32[3]{0:T(128)S(1)} %pad_maximum_fusion.rot_ref, bf16[16,2,3,16,128]{4,3,2,1,0:T(8,128)(2,1)} %collective-permute-done.4.refs_0_, ...), custom_call_target="tpu_custom_call" | custom-call | flops 99999997952 | bytes 4456448 | tf_op jit(solution)/shard_map/correlate/pallas_call | solution.py:134
  87.4 0.7 collective-permute-start.8
  88.1 1.3 collective-permute-start.9
  89.4 1.3 collective-permute-start.10
  90.8 2.6 %collective-permute-start.11 = (bf16[16,3,16,128]{3,2,1,0:T(8,128)(2,1)S(1)}, bf16[16,3,16,128]{3,2,1,0:T(8,128)(2,1)S(1)}, u32[]{:S(2)}, u32[]{:S(2)}) collective-permute-start(bf16[16,3,16,128]{3,2,1,0:T(8,128)(2,1)S(1)} %get-tuple-element.26), channel_id=1, source_target_pairs={{0,130},{1,131},{2,192},{3,193},{4,134},{5,135},{6,196},{7,197},{8... | collective-permute-start | bytes 589832 | tf_op jit(solution)/shard_map/ppermute | solution.py:48
  93.4 0.0 all-to-all-done.2.refs_0_
  93.4 1.0 copy-done.1
  94.4 7.3 %correlate.3 = bf16[16,4,2,16,128]{4,3,2,1,0:T(8,128)(2,1)} custom-call(f32[3]{0:T(128)S(1)} %pad_maximum_fusion.rot_ref, bf16[16,4,2,2,16,128]{5,4,3,2,1,0:T(8,128)(2,1)} %copy-done.1, bf16[4,512,256]{2,1,0:T(8,128)(2,1)} %constant.87.clone.refs_4_.refs_1_, bf16[4,512,256]{2,1,0:T(8,128)(2,1)} %constant.88.clone.refs_5_.refs_2_), custom_call_target="tpu_custom_call" | custom-call | flops 99999997952 | bytes 3670016 | tf_op jit(solution)/shard_map/correlate/pallas_call | solution.py:134
  101.7 7.3 %all-to-all-start.3 = ((bf16[16,4,2,16,128]{4,3,2,1,0:T(8,128)(2,1)}), bf16[16,4,2,16,128]{4,3,2,1,0:T(8,128)(2,1)S(1)}, u32[]{:S(2)}, u32[]{:S(2)}) async-start(bf16[16,4,2,16,128]{4,3,2,1,0:T(8,128)(2,1)} %correlate.3), calls=%async_computation.3 | async-start | bytes 1048576 | tf_op jit(solution)/shard_map/all_to_all | solution.py:352
  109.0 0.0 collective-permute-done.8.refs_0_
  109.0 0.0 collective-permute-done.9.refs_1_
  109.0 0.0 collective-permute-done.10.refs_2_
  109.1 0.0 collective-permute-done.11.refs_3_
  109.1 0.9 gather.3
  110.0 8.0 %all-to-all-done.3 = bf16[16,4,2,16,128]{4,3,2,1,0:T(8,128)(2,1)S(1)} async-done(((bf16[16,4,2,16,128]{4,3,2,1,0:T(8,128)(2,1)}), bf16[16,4,2,16,128]{4,3,2,1,0:T(8,128)(2,1)S(1)}, u32[]{:S(2)}, u32[]{:S(2)}) %all-to-all-start.3) | async-done | bytes 524320 | tf_op jit(solution)/shard_map/all_to_all | solution.py:352
  118.1 2.2 %collective-permute-start.15 = (bf16[16,2,16,128]{3,2,1,0:T(8,128)(2,1)S(1)}, bf16[16,2,16,128]{3,2,1,0:T(8,128)(2,1)S(1)}, u32[]{:S(2)}, u32[]{:S(2)}) collective-permute-start(bf16[16,2,16,128]{3,2,1,0:T(8,128)(2,1)S(1)} %get-tuple-element.33), channel_id=1, source_target_pairs={{0,130},{1,131},{2,192},{3,193},{4,134},{5,135},{6,196},{7,197},{8... | collective-permute-start | bytes 393224 | tf_op jit(solution)/shard_map/ppermute | solution.py:48
  120.2 1.1 collective-permute-start.14
  121.4 0.3 collective-permute-start.13
  121.7 2.4 %collective-permute-start.12 = (bf16[16,2,16,128]{3,2,1,0:T(8,128)(2,1)S(1)}, bf16[16,2,16,128]{3,2,1,0:T(8,128)(2,1)S(1)}, u32[]{:S(2)}, u32[]{:S(2)}) collective-permute-start(bf16[16,2,16,128]{3,2,1,0:T(8,128)(2,1)S(1)} %get-tuple-element.36), channel_id=1, source_target_pairs={{0,66},{1,67},{2,128},{3,129},{4,70},{5,71},{6,132},{7,133},{8,74}... | collective-permute-start | bytes 393224 | tf_op jit(solution)/shard_map/ppermute | solution.py:48
  124.1 3.6 %all-to-all-start.1 = ((bf16[16,4,3,16,128]{4,3,2,1,0:T(8,128)(2,1)}), bf16[16,4,3,16,128]{4,3,2,1,0:T(8,128)(2,1)S(1)}, u32[]{:S(2)}, u32[]{:S(2)}) async-start(bf16[16,4,3,16,128]{4,3,2,1,0:T(8,128)(2,1)} %gather.3), calls=%async_computation.1 | async-start | bytes 1572864 | tf_op jit(solution)/shard_map/all_to_all | solution.py:355
  127.7 0.0 collective-permute-done.15.refs_3_
  127.7 0.1 collective-permute-done.14.refs_2_
  127.8 0.0 collective-permute-done.13.refs_1_
  127.9 1.8 %collective-permute-done.12.refs_0_ = bf16[16,2,16,128]{3,2,1,0:T(8,128)(2,1)S(1)} collective-permute-done((bf16[16,2,16,128]{3,2,1,0:T(8,128)(2,1)S(1)}, bf16[16,2,16,128]{3,2,1,0:T(8,128)(2,1)S(1)}, u32[]{:S(2)}, u32[]{:S(2)}) %collective-permute-start.12) | collective-permute-done | bytes 131104 | tf_op jit(solution)/shard_map/ppermute | solution.py:48
  129.7 0.3 settle.2.refs_1_
  130.0 0.0 copy-start.2
  130.0 0.0 copy-start
  130.0 8.2 %all-to-all-done.1.refs_0_ = bf16[16,4,3,16,128]{4,3,2,1,0:T(8,128)(2,1)S(1)} async-done(((bf16[16,4,3,16,128]{4,3,2,1,0:T(8,128)(2,1)}), bf16[16,4,3,16,128]{4,3,2,1,0:T(8,128)(2,1)S(1)}, u32[]{:S(2)}, u32[]{:S(2)}) %all-to-all-start.1) | async-done | bytes 786464 | tf_op jit(solution)/shard_map/all_to_all | solution.py:355
  138.2 0.4 settle.3.own_ref
  138.6 8.5 %collective-permute-start.17 = (bf16[16,5,64,128]{3,2,1,0:T(8,128)(2,1)S(1)}, bf16[16,5,64,128]{3,2,1,0:T(8,128)(2,1)S(1)}, u32[]{:S(2)}, u32[]{:S(2)}) collective-permute-start(bf16[16,5,64,128]{3,2,1,0:T(8,128)(2,1)S(1)} %settle.3.own_ref), channel_id=1, source_target_pairs={{1,0},{2,1},{3,2},{5,4},{6,5},{7,6},{9,8},{10,9},{11,10},{13,12},{... | collective-permute-start | bytes 3932168 | tf_op jit(solution)/shard_map/ppermute | solution.py:358
  147.1 3.5 %collective-permute-start.16 = (bf16[16,5,64,128]{3,2,1,0:T(8,128)(2,1)S(1)}, bf16[16,5,64,128]{3,2,1,0:T(8,128)(2,1)}, u32[]{:S(2)}, u32[]{:S(2)}) collective-permute-start(bf16[16,5,64,128]{3,2,1,0:T(8,128)(2,1)S(1)} %settle.3.own_ref), channel_id=1, source_target_pairs={{0,1},{1,2},{2,3},{4,5},{5,6},{6,7},{8,9},{9,10},{10,11},{12,13},{... | collective-permute-start | bytes 3932168 | tf_op jit(solution)/shard_map/ppermute | solution.py:357
  150.7 0.1 copy.19
  150.9 0.1 add_select_fusion
  150.9 0.2 fusion
  151.2 0.1 copy.30.w_ref
  151.3 12.8 %collective-permute-done.17.down_ref = bf16[16,5,64,128]{3,2,1,0:T(8,128)(2,1)S(1)} collective-permute-done((bf16[16,5,64,128]{3,2,1,0:T(8,128)(2,1)S(1)}, bf16[16,5,64,128]{3,2,1,0:T(8,128)(2,1)S(1)}, u32[]{:S(2)}, u32[]{:S(2)}) %collective-permute-start.17) | collective-permute-done | bytes 1310752 | tf_op jit(solution)/shard_map/ppermute | solution.py:358
  164.0 1.2 collective-permute-done.16.up_ref
  165.2 0.0 copy-done
  165.2 4.2 %screen.1 = bf16[16,5,64,128]{3,2,1,0:T(8,128)(2,1)} custom-call(s32[1]{0:T(128)} %bitcast.row_ref, s32[4,5]{1,0:T(4,128)S(1)} %copy-done, bf16[64,192]{1,0:T(8,128)(2,1)S(1)} %copy.30.w_ref, bf16[16,5,64,128]{3,2,1,0:T(8,128)(2,1)} %collective-permute-done.16.up_ref, bf16[16,5,64,128]{3,2,1,0:T(8,128)(2,1)S(1)} %settle.3.own_ref, ...), custom_call_target="tpu_custom_call" | custom-call | flops 251658240 | bytes 5242880 | tf_op jit(solution)/shard_map/screen/pallas_call | solution.py:300
  (7 shorter events, 0.1 us)
Async XLA Ops:
  4.0 21.5 %collective-permute-start = (bf16[16,2,2,16,128]{4,3,2,1,0:T(8,128)(2,1)}, bf16[16,2,2,16,128]{4,3,2,1,0:T(8,128)(2,1)S(1)}, u32[]{:S(2)}, u32[]{:S(2)}) collective-permute-start(bf16[16,2,2,16,128]{4,3,2,1,0:T(8,128)(2,1)} %get-tuple-element.18), channel_id=1, source_target_pairs={{0,66},{1,67},{2,128},{3,129},{4,70},{5,71},{6,132},{7,133},{8,74}... | collective-permute-start | bytes 786440 | tf_op jit(solution)/shard_map/ppermute | solution.py:48
  9.2 24.7 %collective-permute-start.1 = (bf16[16,2,2,16,128]{4,3,2,1,0:T(8,128)(2,1)}, bf16[16,2,2,16,128]{4,3,2,1,0:T(8,128)(2,1)S(1)}, u32[]{:S(2)}, u32[]{:S(2)}) collective-permute-start(bf16[16,2,2,16,128]{4,3,2,1,0:T(8,128)(2,1)} %get-tuple-element.19), channel_id=1, source_target_pairs={{0,2},{1,3},{2,64},{3,65},{4,6},{5,7},{6,68},{7,69},{8,10},{9,11},... | collective-permute-start | bytes 786440 | tf_op jit(solution)/shard_map/ppermute | solution.py:48
  12.1 21.9 %collective-permute-start.2 = (bf16[16,2,2,16,128]{4,3,2,1,0:T(8,128)(2,1)}, bf16[16,2,2,16,128]{4,3,2,1,0:T(8,128)(2,1)S(1)}, u32[]{:S(2)}, u32[]{:S(2)}) collective-permute-start(bf16[16,2,2,16,128]{4,3,2,1,0:T(8,128)(2,1)} %get-tuple-element.20), channel_id=1, source_target_pairs={{0,194},{1,195},{2,0},{3,1},{4,198},{5,199},{6,4},{7,5},{8,202},{9... | collective-permute-start | bytes 786440 | tf_op jit(solution)/shard_map/ppermute | solution.py:48
  12.1 21.9 %collective-permute-start.3 = (bf16[16,2,2,16,128]{4,3,2,1,0:T(8,128)(2,1)}, bf16[16,2,2,16,128]{4,3,2,1,0:T(8,128)(2,1)S(1)}, u32[]{:S(2)}, u32[]{:S(2)}) collective-permute-start(bf16[16,2,2,16,128]{4,3,2,1,0:T(8,128)(2,1)} %get-tuple-element.21), channel_id=1, source_target_pairs={{0,130},{1,131},{2,192},{3,193},{4,134},{5,135},{6,196},{7,197},{8... | collective-permute-start | bytes 786440 | tf_op jit(solution)/shard_map/ppermute | solution.py:48
  13.7 27.5 %all-to-all-start = ((bf16[16,4,2,3,16,128]{5,4,3,2,1,0:T(8,128)(2,1)}), bf16[16,4,2,3,16,128]{5,4,3,2,1,0:T(8,128)(2,1)S(1)}, u32[]{:S(2)}, u32[]{:S(2)}) async-start(bf16[16,4,2,3,16,128]{5,4,3,2,1,0:T(8,128)(2,1)} %get-tuple-element.17), calls=%async_computation | async-start | bytes 3145728 | tf_op jit(solution)/shard_map/all_to_all | solution.py:342
  41.6 24.0 %collective-permute-start.7 = (bf16[16,2,3,16,128]{4,3,2,1,0:T(8,128)(2,1)S(1)}, bf16[16,2,3,16,128]{4,3,2,1,0:T(8,128)(2,1)S(1)}, u32[]{:S(2)}, u32[]{:S(2)}) collective-permute-start(bf16[16,2,3,16,128]{4,3,2,1,0:T(8,128)(2,1)S(1)} %get-tuple-element.29), channel_id=1, source_target_pairs={{0,130},{1,131},{2,192},{3,193},{4,134},{5,135},{6,196},{7,197},{8... | collective-permute-start | bytes 1179656 | tf_op jit(solution)/shard_map/ppermute | solution.py:48
  44.9 33.4 %collective-permute-start.6 = (bf16[16,2,3,16,128]{4,3,2,1,0:T(8,128)(2,1)S(1)}, bf16[16,2,3,16,128]{4,3,2,1,0:T(8,128)(2,1)S(1)}, u32[]{:S(2)}, u32[]{:S(2)}) collective-permute-start(bf16[16,2,3,16,128]{4,3,2,1,0:T(8,128)(2,1)S(1)} %get-tuple-element.30), channel_id=1, source_target_pairs={{0,194},{1,195},{2,0},{3,1},{4,198},{5,199},{6,4},{7,5},{8,202},{9... | collective-permute-start | bytes 1179656 | tf_op jit(solution)/shard_map/ppermute | solution.py:48
  45.6 32.7 %collective-permute-start.5 = (bf16[16,2,3,16,128]{4,3,2,1,0:T(8,128)(2,1)S(1)}, bf16[16,2,3,16,128]{4,3,2,1,0:T(8,128)(2,1)}, u32[]{:S(2)}, u32[]{:S(2)}) collective-permute-start(bf16[16,2,3,16,128]{4,3,2,1,0:T(8,128)(2,1)S(1)} %get-tuple-element.31), channel_id=1, source_target_pairs={{0,2},{1,3},{2,64},{3,65},{4,6},{5,7},{6,68},{7,69},{8,10},{9,11},... | collective-permute-start | bytes 1179656 | tf_op jit(solution)/shard_map/ppermute | solution.py:48
  46.4 32.7 %collective-permute-start.4 = (bf16[16,2,3,16,128]{4,3,2,1,0:T(8,128)(2,1)S(1)}, bf16[16,2,3,16,128]{4,3,2,1,0:T(8,128)(2,1)}, u32[]{:S(2)}, u32[]{:S(2)}) collective-permute-start(bf16[16,2,3,16,128]{4,3,2,1,0:T(8,128)(2,1)S(1)} %get-tuple-element.32), channel_id=1, source_target_pairs={{0,66},{1,67},{2,128},{3,129},{4,70},{5,71},{6,132},{7,133},{8,74}... | collective-permute-start | bytes 1179656 | tf_op jit(solution)/shard_map/ppermute | solution.py:48
  47.7 45.7 %all-to-all-start.2 = ((bf16[16,4,2,2,16,128]{5,4,3,2,1,0:T(8,128)(2,1)}), bf16[16,4,2,2,16,128]{5,4,3,2,1,0:T(8,128)(2,1)S(1)}, u32[]{:S(2)}, u32[]{:S(2)}) async-start(bf16[16,4,2,2,16,128]{5,4,3,2,1,0:T(8,128)(2,1)} %gather.2), calls=%async_computation.2 | async-start | bytes 2097152 | tf_op jit(solution)/shard_map/all_to_all | solution.py:345
  65.6 13.6 %copy-start.3 = (bf16[16,2,3,16,128]{4,3,2,1,0:T(8,128)(2,1)}, bf16[16,2,3,16,128]{4,3,2,1,0:T(8,128)(2,1)S(1)}, u32[]{:S(2)}) copy-start(bf16[16,2,3,16,128]{4,3,2,1,0:T(8,128)(2,1)S(1)} %collective-permute-done.7.refs_3_) | copy-start | bytes 1179652
  78.3 0.8 copy-start.4
  87.4 21.7 %collective-permute-start.8 = (bf16[16,3,16,128]{3,2,1,0:T(8,128)(2,1)S(1)}, bf16[16,3,16,128]{3,2,1,0:T(8,128)(2,1)S(1)}, u32[]{:S(2)}, u32[]{:S(2)}) collective-permute-start(bf16[16,3,16,128]{3,2,1,0:T(8,128)(2,1)S(1)} %get-tuple-element.23), channel_id=1, source_target_pairs={{0,66},{1,67},{2,128},{3,129},{4,70},{5,71},{6,132},{7,133},{8,74}... | collective-permute-start | bytes 589832 | tf_op jit(solution)/shard_map/ppermute | solution.py:48
  88.1 20.9 %collective-permute-start.9 = (bf16[16,3,16,128]{3,2,1,0:T(8,128)(2,1)S(1)}, bf16[16,3,16,128]{3,2,1,0:T(8,128)(2,1)S(1)}, u32[]{:S(2)}, u32[]{:S(2)}) collective-permute-start(bf16[16,3,16,128]{3,2,1,0:T(8,128)(2,1)S(1)} %get-tuple-element.24), channel_id=1, source_target_pairs={{0,2},{1,3},{2,64},{3,65},{4,6},{5,7},{6,68},{7,69},{8,10},{9,11},... | collective-permute-start | bytes 589832 | tf_op jit(solution)/shard_map/ppermute | solution.py:48
  89.4 19.6 %collective-permute-start.10 = (bf16[16,3,16,128]{3,2,1,0:T(8,128)(2,1)S(1)}, bf16[16,3,16,128]{3,2,1,0:T(8,128)(2,1)S(1)}, u32[]{:S(2)}, u32[]{:S(2)}) collective-permute-start(bf16[16,3,16,128]{3,2,1,0:T(8,128)(2,1)S(1)} %get-tuple-element.25), channel_id=1, source_target_pairs={{0,194},{1,195},{2,0},{3,1},{4,198},{5,199},{6,4},{7,5},{8,202},{9... | collective-permute-start | bytes 589832 | tf_op jit(solution)/shard_map/ppermute | solution.py:48
  90.8 18.3 %collective-permute-start.11 = (bf16[16,3,16,128]{3,2,1,0:T(8,128)(2,1)S(1)}, bf16[16,3,16,128]{3,2,1,0:T(8,128)(2,1)S(1)}, u32[]{:S(2)}, u32[]{:S(2)}) collective-permute-start(bf16[16,3,16,128]{3,2,1,0:T(8,128)(2,1)S(1)} %get-tuple-element.26), channel_id=1, source_target_pairs={{0,130},{1,131},{2,192},{3,193},{4,134},{5,135},{6,196},{7,197},{8... | collective-permute-start | bytes 589832 | tf_op jit(solution)/shard_map/ppermute | solution.py:48
  93.4 1.0 copy-start.1
  101.7 16.3 %all-to-all-start.3 = ((bf16[16,4,2,16,128]{4,3,2,1,0:T(8,128)(2,1)}), bf16[16,4,2,16,128]{4,3,2,1,0:T(8,128)(2,1)S(1)}, u32[]{:S(2)}, u32[]{:S(2)}) async-start(bf16[16,4,2,16,128]{4,3,2,1,0:T(8,128)(2,1)} %correlate.3), calls=%async_computation.3 | async-start | bytes 1048576 | tf_op jit(solution)/shard_map/all_to_all | solution.py:352
  118.1 9.6 %collective-permute-start.15 = (bf16[16,2,16,128]{3,2,1,0:T(8,128)(2,1)S(1)}, bf16[16,2,16,128]{3,2,1,0:T(8,128)(2,1)S(1)}, u32[]{:S(2)}, u32[]{:S(2)}) collective-permute-start(bf16[16,2,16,128]{3,2,1,0:T(8,128)(2,1)S(1)} %get-tuple-element.33), channel_id=1, source_target_pairs={{0,130},{1,131},{2,192},{3,193},{4,134},{5,135},{6,196},{7,197},{8... | collective-permute-start | bytes 393224 | tf_op jit(solution)/shard_map/ppermute | solution.py:48
  120.2 7.6 %collective-permute-start.14 = (bf16[16,2,16,128]{3,2,1,0:T(8,128)(2,1)S(1)}, bf16[16,2,16,128]{3,2,1,0:T(8,128)(2,1)S(1)}, u32[]{:S(2)}, u32[]{:S(2)}) collective-permute-start(bf16[16,2,16,128]{3,2,1,0:T(8,128)(2,1)S(1)} %get-tuple-element.34), channel_id=1, source_target_pairs={{0,194},{1,195},{2,0},{3,1},{4,198},{5,199},{6,4},{7,5},{8,202},{9... | collective-permute-start | bytes 393224 | tf_op jit(solution)/shard_map/ppermute | solution.py:48
  121.4 6.5 %collective-permute-start.13 = (bf16[16,2,16,128]{3,2,1,0:T(8,128)(2,1)S(1)}, bf16[16,2,16,128]{3,2,1,0:T(8,128)(2,1)S(1)}, u32[]{:S(2)}, u32[]{:S(2)}) collective-permute-start(bf16[16,2,16,128]{3,2,1,0:T(8,128)(2,1)S(1)} %get-tuple-element.35), channel_id=1, source_target_pairs={{0,2},{1,3},{2,64},{3,65},{4,6},{5,7},{6,68},{7,69},{8,10},{9,11},... | collective-permute-start | bytes 393224 | tf_op jit(solution)/shard_map/ppermute | solution.py:48
  121.7 7.9 %collective-permute-start.12 = (bf16[16,2,16,128]{3,2,1,0:T(8,128)(2,1)S(1)}, bf16[16,2,16,128]{3,2,1,0:T(8,128)(2,1)S(1)}, u32[]{:S(2)}, u32[]{:S(2)}) collective-permute-start(bf16[16,2,16,128]{3,2,1,0:T(8,128)(2,1)S(1)} %get-tuple-element.36), channel_id=1, source_target_pairs={{0,66},{1,67},{2,128},{3,129},{4,70},{5,71},{6,132},{7,133},{8,74}... | collective-permute-start | bytes 393224 | tf_op jit(solution)/shard_map/ppermute | solution.py:48
  124.1 14.1 %all-to-all-start.1 = ((bf16[16,4,3,16,128]{4,3,2,1,0:T(8,128)(2,1)}), bf16[16,4,3,16,128]{4,3,2,1,0:T(8,128)(2,1)S(1)}, u32[]{:S(2)}, u32[]{:S(2)}) async-start(bf16[16,4,3,16,128]{4,3,2,1,0:T(8,128)(2,1)} %gather.3), calls=%async_computation.1 | async-start | bytes 1572864 | tf_op jit(solution)/shard_map/all_to_all | solution.py:355
  130.0 20.7 %copy-start.2 = (bf16[1,64,192]{2,1,0:T(8,128)(2,1)S(1)}, bf16[1,64,192]{2,1,0:T(8,128)(2,1)}, u32[]{:S(2)}) copy-start(bf16[1,64,192]{2,1,0:T(8,128)(2,1)} %param.8) | copy-start | bytes 73732
  130.0 35.3 %copy-start = (s32[4,5]{1,0:T(4,128)S(1)}, s32[4,5]{1,0:T(4,128)}, u32[]{:S(2)}) copy-start(s32[4,5]{1,0:T(4,128)} %pattern_ref.1) | copy-start | bytes 244
  138.6 25.4 %collective-permute-start.17 = (bf16[16,5,64,128]{3,2,1,0:T(8,128)(2,1)S(1)}, bf16[16,5,64,128]{3,2,1,0:T(8,128)(2,1)S(1)}, u32[]{:S(2)}, u32[]{:S(2)}) collective-permute-start(bf16[16,5,64,128]{3,2,1,0:T(8,128)(2,1)S(1)} %settle.3.own_ref), channel_id=1, source_target_pairs={{1,0},{2,1},{3,2},{5,4},{6,5},{7,6},{9,8},{10,9},{11,10},{13,12},{... | collective-permute-start | bytes 3932168 | tf_op jit(solution)/shard_map/ppermute | solution.py:358
  147.1 18.1 %collective-permute-start.16 = (bf16[16,5,64,128]{3,2,1,0:T(8,128)(2,1)S(1)}, bf16[16,5,64,128]{3,2,1,0:T(8,128)(2,1)}, u32[]{:S(2)}, u32[]{:S(2)}) collective-permute-start(bf16[16,5,64,128]{3,2,1,0:T(8,128)(2,1)S(1)} %settle.3.own_ref), channel_id=1, source_target_pairs={{0,1},{1,2},{2,3},{4,5},{5,6},{6,7},{8,9},{9,10},{10,11},{12,13},{... | collective-permute-start | bytes 3932168 | tf_op jit(solution)/shard_map/ppermute | solution.py:357

commit v4 on v3

--- a/solution.py
+++ b/solution.py
@@ -36,6 +36,10 @@
     forward = np.stack([np.concatenate([r.T, i.T]) for r, i in out])
     inverse = np.stack([np.concatenate([r, i]) for r, i in out])
     return forward, inverse
+
+
+def after(value, other):
+    return lax.optimization_barrier([value, other])[0]
 
 
 def hop(piece, step):
@@ -124,7 +128,7 @@
                     outs[0][p : p + 2, j, s] = v
 
 
-def correlate(rot, inputs, fwd, inv, split):
+def correlate(rot, inputs, fwd, inv, split, flops):
     slots = inputs[0].shape[-3]
     n = slots * 128
     vmem = pl.BlockSpec(memory_space=pltpu.VMEM)
@@ -145,9 +149,9 @@
             pltpu.VMEM((4, 2 * QUART, QUART), jnp.bfloat16),
             pltpu.SemaphoreType.DMA((2, 4)),
         ],
-        compiler_params=pltpu.CompilerParams(vmem_limit_bytes=53 << 20),
+        compiler_params=pltpu.CompilerParams(vmem_limit_bytes=52 << 20),
         cost_estimate=pl.CostEstimate(
-            flops=HEAVY, bytes_accessed=3 * NE * n * 2 + (2 << 20), transcendentals=0
+            flops=flops, bytes_accessed=3 * NE * n * 2 + (2 << 20), transcendentals=0
         ),
         name="correlate",
     )(rot, *inputs, fwd, inv)
@@ -257,6 +261,23 @@
     )(*pieces)
 
 
+def marker(value, pieces, flops):
+    hbm = pl.BlockSpec(memory_space=pl.ANY)
+
+    def kernel(*refs):
+        refs[-1][...] = refs[0][...]
+
+    return pl.pallas_call(
+        kernel,
+        out_shape=jax.ShapeDtypeStruct(value.shape, value.dtype),
+        in_specs=[pl.BlockSpec(memory_space=pltpu.VMEM)] + [hbm] * len(pieces),
+        out_specs=pl.BlockSpec(memory_space=pltpu.VMEM),
+        cost_estimate=pl.CostEstimate(flops=flops, bytes_accessed=4096, transcendentals=0),
+        compiler_params=pltpu.CompilerParams(vmem_limit_bytes=1 << 20),
+        name="marker",
+    )(value, *pieces)
+
+
 def screen_kernel(row_ref, pattern_ref, w_ref, up_ref, own_ref, down_ref, out_ref):
     slots = own_ref.shape[1]
     rows = pattern_ref.shape[0]
@@ -340,18 +361,19 @@
     early, late = prepare((turn % 4).reshape(1), *both, cut)
     late = gather([hop(late[j], STEPS[j]) for j in range(4)], HEAVY)
     early = lax.all_to_all(early, PLANE, split_axis=0, concat_axis=0, tiled=True)
-    early = lax.optimization_barrier([early, late])[0]
+    early = after(early, late)
     early = [hop(early[:, j], STEPS[j]) for j in range(4)]
     late = lax.all_to_all(late, PLANE, split_axis=0, concat_axis=0, tiled=True)
 
-    lo = correlate(rot, early, fwd, inv, True)
-    late = lax.optimization_barrier([late] + list(lo))[0]
-    hi = correlate(rot, [late], fwd, inv, False)
-
+    late, rot = lax.optimization_barrier([late, marker(rot, early[1:3], HEAVY)])
+    hi = correlate(rot, [late], fwd, inv, True, 0)
+    early[0] = after(early[0], hi[0])
+    lo = correlate(rot, early, fwd, inv, True, HEAVY)
+
+    hi = gather([hop(p, STEPS[j]) for j, p in enumerate(hi)], 0)
+    hi = lax.all_to_all(hi, PLANE, split_axis=0, concat_axis=0, tiled=True)
     lo = gather([hop(p, STEPS[j]) for j, p in enumerate(lo)], HEAVY)
-    hi = lax.all_to_all(hi, PLANE, split_axis=0, concat_axis=0, tiled=True)
-    hi = lax.optimization_barrier([hi, lo])[0]
-    hi = settle([hop(hi[:, j], STEPS[j]) for j in range(4)], [], HEAVY)
+    hi = settle([after(hi, lo)], [], 0)
     lo = lax.all_to_all(lo, PLANE, split_axis=0, concat_axis=0, tiled=True)
     own = settle([lo], [hi], 0)
     up = lax.ppermute(own, "s", [(0, 1), (1, 2), (2, 3)])

time: 170 us -> 185 us (1.088)
  waiting for transfers between devices: 76.5 us -> 93.6 us
    all_to_all x1, waiting for transfers between devices: 0.01 us -> 11.6 us  [shards(): late = lax.all_to_all(late, PLANE, split_axis=0, concat_axis=0, tiled=True)]
    ppermute x16, waiting for transfers between devices: 40.1 us -> 43.6 us  [hop(): return lax.ppermute(piece, ALL, perm)]
    ppermute x1, starting transfers between devices: 3.55 us -> 6.95 us  [shards(): up = lax.ppermute(own, 's', [(0, 1), (1, 2), (2, 3)])]
    all_to_all x1, starting transfers between devices: 7.34 us -> 4.49 us  [shards(): hi = lax.all_to_all(hi, PLANE, split_axis=0, concat_axis=0, tiled=True)]
    all_to_all x1, waiting for transfers between devices: 8.22 us -> 10.1 us  [shards(): lo = lax.all_to_all(lo, PLANE, split_axis=0, concat_axis=0, tiled=True)]
    pallas_call x2, Pallas kernels: 15.5 us -> 13.7 us  [correlate(): pl.pallas_call(functools.partial(correlate_kernel, slots, len(inputs), sp...]
  transfers between devices with their start and end apart: 22 -> 22, of which waited for: 11 -> 10; matrix products, arithmetic and copies ran while one was open for 0% -> 0% of each run, Pallas kernels for 11% -> 9%
where the time goes in v4:
time: 185 us; the launch traced here: 184 us
  waiting for transfers between devices  93.6 us (51%)
  starting transfers between devices  63.5 us (34%)
  Pallas kernels  25.4 us (14%)
    ppermute x16, waiting for transfers between devices, hop(): return lax.ppermute(piece, ALL, perm)  43.6 us
    ppermute x16, starting transfers between devices, hop(): return lax.ppermute(piece, ALL, perm)  27.4 us
    pallas_call x2, Pallas kernels, correlate(): pl.pallas_call(functools.partial(correlate_kernel, slots, len(inputs), sp...  13.7 us
    ppermute x1, waiting for transfers between devices, shards(): down = lax.ppermute(own, 's', [(1, 0), (2, 1), (3, 2)])  12.8 us
    all_to_all x1, waiting for transfers between devices, shards(): late = lax.all_to_all(late, PLANE, split_axis=0, concat_axis=0, tiled=True)  11.6 us
    all_to_all x1, waiting for transfers between devices, shards(): lo = lax.all_to_all(lo, PLANE, split_axis=0, concat_axis=0, tiled=True)  10.1 us
    ppermute x1, starting transfers between devices, shards(): down = lax.ppermute(own, 's', [(1, 0), (2, 1), (3, 2)])  8.74 us
    all_to_all x1, waiting for transfers between devices, shards(): hi = lax.all_to_all(hi, PLANE, split_axis=0, concat_axis=0, tiled=True)  8.03 us
  transfers between devices with their start and end apart: 22, of which 10 were waited for; matrix products, arithmetic and copies ran while one was open for 0% of the time, Pallas kernels for 9%

profile of v4, /device:TPU:1, one launch (start us, length us, event | category | flops | bytes accessed | tf_op | source)
XLA Modules:
  0.0 184.5 jit_solution(14988859989685279883)
XLA Ops:
  0.0 4.0 %prepare.1 = (bf16[16,4,2,3,16,128]{5,4,3,2,1,0:T(8,128)(2,1)}, bf16[16,2,2,16,128]{4,3,2,1,0:T(8,128)(2,1)}, bf16[16,2,2,16,128]{4,3,2,1,0:T(8,128)(2,1)}, bf16...) custom-call(s32[1]{0:T(128)} %bitcast.6.turn_ref, bf16[16,5,64,128]{3,2,1,0:T(8,128)(2,1)} %bitcast.27, ...), custom_call_target="tpu_custom_call" | custom-call | bytes 5242880 | tf_op jit(solution)/shard_map/prepare/pallas_call | solution.py:200
  4.0 5.2 %collective-permute-start = (bf16[16,2,2,16,128]{4,3,2,1,0:T(8,128)(2,1)}, bf16[16,2,2,16,128]{4,3,2,1,0:T(8,128)(2,1)S(1)}, u32[]{:S(2)}, u32[]{:S(2)}) collective-permute-start(bf16[16,2,2,16,128]{4,3,2,1,0:T(8,128)(2,1)} %get-tuple-element.23), channel_id=1, source_target_pairs={{0,66},{1,67},{2,128},{3,129},{4,70},{5,71},{6,132},{7,133},{8,74}... | collective-permute-start | bytes 786440 | tf_op jit(solution)/shard_map/ppermute | solution.py:52
  9.2 2.8 %collective-permute-start.1 = (bf16[16,2,2,16,128]{4,3,2,1,0:T(8,128)(2,1)}, bf16[16,2,2,16,128]{4,3,2,1,0:T(8,128)(2,1)S(1)}, u32[]{:S(2)}, u32[]{:S(2)}) collective-permute-start(bf16[16,2,2,16,128]{4,3,2,1,0:T(8,128)(2,1)} %get-tuple-element.24), channel_id=1, source_target_pairs={{0,2},{1,3},{2,64},{3,65},{4,6},{5,7},{6,68},{7,69},{8,10},{9,11},... | collective-permute-start | bytes 786440 | tf_op jit(solution)/shard_map/ppermute | solution.py:52
  12.1 0.0 collective-permute-start.2
  12.1 1.6 collective-permute-start.3
  13.7 6.8 %all-to-all-start.1 = ((bf16[16,4,2,3,16,128]{5,4,3,2,1,0:T(8,128)(2,1)}), bf16[16,4,2,3,16,128]{5,4,3,2,1,0:T(8,128)(2,1)S(1)}, u32[]{:S(2)}, u32[]{:S(2)}) async-start(bf16[16,4,2,3,16,128]{5,4,3,2,1,0:T(8,128)(2,1)} %get-tuple-element.27), calls=%async_computation.1 | async-start | bytes 3145728 | tf_op jit(solution)/shard_map/all_to_all | solution.py:363
  20.5 5.0 %collective-permute-done.refs_0_ = bf16[16,2,2,16,128]{4,3,2,1,0:T(8,128)(2,1)S(1)} collective-permute-done((bf16[16,2,2,16,128]{4,3,2,1,0:T(8,128)(2,1)}, bf16[16,2,2,16,128]{4,3,2,1,0:T(8,128)(2,1)S(1)}, u32[]{:S(2)}, u32[]{:S(2)}) %collective-permute-start) | collective-permute-done | bytes 262176 | tf_op jit(solution)/shard_map/ppermute | solution.py:52
  25.5 8.5 %collective-permute-done.1.refs_1_ = bf16[16,2,2,16,128]{4,3,2,1,0:T(8,128)(2,1)S(1)} collective-permute-done((bf16[16,2,2,16,128]{4,3,2,1,0:T(8,128)(2,1)}, bf16[16,2,2,16,128]{4,3,2,1,0:T(8,128)(2,1)S(1)}, u32[]{:S(2)}, u32[]{:S(2)}) %collective-permute-start.1) | collective-permute-done | bytes 262176 | tf_op jit(solution)/shard_map/ppermute | solution.py:52
  34.0 0.0 collective-permute-done.2.refs_2_
  34.0 0.0 collective-permute-done.3.refs_3_
  34.0 1.0 gather.3
  35.0 6.2 %all-to-all-done.1 = bf16[16,4,2,3,16,128]{5,4,3,2,1,0:T(8,128)(2,1)S(1)} async-done(((bf16[16,4,2,3,16,128]{5,4,3,2,1,0:T(8,128)(2,1)}), bf16[16,4,2,3,16,128]{5,4,3,2,1,0:T(8,128)(2,1)S(1)}, u32[]{:S(2)}, u32[]{:S(2)}) %all-to-all-start.1) | async-done | bytes 1572896 | tf_op jit(solution)/shard_map/all_to_all | solution.py:363
  41.3 1.1 slice_bitcast_fusion
  42.4 2.4 %collective-permute-start.5 = (bf16[16,2,3,16,128]{4,3,2,1,0:T(8,128)(2,1)}, bf16[16,2,3,16,128]{4,3,2,1,0:T(8,128)(2,1)S(1)}, u32[]{:S(2)}, u32[]{:S(2)}) collective-permute-start(bf16[16,2,3,16,128]{4,3,2,1,0:T(8,128)(2,1)} %get-tuple-element.43), channel_id=1, source_target_pairs={{0,194},{1,195},{2,0},{3,1},{4,198},{5,199},{6,4},{7,5},{8,202},{9... | collective-permute-start | bytes 1179656 | tf_op jit(solution)/shard_map/ppermute | solution.py:52
  44.8 0.0 collective-permute-start.4
  44.8 0.1 pad_maximum_fusion.refs_0_
  44.9 5.5 %all-to-all-start = ((bf16[16,4,2,2,16,128]{5,4,3,2,1,0:T(8,128)(2,1)}), bf16[16,4,2,2,16,128]{5,4,3,2,1,0:T(8,128)(2,1)S(1)}, u32[]{:S(2)}, u32[]{:S(2)}) async-start(bf16[16,4,2,2,16,128]{5,4,3,2,1,0:T(8,128)(2,1)} %gather.3), calls=%async_computation | async-start | bytes 2097152 | tf_op jit(solution)/shard_map/all_to_all | solution.py:366
  50.3 2.4 %collective-permute-start.7 = (bf16[16,2,3,16,128]{4,3,2,1,0:T(8,128)(2,1)S(1)}, bf16[16,2,3,16,128]{4,3,2,1,0:T(8,128)(2,1)}, u32[]{:S(2)}, u32[]{:S(2)}) collective-permute-start(bf16[16,2,3,16,128]{4,3,2,1,0:T(8,128)(2,1)S(1)} %get-tuple-element.41), channel_id=1, source_target_pairs={{0,130},{1,131},{2,192},{3,193},{4,134},{5,135},{6,196},{7,197},{8... | collective-permute-start | bytes 1179656 | tf_op jit(solution)/shard_map/ppermute | solution.py:52
  52.8 0.0 copy-done.1
  52.8 0.9 collective-permute-start.6
  53.7 0.0 collective-permute-done.5.refs_2_
  53.7 0.0 collective-permute-done.4.refs_1_
  53.7 11.6 %all-to-all-done.refs_0_ = bf16[16,4,2,2,16,128]{5,4,3,2,1,0:T(8,128)(2,1)S(1)} async-done(((bf16[16,4,2,2,16,128]{5,4,3,2,1,0:T(8,128)(2,1)}), bf16[16,4,2,2,16,128]{5,4,3,2,1,0:T(8,128)(2,1)S(1)}, u32[]{:S(2)}, u32[]{:S(2)}) %all-to-all-start) | async-done | bytes 1048608 | tf_op jit(solution)/shard_map/all_to_all | solution.py:366
  65.3 5.8 %correlate.2 = (bf16[16,2,16,128]{3,2,1,0:T(8,128)(2,1)S(1)}, bf16[16,2,16,128]{3,2,1,0:T(8,128)(2,1)S(1)}, bf16[16,2,16,128]{3,2,1,0:T(8,128)(2,1)S(1)}, bf16[16,2,16,128]{3,2,1,0:T(8,128)(2,1)S(1)}) custom-call(f32[3]{0:T(128)S(1)} %marker.1.rot_ref, bf16[16,4,2,2,16,128]{5,4,3,2,1,0:T(8,128)(2,1)S(1)} %all-to-all-done.refs_0_, ...), custom_call_target="tpu_custom_call" | custom-call | bytes 3670016 | tf_op jit(solution)/shard_map/correlate/pallas_call | solution.py:138
  71.2 11.6 %collective-permute-done.6.refs_0_ = bf16[16,2,3,16,128]{4,3,2,1,0:T(8,128)(2,1)S(1)} collective-permute-done((bf16[16,2,3,16,128]{4,3,2,1,0:T(8,128)(2,1)S(1)}, bf16[16,2,3,16,128]{4,3,2,1,0:T(8,128)(2,1)S(1)}, u32[]{:S(2)}, u32[]{:S(2)}) %collective-permute-start.6) | collective-permute-done | bytes 393248 | tf_op jit(solution)/shard_map/ppermute | solution.py:52
  82.8 0.0 collective-permute-start.13
  82.8 2.7 %collective-permute-start.14 = (bf16[16,2,16,128]{3,2,1,0:T(8,128)(2,1)S(1)}, bf16[16,2,16,128]{3,2,1,0:T(8,128)(2,1)S(1)}, u32[]{:S(2)}, u32[]{:S(2)}) collective-permute-start(bf16[16,2,16,128]{3,2,1,0:T(8,128)(2,1)S(1)} %get-tuple-element.38), channel_id=1, source_target_pairs={{0,194},{1,195},{2,0},{3,1},{4,198},{5,199},{6,4},{7,5},{8,202},{9... | collective-permute-start | bytes 393224 | tf_op jit(solution)/shard_map/ppermute | solution.py:52
  85.4 0.7 collective-permute-start.15
  86.1 0.0 collective-permute-done.7.refs_3_
  86.1 7.9 %correlate.3 = (bf16[16,3,16,128]{3,2,1,0:T(8,128)(2,1)S(1)}, bf16[16,3,16,128]{3,2,1,0:T(8,128)(2,1)S(1)}, bf16[16,3,16,128]{3,2,1,0:T(8,128)(2,1)S(1)}, bf16[16,3,16,128]{3,2,1,0:T(8,128)(2,1)S(1)}) custom-call(f32[3]{0:T(128)S(1)} %marker.1.rot_ref, bf16[16,2,3,16,128]{4,3,2,1,0:T(8,128)(2,1)S(1)} %collective-permute-done.6.refs_0_, ...), custom_call_target="tpu_custom_call" | custom-call | flops 99999997952 | bytes 4456448 | tf_op jit(solution)/shard_map/correlate/pallas_call | solution.py:138
  94.0 2.7 %collective-permute-start.8 = (bf16[16,3,16,128]{3,2,1,0:T(8,128)(2,1)S(1)}, bf16[16,3,16,128]{3,2,1,0:T(8,128)(2,1)S(1)}, u32[]{:S(2)}, u32[]{:S(2)}) collective-permute-start(bf16[16,3,16,128]{3,2,1,0:T(8,128)(2,1)S(1)} %get-tuple-element.33), channel_id=1, source_target_pairs={{0,66},{1,67},{2,128},{3,129},{4,70},{5,71},{6,132},{7,133},{8,74}... | collective-permute-start | bytes 589832 | tf_op jit(solution)/shard_map/ppermute | solution.py:52
  96.7 0.0 collective-permute-start.9
  96.7 0.0 collective-permute-done.13.refs_1_
  96.7 2.7 %collective-permute-start.10 = (bf16[16,3,16,128]{3,2,1,0:T(8,128)(2,1)S(1)}, bf16[16,3,16,128]{3,2,1,0:T(8,128)(2,1)S(1)}, u32[]{:S(2)}, u32[]{:S(2)}) collective-permute-start(bf16[16,3,16,128]{3,2,1,0:T(8,128)(2,1)S(1)} %get-tuple-element.35), channel_id=1, source_target_pairs={{0,194},{1,195},{2,0},{3,1},{4,198},{5,199},{6,4},{7,5},{8,202},{9... | collective-permute-start | bytes 589832 | tf_op jit(solution)/shard_map/ppermute | solution.py:52
  99.4 0.0 collective-permute-done.14.refs_2_
  99.4 0.7 collective-permute-start.11
  100.0 0.0 collective-permute-done.15.refs_3_
  100.0 2.6 %collective-permute-start.12 = (bf16[16,2,16,128]{3,2,1,0:T(8,128)(2,1)S(1)}, bf16[16,2,16,128]{3,2,1,0:T(8,128)(2,1)S(1)}, u32[]{:S(2)}, u32[]{:S(2)}) collective-permute-start(bf16[16,2,16,128]{3,2,1,0:T(8,128)(2,1)S(1)} %get-tuple-element.31), channel_id=1, source_target_pairs={{0,66},{1,67},{2,128},{3,129},{4,70},{5,71},{6,132},{7,133},{8,74}... | collective-permute-start | bytes 393224 | tf_op jit(solution)/shard_map/ppermute | solution.py:52
  102.6 18.5 %collective-permute-done.12.refs_0_ = bf16[16,2,16,128]{3,2,1,0:T(8,128)(2,1)S(1)} collective-permute-done((bf16[16,2,16,128]{3,2,1,0:T(8,128)(2,1)S(1)}, bf16[16,2,16,128]{3,2,1,0:T(8,128)(2,1)S(1)}, u32[]{:S(2)}, u32[]{:S(2)}) %collective-permute-start.12) | collective-permute-done | bytes 131104 | tf_op jit(solution)/shard_map/ppermute | solution.py:52
  121.1 0.8 gather.5
  122.0 4.5 %all-to-all-start.3 = ((bf16[16,4,2,16,128]{4,3,2,1,0:T(8,128)(2,1)}), bf16[16,4,2,16,128]{4,3,2,1,0:T(8,128)(2,1)S(1)}, u32[]{:S(2)}, u32[]{:S(2)}) async-start(bf16[16,4,2,16,128]{4,3,2,1,0:T(8,128)(2,1)} %gather.5), calls=%async_computation.3 | async-start | bytes 1048576 | tf_op jit(solution)/shard_map/all_to_all | solution.py:374
  126.5 0.0 collective-permute-done.8.refs_0_
  126.5 0.0 collective-permute-done.9.refs_1_
  126.5 0.0 collective-permute-done.10.refs_2_
  126.5 0.0 collective-permute-done.11.refs_3_
  126.5 0.9 gather.4
  127.5 8.0 %all-to-all-done.3.refs_0_ = bf16[16,4,2,16,128]{4,3,2,1,0:T(8,128)(2,1)S(1)} async-done(((bf16[16,4,2,16,128]{4,3,2,1,0:T(8,128)(2,1)}), bf16[16,4,2,16,128]{4,3,2,1,0:T(8,128)(2,1)S(1)}, u32[]{:S(2)}, u32[]{:S(2)}) %all-to-all-start.3) | async-done | bytes 524320 | tf_op jit(solution)/shard_map/all_to_all | solution.py:374
  135.5 3.6 %all-to-all-start.2 = ((bf16[16,4,3,16,128]{4,3,2,1,0:T(8,128)(2,1)}), bf16[16,4,3,16,128]{4,3,2,1,0:T(8,128)(2,1)S(1)}, u32[]{:S(2)}, u32[]{:S(2)}) async-start(bf16[16,4,3,16,128]{4,3,2,1,0:T(8,128)(2,1)} %gather.4), calls=%async_computation.2 | async-start | bytes 1572864 | tf_op jit(solution)/shard_map/all_to_all | solution.py:377
  139.1 0.0 copy-start.2
  139.1 0.3 settle.2.refs_1_
  139.4 0.0 copy-start
  139.4 10.1 %all-to-all-done.2.refs_0_ = bf16[16,4,3,16,128]{4,3,2,1,0:T(8,128)(2,1)S(1)} async-done(((bf16[16,4,3,16,128]{4,3,2,1,0:T(8,128)(2,1)}), bf16[16,4,3,16,128]{4,3,2,1,0:T(8,128)(2,1)S(1)}, u32[]{:S(2)}, u32[]{:S(2)}) %all-to-all-start.2) | async-done | bytes 786464 | tf_op jit(solution)/shard_map/all_to_all | solution.py:377
  149.6 0.4 settle.3.own_ref
  150.0 8.7 %collective-permute-start.17 = (bf16[16,5,64,128]{3,2,1,0:T(8,128)(2,1)S(1)}, bf16[16,5,64,128]{3,2,1,0:T(8,128)(2,1)S(1)}, u32[]{:S(2)}, u32[]{:S(2)}) collective-permute-start(bf16[16,5,64,128]{3,2,1,0:T(8,128)(2,1)S(1)} %settle.3.own_ref), channel_id=1, source_target_pairs={{1,0},{2,1},{3,2},{5,4},{6,5},{7,6},{9,8},{10,9},{11,10},{13,12},{... | collective-permute-start | bytes 3932168 | tf_op jit(solution)/shard_map/ppermute | solution.py:380
  158.7 7.0 %collective-permute-start.16 = (bf16[16,5,64,128]{3,2,1,0:T(8,128)(2,1)S(1)}, bf16[16,5,64,128]{3,2,1,0:T(8,128)(2,1)}, u32[]{:S(2)}, u32[]{:S(2)}) collective-permute-start(bf16[16,5,64,128]{3,2,1,0:T(8,128)(2,1)S(1)} %settle.3.own_ref), channel_id=1, source_target_pairs={{0,1},{1,2},{2,3},{4,5},{5,6},{6,7},{8,9},{9,10},{10,11},{12,13},{... | collective-permute-start | bytes 3932168 | tf_op jit(solution)/shard_map/ppermute | solution.py:379
  165.7 0.0 copy-done.2
  165.7 0.1 copy.17
  165.9 0.1 add_select_fusion
  165.9 0.2 fusion
  166.2 0.1 copy.24.w_ref
  166.3 12.8 %collective-permute-done.17.down_ref = bf16[16,5,64,128]{3,2,1,0:T(8,128)(2,1)S(1)} collective-permute-done((bf16[16,5,64,128]{3,2,1,0:T(8,128)(2,1)S(1)}, bf16[16,5,64,128]{3,2,1,0:T(8,128)(2,1)S(1)}, u32[]{:S(2)}, u32[]{:S(2)}) %collective-permute-start.17) | collective-permute-done | bytes 1310752 | tf_op jit(solution)/shard_map/ppermute | solution.py:380
  179.0 1.2 collective-permute-done.16.up_ref
  180.2 0.0 copy-done
  180.2 4.2 %screen.1 = bf16[16,5,64,128]{3,2,1,0:T(8,128)(2,1)} custom-call(s32[1]{0:T(128)} %bitcast.row_ref, s32[4,5]{1,0:T(4,128)S(1)} %copy-done, bf16[64,192]{1,0:T(8,128)(2,1)S(1)} %copy.24.w_ref, bf16[16,5,64,128]{3,2,1,0:T(8,128)(2,1)} %collective-permute-done.16.up_ref, bf16[16,5,64,128]{3,2,1,0:T(8,128)(2,1)S(1)} %settle.3.own_ref, ...), custom_call_target="tpu_custom_call" | custom-call | flops 251658240 | bytes 5242880 | tf_op jit(solution)/shard_map/screen/pallas_call | solution.py:321
  (4 shorter events, 0.0 us)
Async XLA Ops:
  4.0 21.5 %collective-permute-start = (bf16[16,2,2,16,128]{4,3,2,1,0:T(8,128)(2,1)}, bf16[16,2,2,16,128]{4,3,2,1,0:T(8,128)(2,1)S(1)}, u32[]{:S(2)}, u32[]{:S(2)}) collective-permute-start(bf16[16,2,2,16,128]{4,3,2,1,0:T(8,128)(2,1)} %get-tuple-element.23), channel_id=1, source_target_pairs={{0,66},{1,67},{2,128},{3,129},{4,70},{5,71},{6,132},{7,133},{8,74}... | collective-permute-start | bytes 786440 | tf_op jit(solution)/shard_map/ppermute | solution.py:52
  9.2 24.7 %collective-permute-start.1 = (bf16[16,2,2,16,128]{4,3,2,1,0:T(8,128)(2,1)}, bf16[16,2,2,16,128]{4,3,2,1,0:T(8,128)(2,1)S(1)}, u32[]{:S(2)}, u32[]{:S(2)}) collective-permute-start(bf16[16,2,2,16,128]{4,3,2,1,0:T(8,128)(2,1)} %get-tuple-element.24), channel_id=1, source_target_pairs={{0,2},{1,3},{2,64},{3,65},{4,6},{5,7},{6,68},{7,69},{8,10},{9,11},... | collective-permute-start | bytes 786440 | tf_op jit(solution)/shard_map/ppermute | solution.py:52
  12.1 21.9 %collective-permute-start.2 = (bf16[16,2,2,16,128]{4,3,2,1,0:T(8,128)(2,1)}, bf16[16,2,2,16,128]{4,3,2,1,0:T(8,128)(2,1)S(1)}, u32[]{:S(2)}, u32[]{:S(2)}) collective-permute-start(bf16[16,2,2,16,128]{4,3,2,1,0:T(8,128)(2,1)} %get-tuple-element.25), channel_id=1, source_target_pairs={{0,194},{1,195},{2,0},{3,1},{4,198},{5,199},{6,4},{7,5},{8,202},{9... | collective-permute-start | bytes 786440 | tf_op jit(solution)/shard_map/ppermute | solution.py:52
  12.1 21.9 %collective-permute-start.3 = (bf16[16,2,2,16,128]{4,3,2,1,0:T(8,128)(2,1)}, bf16[16,2,2,16,128]{4,3,2,1,0:T(8,128)(2,1)S(1)}, u32[]{:S(2)}, u32[]{:S(2)}) collective-permute-start(bf16[16,2,2,16,128]{4,3,2,1,0:T(8,128)(2,1)} %get-tuple-element.26), channel_id=1, source_target_pairs={{0,130},{1,131},{2,192},{3,193},{4,134},{5,135},{6,196},{7,197},{8... | collective-permute-start | bytes 786440 | tf_op jit(solution)/shard_map/ppermute | solution.py:52
  13.7 27.5 %all-to-all-start.1 = ((bf16[16,4,2,3,16,128]{5,4,3,2,1,0:T(8,128)(2,1)}), bf16[16,4,2,3,16,128]{5,4,3,2,1,0:T(8,128)(2,1)S(1)}, u32[]{:S(2)}, u32[]{:S(2)}) async-start(bf16[16,4,2,3,16,128]{5,4,3,2,1,0:T(8,128)(2,1)} %get-tuple-element.27), calls=%async_computation.1 | async-start | bytes 3145728 | tf_op jit(solution)/shard_map/all_to_all | solution.py:363
  42.4 10.4 %copy-start.1 = (bf16[16,2,3,16,128]{4,3,2,1,0:T(8,128)(2,1)S(1)}, bf16[16,2,3,16,128]{4,3,2,1,0:T(8,128)(2,1)}, u32[]{:S(2)}) copy-start(bf16[16,2,3,16,128]{4,3,2,1,0:T(8,128)(2,1)} %get-tuple-element.42) | copy-start | bytes 1179652
  42.4 11.3 %collective-permute-start.5 = (bf16[16,2,3,16,128]{4,3,2,1,0:T(8,128)(2,1)}, bf16[16,2,3,16,128]{4,3,2,1,0:T(8,128)(2,1)S(1)}, u32[]{:S(2)}, u32[]{:S(2)}) collective-permute-start(bf16[16,2,3,16,128]{4,3,2,1,0:T(8,128)(2,1)} %get-tuple-element.43), channel_id=1, source_target_pairs={{0,194},{1,195},{2,0},{3,1},{4,198},{5,199},{6,4},{7,5},{8,202},{9... | collective-permute-start | bytes 1179656 | tf_op jit(solution)/shard_map/ppermute | solution.py:52
  44.8 8.9 %collective-permute-start.4 = (bf16[16,2,3,16,128]{4,3,2,1,0:T(8,128)(2,1)}, bf16[16,2,3,16,128]{4,3,2,1,0:T(8,128)(2,1)S(1)}, u32[]{:S(2)}, u32[]{:S(2)}) collective-permute-start(bf16[16,2,3,16,128]{4,3,2,1,0:T(8,128)(2,1)} %get-tuple-element.44), channel_id=1, source_target_pairs={{0,2},{1,3},{2,64},{3,65},{4,6},{5,7},{6,68},{7,69},{8,10},{9,11},... | collective-permute-start | bytes 1179656 | tf_op jit(solution)/shard_map/ppermute | solution.py:52
  44.9 20.5 %all-to-all-start = ((bf16[16,4,2,2,16,128]{5,4,3,2,1,0:T(8,128)(2,1)}), bf16[16,4,2,2,16,128]{5,4,3,2,1,0:T(8,128)(2,1)S(1)}, u32[]{:S(2)}, u32[]{:S(2)}) async-start(bf16[16,4,2,2,16,128]{5,4,3,2,1,0:T(8,128)(2,1)} %gather.3), calls=%async_computation | async-start | bytes 2097152 | tf_op jit(solution)/shard_map/all_to_all | solution.py:366
  50.3 35.8 %collective-permute-start.7 = (bf16[16,2,3,16,128]{4,3,2,1,0:T(8,128)(2,1)S(1)}, bf16[16,2,3,16,128]{4,3,2,1,0:T(8,128)(2,1)}, u32[]{:S(2)}, u32[]{:S(2)}) collective-permute-start(bf16[16,2,3,16,128]{4,3,2,1,0:T(8,128)(2,1)S(1)} %get-tuple-element.41), channel_id=1, source_target_pairs={{0,130},{1,131},{2,192},{3,193},{4,134},{5,135},{6,196},{7,197},{8... | collective-permute-start | bytes 1179656 | tf_op jit(solution)/shard_map/ppermute | solution.py:52
  52.8 30.0 %collective-permute-start.6 = (bf16[16,2,3,16,128]{4,3,2,1,0:T(8,128)(2,1)S(1)}, bf16[16,2,3,16,128]{4,3,2,1,0:T(8,128)(2,1)S(1)}, u32[]{:S(2)}, u32[]{:S(2)}) collective-permute-start(bf16[16,2,3,16,128]{4,3,2,1,0:T(8,128)(2,1)S(1)} %copy-done.1), channel_id=1, source_target_pairs={{0,66},{1,67},{2,128},{3,129},{4,70},{5,71},{6,132},{7,133},{8,74}... | collective-permute-start | bytes 1179656 | tf_op jit(solution)/shard_map/ppermute | solution.py:52
  82.8 13.9 %collective-permute-start.13 = (bf16[16,2,16,128]{3,2,1,0:T(8,128)(2,1)S(1)}, bf16[16,2,16,128]{3,2,1,0:T(8,128)(2,1)S(1)}, u32[]{:S(2)}, u32[]{:S(2)}) collective-permute-start(bf16[16,2,16,128]{3,2,1,0:T(8,128)(2,1)S(1)} %get-tuple-element.37), channel_id=1, source_target_pairs={{0,2},{1,3},{2,64},{3,65},{4,6},{5,7},{6,68},{7,69},{8,10},{9,11},... | collective-permute-start | bytes 393224 | tf_op jit(solution)/shard_map/ppermute | solution.py:52
  82.8 16.6 %collective-permute-start.14 = (bf16[16,2,16,128]{3,2,1,0:T(8,128)(2,1)S(1)}, bf16[16,2,16,128]{3,2,1,0:T(8,128)(2,1)S(1)}, u32[]{:S(2)}, u32[]{:S(2)}) collective-permute-start(bf16[16,2,16,128]{3,2,1,0:T(8,128)(2,1)S(1)} %get-tuple-element.38), channel_id=1, source_target_pairs={{0,194},{1,195},{2,0},{3,1},{4,198},{5,199},{6,4},{7,5},{8,202},{9... | collective-permute-start | bytes 393224 | tf_op jit(solution)/shard_map/ppermute | solution.py:52
  85.4 14.6 %collective-permute-start.15 = (bf16[16,2,16,128]{3,2,1,0:T(8,128)(2,1)S(1)}, bf16[16,2,16,128]{3,2,1,0:T(8,128)(2,1)S(1)}, u32[]{:S(2)}, u32[]{:S(2)}) collective-permute-start(bf16[16,2,16,128]{3,2,1,0:T(8,128)(2,1)S(1)} %get-tuple-element.39), channel_id=1, source_target_pairs={{0,130},{1,131},{2,192},{3,193},{4,134},{5,135},{6,196},{7,197},{8... | collective-permute-start | bytes 393224 | tf_op jit(solution)/shard_map/ppermute | solution.py:52
  94.0 32.5 %collective-permute-start.8 = (bf16[16,3,16,128]{3,2,1,0:T(8,128)(2,1)S(1)}, bf16[16,3,16,128]{3,2,1,0:T(8,128)(2,1)S(1)}, u32[]{:S(2)}, u32[]{:S(2)}) collective-permute-start(bf16[16,3,16,128]{3,2,1,0:T(8,128)(2,1)S(1)} %get-tuple-element.33), channel_id=1, source_target_pairs={{0,66},{1,67},{2,128},{3,129},{4,70},{5,71},{6,132},{7,133},{8,74}... | collective-permute-start | bytes 589832 | tf_op jit(solution)/shard_map/ppermute | solution.py:52
  96.7 29.8 %collective-permute-start.9 = (bf16[16,3,16,128]{3,2,1,0:T(8,128)(2,1)S(1)}, bf16[16,3,16,128]{3,2,1,0:T(8,128)(2,1)S(1)}, u32[]{:S(2)}, u32[]{:S(2)}) collective-permute-start(bf16[16,3,16,128]{3,2,1,0:T(8,128)(2,1)S(1)} %get-tuple-element.34), channel_id=1, source_target_pairs={{0,2},{1,3},{2,64},{3,65},{4,6},{5,7},{6,68},{7,69},{8,10},{9,11},... | collective-permute-start | bytes 589832 | tf_op jit(solution)/shard_map/ppermute | solution.py:52
  96.7 29.8 %collective-permute-start.10 = (bf16[16,3,16,128]{3,2,1,0:T(8,128)(2,1)S(1)}, bf16[16,3,16,128]{3,2,1,0:T(8,128)(2,1)S(1)}, u32[]{:S(2)}, u32[]{:S(2)}) collective-permute-start(bf16[16,3,16,128]{3,2,1,0:T(8,128)(2,1)S(1)} %get-tuple-element.35), channel_id=1, source_target_pairs={{0,194},{1,195},{2,0},{3,1},{4,198},{5,199},{6,4},{7,5},{8,202},{9... | collective-permute-start | bytes 589832 | tf_op jit(solution)/shard_map/ppermute | solution.py:52
  99.4 27.2 %collective-permute-start.11 = (bf16[16,3,16,128]{3,2,1,0:T(8,128)(2,1)S(1)}, bf16[16,3,16,128]{3,2,1,0:T(8,128)(2,1)S(1)}, u32[]{:S(2)}, u32[]{:S(2)}) collective-permute-start(bf16[16,3,16,128]{3,2,1,0:T(8,128)(2,1)S(1)} %get-tuple-element.36), channel_id=1, source_target_pairs={{0,130},{1,131},{2,192},{3,193},{4,134},{5,135},{6,196},{7,197},{8... | collective-permute-start | bytes 589832 | tf_op jit(solution)/shard_map/ppermute | solution.py:52
  100.0 21.1 %collective-permute-start.12 = (bf16[16,2,16,128]{3,2,1,0:T(8,128)(2,1)S(1)}, bf16[16,2,16,128]{3,2,1,0:T(8,128)(2,1)S(1)}, u32[]{:S(2)}, u32[]{:S(2)}) collective-permute-start(bf16[16,2,16,128]{3,2,1,0:T(8,128)(2,1)S(1)} %get-tuple-element.31), channel_id=1, source_target_pairs={{0,66},{1,67},{2,128},{3,129},{4,70},{5,71},{6,132},{7,133},{8,74}... | collective-permute-start | bytes 393224 | tf_op jit(solution)/shard_map/ppermute | solution.py:52
  122.0 13.5 %all-to-all-start.3 = ((bf16[16,4,2,16,128]{4,3,2,1,0:T(8,128)(2,1)}), bf16[16,4,2,16,128]{4,3,2,1,0:T(8,128)(2,1)S(1)}, u32[]{:S(2)}, u32[]{:S(2)}) async-start(bf16[16,4,2,16,128]{4,3,2,1,0:T(8,128)(2,1)} %gather.5), calls=%async_computation.3 | async-start | bytes 1048576 | tf_op jit(solution)/shard_map/all_to_all | solution.py:374
  135.5 14.1 %all-to-all-start.2 = ((bf16[16,4,3,16,128]{4,3,2,1,0:T(8,128)(2,1)}), bf16[16,4,3,16,128]{4,3,2,1,0:T(8,128)(2,1)S(1)}, u32[]{:S(2)}, u32[]{:S(2)}) async-start(bf16[16,4,3,16,128]{4,3,2,1,0:T(8,128)(2,1)} %gather.4), calls=%async_computation.2 | async-start | bytes 1572864 | tf_op jit(solution)/shard_map/all_to_all | solution.py:377
  139.1 26.6 %copy-start.2 = (bf16[1,64,192]{2,1,0:T(8,128)(2,1)S(1)}, bf16[1,64,192]{2,1,0:T(8,128)(2,1)}, u32[]{:S(2)}) copy-start(bf16[1,64,192]{2,1,0:T(8,128)(2,1)} %param.8) | copy-start | bytes 73732
  139.4 40.8 %copy-start = (s32[4,5]{1,0:T(4,128)S(1)}, s32[4,5]{1,0:T(4,128)}, u32[]{:S(2)}) copy-start(s32[4,5]{1,0:T(4,128)} %pattern_ref.1) | copy-start | bytes 244
  150.0 29.1 %collective-permute-start.17 = (bf16[16,5,64,128]{3,2,1,0:T(8,128)(2,1)S(1)}, bf16[16,5,64,128]{3,2,1,0:T(8,128)(2,1)S(1)}, u32[]{:S(2)}, u32[]{:S(2)}) collective-permute-start(bf16[16,5,64,128]{3,2,1,0:T(8,128)(2,1)S(1)} %settle.3.own_ref), channel_id=1, source_target_pairs={{1,0},{2,1},{3,2},{5,4},{6,5},{7,6},{9,8},{10,9},{11,10},{13,12},{... | collective-permute-start | bytes 3932168 | tf_op jit(solution)/shard_map/ppermute | solution.py:380
  158.7 21.5 %collective-permute-start.16 = (bf16[16,5,64,128]{3,2,1,0:T(8,128)(2,1)S(1)}, bf16[16,5,64,128]{3,2,1,0:T(8,128)(2,1)}, u32[]{:S(2)}, u32[]{:S(2)}) collective-permute-start(bf16[16,5,64,128]{3,2,1,0:T(8,128)(2,1)S(1)} %settle.3.own_ref), channel_id=1, source_target_pairs={{0,1},{1,2},{2,3},{4,5},{5,6},{6,7},{8,9},{9,10},{10,11},{12,13},{... | collective-permute-start | bytes 3932168 | tf_op jit(solution)/shard_map/ppermute | solution.py:379

commit v5 on v4

--- a/solution.py
+++ b/solution.py
@@ -366,14 +366,13 @@
     late = lax.all_to_all(late, PLANE, split_axis=0, concat_axis=0, tiled=True)
 
     late, rot = lax.optimization_barrier([late, marker(rot, early[1:3], HEAVY)])
-    hi = correlate(rot, [late], fwd, inv, True, 0)
-    early[0] = after(early[0], hi[0])
+    hi = correlate(rot, [late], fwd, inv, False, 0)
+    early[0] = after(early[0], hi)
     lo = correlate(rot, early, fwd, inv, True, HEAVY)
 
-    hi = gather([hop(p, STEPS[j]) for j, p in enumerate(hi)], 0)
     hi = lax.all_to_all(hi, PLANE, split_axis=0, concat_axis=0, tiled=True)
-    lo = gather([hop(p, STEPS[j]) for j, p in enumerate(lo)], HEAVY)
-    hi = settle([after(hi, lo)], [], 0)
+    lo = gather([hop(p, STEPS[j]) for j, p in enumerate(lo)], 0)
+    hi = settle([hop(hi[:, j], STEPS[j]) for j in range(4)], [], 0)
     lo = lax.all_to_all(lo, PLANE, split_axis=0, concat_axis=0, tiled=True)
     own = settle([lo], [hi], 0)
     up = lax.ppermute(own, "s", [(0, 1), (1, 2), (2, 3)])

time: 185 us -> 163 us (0.88)
  waiting for transfers between devices: 93.6 us -> 72.3 us
    all_to_all x1, waiting for transfers between devices: 10.1 us -> 0.01 us  [shards(): lo = lax.all_to_all(lo, PLANE, split_axis=0, concat_axis=0, tiled=True)]
    all_to_all x1, waiting for transfers between devices: 8.03 us -> 0.01 us  [shards(): hi = lax.all_to_all(hi, PLANE, split_axis=0, concat_axis=0, tiled=True)]
    ppermute x1, starting transfers between devices: 6.95 us -> 1.92 us  [shards(): up = lax.ppermute(own, 's', [(0, 1), (1, 2), (2, 3)])]
    ppermute x16, starting transfers between devices: 27.4 us -> 31.9 us  [hop(): return lax.ppermute(piece, ALL, perm)]
    ppermute x16, waiting for transfers between devices: 43.6 us -> 40.5 us  [hop(): return lax.ppermute(piece, ALL, perm)]
    ppermute x1, starting transfers between devices: 8.74 us -> 5.84 us  [shards(): down = lax.ppermute(own, 's', [(1, 0), (2, 1), (3, 2)])]
    all_to_all x1, starting transfers between devices: 3.61 us -> 6.26 us  [shards(): lo = lax.all_to_all(lo, PLANE, split_axis=0, concat_axis=0, tiled=True)]
  transfers between devices with their start and end apart: 22 -> 22, of which waited for: 10 -> 11; matrix products, arithmetic and copies ran while one was open for 0% -> 0% of each run, Pallas kernels for 9% -> 10%
where the time goes in v5:
time: 163 us; the launch traced here: 162 us
  waiting for transfers between devices  72.3 us (44%)
  starting transfers between devices  62.2 us (38%)
  Pallas kernels  25.4 us (16%)
    ppermute x16, waiting for transfers between devices, hop(): return lax.ppermute(piece, ALL, perm)  40.5 us
    ppermute x16, starting transfers between devices, hop(): return lax.ppermute(piece, ALL, perm)  31.9 us
    pallas_call x2, Pallas kernels, correlate(): pl.pallas_call(functools.partial(correlate_kernel, slots, len(inputs), sp...  14.5 us
    ppermute x1, waiting for transfers between devices, shards(): down = lax.ppermute(own, 's', [(1, 0), (2, 1), (3, 2)])  12.6 us
    all_to_all x1, waiting for transfers between devices, shards(): late = lax.all_to_all(late, PLANE, split_axis=0, concat_axis=0, tiled=True)  11.6 us
    all_to_all x1, starting transfers between devices, shards(): lax.all_to_all(early, PLANE, split_axis=0, concat_axis=0, tiled=True)  6.76 us
    all_to_all x1, starting transfers between devices, shards(): lo = lax.all_to_all(lo, PLANE, split_axis=0, concat_axis=0, tiled=True)  6.26 us
    all_to_all x1, waiting for transfers between devices, shards(): lax.all_to_all(early, PLANE, split_axis=0, concat_axis=0, tiled=True)  6.24 us
  transfers between devices with their start and end apart: 22, of which 11 were waited for; matrix products, arithmetic and copies ran while one was open for 0% of the time, Pallas kernels for 10%

profile of v5, /device:TPU:1, one launch (start us, length us, event | category | flops | bytes accessed | tf_op | source)
XLA Modules:
  0.0 161.9 jit_solution(2964272323761591783)
XLA Ops:
  0.0 4.0 %prepare.1 = (bf16[16,4,2,3,16,128]{5,4,3,2,1,0:T(8,128)(2,1)}, bf16[16,2,2,16,128]{4,3,2,1,0:T(8,128)(2,1)}, bf16[16,2,2,16,128]{4,3,2,1,0:T(8,128)(2,1)}, bf16...) custom-call(s32[1]{0:T(128)} %bitcast.6.turn_ref, bf16[16,5,64,128]{3,2,1,0:T(8,128)(2,1)} %bitcast.43, ...), custom_call_target="tpu_custom_call" | custom-call | bytes 5242880 | tf_op jit(solution)/shard_map/prepare/pallas_call | solution.py:200
  4.0 5.2 %collective-permute-start = (bf16[16,2,2,16,128]{4,3,2,1,0:T(8,128)(2,1)}, bf16[16,2,2,16,128]{4,3,2,1,0:T(8,128)(2,1)S(1)}, u32[]{:S(2)}, u32[]{:S(2)}) collective-permute-start(bf16[16,2,2,16,128]{4,3,2,1,0:T(8,128)(2,1)} %get-tuple-element.18), channel_id=1, source_target_pairs={{0,66},{1,67},{2,128},{3,129},{4,70},{5,71},{6,132},{7,133},{8,74}... | collective-permute-start | bytes 786440 | tf_op jit(solution)/shard_map/ppermute | solution.py:52
  9.2 2.8 %collective-permute-start.1 = (bf16[16,2,2,16,128]{4,3,2,1,0:T(8,128)(2,1)}, bf16[16,2,2,16,128]{4,3,2,1,0:T(8,128)(2,1)S(1)}, u32[]{:S(2)}, u32[]{:S(2)}) collective-permute-start(bf16[16,2,2,16,128]{4,3,2,1,0:T(8,128)(2,1)} %get-tuple-element.19), channel_id=1, source_target_pairs={{0,2},{1,3},{2,64},{3,65},{4,6},{5,7},{6,68},{7,69},{8,10},{9,11},... | collective-permute-start | bytes 786440 | tf_op jit(solution)/shard_map/ppermute | solution.py:52
  12.1 0.0 collective-permute-start.2
  12.1 1.6 %collective-permute-start.3 = (bf16[16,2,2,16,128]{4,3,2,1,0:T(8,128)(2,1)}, bf16[16,2,2,16,128]{4,3,2,1,0:T(8,128)(2,1)S(1)}, u32[]{:S(2)}, u32[]{:S(2)}) collective-permute-start(bf16[16,2,2,16,128]{4,3,2,1,0:T(8,128)(2,1)} %get-tuple-element.21), channel_id=1, source_target_pairs={{0,130},{1,131},{2,192},{3,193},{4,134},{5,135},{6,196},{7,197},{8... | collective-permute-start | bytes 786440 | tf_op jit(solution)/shard_map/ppermute | solution.py:52
  13.7 6.8 %all-to-all-start.1 = ((bf16[16,4,2,3,16,128]{5,4,3,2,1,0:T(8,128)(2,1)}), bf16[16,4,2,3,16,128]{5,4,3,2,1,0:T(8,128)(2,1)S(1)}, u32[]{:S(2)}, u32[]{:S(2)}) async-start(bf16[16,4,2,3,16,128]{5,4,3,2,1,0:T(8,128)(2,1)} %get-tuple-element.22), calls=%async_computation.1 | async-start | bytes 3145728 | tf_op jit(solution)/shard_map/all_to_all | solution.py:363
  20.5 5.0 %collective-permute-done.refs_0_ = bf16[16,2,2,16,128]{4,3,2,1,0:T(8,128)(2,1)S(1)} collective-permute-done((bf16[16,2,2,16,128]{4,3,2,1,0:T(8,128)(2,1)}, bf16[16,2,2,16,128]{4,3,2,1,0:T(8,128)(2,1)S(1)}, u32[]{:S(2)}, u32[]{:S(2)}) %collective-permute-start) | collective-permute-done | bytes 262176 | tf_op jit(solution)/shard_map/ppermute | solution.py:52
  25.5 8.5 %collective-permute-done.1.refs_1_ = bf16[16,2,2,16,128]{4,3,2,1,0:T(8,128)(2,1)S(1)} collective-permute-done((bf16[16,2,2,16,128]{4,3,2,1,0:T(8,128)(2,1)}, bf16[16,2,2,16,128]{4,3,2,1,0:T(8,128)(2,1)S(1)}, u32[]{:S(2)}, u32[]{:S(2)}) %collective-permute-start.1) | collective-permute-done | bytes 262176 | tf_op jit(solution)/shard_map/ppermute | solution.py:52
  34.0 0.0 collective-permute-done.2.refs_2_
  34.0 0.0 collective-permute-done.3.refs_3_
  34.0 1.0 gather.2
  35.0 6.2 %all-to-all-done.1 = bf16[16,4,2,3,16,128]{5,4,3,2,1,0:T(8,128)(2,1)S(1)} async-done(((bf16[16,4,2,3,16,128]{5,4,3,2,1,0:T(8,128)(2,1)}), bf16[16,4,2,3,16,128]{5,4,3,2,1,0:T(8,128)(2,1)S(1)}, u32[]{:S(2)}, u32[]{:S(2)}) %all-to-all-start.1) | async-done | bytes 1572896 | tf_op jit(solution)/shard_map/all_to_all | solution.py:363
  41.3 1.2 slice_bitcast_fusion
  42.4 2.4 %collective-permute-start.5 = (bf16[16,2,3,16,128]{4,3,2,1,0:T(8,128)(2,1)}, bf16[16,2,3,16,128]{4,3,2,1,0:T(8,128)(2,1)S(1)}, u32[]{:S(2)}, u32[]{:S(2)}) collective-permute-start(bf16[16,2,3,16,128]{4,3,2,1,0:T(8,128)(2,1)} %get-tuple-element.33), channel_id=1, source_target_pairs={{0,194},{1,195},{2,0},{3,1},{4,198},{5,199},{6,4},{7,5},{8,202},{9... | collective-permute-start | bytes 1179656 | tf_op jit(solution)/shard_map/ppermute | solution.py:52
  44.8 0.0 collective-permute-start.4
  44.8 0.1 pad_maximum_fusion.refs_0_
  44.9 5.5 %all-to-all-start = ((bf16[16,4,2,2,16,128]{5,4,3,2,1,0:T(8,128)(2,1)}), bf16[16,4,2,2,16,128]{5,4,3,2,1,0:T(8,128)(2,1)S(1)}, u32[]{:S(2)}, u32[]{:S(2)}) async-start(bf16[16,4,2,2,16,128]{5,4,3,2,1,0:T(8,128)(2,1)} %gather.2), calls=%async_computation | async-start | bytes 2097152 | tf_op jit(solution)/shard_map/all_to_all | solution.py:366
  50.4 2.4 %collective-permute-start.7 = (bf16[16,2,3,16,128]{4,3,2,1,0:T(8,128)(2,1)S(1)}, bf16[16,2,3,16,128]{4,3,2,1,0:T(8,128)(2,1)}, u32[]{:S(2)}, u32[]{:S(2)}) collective-permute-start(bf16[16,2,3,16,128]{4,3,2,1,0:T(8,128)(2,1)S(1)} %get-tuple-element.31), channel_id=1, source_target_pairs={{0,130},{1,131},{2,192},{3,193},{4,134},{5,135},{6,196},{7,197},{8... | collective-permute-start | bytes 1179656 | tf_op jit(solution)/shard_map/ppermute | solution.py:52
  52.8 0.9 collective-permute-start.6
  53.7 0.0 collective-permute-done.5.refs_2_
  53.7 0.0 collective-permute-done.4.refs_1_
  53.7 11.6 %all-to-all-done.refs_0_ = bf16[16,4,2,2,16,128]{5,4,3,2,1,0:T(8,128)(2,1)S(1)} async-done(((bf16[16,4,2,2,16,128]{5,4,3,2,1,0:T(8,128)(2,1)}), bf16[16,4,2,2,16,128]{5,4,3,2,1,0:T(8,128)(2,1)S(1)}, u32[]{:S(2)}, u32[]{:S(2)}) %all-to-all-start) | async-done | bytes 1048608 | tf_op jit(solution)/shard_map/all_to_all | solution.py:366
  65.4 6.6 %correlate.2 = bf16[16,4,2,16,128]{4,3,2,1,0:T(8,128)(2,1)} custom-call(f32[3]{0:T(128)S(1)} %marker.1.rot_ref, bf16[16,4,2,2,16,128]{5,4,3,2,1,0:T(8,128)(2,1)S(1)} %all-to-all-done.refs_0_, bf16[4,512,256]{2,1,0:T(8,128)(2,1)} %constant.87.clone.refs_1_.refs_4_, bf16[4,512,256]{2,1,0:T(8,128)(2,1)} %constant.88.clone.refs_2_.refs_5_), custom_call_target="tpu_custom_call" | custom-call | bytes 3670016 | tf_op jit(solution)/shard_map/correlate/pallas_call | solution.py:138
  72.0 4.0 %all-to-all-start.3 = ((bf16[16,4,2,16,128]{4,3,2,1,0:T(8,128)(2,1)}), bf16[16,4,2,16,128]{4,3,2,1,0:T(8,128)(2,1)S(1)}, u32[]{:S(2)}, u32[]{:S(2)}) async-start(bf16[16,4,2,16,128]{4,3,2,1,0:T(8,128)(2,1)} %correlate.2), calls=%async_computation.3 | async-start | bytes 1048576 | tf_op jit(solution)/shard_map/all_to_all | solution.py:373
  76.1 6.7 %collective-permute-done.6.refs_0_ = bf16[16,2,3,16,128]{4,3,2,1,0:T(8,128)(2,1)S(1)} collective-permute-done((bf16[16,2,3,16,128]{4,3,2,1,0:T(8,128)(2,1)S(1)}, bf16[16,2,3,16,128]{4,3,2,1,0:T(8,128)(2,1)S(1)}, u32[]{:S(2)}, u32[]{:S(2)}) %collective-permute-start.6) | collective-permute-done | bytes 393248 | tf_op jit(solution)/shard_map/ppermute | solution.py:52
  82.8 0.0 collective-permute-done.7.refs_3_
  82.8 7.9 %correlate.3 = (bf16[16,3,16,128]{3,2,1,0:T(8,128)(2,1)S(1)}, bf16[16,3,16,128]{3,2,1,0:T(8,128)(2,1)S(1)}, bf16[16,3,16,128]{3,2,1,0:T(8,128)(2,1)S(1)}, bf16[16,3,16,128]{3,2,1,0:T(8,128)(2,1)S(1)}) custom-call(f32[3]{0:T(128)S(1)} %marker.1.rot_ref, bf16[16,2,3,16,128]{4,3,2,1,0:T(8,128)(2,1)S(1)} %collective-permute-done.6.refs_0_, ...), custom_call_target="tpu_custom_call" | custom-call | flops 99999997952 | bytes 4456448 | tf_op jit(solution)/shard_map/correlate/pallas_call | solution.py:138
  90.7 0.1 collective-permute-start.8
  90.8 0.4 collective-permute-start.9
  91.2 2.4 %collective-permute-start.10 = (bf16[16,3,16,128]{3,2,1,0:T(8,128)(2,1)S(1)}, bf16[16,3,16,128]{3,2,1,0:T(8,128)(2,1)S(1)}, u32[]{:S(2)}, u32[]{:S(2)}) collective-permute-start(bf16[16,3,16,128]{3,2,1,0:T(8,128)(2,1)S(1)} %get-tuple-element.29), channel_id=1, source_target_pairs={{0,194},{1,195},{2,0},{3,1},{4,198},{5,199},{6,4},{7,5},{8,202},{9... | collective-permute-start | bytes 589832 | tf_op jit(solution)/shard_map/ppermute | solution.py:52
  93.5 3.2 %collective-permute-start.11 = (bf16[16,3,16,128]{3,2,1,0:T(8,128)(2,1)S(1)}, bf16[16,3,16,128]{3,2,1,0:T(8,128)(2,1)S(1)}, u32[]{:S(2)}, u32[]{:S(2)}) collective-permute-start(bf16[16,3,16,128]{3,2,1,0:T(8,128)(2,1)S(1)} %get-tuple-element.30), channel_id=1, source_target_pairs={{0,130},{1,131},{2,192},{3,193},{4,134},{5,135},{6,196},{7,197},{8... | collective-permute-start | bytes 589832 | tf_op jit(solution)/shard_map/ppermute | solution.py:52
  96.7 7.0 %collective-permute-done.8.refs_0_ = bf16[16,3,16,128]{3,2,1,0:T(8,128)(2,1)S(1)} collective-permute-done((bf16[16,3,16,128]{3,2,1,0:T(8,128)(2,1)S(1)}, bf16[16,3,16,128]{3,2,1,0:T(8,128)(2,1)S(1)}, u32[]{:S(2)}, u32[]{:S(2)}) %collective-permute-start.8) | collective-permute-done | bytes 196640 | tf_op jit(solution)/shard_map/ppermute | solution.py:52
  103.7 3.4 %collective-permute-done.9.refs_1_ = bf16[16,3,16,128]{3,2,1,0:T(8,128)(2,1)S(1)} collective-permute-done((bf16[16,3,16,128]{3,2,1,0:T(8,128)(2,1)S(1)}, bf16[16,3,16,128]{3,2,1,0:T(8,128)(2,1)S(1)}, u32[]{:S(2)}, u32[]{:S(2)}) %collective-permute-start.9) | collective-permute-done | bytes 196640 | tf_op jit(solution)/shard_map/ppermute | solution.py:52
  107.2 0.0 collective-permute-done.10.refs_2_
  107.2 0.0 collective-permute-done.11.refs_3_
  107.2 0.9 gather.3
  108.1 0.0 all-to-all-done.3
  108.1 6.3 %all-to-all-start.2 = ((bf16[16,4,3,16,128]{4,3,2,1,0:T(8,128)(2,1)}), bf16[16,4,3,16,128]{4,3,2,1,0:T(8,128)(2,1)S(1)}, u32[]{:S(2)}, u32[]{:S(2)}) async-start(bf16[16,4,3,16,128]{4,3,2,1,0:T(8,128)(2,1)} %gather.3), calls=%async_computation.2 | async-start | bytes 1572864 | tf_op jit(solution)/shard_map/all_to_all | solution.py:376
  114.4 4.0 %collective-permute-start.15 = (bf16[16,2,16,128]{3,2,1,0:T(8,128)(2,1)S(1)}, bf16[16,2,16,128]{3,2,1,0:T(8,128)(2,1)S(1)}, u32[]{:S(2)}, u32[]{:S(2)}) collective-permute-start(bf16[16,2,16,128]{3,2,1,0:T(8,128)(2,1)S(1)} %get-tuple-element.35), channel_id=1, source_target_pairs={{0,130},{1,131},{2,192},{3,193},{4,134},{5,135},{6,196},{7,197},{8... | collective-permute-start | bytes 393224 | tf_op jit(solution)/shard_map/ppermute | solution.py:52
  118.5 3.2 %collective-permute-start.14 = (bf16[16,2,16,128]{3,2,1,0:T(8,128)(2,1)S(1)}, bf16[16,2,16,128]{3,2,1,0:T(8,128)(2,1)S(1)}, u32[]{:S(2)}, u32[]{:S(2)}) collective-permute-start(bf16[16,2,16,128]{3,2,1,0:T(8,128)(2,1)S(1)} %get-tuple-element.36), channel_id=1, source_target_pairs={{0,194},{1,195},{2,0},{3,1},{4,198},{5,199},{6,4},{7,5},{8,202},{9... | collective-permute-start | bytes 393224 | tf_op jit(solution)/shard_map/ppermute | solution.py:52
  121.7 0.0 collective-permute-start.13
  121.7 0.0 copy-start.1
  121.7 3.2 %collective-permute-start.12 = (bf16[16,2,16,128]{3,2,1,0:T(8,128)(2,1)S(1)}, bf16[16,2,16,128]{3,2,1,0:T(8,128)(2,1)S(1)}, u32[]{:S(2)}, u32[]{:S(2)}) collective-permute-start(bf16[16,2,16,128]{3,2,1,0:T(8,128)(2,1)S(1)} %get-tuple-element.38), channel_id=1, source_target_pairs={{0,66},{1,67},{2,128},{3,129},{4,70},{5,71},{6,132},{7,133},{8,74}... | collective-permute-start | bytes 393224 | tf_op jit(solution)/shard_map/ppermute | solution.py:52
  124.8 0.0 collective-permute-done.15.refs_3_
  124.8 0.0 collective-permute-done.14.refs_2_
  124.8 2.1 %collective-permute-done.13.refs_1_ = bf16[16,2,16,128]{3,2,1,0:T(8,128)(2,1)S(1)} collective-permute-done((bf16[16,2,16,128]{3,2,1,0:T(8,128)(2,1)S(1)}, bf16[16,2,16,128]{3,2,1,0:T(8,128)(2,1)S(1)}, u32[]{:S(2)}, u32[]{:S(2)}) %collective-permute-start.13) | collective-permute-done | bytes 131104 | tf_op jit(solution)/shard_map/ppermute | solution.py:52
  127.0 7.7 %collective-permute-done.12.refs_0_ = bf16[16,2,16,128]{3,2,1,0:T(8,128)(2,1)S(1)} collective-permute-done((bf16[16,2,16,128]{3,2,1,0:T(8,128)(2,1)S(1)}, bf16[16,2,16,128]{3,2,1,0:T(8,128)(2,1)S(1)}, u32[]{:S(2)}, u32[]{:S(2)}) %collective-permute-start.12) | collective-permute-done | bytes 131104 | tf_op jit(solution)/shard_map/ppermute | solution.py:52
  134.6 0.3 settle.2.refs_1_
  134.9 0.0 copy-start
  135.0 0.0 all-to-all-done.2.refs_0_
  135.0 0.4 settle.3.own_ref
  135.4 5.8 %collective-permute-start.17 = (bf16[16,5,64,128]{3,2,1,0:T(8,128)(2,1)S(1)}, bf16[16,5,64,128]{3,2,1,0:T(8,128)(2,1)S(1)}, u32[]{:S(2)}, u32[]{:S(2)}) collective-permute-start(bf16[16,5,64,128]{3,2,1,0:T(8,128)(2,1)S(1)} %settle.3.own_ref), channel_id=1, source_target_pairs={{1,0},{2,1},{3,2},{5,4},{6,5},{7,6},{9,8},{10,9},{11,10},{13,12},{... | collective-permute-start | bytes 3932168 | tf_op jit(solution)/shard_map/ppermute | solution.py:379
  141.3 1.9 %collective-permute-start.16 = (bf16[16,5,64,128]{3,2,1,0:T(8,128)(2,1)S(1)}, bf16[16,5,64,128]{3,2,1,0:T(8,128)(2,1)}, u32[]{:S(2)}, u32[]{:S(2)}) collective-permute-start(bf16[16,5,64,128]{3,2,1,0:T(8,128)(2,1)S(1)} %settle.3.own_ref), channel_id=1, source_target_pairs={{0,1},{1,2},{2,3},{4,5},{5,6},{6,7},{8,9},{9,10},{10,11},{12,13},{... | collective-permute-start | bytes 3932168 | tf_op jit(solution)/shard_map/ppermute | solution.py:378
  143.2 0.0 copy-done.1
  143.2 0.1 copy.19
  143.3 0.1 add_select_fusion
  143.4 0.2 fusion
  143.7 0.1 copy.30.w_ref
  143.8 12.6 %collective-permute-done.17.down_ref = bf16[16,5,64,128]{3,2,1,0:T(8,128)(2,1)S(1)} collective-permute-done((bf16[16,5,64,128]{3,2,1,0:T(8,128)(2,1)S(1)}, bf16[16,5,64,128]{3,2,1,0:T(8,128)(2,1)S(1)}, u32[]{:S(2)}, u32[]{:S(2)}) %collective-permute-start.17) | collective-permute-done | bytes 1310752 | tf_op jit(solution)/shard_map/ppermute | solution.py:379
  156.3 1.4 collective-permute-done.16.up_ref
  157.7 0.0 copy-done
  157.7 4.2 %screen.1 = bf16[16,5,64,128]{3,2,1,0:T(8,128)(2,1)} custom-call(s32[1]{0:T(128)} %bitcast.row_ref, s32[4,5]{1,0:T(4,128)S(1)} %copy-done, bf16[64,192]{1,0:T(8,128)(2,1)S(1)} %copy.30.w_ref, bf16[16,5,64,128]{3,2,1,0:T(8,128)(2,1)} %collective-permute-done.16.up_ref, bf16[16,5,64,128]{3,2,1,0:T(8,128)(2,1)S(1)} %settle.3.own_ref, ...), custom_call_target="tpu_custom_call" | custom-call | flops 251658240 | bytes 5242880 | tf_op jit(solution)/shard_map/screen/pallas_call | solution.py:321
  (4 shorter events, 0.1 us)
Async XLA Ops:
  4.0 21.5 %collective-permute-start = (bf16[16,2,2,16,128]{4,3,2,1,0:T(8,128)(2,1)}, bf16[16,2,2,16,128]{4,3,2,1,0:T(8,128)(2,1)S(1)}, u32[]{:S(2)}, u32[]{:S(2)}) collective-permute-start(bf16[16,2,2,16,128]{4,3,2,1,0:T(8,128)(2,1)} %get-tuple-element.18), channel_id=1, source_target_pairs={{0,66},{1,67},{2,128},{3,129},{4,70},{5,71},{6,132},{7,133},{8,74}... | collective-permute-start | bytes 786440 | tf_op jit(solution)/shard_map/ppermute | solution.py:52
  9.2 24.7 %collective-permute-start.1 = (bf16[16,2,2,16,128]{4,3,2,1,0:T(8,128)(2,1)}, bf16[16,2,2,16,128]{4,3,2,1,0:T(8,128)(2,1)S(1)}, u32[]{:S(2)}, u32[]{:S(2)}) collective-permute-start(bf16[16,2,2,16,128]{4,3,2,1,0:T(8,128)(2,1)} %get-tuple-element.19), channel_id=1, source_target_pairs={{0,2},{1,3},{2,64},{3,65},{4,6},{5,7},{6,68},{7,69},{8,10},{9,11},... | collective-permute-start | bytes 786440 | tf_op jit(solution)/shard_map/ppermute | solution.py:52
  12.1 21.9 %collective-permute-start.2 = (bf16[16,2,2,16,128]{4,3,2,1,0:T(8,128)(2,1)}, bf16[16,2,2,16,128]{4,3,2,1,0:T(8,128)(2,1)S(1)}, u32[]{:S(2)}, u32[]{:S(2)}) collective-permute-start(bf16[16,2,2,16,128]{4,3,2,1,0:T(8,128)(2,1)} %get-tuple-element.20), channel_id=1, source_target_pairs={{0,194},{1,195},{2,0},{3,1},{4,198},{5,199},{6,4},{7,5},{8,202},{9... | collective-permute-start | bytes 786440 | tf_op jit(solution)/shard_map/ppermute | solution.py:52
  12.1 21.9 %collective-permute-start.3 = (bf16[16,2,2,16,128]{4,3,2,1,0:T(8,128)(2,1)}, bf16[16,2,2,16,128]{4,3,2,1,0:T(8,128)(2,1)S(1)}, u32[]{:S(2)}, u32[]{:S(2)}) collective-permute-start(bf16[16,2,2,16,128]{4,3,2,1,0:T(8,128)(2,1)} %get-tuple-element.21), channel_id=1, source_target_pairs={{0,130},{1,131},{2,192},{3,193},{4,134},{5,135},{6,196},{7,197},{8... | collective-permute-start | bytes 786440 | tf_op jit(solution)/shard_map/ppermute | solution.py:52
  13.7 27.5 %all-to-all-start.1 = ((bf16[16,4,2,3,16,128]{5,4,3,2,1,0:T(8,128)(2,1)}), bf16[16,4,2,3,16,128]{5,4,3,2,1,0:T(8,128)(2,1)S(1)}, u32[]{:S(2)}, u32[]{:S(2)}) async-start(bf16[16,4,2,3,16,128]{5,4,3,2,1,0:T(8,128)(2,1)} %get-tuple-element.22), calls=%async_computation.1 | async-start | bytes 3145728 | tf_op jit(solution)/shard_map/all_to_all | solution.py:363
  42.4 11.3 %collective-permute-start.5 = (bf16[16,2,3,16,128]{4,3,2,1,0:T(8,128)(2,1)}, bf16[16,2,3,16,128]{4,3,2,1,0:T(8,128)(2,1)S(1)}, u32[]{:S(2)}, u32[]{:S(2)}) collective-permute-start(bf16[16,2,3,16,128]{4,3,2,1,0:T(8,128)(2,1)} %get-tuple-element.33), channel_id=1, source_target_pairs={{0,194},{1,195},{2,0},{3,1},{4,198},{5,199},{6,4},{7,5},{8,202},{9... | collective-permute-start | bytes 1179656 | tf_op jit(solution)/shard_map/ppermute | solution.py:52
  44.8 8.9 %collective-permute-start.4 = (bf16[16,2,3,16,128]{4,3,2,1,0:T(8,128)(2,1)}, bf16[16,2,3,16,128]{4,3,2,1,0:T(8,128)(2,1)S(1)}, u32[]{:S(2)}, u32[]{:S(2)}) collective-permute-start(bf16[16,2,3,16,128]{4,3,2,1,0:T(8,128)(2,1)} %get-tuple-element.34), channel_id=1, source_target_pairs={{0,2},{1,3},{2,64},{3,65},{4,6},{5,7},{6,68},{7,69},{8,10},{9,11},... | collective-permute-start | bytes 1179656 | tf_op jit(solution)/shard_map/ppermute | solution.py:52
  44.9 20.5 %all-to-all-start = ((bf16[16,4,2,2,16,128]{5,4,3,2,1,0:T(8,128)(2,1)}), bf16[16,4,2,2,16,128]{5,4,3,2,1,0:T(8,128)(2,1)S(1)}, u32[]{:S(2)}, u32[]{:S(2)}) async-start(bf16[16,4,2,2,16,128]{5,4,3,2,1,0:T(8,128)(2,1)} %gather.2), calls=%async_computation | async-start | bytes 2097152 | tf_op jit(solution)/shard_map/all_to_all | solution.py:366
  50.4 32.4 %collective-permute-start.7 = (bf16[16,2,3,16,128]{4,3,2,1,0:T(8,128)(2,1)S(1)}, bf16[16,2,3,16,128]{4,3,2,1,0:T(8,128)(2,1)}, u32[]{:S(2)}, u32[]{:S(2)}) collective-permute-start(bf16[16,2,3,16,128]{4,3,2,1,0:T(8,128)(2,1)S(1)} %get-tuple-element.31), channel_id=1, source_target_pairs={{0,130},{1,131},{2,192},{3,193},{4,134},{5,135},{6,196},{7,197},{8... | collective-permute-start | bytes 1179656 | tf_op jit(solution)/shard_map/ppermute | solution.py:52
  52.8 30.0 %collective-permute-start.6 = (bf16[16,2,3,16,128]{4,3,2,1,0:T(8,128)(2,1)S(1)}, bf16[16,2,3,16,128]{4,3,2,1,0:T(8,128)(2,1)S(1)}, u32[]{:S(2)}, u32[]{:S(2)}) collective-permute-start(bf16[16,2,3,16,128]{4,3,2,1,0:T(8,128)(2,1)S(1)} %get-tuple-element.32), channel_id=1, source_target_pairs={{0,66},{1,67},{2,128},{3,129},{4,70},{5,71},{6,132},{7,133},{8,74}... | collective-permute-start | bytes 1179656 | tf_op jit(solution)/shard_map/ppermute | solution.py:52
  72.0 36.1 %all-to-all-start.3 = ((bf16[16,4,2,16,128]{4,3,2,1,0:T(8,128)(2,1)}), bf16[16,4,2,16,128]{4,3,2,1,0:T(8,128)(2,1)S(1)}, u32[]{:S(2)}, u32[]{:S(2)}) async-start(bf16[16,4,2,16,128]{4,3,2,1,0:T(8,128)(2,1)} %correlate.2), calls=%async_computation.3 | async-start | bytes 1048576 | tf_op jit(solution)/shard_map/all_to_all | solution.py:373
  90.7 13.0 %collective-permute-start.8 = (bf16[16,3,16,128]{3,2,1,0:T(8,128)(2,1)S(1)}, bf16[16,3,16,128]{3,2,1,0:T(8,128)(2,1)S(1)}, u32[]{:S(2)}, u32[]{:S(2)}) collective-permute-start(bf16[16,3,16,128]{3,2,1,0:T(8,128)(2,1)S(1)} %get-tuple-element.27), channel_id=1, source_target_pairs={{0,66},{1,67},{2,128},{3,129},{4,70},{5,71},{6,132},{7,133},{8,74}... | collective-permute-start | bytes 589832 | tf_op jit(solution)/shard_map/ppermute | solution.py:52
  90.8 16.4 %collective-permute-start.9 = (bf16[16,3,16,128]{3,2,1,0:T(8,128)(2,1)S(1)}, bf16[16,3,16,128]{3,2,1,0:T(8,128)(2,1)S(1)}, u32[]{:S(2)}, u32[]{:S(2)}) collective-permute-start(bf16[16,3,16,128]{3,2,1,0:T(8,128)(2,1)S(1)} %get-tuple-element.28), channel_id=1, source_target_pairs={{0,2},{1,3},{2,64},{3,65},{4,6},{5,7},{6,68},{7,69},{8,10},{9,11},... | collective-permute-start | bytes 589832 | tf_op jit(solution)/shard_map/ppermute | solution.py:52
  91.2 16.0 %collective-permute-start.10 = (bf16[16,3,16,128]{3,2,1,0:T(8,128)(2,1)S(1)}, bf16[16,3,16,128]{3,2,1,0:T(8,128)(2,1)S(1)}, u32[]{:S(2)}, u32[]{:S(2)}) collective-permute-start(bf16[16,3,16,128]{3,2,1,0:T(8,128)(2,1)S(1)} %get-tuple-element.29), channel_id=1, source_target_pairs={{0,194},{1,195},{2,0},{3,1},{4,198},{5,199},{6,4},{7,5},{8,202},{9... | collective-permute-start | bytes 589832 | tf_op jit(solution)/shard_map/ppermute | solution.py:52
  93.5 13.6 %collective-permute-start.11 = (bf16[16,3,16,128]{3,2,1,0:T(8,128)(2,1)S(1)}, bf16[16,3,16,128]{3,2,1,0:T(8,128)(2,1)S(1)}, u32[]{:S(2)}, u32[]{:S(2)}) collective-permute-start(bf16[16,3,16,128]{3,2,1,0:T(8,128)(2,1)S(1)} %get-tuple-element.30), channel_id=1, source_target_pairs={{0,130},{1,131},{2,192},{3,193},{4,134},{5,135},{6,196},{7,197},{8... | collective-permute-start | bytes 589832 | tf_op jit(solution)/shard_map/ppermute | solution.py:52
  108.1 26.9 %all-to-all-start.2 = ((bf16[16,4,3,16,128]{4,3,2,1,0:T(8,128)(2,1)}), bf16[16,4,3,16,128]{4,3,2,1,0:T(8,128)(2,1)S(1)}, u32[]{:S(2)}, u32[]{:S(2)}) async-start(bf16[16,4,3,16,128]{4,3,2,1,0:T(8,128)(2,1)} %gather.3), calls=%async_computation.2 | async-start | bytes 1572864 | tf_op jit(solution)/shard_map/all_to_all | solution.py:376
  114.4 10.4 %collective-permute-start.15 = (bf16[16,2,16,128]{3,2,1,0:T(8,128)(2,1)S(1)}, bf16[16,2,16,128]{3,2,1,0:T(8,128)(2,1)S(1)}, u32[]{:S(2)}, u32[]{:S(2)}) collective-permute-start(bf16[16,2,16,128]{3,2,1,0:T(8,128)(2,1)S(1)} %get-tuple-element.35), channel_id=1, source_target_pairs={{0,130},{1,131},{2,192},{3,193},{4,134},{5,135},{6,196},{7,197},{8... | collective-permute-start | bytes 393224 | tf_op jit(solution)/shard_map/ppermute | solution.py:52
  118.5 6.4 %collective-permute-start.14 = (bf16[16,2,16,128]{3,2,1,0:T(8,128)(2,1)S(1)}, bf16[16,2,16,128]{3,2,1,0:T(8,128)(2,1)S(1)}, u32[]{:S(2)}, u32[]{:S(2)}) collective-permute-start(bf16[16,2,16,128]{3,2,1,0:T(8,128)(2,1)S(1)} %get-tuple-element.36), channel_id=1, source_target_pairs={{0,194},{1,195},{2,0},{3,1},{4,198},{5,199},{6,4},{7,5},{8,202},{9... | collective-permute-start | bytes 393224 | tf_op jit(solution)/shard_map/ppermute | solution.py:52
  121.7 5.3 %collective-permute-start.13 = (bf16[16,2,16,128]{3,2,1,0:T(8,128)(2,1)S(1)}, bf16[16,2,16,128]{3,2,1,0:T(8,128)(2,1)S(1)}, u32[]{:S(2)}, u32[]{:S(2)}) collective-permute-start(bf16[16,2,16,128]{3,2,1,0:T(8,128)(2,1)S(1)} %get-tuple-element.37), channel_id=1, source_target_pairs={{0,2},{1,3},{2,64},{3,65},{4,6},{5,7},{6,68},{7,69},{8,10},{9,11},... | collective-permute-start | bytes 393224 | tf_op jit(solution)/shard_map/ppermute | solution.py:52
  121.7 21.5 %copy-start.1 = (bf16[1,64,192]{2,1,0:T(8,128)(2,1)S(1)}, bf16[1,64,192]{2,1,0:T(8,128)(2,1)}, u32[]{:S(2)}) copy-start(bf16[1,64,192]{2,1,0:T(8,128)(2,1)} %param.8) | copy-start | bytes 73732
  121.7 13.0 %collective-permute-start.12 = (bf16[16,2,16,128]{3,2,1,0:T(8,128)(2,1)S(1)}, bf16[16,2,16,128]{3,2,1,0:T(8,128)(2,1)S(1)}, u32[]{:S(2)}, u32[]{:S(2)}) collective-permute-start(bf16[16,2,16,128]{3,2,1,0:T(8,128)(2,1)S(1)} %get-tuple-element.38), channel_id=1, source_target_pairs={{0,66},{1,67},{2,128},{3,129},{4,70},{5,71},{6,132},{7,133},{8,74}... | collective-permute-start | bytes 393224 | tf_op jit(solution)/shard_map/ppermute | solution.py:52
  134.9 22.8 %copy-start = (s32[4,5]{1,0:T(4,128)S(1)}, s32[4,5]{1,0:T(4,128)}, u32[]{:S(2)}) copy-start(s32[4,5]{1,0:T(4,128)} %pattern_ref.1) | copy-start | bytes 244
  135.4 20.9 %collective-permute-start.17 = (bf16[16,5,64,128]{3,2,1,0:T(8,128)(2,1)S(1)}, bf16[16,5,64,128]{3,2,1,0:T(8,128)(2,1)S(1)}, u32[]{:S(2)}, u32[]{:S(2)}) collective-permute-start(bf16[16,5,64,128]{3,2,1,0:T(8,128)(2,1)S(1)} %settle.3.own_ref), channel_id=1, source_target_pairs={{1,0},{2,1},{3,2},{5,4},{6,5},{7,6},{9,8},{10,9},{11,10},{13,12},{... | collective-permute-start | bytes 3932168 | tf_op jit(solution)/shard_map/ppermute | solution.py:379
  141.3 16.5 %collective-permute-start.16 = (bf16[16,5,64,128]{3,2,1,0:T(8,128)(2,1)S(1)}, bf16[16,5,64,128]{3,2,1,0:T(8,128)(2,1)}, u32[]{:S(2)}, u32[]{:S(2)}) collective-permute-start(bf16[16,5,64,128]{3,2,1,0:T(8,128)(2,1)S(1)} %settle.3.own_ref), channel_id=1, source_target_pairs={{0,1},{1,2},{2,3},{4,5},{5,6},{6,7},{8,9},{9,10},{10,11},{12,13},{... | collective-permute-start | bytes 3932168 | tf_op jit(solution)/shard_map/ppermute | solution.py:378

commit v6 on v5

--- a/solution.py
+++ b/solution.py
@@ -18,6 +18,7 @@
 ALL = ("z", "y", "x", "s")
 PLANE = ("y", "x")
 CUT = 3
+ORDER = (0, 3, 1, 2)
 BUF = 2
 HEAVY = 100 * 10**9
 STEPS = (3, 1, -1, -3)
@@ -215,36 +216,33 @@
 
 
 def settle_kernel(slots, pieces, *refs):
-    in_refs, more, out_ref, turn = refs[:pieces], refs[pieces:-2], refs[-2], refs[-1]
+    in_refs, out_ref, turn = refs[:pieces], refs[-2], refs[-1]
     turn[...] = turning()
-    for j in range(4):
-        x = [(in_refs[j][:, s] if pieces == 4 else in_refs[0][:, j, s]).reshape(256, 128) for s in range(slots)]
+    for k, j in enumerate(ORDER[::-1]):
+        x = [(in_refs[k][:, s] if pieces == 4 else in_refs[0][:, j, s]).reshape(256, 128) for s in range(slots)]
         x = jnp.dot(turn[...], jnp.concatenate(x, 1), preferred_element_type=jnp.float32).astype(jnp.bfloat16)
         for s in range(slots):
             out_ref[:, s, j * NP : (j + 1) * NP] = x[:, s * 128 : (s + 1) * 128].reshape(NL, NP, 128)
-    for ref in more:
-        out_ref[:, slots:] = ref[...]
-
-
-def settle(inputs, more, flops):
+
+
+def settle(inputs, flops):
     slots = inputs[0].shape[-3]
-    total = slots + sum(m.shape[1] for m in more)
     vmem = pl.BlockSpec(memory_space=pltpu.VMEM)
     return pl.pallas_call(
         functools.partial(settle_kernel, slots, len(inputs)),
-        out_shape=jax.ShapeDtypeStruct((NL, total, 64, 128), jnp.bfloat16),
-        in_specs=[vmem] * (len(inputs) + len(more)),
+        out_shape=jax.ShapeDtypeStruct((NL, slots, 64, 128), jnp.bfloat16),
+        in_specs=[vmem] * len(inputs),
         out_specs=vmem,
         scratch_shapes=[pltpu.VMEM((256, 256), jnp.bfloat16)],
-        cost_estimate=pl.CostEstimate(flops=flops, bytes_accessed=NL * total * 64 * 128 * 4, transcendentals=0),
+        cost_estimate=pl.CostEstimate(flops=flops, bytes_accessed=NL * slots * 64 * 128 * 4, transcendentals=0),
         compiler_params=pltpu.CompilerParams(vmem_limit_bytes=12 << 20),
         name="settle",
-    )(*inputs, *more)
+    )(*(inputs[j] for j in ORDER[::-1]) if len(inputs) == 4 else inputs)
 
 
 def gather_kernel(*refs):
-    for j in range(4):
-        refs[4][:, j] = refs[j][...]
+    for k, j in enumerate(ORDER):
+        refs[4][:, j] = refs[k][...]
 
 
 def gather(pieces, flops):
@@ -258,7 +256,7 @@
         cost_estimate=pl.CostEstimate(flops=flops, bytes_accessed=8 * pieces[0].size * 2, transcendentals=0),
         compiler_params=pltpu.CompilerParams(vmem_limit_bytes=12 << 20),
         name="gather",
-    )(*pieces)
+    )(*(pieces[j] for j in ORDER))
 
 
 def marker(value, pieces, flops):
@@ -278,8 +276,9 @@
     )(value, *pieces)
 
 
-def screen_kernel(row_ref, pattern_ref, w_ref, up_ref, own_ref, down_ref, out_ref):
-    slots = own_ref.shape[1]
+def screen_kernel(row_ref, pattern_ref, w_ref, *refs):
+    pairs, out_ref = (refs[0:2], refs[2:4], refs[4:6]), refs[6]
+    slots = out_ref.shape[1]
     rows = pattern_ref.shape[0]
     row = row_ref[0]
     found = {}
@@ -296,16 +295,19 @@
                 hit = jnp.where(same, 1, hit)
             found[d, s] = at, hit
     w = w_ref[...]
-    for l in range(own_ref.shape[0]):
+    for l in range(out_ref.shape[0]):
         cols = []
         for s in range(slots):
             blocks = []
-            for d, ref in enumerate((up_ref, own_ref, down_ref)):
+            for d, (low, high) in enumerate(pairs):
+                cut = low.shape[1]
                 if d == 1:
-                    blocks.append(ref[l, s])
+                    blocks.append(low[l, s] if s < cut else high[l, s - cut])
                 else:
                     at, hit = found[d, s]
-                    got = ref[l, at]
+                    one = low[l, jnp.minimum(at, cut - 1)]
+                    two = high[l, jnp.maximum(at - cut, 0)]
+                    got = jnp.where(at < cut, one, two)
                     blocks.append(jnp.where(hit > 0, got, jnp.zeros_like(got)))
             cols.append(jnp.concatenate(blocks, 0))
         res = jnp.dot(w, jnp.concatenate(cols, 1), preferred_element_type=jnp.float32)
@@ -314,22 +316,24 @@
 
 
 def screen(row, pattern, weights, up, own, down):
-    el, slots, bi, wide = own.shape
     step = 4
-    block = pl.BlockSpec((step, slots, bi, wide), lambda i: (i, 0, 0, 0))
     smem = pl.BlockSpec(memory_space=pltpu.SMEM)
+    arrays = [*up, *own, *down]
+    blocks = [pl.BlockSpec((step, *a.shape[1:]), lambda i: (i, 0, 0, 0)) for a in arrays]
+    el, _, bi, wide = own[0].shape
+    slots = own[0].shape[1] + own[1].shape[1]
     return pl.pallas_call(
         screen_kernel,
         grid=(el // step,),
-        out_shape=jax.ShapeDtypeStruct(own.shape, jnp.bfloat16),
-        in_specs=[smem, smem, pl.BlockSpec(weights.shape, lambda i: (0, 0)), block, block, block],
-        out_specs=block,
+        out_shape=jax.ShapeDtypeStruct((el, slots, bi, wide), jnp.bfloat16),
+        in_specs=[smem, smem, pl.BlockSpec(weights.shape, lambda i: (0, 0)), *blocks],
+        out_specs=pl.BlockSpec((step, slots, bi, wide), lambda i: (i, 0, 0, 0)),
         cost_estimate=pl.CostEstimate(
-            flops=2 * el * slots * bi * 3 * bi * wide, bytes_accessed=4 * own.size * 2, transcendentals=0
+            flops=2 * el * slots * bi * 3 * bi * wide, bytes_accessed=8 * el * slots * bi * wide, transcendentals=0
         ),
         compiler_params=pltpu.CompilerParams(vmem_limit_bytes=12 << 20),
         name="screen",
-    )(row, pattern, weights, up, own, down)
+    )(row, pattern, weights, *arrays)
 
 
 def shards(g_less, g_greater, coulomb, pattern):
@@ -372,12 +376,19 @@
 
     hi = lax.all_to_all(hi, PLANE, split_axis=0, concat_axis=0, tiled=True)
     lo = gather([hop(p, STEPS[j]) for j, p in enumerate(lo)], 0)
-    hi = settle([hop(hi[:, j], STEPS[j]) for j in range(4)], [], 0)
+    hi = settle([hop(hi[:, j], STEPS[j]) for j in range(4)], HEAVY)
     lo = lax.all_to_all(lo, PLANE, split_axis=0, concat_axis=0, tiled=True)
-    own = settle([lo], [hi], 0)
-    up = lax.ppermute(own, "s", [(0, 1), (1, 2), (2, 3)])
-    down = lax.ppermute(own, "s", [(1, 0), (2, 1), (3, 2)])
-    return screen(s_row.reshape(1), pattern, weights, up, own, down)[:, None]
+    lo = settle([after(lo, hi)], 0)
+
+    def halo(cells):
+        up = lax.ppermute(cells, "s", [(0, 1), (1, 2), (2, 3)])
+        down = lax.ppermute(cells, "s", [(1, 0), (2, 1), (3, 2)])
+        return up, down
+
+    up_hi, down_hi = halo(hi)
+    lo = lax.optimization_barrier([lo, up_hi, down_hi])[0]
+    up_lo, down_lo = halo(lo)
+    return screen(s_row.reshape(1), pattern, weights, (up_lo, up_hi), (lo, hi), (down_lo, down_hi))[:, None]
 
 
 def solution(mesh):

time: 163 us -> 157 us (0.963)
  waiting for transfers between devices: 72.3 us -> 59.7 us
  starting transfers between devices: 62.2 us -> 68.7 us
  local copies, waits for them, and re-layouts: 1.43 us -> 3.22 us
    ppermute x16, waiting for transfers between devices: 40.5 us -> 29.3 us  [hop(): return lax.ppermute(piece, ALL, perm)]
    ppermute x2 -> x4, starting transfers between devices: 7.77 us -> 14.4 us  [the longest x2 9.77 us: halo(): down = lax.ppermute(cells, 's', [(1, 0), (2, 1), (3, 2)])]
    unnamed x5 -> x9, local copies, waits for them, and re-layouts: 0.12 us -> 1.95 us
    ppermute x2 -> x4, waiting for transfers between devices: 14 us -> 13.8 us  [the longest x2 11.3 us: halo(): down = lax.ppermute(cells, 's', [(1, 0), (2, 1), (3, 2)])]
  transfers between devices with their start and end apart: 22 -> 24, of which waited for: 11 -> 15; matrix products, arithmetic and copies ran while one was open for 0% -> 0% of each run, Pallas kernels for 10% -> 11%
where the time goes in v6:
time: 157 us
  starting transfers between devices  68.7 us (44%)
  waiting for transfers between devices  59.7 us (38%)
  Pallas kernels  24.5 us (16%)
  local copies, waits for them, and re-layouts  3.22 us (2%)
    ppermute x16, starting transfers between devices, hop(): return lax.ppermute(piece, ALL, perm)  30.7 us
    ppermute x16, waiting for transfers between devices, hop(): return lax.ppermute(piece, ALL, perm)  29.3 us
    pallas_call x2, Pallas kernels, correlate(): pl.pallas_call(functools.partial(correlate_kernel, slots, len(inputs), sp...  14.5 us
    all_to_all x1, waiting for transfers between devices, shards(): late = lax.all_to_all(late, PLANE, split_axis=0, concat_axis=0, tiled=True)  11.4 us
    ppermute x2, waiting for transfers between devices, halo(): down = lax.ppermute(cells, 's', [(1, 0), (2, 1), (3, 2)])  11.3 us
    ppermute x2, starting transfers between devices, halo(): down = lax.ppermute(cells, 's', [(1, 0), (2, 1), (3, 2)])  9.77 us
    all_to_all x1, starting transfers between devices, shards(): lax.all_to_all(early, PLANE, split_axis=0, concat_axis=0, tiled=True)  6.76 us
    all_to_all x1, starting transfers between devices, shards(): late = lax.all_to_all(late, PLANE, split_axis=0, concat_axis=0, tiled=True)  6.02 us
  transfers between devices with their start and end apart: 24, of which 15 were waited for; matrix products, arithmetic and copies ran while one was open for 0% of the time, Pallas kernels for 11%

profile of v6, /device:TPU:1, one launch (start us, length us, event | category | flops | bytes accessed | tf_op | source)
XLA Modules:
  0.0 156.8 jit_solution(15077236316021540686)
XLA Ops:
  0.0 4.0 %prepare.1 = (bf16[16,4,2,3,16,128]{5,4,3,2,1,0:T(8,128)(2,1)}, bf16[16,2,2,16,128]{4,3,2,1,0:T(8,128)(2,1)}, bf16[16,2,2,16,128]{4,3,2,1,0:T(8,128)(2,1)}, bf16...) custom-call(s32[1]{0:T(128)} %bitcast.6.turn_ref, bf16[16,5,64,128]{3,2,1,0:T(8,128)(2,1)} %bitcast.43, ...), custom_call_target="tpu_custom_call" | custom-call | bytes 5242880 | tf_op jit(solution)/shard_map/prepare/pallas_call | solution.py:201
  4.0 5.2 %collective-permute-start = (bf16[16,2,2,16,128]{4,3,2,1,0:T(8,128)(2,1)}, bf16[16,2,2,16,128]{4,3,2,1,0:T(8,128)(2,1)S(1)}, u32[]{:S(2)}, u32[]{:S(2)}) collective-permute-start(bf16[16,2,2,16,128]{4,3,2,1,0:T(8,128)(2,1)} %get-tuple-element.20), channel_id=1, source_target_pairs={{0,66},{1,67},{2,128},{3,129},{4,70},{5,71},{6,132},{7,133},{8,74}... | collective-permute-start | bytes 786440 | tf_op jit(solution)/shard_map/ppermute | solution.py:53
  9.2 2.2 %collective-permute-start.1 = (bf16[16,2,2,16,128]{4,3,2,1,0:T(8,128)(2,1)}, bf16[16,2,2,16,128]{4,3,2,1,0:T(8,128)(2,1)S(1)}, u32[]{:S(2)}, u32[]{:S(2)}) collective-permute-start(bf16[16,2,2,16,128]{4,3,2,1,0:T(8,128)(2,1)} %get-tuple-element.21), channel_id=1, source_target_pairs={{0,130},{1,131},{2,192},{3,193},{4,134},{5,135},{6,196},{7,197},{8... | collective-permute-start | bytes 786440 | tf_op jit(solution)/shard_map/ppermute | solution.py:53
  11.4 0.7 collective-permute-start.2
  12.2 1.9 %collective-permute-start.3 = (bf16[16,2,2,16,128]{4,3,2,1,0:T(8,128)(2,1)}, bf16[16,2,2,16,128]{4,3,2,1,0:T(8,128)(2,1)S(1)}, u32[]{:S(2)}, u32[]{:S(2)}) collective-permute-start(bf16[16,2,2,16,128]{4,3,2,1,0:T(8,128)(2,1)} %get-tuple-element.23), channel_id=1, source_target_pairs={{0,194},{1,195},{2,0},{3,1},{4,198},{5,199},{6,4},{7,5},{8,202},{9... | collective-permute-start | bytes 786440 | tf_op jit(solution)/shard_map/ppermute | solution.py:53
  14.1 6.8 %all-to-all-start.1 = ((bf16[16,4,2,3,16,128]{5,4,3,2,1,0:T(8,128)(2,1)}), bf16[16,4,2,3,16,128]{5,4,3,2,1,0:T(8,128)(2,1)S(1)}, u32[]{:S(2)}, u32[]{:S(2)}) async-start(bf16[16,4,2,3,16,128]{5,4,3,2,1,0:T(8,128)(2,1)} %get-tuple-element.24), calls=%async_computation.1 | async-start | bytes 3145728 | tf_op jit(solution)/shard_map/all_to_all | solution.py:367
  20.9 4.6 %collective-permute-done.refs_0_ = bf16[16,2,2,16,128]{4,3,2,1,0:T(8,128)(2,1)S(1)} collective-permute-done((bf16[16,2,2,16,128]{4,3,2,1,0:T(8,128)(2,1)}, bf16[16,2,2,16,128]{4,3,2,1,0:T(8,128)(2,1)S(1)}, u32[]{:S(2)}, u32[]{:S(2)}) %collective-permute-start) | collective-permute-done | bytes 262176 | tf_op jit(solution)/shard_map/ppermute | solution.py:53
  25.5 0.0 collective-permute-done.1.refs_1_
  25.5 8.5 %collective-permute-done.2.refs_2_ = bf16[16,2,2,16,128]{4,3,2,1,0:T(8,128)(2,1)S(1)} collective-permute-done((bf16[16,2,2,16,128]{4,3,2,1,0:T(8,128)(2,1)}, bf16[16,2,2,16,128]{4,3,2,1,0:T(8,128)(2,1)S(1)}, u32[]{:S(2)}, u32[]{:S(2)}) %collective-permute-start.2) | collective-permute-done | bytes 262176 | tf_op jit(solution)/shard_map/ppermute | solution.py:53
  34.0 1.7 %collective-permute-done.3.refs_3_ = bf16[16,2,2,16,128]{4,3,2,1,0:T(8,128)(2,1)S(1)} collective-permute-done((bf16[16,2,2,16,128]{4,3,2,1,0:T(8,128)(2,1)}, bf16[16,2,2,16,128]{4,3,2,1,0:T(8,128)(2,1)S(1)}, u32[]{:S(2)}, u32[]{:S(2)}) %collective-permute-start.3) | collective-permute-done | bytes 262176 | tf_op jit(solution)/shard_map/ppermute | solution.py:53
  35.6 1.0 gather.2
  36.7 5.0 %all-to-all-done.1 = bf16[16,4,2,3,16,128]{5,4,3,2,1,0:T(8,128)(2,1)S(1)} async-done(((bf16[16,4,2,3,16,128]{5,4,3,2,1,0:T(8,128)(2,1)}), bf16[16,4,2,3,16,128]{5,4,3,2,1,0:T(8,128)(2,1)S(1)}, u32[]{:S(2)}, u32[]{:S(2)}) %all-to-all-start.1) | async-done | bytes 1572896 | tf_op jit(solution)/shard_map/all_to_all | solution.py:367
  41.6 1.1 slice_bitcast_fusion
  42.8 1.5 collective-permute-start.5
  44.3 0.0 collective-permute-start.4
  44.3 0.1 pad_maximum_fusion.refs_0_
  44.4 6.0 %all-to-all-start = ((bf16[16,4,2,2,16,128]{5,4,3,2,1,0:T(8,128)(2,1)}), bf16[16,4,2,2,16,128]{5,4,3,2,1,0:T(8,128)(2,1)S(1)}, u32[]{:S(2)}, u32[]{:S(2)}) async-start(bf16[16,4,2,2,16,128]{5,4,3,2,1,0:T(8,128)(2,1)} %gather.2), calls=%async_computation | async-start | bytes 2097152 | tf_op jit(solution)/shard_map/all_to_all | solution.py:370
  50.4 2.8 %collective-permute-start.7 = (bf16[16,2,3,16,128]{4,3,2,1,0:T(8,128)(2,1)S(1)}, bf16[16,2,3,16,128]{4,3,2,1,0:T(8,128)(2,1)}, u32[]{:S(2)}, u32[]{:S(2)}) collective-permute-start(bf16[16,2,3,16,128]{4,3,2,1,0:T(8,128)(2,1)S(1)} %get-tuple-element.35), channel_id=1, source_target_pairs={{0,130},{1,131},{2,192},{3,193},{4,134},{5,135},{6,196},{7,197},{8... | collective-permute-start | bytes 1179656 | tf_op jit(solution)/shard_map/ppermute | solution.py:53
  53.2 0.9 collective-permute-start.6
  54.2 0.0 collective-permute-done.5.refs_2_
  54.2 0.0 collective-permute-done.4.refs_1_
  54.2 11.4 %all-to-all-done.refs_0_ = bf16[16,4,2,2,16,128]{5,4,3,2,1,0:T(8,128)(2,1)S(1)} async-done(((bf16[16,4,2,2,16,128]{5,4,3,2,1,0:T(8,128)(2,1)}), bf16[16,4,2,2,16,128]{5,4,3,2,1,0:T(8,128)(2,1)S(1)}, u32[]{:S(2)}, u32[]{:S(2)}) %all-to-all-start) | async-done | bytes 1048608 | tf_op jit(solution)/shard_map/all_to_all | solution.py:370
  65.6 6.6 %correlate.2 = bf16[16,4,2,16,128]{4,3,2,1,0:T(8,128)(2,1)} custom-call(f32[3]{0:T(128)S(1)} %marker.1.rot_ref, bf16[16,4,2,2,16,128]{5,4,3,2,1,0:T(8,128)(2,1)S(1)} %all-to-all-done.refs_0_, bf16[4,512,256]{2,1,0:T(8,128)(2,1)} %constant.87.clone.refs_1_.refs_4_, bf16[4,512,256]{2,1,0:T(8,128)(2,1)} %constant.88.clone.refs_2_.refs_5_), custom_call_target="tpu_custom_call" | custom-call | bytes 3670016 | tf_op jit(solution)/shard_map/correlate/pallas_call | solution.py:139
  72.2 5.0 %all-to-all-start.3 = ((bf16[16,4,2,16,128]{4,3,2,1,0:T(8,128)(2,1)}), bf16[16,4,2,16,128]{4,3,2,1,0:T(8,128)(2,1)S(1)}, u32[]{:S(2)}, u32[]{:S(2)}) async-start(bf16[16,4,2,16,128]{4,3,2,1,0:T(8,128)(2,1)} %correlate.2), calls=%async_computation.3 | async-start | bytes 1048576 | tf_op jit(solution)/shard_map/all_to_all | solution.py:377
  77.2 5.6 %collective-permute-done.6.refs_0_ = bf16[16,2,3,16,128]{4,3,2,1,0:T(8,128)(2,1)S(1)} collective-permute-done((bf16[16,2,3,16,128]{4,3,2,1,0:T(8,128)(2,1)}, bf16[16,2,3,16,128]{4,3,2,1,0:T(8,128)(2,1)S(1)}, u32[]{:S(2)}, u32[]{:S(2)}) %collective-permute-start.6) | collective-permute-done | bytes 393248 | tf_op jit(solution)/shard_map/ppermute | solution.py:53
  82.8 0.0 collective-permute-done.7.refs_3_
  82.8 7.9 %correlate.3 = (bf16[16,3,16,128]{3,2,1,0:T(8,128)(2,1)S(1)}, bf16[16,3,16,128]{3,2,1,0:T(8,128)(2,1)S(1)}, bf16[16,3,16,128]{3,2,1,0:T(8,128)(2,1)S(1)}, bf16[16,3,16,128]{3,2,1,0:T(8,128)(2,1)S(1)}) custom-call(f32[3]{0:T(128)S(1)} %marker.1.rot_ref, bf16[16,2,3,16,128]{4,3,2,1,0:T(8,128)(2,1)S(1)} %collective-permute-done.6.refs_0_, ...), custom_call_target="tpu_custom_call" | custom-call | flops 99999997952 | bytes 4456448 | tf_op jit(solution)/shard_map/correlate/pallas_call | solution.py:139
  90.7 0.1 collective-permute-start.8
  90.8 4.5 %collective-permute-start.9 = (bf16[16,3,16,128]{3,2,1,0:T(8,128)(2,1)S(1)}, bf16[16,3,16,128]{3,2,1,0:T(8,128)(2,1)S(1)}, u32[]{:S(2)}, u32[]{:S(2)}) collective-permute-start(bf16[16,3,16,128]{3,2,1,0:T(8,128)(2,1)S(1)} %get-tuple-element.30), channel_id=1, source_target_pairs={{0,130},{1,131},{2,192},{3,193},{4,134},{5,135},{6,196},{7,197},{8... | collective-permute-start | bytes 589832 | tf_op jit(solution)/shard_map/ppermute | solution.py:53
  95.2 0.0 collective-permute-start.10
  95.2 2.7 %collective-permute-start.11 = (bf16[16,3,16,128]{3,2,1,0:T(8,128)(2,1)S(1)}, bf16[16,3,16,128]{3,2,1,0:T(8,128)(2,1)S(1)}, u32[]{:S(2)}, u32[]{:S(2)}) collective-permute-start(bf16[16,3,16,128]{3,2,1,0:T(8,128)(2,1)S(1)} %get-tuple-element.32), channel_id=1, source_target_pairs={{0,194},{1,195},{2,0},{3,1},{4,198},{5,199},{6,4},{7,5},{8,202},{9... | collective-permute-start | bytes 589832 | tf_op jit(solution)/shard_map/ppermute | solution.py:53
  98.0 0.1 collective-permute-start.15
  98.0 6.7 %collective-permute-done.8.refs_0_ = bf16[16,3,16,128]{3,2,1,0:T(8,128)(2,1)S(1)} collective-permute-done((bf16[16,3,16,128]{3,2,1,0:T(8,128)(2,1)S(1)}, bf16[16,3,16,128]{3,2,1,0:T(8,128)(2,1)S(1)}, u32[]{:S(2)}, u32[]{:S(2)}) %collective-permute-start.8) | collective-permute-done | bytes 196640 | tf_op jit(solution)/shard_map/ppermute | solution.py:53
  104.8 5.8 %collective-permute-start.14 = (bf16[16,2,16,128]{3,2,1,0:T(8,128)(2,1)S(1)}, bf16[16,2,16,128]{3,2,1,0:T(8,128)(2,1)S(1)}, u32[]{:S(2)}, u32[]{:S(2)}) collective-permute-start(bf16[16,2,16,128]{3,2,1,0:T(8,128)(2,1)S(1)} %get-tuple-element.40), channel_id=1, source_target_pairs={{0,130},{1,131},{2,192},{3,193},{4,134},{5,135},{6,196},{7,197},{8... | collective-permute-start | bytes 393224 | tf_op jit(solution)/shard_map/ppermute | solution.py:53
  110.5 0.0 collective-permute-done.9.refs_1_
  110.5 0.0 collective-permute-start.13
  110.5 0.4 collective-permute-done.10.refs_2_
  111.0 2.2 %collective-permute-start.12 = (bf16[16,2,16,128]{3,2,1,0:T(8,128)(2,1)S(1)}, bf16[16,2,16,128]{3,2,1,0:T(8,128)(2,1)S(1)}, u32[]{:S(2)}, u32[]{:S(2)}) collective-permute-start(bf16[16,2,16,128]{3,2,1,0:T(8,128)(2,1)S(1)} %get-tuple-element.42), channel_id=1, source_target_pairs={{0,194},{1,195},{2,0},{3,1},{4,198},{5,199},{6,4},{7,5},{8,202},{9... | collective-permute-start | bytes 393224 | tf_op jit(solution)/shard_map/ppermute | solution.py:53
  113.2 0.0 collective-permute-done.11.refs_3_
  113.2 0.9 gather.3
  114.1 5.8 %all-to-all-start.2 = ((bf16[16,4,3,16,128]{4,3,2,1,0:T(8,128)(2,1)}), bf16[16,4,3,16,128]{4,3,2,1,0:T(8,128)(2,1)S(1)}, u32[]{:S(2)}, u32[]{:S(2)}) async-start(bf16[16,4,3,16,128]{4,3,2,1,0:T(8,128)(2,1)} %gather.3), calls=%async_computation.2 | async-start | bytes 1572864 | tf_op jit(solution)/shard_map/all_to_all | solution.py:380
  120.0 0.0 collective-permute-done.14.refs_2_
  120.0 1.5 collective-permute-done.13.refs_1_
  121.5 0.3 collective-permute-done.12.refs_0_
  121.8 0.3 settle.2.refs_3_
  122.1 0.0 copy-start.3
  122.1 0.0 copy-start.2
  122.1 6.2 %collective-permute-start.17 = (bf16[16,2,64,128]{3,2,1,0:T(8,128)(2,1)S(1)}, bf16[16,2,64,128]{3,2,1,0:T(8,128)(2,1)S(1)}, u32[]{:S(2)}, u32[]{:S(2)}) collective-permute-start(bf16[16,2,64,128]{3,2,1,0:T(8,128)(2,1)S(1)} %settle.2.refs_3_), channel_id=1, source_target_pairs={{1,0},{2,1},{3,2},{5,4},{6,5},{7,6},{9,8},{10,9},{11,10},{13,12},{... | collective-permute-start | bytes 1572872 | tf_op jit(solution)/shard_map/ppermute | solution.py:385
  128.3 1.9 %collective-permute-start.16 = (bf16[16,2,64,128]{3,2,1,0:T(8,128)(2,1)S(1)}, bf16[16,2,64,128]{3,2,1,0:T(8,128)(2,1)S(1)}, u32[]{:S(2)}, u32[]{:S(2)}) collective-permute-start(bf16[16,2,64,128]{3,2,1,0:T(8,128)(2,1)S(1)} %settle.2.refs_3_), channel_id=1, source_target_pairs={{0,1},{1,2},{2,3},{4,5},{5,6},{6,7},{8,9},{9,10},{10,11},{12,13},{... | collective-permute-start | bytes 1572872 | tf_op jit(solution)/shard_map/ppermute | solution.py:384
  130.2 0.2 all-to-all-done.2.refs_0_
  130.4 0.4 settle.3.refs_2_
  130.9 4.2 %collective-permute-done.17.refs_5_ = bf16[16,2,64,128]{3,2,1,0:T(8,128)(2,1)S(1)} collective-permute-done((bf16[16,2,64,128]{3,2,1,0:T(8,128)(2,1)S(1)}, bf16[16,2,64,128]{3,2,1,0:T(8,128)(2,1)S(1)}, u32[]{:S(2)}, u32[]{:S(2)}) %collective-permute-start.17) | collective-permute-done | bytes 524320 | tf_op jit(solution)/shard_map/ppermute | solution.py:385
  135.0 1.3 collective-permute-done.16.refs_1_
  136.3 0.8 copy-done
  137.1 3.6 %collective-permute-start.19 = (bf16[16,3,64,128]{3,2,1,0:T(8,128)(2,1)S(1)}, bf16[16,3,64,128]{3,2,1,0:T(8,128)(2,1)S(1)}, u32[]{:S(2)}, u32[]{:S(2)}) collective-permute-start(bf16[16,3,64,128]{3,2,1,0:T(8,128)(2,1)S(1)} %settle.3.refs_2_), channel_id=1, source_target_pairs={{1,0},{2,1},{3,2},{5,4},{6,5},{7,6},{9,8},{10,9},{11,10},{13,12},{... | collective-permute-start | bytes 2359304 | tf_op jit(solution)/shard_map/ppermute | solution.py:385
  140.7 2.7 %collective-permute-start.18 = (bf16[16,3,64,128]{3,2,1,0:T(8,128)(2,1)S(1)}, bf16[16,3,64,128]{3,2,1,0:T(8,128)(2,1)S(1)}, u32[]{:S(2)}, u32[]{:S(2)}) collective-permute-start(bf16[16,3,64,128]{3,2,1,0:T(8,128)(2,1)S(1)} %settle.3.refs_2_), channel_id=1, source_target_pairs={{0,1},{1,2},{2,3},{4,5},{5,6},{6,7},{8,9},{9,10},{10,11},{12,13},{... | collective-permute-start | bytes 2359304 | tf_op jit(solution)/shard_map/ppermute | solution.py:384
  143.4 0.1 copy.19
  143.6 0.1 add_select_fusion
  143.6 0.2 fusion
  143.9 0.1 copy.30.w_ref
  144.0 7.2 %collective-permute-done.19.refs_4_ = bf16[16,3,64,128]{3,2,1,0:T(8,128)(2,1)S(1)} collective-permute-done((bf16[16,3,64,128]{3,2,1,0:T(8,128)(2,1)S(1)}, bf16[16,3,64,128]{3,2,1,0:T(8,128)(2,1)S(1)}, u32[]{:S(2)}, u32[]{:S(2)}) %collective-permute-start.19) | collective-permute-done | bytes 786464 | tf_op jit(solution)/shard_map/ppermute | solution.py:385
  151.1 1.2 collective-permute-done.18.refs_0_
  152.3 1.0 copy-done.1
  153.4 3.4 %screen.1 = bf16[16,5,64,128]{3,2,1,0:T(8,128)(2,1)} custom-call(s32[1]{0:T(128)} %bitcast.row_ref, s32[4,5]{1,0:T(4,128)S(1)} %copy-done.2, bf16[64,192]{1,0:T(8,128)(2,1)S(1)} %copy.30.w_ref, bf16[16,3,64,128]{3,2,1,0:T(8,128)(2,1)S(1)} %collective-permute-done.18.refs_0_, bf16[16,2,64,128]{3,2,1,0:T(8,128)(2,1)S(1)} %copy-done.1, ...), custom_call_target="tpu_custom_call" | custom-call | flops 251658240 | bytes 5242880 | tf_op jit(solution)/shard_map/screen/pallas_call | solution.py:325
  (10 shorter events, 0.1 us)
Async XLA Ops:
  4.0 21.5 %collective-permute-start = (bf16[16,2,2,16,128]{4,3,2,1,0:T(8,128)(2,1)}, bf16[16,2,2,16,128]{4,3,2,1,0:T(8,128)(2,1)S(1)}, u32[]{:S(2)}, u32[]{:S(2)}) collective-permute-start(bf16[16,2,2,16,128]{4,3,2,1,0:T(8,128)(2,1)} %get-tuple-element.20), channel_id=1, source_target_pairs={{0,66},{1,67},{2,128},{3,129},{4,70},{5,71},{6,132},{7,133},{8,74}... | collective-permute-start | bytes 786440 | tf_op jit(solution)/shard_map/ppermute | solution.py:53
  9.2 16.3 %collective-permute-start.1 = (bf16[16,2,2,16,128]{4,3,2,1,0:T(8,128)(2,1)}, bf16[16,2,2,16,128]{4,3,2,1,0:T(8,128)(2,1)S(1)}, u32[]{:S(2)}, u32[]{:S(2)}) collective-permute-start(bf16[16,2,2,16,128]{4,3,2,1,0:T(8,128)(2,1)} %get-tuple-element.21), channel_id=1, source_target_pairs={{0,130},{1,131},{2,192},{3,193},{4,134},{5,135},{6,196},{7,197},{8... | collective-permute-start | bytes 786440 | tf_op jit(solution)/shard_map/ppermute | solution.py:53
  11.4 22.5 %collective-permute-start.2 = (bf16[16,2,2,16,128]{4,3,2,1,0:T(8,128)(2,1)}, bf16[16,2,2,16,128]{4,3,2,1,0:T(8,128)(2,1)S(1)}, u32[]{:S(2)}, u32[]{:S(2)}) collective-permute-start(bf16[16,2,2,16,128]{4,3,2,1,0:T(8,128)(2,1)} %get-tuple-element.22), channel_id=1, source_target_pairs={{0,2},{1,3},{2,64},{3,65},{4,6},{5,7},{6,68},{7,69},{8,10},{9,11},... | collective-permute-start | bytes 786440 | tf_op jit(solution)/shard_map/ppermute | solution.py:53
  12.2 23.4 %collective-permute-start.3 = (bf16[16,2,2,16,128]{4,3,2,1,0:T(8,128)(2,1)}, bf16[16,2,2,16,128]{4,3,2,1,0:T(8,128)(2,1)S(1)}, u32[]{:S(2)}, u32[]{:S(2)}) collective-permute-start(bf16[16,2,2,16,128]{4,3,2,1,0:T(8,128)(2,1)} %get-tuple-element.23), channel_id=1, source_target_pairs={{0,194},{1,195},{2,0},{3,1},{4,198},{5,199},{6,4},{7,5},{8,202},{9... | collective-permute-start | bytes 786440 | tf_op jit(solution)/shard_map/ppermute | solution.py:53
  14.1 27.5 %all-to-all-start.1 = ((bf16[16,4,2,3,16,128]{5,4,3,2,1,0:T(8,128)(2,1)}), bf16[16,4,2,3,16,128]{5,4,3,2,1,0:T(8,128)(2,1)S(1)}, u32[]{:S(2)}, u32[]{:S(2)}) async-start(bf16[16,4,2,3,16,128]{5,4,3,2,1,0:T(8,128)(2,1)} %get-tuple-element.24), calls=%async_computation.1 | async-start | bytes 3145728 | tf_op jit(solution)/shard_map/all_to_all | solution.py:367
  42.8 11.4 %collective-permute-start.5 = (bf16[16,2,3,16,128]{4,3,2,1,0:T(8,128)(2,1)}, bf16[16,2,3,16,128]{4,3,2,1,0:T(8,128)(2,1)S(1)}, u32[]{:S(2)}, u32[]{:S(2)}) collective-permute-start(bf16[16,2,3,16,128]{4,3,2,1,0:T(8,128)(2,1)} %get-tuple-element.37), channel_id=1, source_target_pairs={{0,194},{1,195},{2,0},{3,1},{4,198},{5,199},{6,4},{7,5},{8,202},{9... | collective-permute-start | bytes 1179656 | tf_op jit(solution)/shard_map/ppermute | solution.py:53
  44.3 9.8 %collective-permute-start.4 = (bf16[16,2,3,16,128]{4,3,2,1,0:T(8,128)(2,1)}, bf16[16,2,3,16,128]{4,3,2,1,0:T(8,128)(2,1)S(1)}, u32[]{:S(2)}, u32[]{:S(2)}) collective-permute-start(bf16[16,2,3,16,128]{4,3,2,1,0:T(8,128)(2,1)} %get-tuple-element.38), channel_id=1, source_target_pairs={{0,2},{1,3},{2,64},{3,65},{4,6},{5,7},{6,68},{7,69},{8,10},{9,11},... | collective-permute-start | bytes 1179656 | tf_op jit(solution)/shard_map/ppermute | solution.py:53
  44.4 21.2 %all-to-all-start = ((bf16[16,4,2,2,16,128]{5,4,3,2,1,0:T(8,128)(2,1)}), bf16[16,4,2,2,16,128]{5,4,3,2,1,0:T(8,128)(2,1)S(1)}, u32[]{:S(2)}, u32[]{:S(2)}) async-start(bf16[16,4,2,2,16,128]{5,4,3,2,1,0:T(8,128)(2,1)} %gather.2), calls=%async_computation | async-start | bytes 2097152 | tf_op jit(solution)/shard_map/all_to_all | solution.py:370
  50.4 32.4 %collective-permute-start.7 = (bf16[16,2,3,16,128]{4,3,2,1,0:T(8,128)(2,1)S(1)}, bf16[16,2,3,16,128]{4,3,2,1,0:T(8,128)(2,1)}, u32[]{:S(2)}, u32[]{:S(2)}) collective-permute-start(bf16[16,2,3,16,128]{4,3,2,1,0:T(8,128)(2,1)S(1)} %get-tuple-element.35), channel_id=1, source_target_pairs={{0,130},{1,131},{2,192},{3,193},{4,134},{5,135},{6,196},{7,197},{8... | collective-permute-start | bytes 1179656 | tf_op jit(solution)/shard_map/ppermute | solution.py:53
  53.2 29.6 %collective-permute-start.6 = (bf16[16,2,3,16,128]{4,3,2,1,0:T(8,128)(2,1)}, bf16[16,2,3,16,128]{4,3,2,1,0:T(8,128)(2,1)S(1)}, u32[]{:S(2)}, u32[]{:S(2)}) collective-permute-start(bf16[16,2,3,16,128]{4,3,2,1,0:T(8,128)(2,1)} %get-tuple-element.36), channel_id=1, source_target_pairs={{0,66},{1,67},{2,128},{3,129},{4,70},{5,71},{6,132},{7,133},{8,74}... | collective-permute-start | bytes 1179656 | tf_op jit(solution)/shard_map/ppermute | solution.py:53
  72.2 25.7 %all-to-all-start.3 = ((bf16[16,4,2,16,128]{4,3,2,1,0:T(8,128)(2,1)}), bf16[16,4,2,16,128]{4,3,2,1,0:T(8,128)(2,1)S(1)}, u32[]{:S(2)}, u32[]{:S(2)}) async-start(bf16[16,4,2,16,128]{4,3,2,1,0:T(8,128)(2,1)} %correlate.2), calls=%async_computation.3 | async-start | bytes 1048576 | tf_op jit(solution)/shard_map/all_to_all | solution.py:377
  90.7 14.1 %collective-permute-start.8 = (bf16[16,3,16,128]{3,2,1,0:T(8,128)(2,1)S(1)}, bf16[16,3,16,128]{3,2,1,0:T(8,128)(2,1)S(1)}, u32[]{:S(2)}, u32[]{:S(2)}) collective-permute-start(bf16[16,3,16,128]{3,2,1,0:T(8,128)(2,1)S(1)} %get-tuple-element.29), channel_id=1, source_target_pairs={{0,66},{1,67},{2,128},{3,129},{4,70},{5,71},{6,132},{7,133},{8,74}... | collective-permute-start | bytes 589832 | tf_op jit(solution)/shard_map/ppermute | solution.py:53
  90.8 19.7 %collective-permute-start.9 = (bf16[16,3,16,128]{3,2,1,0:T(8,128)(2,1)S(1)}, bf16[16,3,16,128]{3,2,1,0:T(8,128)(2,1)S(1)}, u32[]{:S(2)}, u32[]{:S(2)}) collective-permute-start(bf16[16,3,16,128]{3,2,1,0:T(8,128)(2,1)S(1)} %get-tuple-element.30), channel_id=1, source_target_pairs={{0,130},{1,131},{2,192},{3,193},{4,134},{5,135},{6,196},{7,197},{8... | collective-permute-start | bytes 589832 | tf_op jit(solution)/shard_map/ppermute | solution.py:53
  95.2 15.7 %collective-permute-start.10 = (bf16[16,3,16,128]{3,2,1,0:T(8,128)(2,1)S(1)}, bf16[16,3,16,128]{3,2,1,0:T(8,128)(2,1)S(1)}, u32[]{:S(2)}, u32[]{:S(2)}) collective-permute-start(bf16[16,3,16,128]{3,2,1,0:T(8,128)(2,1)S(1)} %get-tuple-element.31), channel_id=1, source_target_pairs={{0,2},{1,3},{2,64},{3,65},{4,6},{5,7},{6,68},{7,69},{8,10},{9,11},... | collective-permute-start | bytes 589832 | tf_op jit(solution)/shard_map/ppermute | solution.py:53
  95.2 18.0 %collective-permute-start.11 = (bf16[16,3,16,128]{3,2,1,0:T(8,128)(2,1)S(1)}, bf16[16,3,16,128]{3,2,1,0:T(8,128)(2,1)S(1)}, u32[]{:S(2)}, u32[]{:S(2)}) collective-permute-start(bf16[16,3,16,128]{3,2,1,0:T(8,128)(2,1)S(1)} %get-tuple-element.32), channel_id=1, source_target_pairs={{0,194},{1,195},{2,0},{3,1},{4,198},{5,199},{6,4},{7,5},{8,202},{9... | collective-permute-start | bytes 589832 | tf_op jit(solution)/shard_map/ppermute | solution.py:53
  98.0 22.0 %collective-permute-start.15 = (bf16[16,2,16,128]{3,2,1,0:T(8,128)(2,1)S(1)}, bf16[16,2,16,128]{3,2,1,0:T(8,128)(2,1)S(1)}, u32[]{:S(2)}, u32[]{:S(2)}) collective-permute-start(bf16[16,2,16,128]{3,2,1,0:T(8,128)(2,1)S(1)} %get-tuple-element.39), channel_id=1, source_target_pairs={{0,66},{1,67},{2,128},{3,129},{4,70},{5,71},{6,132},{7,133},{8,74}... | collective-permute-start | bytes 393224 | tf_op jit(solution)/shard_map/ppermute | solution.py:53
  104.8 15.2 %collective-permute-start.14 = (bf16[16,2,16,128]{3,2,1,0:T(8,128)(2,1)S(1)}, bf16[16,2,16,128]{3,2,1,0:T(8,128)(2,1)S(1)}, u32[]{:S(2)}, u32[]{:S(2)}) collective-permute-start(bf16[16,2,16,128]{3,2,1,0:T(8,128)(2,1)S(1)} %get-tuple-element.40), channel_id=1, source_target_pairs={{0,130},{1,131},{2,192},{3,193},{4,134},{5,135},{6,196},{7,197},{8... | collective-permute-start | bytes 393224 | tf_op jit(solution)/shard_map/ppermute | solution.py:53
  110.5 11.0 %collective-permute-start.13 = (bf16[16,2,16,128]{3,2,1,0:T(8,128)(2,1)S(1)}, bf16[16,2,16,128]{3,2,1,0:T(8,128)(2,1)S(1)}, u32[]{:S(2)}, u32[]{:S(2)}) collective-permute-start(bf16[16,2,16,128]{3,2,1,0:T(8,128)(2,1)S(1)} %get-tuple-element.41), channel_id=1, source_target_pairs={{0,2},{1,3},{2,64},{3,65},{4,6},{5,7},{6,68},{7,69},{8,10},{9,11},... | collective-permute-start | bytes 393224 | tf_op jit(solution)/shard_map/ppermute | solution.py:53
  111.0 10.8 %collective-permute-start.12 = (bf16[16,2,16,128]{3,2,1,0:T(8,128)(2,1)S(1)}, bf16[16,2,16,128]{3,2,1,0:T(8,128)(2,1)S(1)}, u32[]{:S(2)}, u32[]{:S(2)}) collective-permute-start(bf16[16,2,16,128]{3,2,1,0:T(8,128)(2,1)S(1)} %get-tuple-element.42), channel_id=1, source_target_pairs={{0,194},{1,195},{2,0},{3,1},{4,198},{5,199},{6,4},{7,5},{8,202},{9... | collective-permute-start | bytes 393224 | tf_op jit(solution)/shard_map/ppermute | solution.py:53
  114.1 16.3 %all-to-all-start.2 = ((bf16[16,4,3,16,128]{4,3,2,1,0:T(8,128)(2,1)}), bf16[16,4,3,16,128]{4,3,2,1,0:T(8,128)(2,1)S(1)}, u32[]{:S(2)}, u32[]{:S(2)}) async-start(bf16[16,4,3,16,128]{4,3,2,1,0:T(8,128)(2,1)} %gather.3), calls=%async_computation.2 | async-start | bytes 1572864 | tf_op jit(solution)/shard_map/all_to_all | solution.py:380
  122.1 21.3 %copy-start.3 = (bf16[1,64,192]{2,1,0:T(8,128)(2,1)S(1)}, bf16[1,64,192]{2,1,0:T(8,128)(2,1)}, u32[]{:S(2)}) copy-start(bf16[1,64,192]{2,1,0:T(8,128)(2,1)} %param.8) | copy-start | bytes 73732
  122.1 30.2 %copy-start.2 = (s32[4,5]{1,0:T(4,128)S(1)}, s32[4,5]{1,0:T(4,128)}, u32[]{:S(2)}) copy-start(s32[4,5]{1,0:T(4,128)} %pattern_ref.1) | copy-start | bytes 244
  122.1 12.9 %collective-permute-start.17 = (bf16[16,2,64,128]{3,2,1,0:T(8,128)(2,1)S(1)}, bf16[16,2,64,128]{3,2,1,0:T(8,128)(2,1)S(1)}, u32[]{:S(2)}, u32[]{:S(2)}) collective-permute-start(bf16[16,2,64,128]{3,2,1,0:T(8,128)(2,1)S(1)} %settle.2.refs_3_), channel_id=1, source_target_pairs={{1,0},{2,1},{3,2},{5,4},{6,5},{7,6},{9,8},{10,9},{11,10},{13,12},{... | collective-permute-start | bytes 1572872 | tf_op jit(solution)/shard_map/ppermute | solution.py:385
  128.3 8.0 %collective-permute-start.16 = (bf16[16,2,64,128]{3,2,1,0:T(8,128)(2,1)S(1)}, bf16[16,2,64,128]{3,2,1,0:T(8,128)(2,1)S(1)}, u32[]{:S(2)}, u32[]{:S(2)}) collective-permute-start(bf16[16,2,64,128]{3,2,1,0:T(8,128)(2,1)S(1)} %settle.2.refs_3_), channel_id=1, source_target_pairs={{0,1},{1,2},{2,3},{4,5},{5,6},{6,7},{8,9},{9,10},{10,11},{12,13},{... | collective-permute-start | bytes 1572872 | tf_op jit(solution)/shard_map/ppermute | solution.py:384
  136.3 0.8 copy-start
  137.1 14.0 %collective-permute-start.19 = (bf16[16,3,64,128]{3,2,1,0:T(8,128)(2,1)S(1)}, bf16[16,3,64,128]{3,2,1,0:T(8,128)(2,1)S(1)}, u32[]{:S(2)}, u32[]{:S(2)}) collective-permute-start(bf16[16,3,64,128]{3,2,1,0:T(8,128)(2,1)S(1)} %settle.3.refs_2_), channel_id=1, source_target_pairs={{1,0},{2,1},{3,2},{5,4},{6,5},{7,6},{9,8},{10,9},{11,10},{13,12},{... | collective-permute-start | bytes 2359304 | tf_op jit(solution)/shard_map/ppermute | solution.py:385
  140.7 11.6 %collective-permute-start.18 = (bf16[16,3,64,128]{3,2,1,0:T(8,128)(2,1)S(1)}, bf16[16,3,64,128]{3,2,1,0:T(8,128)(2,1)S(1)}, u32[]{:S(2)}, u32[]{:S(2)}) collective-permute-start(bf16[16,3,64,128]{3,2,1,0:T(8,128)(2,1)S(1)} %settle.3.refs_2_), channel_id=1, source_target_pairs={{0,1},{1,2},{2,3},{4,5},{5,6},{6,7},{8,9},{9,10},{10,11},{12,13},{... | collective-permute-start | bytes 2359304 | tf_op jit(solution)/shard_map/ppermute | solution.py:384
  152.3 1.0 copy-start.1

commit v7 on v6

--- a/solution.py
+++ b/solution.py
@@ -363,7 +363,9 @@
     cut = CUT
     both = (g_less.reshape(el, slots, bi, wide), g_greater.reshape(el, slots, bi, wide))
     early, late = prepare((turn % 4).reshape(1), *both, cut)
-    late = gather([hop(late[j], STEPS[j]) for j in range(4)], HEAVY)
+    late = [hop(late[j], STEPS[j]) for j in range(4)]
+    late[1], rot = lax.optimization_barrier([late[1], marker(rot, [late[0], late[3]], HEAVY)])
+    late = gather(late, 0)
     early = lax.all_to_all(early, PLANE, split_axis=0, concat_axis=0, tiled=True)
     early = after(early, late)
     early = [hop(early[:, j], STEPS[j]) for j in range(4)]

time: 157 us -> 157 us (level)
  starting transfers between devices: 68.7 us -> 58.3 us
  waiting for transfers between devices: 59.7 us -> 67.5 us
  local copies, waits for them, and re-layouts: 3.22 us -> 5.19 us
    ppermute x16, waiting for transfers between devices: 29.3 us -> 38.1 us  [hop(): return lax.ppermute(piece, ALL, perm)]
    ppermute x16, starting transfers between devices: 30.7 us -> 23 us  [hop(): return lax.ppermute(piece, ALL, perm)]
    ppermute x2, starting transfers between devices: 9.77 us -> 8.11 us  [halo(): down = lax.ppermute(cells, 's', [(1, 0), (2, 1), (3, 2)])]
  transfers between devices with their start and end apart: 24 -> 24, of which waited for: 15 -> 16; matrix products, arithmetic and copies ran while one was open for 0% -> 1% of each run, Pallas kernels for 11% -> 11%
where the time goes in v7:
time: 157 us; the launch traced here: 156 us
  waiting for transfers between devices  67.5 us (43%)
  starting transfers between devices  58.3 us (37%)
  Pallas kernels  24.5 us (16%)
  local copies, waits for them, and re-layouts  5.19 us (3%)
    ppermute x16, waiting for transfers between devices, hop(): return lax.ppermute(piece, ALL, perm)  38.1 us
    ppermute x16, starting transfers between devices, hop(): return lax.ppermute(piece, ALL, perm)  23 us
    pallas_call x2, Pallas kernels, correlate(): pl.pallas_call(functools.partial(correlate_kernel, slots, len(inputs), sp...  14.5 us
    all_to_all x1, waiting for transfers between devices, shards(): late = lax.all_to_all(late, PLANE, split_axis=0, concat_axis=0, tiled=True)  11.8 us
    ppermute x2, waiting for transfers between devices, halo(): down = lax.ppermute(cells, 's', [(1, 0), (2, 1), (3, 2)])  11.1 us
    ppermute x2, starting transfers between devices, halo(): down = lax.ppermute(cells, 's', [(1, 0), (2, 1), (3, 2)])  8.11 us
    all_to_all x1, starting transfers between devices, shards(): lax.all_to_all(early, PLANE, split_axis=0, concat_axis=0, tiled=True)  6.94 us
    all_to_all x1, starting transfers between devices, shards(): late = lax.all_to_all(late, PLANE, split_axis=0, concat_axis=0, tiled=True)  6.2 us
  transfers between devices with their start and end apart: 24, of which 16 were waited for; matrix products, arithmetic and copies ran while one was open for 1% of the time, Pallas kernels for 11%

profile of v7, /device:TPU:1, one launch (start us, length us, event | category | flops | bytes accessed | tf_op | source)
XLA Modules:
  0.0 156.1 jit_solution(1050214629689752148)
XLA Ops:
  0.0 3.9 %prepare.1 = (bf16[16,4,2,3,16,128]{5,4,3,2,1,0:T(8,128)(2,1)}, bf16[16,2,2,16,128]{4,3,2,1,0:T(8,128)(2,1)}, bf16[16,2,2,16,128]{4,3,2,1,0:T(8,128)(2,1)}, bf16...) custom-call(s32[1]{0:T(128)} %bitcast.6.turn_ref, bf16[16,5,64,128]{3,2,1,0:T(8,128)(2,1)} %bitcast.43, ...), custom_call_target="tpu_custom_call" | custom-call | bytes 5242880 | tf_op jit(solution)/shard_map/prepare/pallas_call | solution.py:201
  4.0 5.2 %collective-permute-start = (bf16[16,2,2,16,128]{4,3,2,1,0:T(8,128)(2,1)}, bf16[16,2,2,16,128]{4,3,2,1,0:T(8,128)(2,1)S(1)}, u32[]{:S(2)}, u32[]{:S(2)}) collective-permute-start(bf16[16,2,2,16,128]{4,3,2,1,0:T(8,128)(2,1)} %get-tuple-element.22), channel_id=1, source_target_pairs={{0,66},{1,67},{2,128},{3,129},{4,70},{5,71},{6,132},{7,133},{8,74}... | collective-permute-start | bytes 786440 | tf_op jit(solution)/shard_map/ppermute | solution.py:53
  9.2 2.2 %collective-permute-start.1 = (bf16[16,2,2,16,128]{4,3,2,1,0:T(8,128)(2,1)}, bf16[16,2,2,16,128]{4,3,2,1,0:T(8,128)(2,1)S(1)}, u32[]{:S(2)}, u32[]{:S(2)}) collective-permute-start(bf16[16,2,2,16,128]{4,3,2,1,0:T(8,128)(2,1)} %get-tuple-element.23), channel_id=1, source_target_pairs={{0,130},{1,131},{2,192},{3,193},{4,134},{5,135},{6,196},{7,197},{8... | collective-permute-start | bytes 786440 | tf_op jit(solution)/shard_map/ppermute | solution.py:53
  11.4 6.9 %all-to-all-start.1 = ((bf16[16,4,2,3,16,128]{5,4,3,2,1,0:T(8,128)(2,1)}), bf16[16,4,2,3,16,128]{5,4,3,2,1,0:T(8,128)(2,1)}, u32[]{:S(2)}, u32[]{:S(2)}) async-start(bf16[16,4,2,3,16,128]{5,4,3,2,1,0:T(8,128)(2,1)} %get-tuple-element.28), calls=%async_computation.1 | async-start | bytes 3145728 | tf_op jit(solution)/shard_map/all_to_all | solution.py:369
  18.4 0.8 collective-permute-start.2
  19.2 1.9 %collective-permute-start.3 = (bf16[16,2,2,16,128]{4,3,2,1,0:T(8,128)(2,1)S(1)}, bf16[16,2,2,16,128]{4,3,2,1,0:T(8,128)(2,1)S(1)}, u32[]{:S(2)}, u32[]{:S(2)}) collective-permute-start(bf16[16,2,2,16,128]{4,3,2,1,0:T(8,128)(2,1)S(1)} %copy-done.4), channel_id=1, source_target_pairs={{0,194},{1,195},{2,0},{3,1},{4,198},{5,199},{6,4},{7,5},{8,202},{9... | collective-permute-start | bytes 786440 | tf_op jit(solution)/shard_map/ppermute | solution.py:53
  21.1 0.1 pad_maximum_fusion.refs_0_
  21.2 4.2 %collective-permute-done.refs_1_.refs_0_ = bf16[16,2,2,16,128]{4,3,2,1,0:T(8,128)(2,1)S(1)} collective-permute-done((bf16[16,2,2,16,128]{4,3,2,1,0:T(8,128)(2,1)}, bf16[16,2,2,16,128]{4,3,2,1,0:T(8,128)(2,1)S(1)}, u32[]{:S(2)}, u32[]{:S(2)}) %collective-permute-start) | collective-permute-done | bytes 262176 | tf_op jit(solution)/shard_map/ppermute | solution.py:53
  25.5 0.0 collective-permute-done.1.refs_2_.refs_1_
  25.5 8.6 %collective-permute-done.2.refs_2_ = bf16[16,2,2,16,128]{4,3,2,1,0:T(8,128)(2,1)S(1)} collective-permute-done((bf16[16,2,2,16,128]{4,3,2,1,0:T(8,128)(2,1)S(1)}, bf16[16,2,2,16,128]{4,3,2,1,0:T(8,128)(2,1)S(1)}, u32[]{:S(2)}, u32[]{:S(2)}) %collective-permute-start.2) | collective-permute-done | bytes 262176 | tf_op jit(solution)/shard_map/ppermute | solution.py:53
  34.0 1.7 %collective-permute-done.3.refs_3_ = bf16[16,2,2,16,128]{4,3,2,1,0:T(8,128)(2,1)S(1)} collective-permute-done((bf16[16,2,2,16,128]{4,3,2,1,0:T(8,128)(2,1)S(1)}, bf16[16,2,2,16,128]{4,3,2,1,0:T(8,128)(2,1)S(1)}, u32[]{:S(2)}, u32[]{:S(2)}) %collective-permute-start.3) | collective-permute-done | bytes 262176 | tf_op jit(solution)/shard_map/ppermute | solution.py:53
  35.7 1.0 gather.2
  36.7 3.6 %all-to-all-done.1 = bf16[16,4,2,3,16,128]{5,4,3,2,1,0:T(8,128)(2,1)} async-done(((bf16[16,4,2,3,16,128]{5,4,3,2,1,0:T(8,128)(2,1)}), bf16[16,4,2,3,16,128]{5,4,3,2,1,0:T(8,128)(2,1)}, u32[]{:S(2)}, u32[]{:S(2)}) %all-to-all-start.1) | async-done | bytes 1572896 | tf_op jit(solution)/shard_map/all_to_all | solution.py:369
  40.3 2.4 %slice_bitcast_fusion = (bf16[16,2,3,16,128]{4,3,2,1,0:T(8,128)(2,1)S(1)}, bf16[16,2,3,16,128]{4,3,2,1,0:T(8,128)(2,1)}, bf16[16,2,3,16,128]{4,3,2,1,0:T(8,128)(2,1)S(1)}, bf16[16,2,3,16,128]{4,3,2,1,0:T(8,128)(2,1)S(1)}) fusion(bf16[16,4,2,3,16,128]{5,4,3,2,1,0:T(8,128)(2,1)} %all-to-all-done.1), kind=kLoop, calls=%fused_computation.2 | loop fusion | bytes 3145728 | tf_op jit(solution)/shard_map/squeeze | solution.py:371
  42.7 1.4 collective-permute-start.5
  44.2 0.1 collective-permute-start.4
  44.2 6.2 %all-to-all-start = ((bf16[16,4,2,2,16,128]{5,4,3,2,1,0:T(8,128)(2,1)}), bf16[16,4,2,2,16,128]{5,4,3,2,1,0:T(8,128)(2,1)S(1)}, u32[]{:S(2)}, u32[]{:S(2)}) async-start(bf16[16,4,2,2,16,128]{5,4,3,2,1,0:T(8,128)(2,1)} %gather.2), calls=%async_computation | async-start | bytes 2097152 | tf_op jit(solution)/shard_map/all_to_all | solution.py:372
  50.4 3.6 %collective-permute-start.7 = (bf16[16,2,3,16,128]{4,3,2,1,0:T(8,128)(2,1)S(1)}, bf16[16,2,3,16,128]{4,3,2,1,0:T(8,128)(2,1)}, u32[]{:S(2)}, u32[]{:S(2)}) collective-permute-start(bf16[16,2,3,16,128]{4,3,2,1,0:T(8,128)(2,1)S(1)} %get-tuple-element.39), channel_id=1, source_target_pairs={{0,130},{1,131},{2,192},{3,193},{4,134},{5,135},{6,196},{7,197},{8... | collective-permute-start | bytes 1179656 | tf_op jit(solution)/shard_map/ppermute | solution.py:53
  54.1 0.0 collective-permute-start.6
  54.1 0.0 collective-permute-done.5.refs_2_
  54.1 0.0 collective-permute-done.4.refs_1_
  54.1 11.8 %all-to-all-done.refs_0_ = bf16[16,4,2,2,16,128]{5,4,3,2,1,0:T(8,128)(2,1)S(1)} async-done(((bf16[16,4,2,2,16,128]{5,4,3,2,1,0:T(8,128)(2,1)}), bf16[16,4,2,2,16,128]{5,4,3,2,1,0:T(8,128)(2,1)S(1)}, u32[]{:S(2)}, u32[]{:S(2)}) %all-to-all-start) | async-done | bytes 1048608 | tf_op jit(solution)/shard_map/all_to_all | solution.py:372
  65.8 6.6 %correlate.2 = bf16[16,4,2,16,128]{4,3,2,1,0:T(8,128)(2,1)} custom-call(f32[3]{0:T(128)S(1)} %marker.3.rot_ref, bf16[16,4,2,2,16,128]{5,4,3,2,1,0:T(8,128)(2,1)S(1)} %all-to-all-done.refs_0_, bf16[4,512,256]{2,1,0:T(8,128)(2,1)} %constant.87.clone.refs_1_.refs_4_, bf16[4,512,256]{2,1,0:T(8,128)(2,1)} %constant.88.clone.refs_2_.refs_5_), custom_call_target="tpu_custom_call" | custom-call | bytes 3670016 | tf_op jit(solution)/shard_map/correlate/pallas_call | solution.py:139
  72.5 4.5 %all-to-all-start.3 = ((bf16[16,4,2,16,128]{4,3,2,1,0:T(8,128)(2,1)}), bf16[16,4,2,16,128]{4,3,2,1,0:T(8,128)(2,1)S(1)}, u32[]{:S(2)}, u32[]{:S(2)}) async-start(bf16[16,4,2,16,128]{4,3,2,1,0:T(8,128)(2,1)} %correlate.2), calls=%async_computation.3 | async-start | bytes 1048576 | tf_op jit(solution)/shard_map/all_to_all | solution.py:379
  77.0 6.3 %collective-permute-done.6.refs_0_ = bf16[16,2,3,16,128]{4,3,2,1,0:T(8,128)(2,1)S(1)} collective-permute-done((bf16[16,2,3,16,128]{4,3,2,1,0:T(8,128)(2,1)}, bf16[16,2,3,16,128]{4,3,2,1,0:T(8,128)(2,1)S(1)}, u32[]{:S(2)}, u32[]{:S(2)}) %collective-permute-start.6) | collective-permute-done | bytes 393248 | tf_op jit(solution)/shard_map/ppermute | solution.py:53
  83.3 0.0 collective-permute-done.7.refs_3_
  83.3 7.9 %correlate.3 = (bf16[16,3,16,128]{3,2,1,0:T(8,128)(2,1)S(1)}, bf16[16,3,16,128]{3,2,1,0:T(8,128)(2,1)S(1)}, bf16[16,3,16,128]{3,2,1,0:T(8,128)(2,1)S(1)}, bf16[16,3,16,128]{3,2,1,0:T(8,128)(2,1)S(1)}) custom-call(f32[3]{0:T(128)S(1)} %marker.3.rot_ref, bf16[16,2,3,16,128]{4,3,2,1,0:T(8,128)(2,1)S(1)} %collective-permute-done.6.refs_0_, ...), custom_call_target="tpu_custom_call" | custom-call | flops 99999997952 | bytes 4456448 | tf_op jit(solution)/shard_map/correlate/pallas_call | solution.py:139
  91.2 0.1 collective-permute-start.8
  91.3 4.5 %collective-permute-start.9 = (bf16[16,3,16,128]{3,2,1,0:T(8,128)(2,1)S(1)}, bf16[16,3,16,128]{3,2,1,0:T(8,128)(2,1)S(1)}, u32[]{:S(2)}, u32[]{:S(2)}) collective-permute-start(bf16[16,3,16,128]{3,2,1,0:T(8,128)(2,1)S(1)} %get-tuple-element.34), channel_id=1, source_target_pairs={{0,130},{1,131},{2,192},{3,193},{4,134},{5,135},{6,196},{7,197},{8... | collective-permute-start | bytes 589832 | tf_op jit(solution)/shard_map/ppermute | solution.py:53
  95.7 0.0 collective-permute-start.10
  95.7 2.7 %collective-permute-start.11 = (bf16[16,3,16,128]{3,2,1,0:T(8,128)(2,1)S(1)}, bf16[16,3,16,128]{3,2,1,0:T(8,128)(2,1)S(1)}, u32[]{:S(2)}, u32[]{:S(2)}) collective-permute-start(bf16[16,3,16,128]{3,2,1,0:T(8,128)(2,1)S(1)} %get-tuple-element.36), channel_id=1, source_target_pairs={{0,194},{1,195},{2,0},{3,1},{4,198},{5,199},{6,4},{7,5},{8,202},{9... | collective-permute-start | bytes 589832 | tf_op jit(solution)/shard_map/ppermute | solution.py:53
  98.4 0.7 slice_bitcast_fusion.4
  99.1 0.0 collective-permute-start.15
  99.1 5.5 %collective-permute-done.8.refs_0_ = bf16[16,3,16,128]{3,2,1,0:T(8,128)(2,1)S(1)} collective-permute-done((bf16[16,3,16,128]{3,2,1,0:T(8,128)(2,1)S(1)}, bf16[16,3,16,128]{3,2,1,0:T(8,128)(2,1)S(1)}, u32[]{:S(2)}, u32[]{:S(2)}) %collective-permute-start.8) | collective-permute-done | bytes 196640 | tf_op jit(solution)/shard_map/ppermute | solution.py:53
  104.6 0.5 collective-permute-start.14
  105.1 1.1 collective-permute-done.9.refs_1_
  106.2 0.0 collective-permute-start.13
  106.2 4.0 %collective-permute-done.10.refs_2_ = bf16[16,3,16,128]{3,2,1,0:T(8,128)(2,1)S(1)} collective-permute-done((bf16[16,3,16,128]{3,2,1,0:T(8,128)(2,1)S(1)}, bf16[16,3,16,128]{3,2,1,0:T(8,128)(2,1)S(1)}, u32[]{:S(2)}, u32[]{:S(2)}) %collective-permute-start.10) | collective-permute-done | bytes 196640 | tf_op jit(solution)/shard_map/ppermute | solution.py:53
  110.2 2.4 %collective-permute-done.11.refs_3_ = bf16[16,3,16,128]{3,2,1,0:T(8,128)(2,1)S(1)} collective-permute-done((bf16[16,3,16,128]{3,2,1,0:T(8,128)(2,1)S(1)}, bf16[16,3,16,128]{3,2,1,0:T(8,128)(2,1)S(1)}, u32[]{:S(2)}, u32[]{:S(2)}) %collective-permute-start.11) | collective-permute-done | bytes 196640 | tf_op jit(solution)/shard_map/ppermute | solution.py:53
  112.6 0.9 gather.3
  113.5 4.9 %all-to-all-start.2 = ((bf16[16,4,3,16,128]{4,3,2,1,0:T(8,128)(2,1)}), bf16[16,4,3,16,128]{4,3,2,1,0:T(8,128)(2,1)S(1)}, u32[]{:S(2)}, u32[]{:S(2)}) async-start(bf16[16,4,3,16,128]{4,3,2,1,0:T(8,128)(2,1)} %gather.3), calls=%async_computation.2 | async-start | bytes 1572864 | tf_op jit(solution)/shard_map/all_to_all | solution.py:382
  118.4 0.0 collective-permute-done.15.refs_3_
  118.4 0.0 collective-permute-done.14.refs_2_
  118.4 2.2 %collective-permute-done.13.refs_1_ = bf16[16,2,16,128]{3,2,1,0:T(8,128)(2,1)S(1)} collective-permute-done((bf16[16,2,16,128]{3,2,1,0:T(8,128)(2,1)S(1)}, bf16[16,2,16,128]{3,2,1,0:T(8,128)(2,1)S(1)}, u32[]{:S(2)}, u32[]{:S(2)}) %collective-permute-start.13) | collective-permute-done | bytes 131104 | tf_op jit(solution)/shard_map/ppermute | solution.py:53
  120.6 2.1 %collective-permute-done.12.refs_0_ = bf16[16,2,16,128]{3,2,1,0:T(8,128)(2,1)S(1)} collective-permute-done((bf16[16,2,16,128]{3,2,1,0:T(8,128)(2,1)S(1)}, bf16[16,2,16,128]{3,2,1,0:T(8,128)(2,1)S(1)}, u32[]{:S(2)}, u32[]{:S(2)}) %collective-permute-start.12) | collective-permute-done | bytes 131104 | tf_op jit(solution)/shard_map/ppermute | solution.py:53
  122.8 0.3 settle.2.refs_3_
  123.1 0.0 copy-start.3
  123.1 0.0 copy-start.2
  123.1 4.5 %collective-permute-start.17 = (bf16[16,2,64,128]{3,2,1,0:T(8,128)(2,1)S(1)}, bf16[16,2,64,128]{3,2,1,0:T(8,128)(2,1)S(1)}, u32[]{:S(2)}, u32[]{:S(2)}) collective-permute-start(bf16[16,2,64,128]{3,2,1,0:T(8,128)(2,1)S(1)} %settle.2.refs_3_), channel_id=1, source_target_pairs={{1,0},{2,1},{3,2},{5,4},{6,5},{7,6},{9,8},{10,9},{11,10},{13,12},{... | collective-permute-start | bytes 1572872 | tf_op jit(solution)/shard_map/ppermute | solution.py:387
  127.6 1.9 %collective-permute-start.16 = (bf16[16,2,64,128]{3,2,1,0:T(8,128)(2,1)S(1)}, bf16[16,2,64,128]{3,2,1,0:T(8,128)(2,1)S(1)}, u32[]{:S(2)}, u32[]{:S(2)}) collective-permute-start(bf16[16,2,64,128]{3,2,1,0:T(8,128)(2,1)S(1)} %settle.2.refs_3_), channel_id=1, source_target_pairs={{0,1},{1,2},{2,3},{4,5},{5,6},{6,7},{8,9},{9,10},{10,11},{12,13},{... | collective-permute-start | bytes 1572872 | tf_op jit(solution)/shard_map/ppermute | solution.py:386
  129.5 0.4 settle.3.refs_2_
  130.0 3.9 %collective-permute-done.17.refs_5_ = bf16[16,2,64,128]{3,2,1,0:T(8,128)(2,1)S(1)} collective-permute-done((bf16[16,2,64,128]{3,2,1,0:T(8,128)(2,1)S(1)}, bf16[16,2,64,128]{3,2,1,0:T(8,128)(2,1)S(1)}, u32[]{:S(2)}, u32[]{:S(2)}) %collective-permute-start.17) | collective-permute-done | bytes 524320 | tf_op jit(solution)/shard_map/ppermute | solution.py:387
  133.9 1.7 %collective-permute-done.16.refs_1_ = bf16[16,2,64,128]{3,2,1,0:T(8,128)(2,1)S(1)} collective-permute-done((bf16[16,2,64,128]{3,2,1,0:T(8,128)(2,1)S(1)}, bf16[16,2,64,128]{3,2,1,0:T(8,128)(2,1)S(1)}, u32[]{:S(2)}, u32[]{:S(2)}) %collective-permute-start.16) | collective-permute-done | bytes 524320 | tf_op jit(solution)/shard_map/ppermute | solution.py:386
  135.6 0.8 copy-done
  136.4 3.6 %collective-permute-start.19 = (bf16[16,3,64,128]{3,2,1,0:T(8,128)(2,1)S(1)}, bf16[16,3,64,128]{3,2,1,0:T(8,128)(2,1)S(1)}, u32[]{:S(2)}, u32[]{:S(2)}) collective-permute-start(bf16[16,3,64,128]{3,2,1,0:T(8,128)(2,1)S(1)} %settle.3.refs_2_), channel_id=1, source_target_pairs={{1,0},{2,1},{3,2},{5,4},{6,5},{7,6},{9,8},{10,9},{11,10},{13,12},{... | collective-permute-start | bytes 2359304 | tf_op jit(solution)/shard_map/ppermute | solution.py:387
  140.0 2.7 %collective-permute-start.18 = (bf16[16,3,64,128]{3,2,1,0:T(8,128)(2,1)S(1)}, bf16[16,3,64,128]{3,2,1,0:T(8,128)(2,1)S(1)}, u32[]{:S(2)}, u32[]{:S(2)}) collective-permute-start(bf16[16,3,64,128]{3,2,1,0:T(8,128)(2,1)S(1)} %settle.3.refs_2_), channel_id=1, source_target_pairs={{0,1},{1,2},{2,3},{4,5},{5,6},{6,7},{8,9},{9,10},{10,11},{12,13},{... | collective-permute-start | bytes 2359304 | tf_op jit(solution)/shard_map/ppermute | solution.py:386
  142.8 0.1 copy.19
  142.9 0.1 add_select_fusion
  143.0 0.2 fusion
  143.2 0.1 copy.30.w_ref
  143.3 7.2 %collective-permute-done.19.refs_4_ = bf16[16,3,64,128]{3,2,1,0:T(8,128)(2,1)S(1)} collective-permute-done((bf16[16,3,64,128]{3,2,1,0:T(8,128)(2,1)S(1)}, bf16[16,3,64,128]{3,2,1,0:T(8,128)(2,1)S(1)}, u32[]{:S(2)}, u32[]{:S(2)}) %collective-permute-start.19) | collective-permute-done | bytes 786464 | tf_op jit(solution)/shard_map/ppermute | solution.py:387
  150.5 1.2 collective-permute-done.18.refs_0_
  151.7 1.0 copy-done.1
  152.7 3.4 %screen.1 = bf16[16,5,64,128]{3,2,1,0:T(8,128)(2,1)} custom-call(s32[1]{0:T(128)} %bitcast.row_ref, s32[4,5]{1,0:T(4,128)S(1)} %copy-done.2, bf16[64,192]{1,0:T(8,128)(2,1)S(1)} %copy.30.w_ref, bf16[16,3,64,128]{3,2,1,0:T(8,128)(2,1)S(1)} %collective-permute-done.18.refs_0_, bf16[16,2,64,128]{3,2,1,0:T(8,128)(2,1)S(1)} %copy-done.1, ...), custom_call_target="tpu_custom_call" | custom-call | flops 251658240 | bytes 5242880 | tf_op jit(solution)/shard_map/screen/pallas_call | solution.py:325
  (15 shorter events, 0.1 us)
Async XLA Ops:
  4.0 21.5 %collective-permute-start = (bf16[16,2,2,16,128]{4,3,2,1,0:T(8,128)(2,1)}, bf16[16,2,2,16,128]{4,3,2,1,0:T(8,128)(2,1)S(1)}, u32[]{:S(2)}, u32[]{:S(2)}) collective-permute-start(bf16[16,2,2,16,128]{4,3,2,1,0:T(8,128)(2,1)} %get-tuple-element.22), channel_id=1, source_target_pairs={{0,66},{1,67},{2,128},{3,129},{4,70},{5,71},{6,132},{7,133},{8,74}... | collective-permute-start | bytes 786440 | tf_op jit(solution)/shard_map/ppermute | solution.py:53
  9.2 16.3 %collective-permute-start.1 = (bf16[16,2,2,16,128]{4,3,2,1,0:T(8,128)(2,1)}, bf16[16,2,2,16,128]{4,3,2,1,0:T(8,128)(2,1)S(1)}, u32[]{:S(2)}, u32[]{:S(2)}) collective-permute-start(bf16[16,2,2,16,128]{4,3,2,1,0:T(8,128)(2,1)} %get-tuple-element.23), channel_id=1, source_target_pairs={{0,130},{1,131},{2,192},{3,193},{4,134},{5,135},{6,196},{7,197},{8... | collective-permute-start | bytes 786440 | tf_op jit(solution)/shard_map/ppermute | solution.py:53
  11.4 7.0 %copy-start.5 = (bf16[16,2,2,16,128]{4,3,2,1,0:T(8,128)(2,1)S(1)}, bf16[16,2,2,16,128]{4,3,2,1,0:T(8,128)(2,1)}, u32[]{:S(2)}) copy-start(bf16[16,2,2,16,128]{4,3,2,1,0:T(8,128)(2,1)} %get-tuple-element.24) | copy-start | bytes 786436
  11.4 7.8 %copy-start.4 = (bf16[16,2,2,16,128]{4,3,2,1,0:T(8,128)(2,1)S(1)}, bf16[16,2,2,16,128]{4,3,2,1,0:T(8,128)(2,1)}, u32[]{:S(2)}) copy-start(bf16[16,2,2,16,128]{4,3,2,1,0:T(8,128)(2,1)} %get-tuple-element.26) | copy-start | bytes 786436
  11.4 28.9 %all-to-all-start.1 = ((bf16[16,4,2,3,16,128]{5,4,3,2,1,0:T(8,128)(2,1)}), bf16[16,4,2,3,16,128]{5,4,3,2,1,0:T(8,128)(2,1)}, u32[]{:S(2)}, u32[]{:S(2)}) async-start(bf16[16,4,2,3,16,128]{5,4,3,2,1,0:T(8,128)(2,1)} %get-tuple-element.28), calls=%async_computation.1 | async-start | bytes 3145728 | tf_op jit(solution)/shard_map/all_to_all | solution.py:369
  18.4 15.7 %collective-permute-start.2 = (bf16[16,2,2,16,128]{4,3,2,1,0:T(8,128)(2,1)S(1)}, bf16[16,2,2,16,128]{4,3,2,1,0:T(8,128)(2,1)S(1)}, u32[]{:S(2)}, u32[]{:S(2)}) collective-permute-start(bf16[16,2,2,16,128]{4,3,2,1,0:T(8,128)(2,1)S(1)} %copy-done.5), channel_id=1, source_target_pairs={{0,2},{1,3},{2,64},{3,65},{4,6},{5,7},{6,68},{7,69},{8,10},{9,11},... | collective-permute-start | bytes 786440 | tf_op jit(solution)/shard_map/ppermute | solution.py:53
  19.2 16.5 %collective-permute-start.3 = (bf16[16,2,2,16,128]{4,3,2,1,0:T(8,128)(2,1)S(1)}, bf16[16,2,2,16,128]{4,3,2,1,0:T(8,128)(2,1)S(1)}, u32[]{:S(2)}, u32[]{:S(2)}) collective-permute-start(bf16[16,2,2,16,128]{4,3,2,1,0:T(8,128)(2,1)S(1)} %copy-done.4), channel_id=1, source_target_pairs={{0,194},{1,195},{2,0},{3,1},{4,198},{5,199},{6,4},{7,5},{8,202},{9... | collective-permute-start | bytes 786440 | tf_op jit(solution)/shard_map/ppermute | solution.py:53
  42.7 11.3 %collective-permute-start.5 = (bf16[16,2,3,16,128]{4,3,2,1,0:T(8,128)(2,1)S(1)}, bf16[16,2,3,16,128]{4,3,2,1,0:T(8,128)(2,1)S(1)}, u32[]{:S(2)}, u32[]{:S(2)}) collective-permute-start(bf16[16,2,3,16,128]{4,3,2,1,0:T(8,128)(2,1)S(1)} %get-tuple-element.41), channel_id=1, source_target_pairs={{0,194},{1,195},{2,0},{3,1},{4,198},{5,199},{6,4},{7,5},{8,202},{9... | collective-permute-start | bytes 1179656 | tf_op jit(solution)/shard_map/ppermute | solution.py:53
  44.2 9.9 %collective-permute-start.4 = (bf16[16,2,3,16,128]{4,3,2,1,0:T(8,128)(2,1)S(1)}, bf16[16,2,3,16,128]{4,3,2,1,0:T(8,128)(2,1)S(1)}, u32[]{:S(2)}, u32[]{:S(2)}) collective-permute-start(bf16[16,2,3,16,128]{4,3,2,1,0:T(8,128)(2,1)S(1)} %get-tuple-element.42), channel_id=1, source_target_pairs={{0,2},{1,3},{2,64},{3,65},{4,6},{5,7},{6,68},{7,69},{8,10},{9,11},... | collective-permute-start | bytes 1179656 | tf_op jit(solution)/shard_map/ppermute | solution.py:53
  44.2 21.6 %all-to-all-start = ((bf16[16,4,2,2,16,128]{5,4,3,2,1,0:T(8,128)(2,1)}), bf16[16,4,2,2,16,128]{5,4,3,2,1,0:T(8,128)(2,1)S(1)}, u32[]{:S(2)}, u32[]{:S(2)}) async-start(bf16[16,4,2,2,16,128]{5,4,3,2,1,0:T(8,128)(2,1)} %gather.2), calls=%async_computation | async-start | bytes 2097152 | tf_op jit(solution)/shard_map/all_to_all | solution.py:372
  50.4 32.9 %collective-permute-start.7 = (bf16[16,2,3,16,128]{4,3,2,1,0:T(8,128)(2,1)S(1)}, bf16[16,2,3,16,128]{4,3,2,1,0:T(8,128)(2,1)}, u32[]{:S(2)}, u32[]{:S(2)}) collective-permute-start(bf16[16,2,3,16,128]{4,3,2,1,0:T(8,128)(2,1)S(1)} %get-tuple-element.39), channel_id=1, source_target_pairs={{0,130},{1,131},{2,192},{3,193},{4,134},{5,135},{6,196},{7,197},{8... | collective-permute-start | bytes 1179656 | tf_op jit(solution)/shard_map/ppermute | solution.py:53
  54.1 29.2 %collective-permute-start.6 = (bf16[16,2,3,16,128]{4,3,2,1,0:T(8,128)(2,1)}, bf16[16,2,3,16,128]{4,3,2,1,0:T(8,128)(2,1)S(1)}, u32[]{:S(2)}, u32[]{:S(2)}) collective-permute-start(bf16[16,2,3,16,128]{4,3,2,1,0:T(8,128)(2,1)} %get-tuple-element.40), channel_id=1, source_target_pairs={{0,66},{1,67},{2,128},{3,129},{4,70},{5,71},{6,132},{7,133},{8,74}... | collective-permute-start | bytes 1179656 | tf_op jit(solution)/shard_map/ppermute | solution.py:53
  72.5 26.0 %all-to-all-start.3 = ((bf16[16,4,2,16,128]{4,3,2,1,0:T(8,128)(2,1)}), bf16[16,4,2,16,128]{4,3,2,1,0:T(8,128)(2,1)S(1)}, u32[]{:S(2)}, u32[]{:S(2)}) async-start(bf16[16,4,2,16,128]{4,3,2,1,0:T(8,128)(2,1)} %correlate.2), calls=%async_computation.3 | async-start | bytes 1048576 | tf_op jit(solution)/shard_map/all_to_all | solution.py:379
  91.2 13.5 %collective-permute-start.8 = (bf16[16,3,16,128]{3,2,1,0:T(8,128)(2,1)S(1)}, bf16[16,3,16,128]{3,2,1,0:T(8,128)(2,1)S(1)}, u32[]{:S(2)}, u32[]{:S(2)}) collective-permute-start(bf16[16,3,16,128]{3,2,1,0:T(8,128)(2,1)S(1)} %get-tuple-element.33), channel_id=1, source_target_pairs={{0,66},{1,67},{2,128},{3,129},{4,70},{5,71},{6,132},{7,133},{8,74}... | collective-permute-start | bytes 589832 | tf_op jit(solution)/shard_map/ppermute | solution.py:53
  91.3 14.9 %collective-permute-start.9 = (bf16[16,3,16,128]{3,2,1,0:T(8,128)(2,1)S(1)}, bf16[16,3,16,128]{3,2,1,0:T(8,128)(2,1)S(1)}, u32[]{:S(2)}, u32[]{:S(2)}) collective-permute-start(bf16[16,3,16,128]{3,2,1,0:T(8,128)(2,1)S(1)} %get-tuple-element.34), channel_id=1, source_target_pairs={{0,130},{1,131},{2,192},{3,193},{4,134},{5,135},{6,196},{7,197},{8... | collective-permute-start | bytes 589832 | tf_op jit(solution)/shard_map/ppermute | solution.py:53
  95.7 14.5 %collective-permute-start.10 = (bf16[16,3,16,128]{3,2,1,0:T(8,128)(2,1)S(1)}, bf16[16,3,16,128]{3,2,1,0:T(8,128)(2,1)S(1)}, u32[]{:S(2)}, u32[]{:S(2)}) collective-permute-start(bf16[16,3,16,128]{3,2,1,0:T(8,128)(2,1)S(1)} %get-tuple-element.35), channel_id=1, source_target_pairs={{0,2},{1,3},{2,64},{3,65},{4,6},{5,7},{6,68},{7,69},{8,10},{9,11},... | collective-permute-start | bytes 589832 | tf_op jit(solution)/shard_map/ppermute | solution.py:53
  95.7 16.8 %collective-permute-start.11 = (bf16[16,3,16,128]{3,2,1,0:T(8,128)(2,1)S(1)}, bf16[16,3,16,128]{3,2,1,0:T(8,128)(2,1)S(1)}, u32[]{:S(2)}, u32[]{:S(2)}) collective-permute-start(bf16[16,3,16,128]{3,2,1,0:T(8,128)(2,1)S(1)} %get-tuple-element.36), channel_id=1, source_target_pairs={{0,194},{1,195},{2,0},{3,1},{4,198},{5,199},{6,4},{7,5},{8,202},{9... | collective-permute-start | bytes 589832 | tf_op jit(solution)/shard_map/ppermute | solution.py:53
  99.1 19.3 %collective-permute-start.15 = (bf16[16,2,16,128]{3,2,1,0:T(8,128)(2,1)}, bf16[16,2,16,128]{3,2,1,0:T(8,128)(2,1)S(1)}, u32[]{:S(2)}, u32[]{:S(2)}) collective-permute-start(bf16[16,2,16,128]{3,2,1,0:T(8,128)(2,1)} %get-tuple-element.43), channel_id=1, source_target_pairs={{0,66},{1,67},{2,128},{3,129},{4,70},{5,71},{6,132},{7,133},{8,74}... | collective-permute-start | bytes 393224 | tf_op jit(solution)/shard_map/ppermute | solution.py:53
  104.6 13.8 %collective-permute-start.14 = (bf16[16,2,16,128]{3,2,1,0:T(8,128)(2,1)}, bf16[16,2,16,128]{3,2,1,0:T(8,128)(2,1)S(1)}, u32[]{:S(2)}, u32[]{:S(2)}) collective-permute-start(bf16[16,2,16,128]{3,2,1,0:T(8,128)(2,1)} %get-tuple-element.44), channel_id=1, source_target_pairs={{0,130},{1,131},{2,192},{3,193},{4,134},{5,135},{6,196},{7,197},{8... | collective-permute-start | bytes 393224 | tf_op jit(solution)/shard_map/ppermute | solution.py:53
  106.2 14.4 %collective-permute-start.13 = (bf16[16,2,16,128]{3,2,1,0:T(8,128)(2,1)S(1)}, bf16[16,2,16,128]{3,2,1,0:T(8,128)(2,1)S(1)}, u32[]{:S(2)}, u32[]{:S(2)}) collective-permute-start(bf16[16,2,16,128]{3,2,1,0:T(8,128)(2,1)S(1)} %get-tuple-element.45), channel_id=1, source_target_pairs={{0,2},{1,3},{2,64},{3,65},{4,6},{5,7},{6,68},{7,69},{8,10},{9,11},... | collective-permute-start | bytes 393224 | tf_op jit(solution)/shard_map/ppermute | solution.py:53
  110.2 12.5 %collective-permute-start.12 = (bf16[16,2,16,128]{3,2,1,0:T(8,128)(2,1)S(1)}, bf16[16,2,16,128]{3,2,1,0:T(8,128)(2,1)S(1)}, u32[]{:S(2)}, u32[]{:S(2)}) collective-permute-start(bf16[16,2,16,128]{3,2,1,0:T(8,128)(2,1)S(1)} %get-tuple-element.46), channel_id=1, source_target_pairs={{0,194},{1,195},{2,0},{3,1},{4,198},{5,199},{6,4},{7,5},{8,202},{9... | collective-permute-start | bytes 393224 | tf_op jit(solution)/shard_map/ppermute | solution.py:53
  113.5 16.0 %all-to-all-start.2 = ((bf16[16,4,3,16,128]{4,3,2,1,0:T(8,128)(2,1)}), bf16[16,4,3,16,128]{4,3,2,1,0:T(8,128)(2,1)S(1)}, u32[]{:S(2)}, u32[]{:S(2)}) async-start(bf16[16,4,3,16,128]{4,3,2,1,0:T(8,128)(2,1)} %gather.3), calls=%async_computation.2 | async-start | bytes 1572864 | tf_op jit(solution)/shard_map/all_to_all | solution.py:382
  123.1 19.7 %copy-start.3 = (bf16[1,64,192]{2,1,0:T(8,128)(2,1)S(1)}, bf16[1,64,192]{2,1,0:T(8,128)(2,1)}, u32[]{:S(2)}) copy-start(bf16[1,64,192]{2,1,0:T(8,128)(2,1)} %param.8) | copy-start | bytes 73732
  123.1 28.6 %copy-start.2 = (s32[4,5]{1,0:T(4,128)S(1)}, s32[4,5]{1,0:T(4,128)}, u32[]{:S(2)}) copy-start(s32[4,5]{1,0:T(4,128)} %pattern_ref.1) | copy-start | bytes 244
  123.1 10.8 %collective-permute-start.17 = (bf16[16,2,64,128]{3,2,1,0:T(8,128)(2,1)S(1)}, bf16[16,2,64,128]{3,2,1,0:T(8,128)(2,1)S(1)}, u32[]{:S(2)}, u32[]{:S(2)}) collective-permute-start(bf16[16,2,64,128]{3,2,1,0:T(8,128)(2,1)S(1)} %settle.2.refs_3_), channel_id=1, source_target_pairs={{1,0},{2,1},{3,2},{5,4},{6,5},{7,6},{9,8},{10,9},{11,10},{13,12},{... | collective-permute-start | bytes 1572872 | tf_op jit(solution)/shard_map/ppermute | solution.py:387
  127.6 8.0 %collective-permute-start.16 = (bf16[16,2,64,128]{3,2,1,0:T(8,128)(2,1)S(1)}, bf16[16,2,64,128]{3,2,1,0:T(8,128)(2,1)S(1)}, u32[]{:S(2)}, u32[]{:S(2)}) collective-permute-start(bf16[16,2,64,128]{3,2,1,0:T(8,128)(2,1)S(1)} %settle.2.refs_3_), channel_id=1, source_target_pairs={{0,1},{1,2},{2,3},{4,5},{5,6},{6,7},{8,9},{9,10},{10,11},{12,13},{... | collective-permute-start | bytes 1572872 | tf_op jit(solution)/shard_map/ppermute | solution.py:386
  135.6 0.8 copy-start
  136.4 14.0 %collective-permute-start.19 = (bf16[16,3,64,128]{3,2,1,0:T(8,128)(2,1)S(1)}, bf16[16,3,64,128]{3,2,1,0:T(8,128)(2,1)S(1)}, u32[]{:S(2)}, u32[]{:S(2)}) collective-permute-start(bf16[16,3,64,128]{3,2,1,0:T(8,128)(2,1)S(1)} %settle.3.refs_2_), channel_id=1, source_target_pairs={{1,0},{2,1},{3,2},{5,4},{6,5},{7,6},{9,8},{10,9},{11,10},{13,12},{... | collective-permute-start | bytes 2359304 | tf_op jit(solution)/shard_map/ppermute | solution.py:387
  140.0 11.6 %collective-permute-start.18 = (bf16[16,3,64,128]{3,2,1,0:T(8,128)(2,1)S(1)}, bf16[16,3,64,128]{3,2,1,0:T(8,128)(2,1)S(1)}, u32[]{:S(2)}, u32[]{:S(2)}) collective-permute-start(bf16[16,3,64,128]{3,2,1,0:T(8,128)(2,1)S(1)} %settle.3.refs_2_), channel_id=1, source_target_pairs={{0,1},{1,2},{2,3},{4,5},{5,6},{6,7},{8,9},{9,10},{10,11},{12,13},{... | collective-permute-start | bytes 2359304 | tf_op jit(solution)/shard_map/ppermute | solution.py:386
  151.7 1.0 copy-start.1

commit v8 on v7

--- a/solution.py
+++ b/solution.py
@@ -20,6 +20,7 @@
 CUT = 3
 ORDER = (0, 3, 1, 2)
 BUF = 2
+ROOM_HI, ROOM_LO = 52, 52
 HEAVY = 100 * 10**9
 STEPS = (3, 1, -1, -3)
 
@@ -129,7 +130,7 @@
                     outs[0][p : p + 2, j, s] = v
 
 
-def correlate(rot, inputs, fwd, inv, split, flops):
+def correlate(rot, inputs, fwd, inv, split, flops, room):
     slots = inputs[0].shape[-3]
     n = slots * 128
     vmem = pl.BlockSpec(memory_space=pltpu.VMEM)
@@ -150,7 +151,7 @@
             pltpu.VMEM((4, 2 * QUART, QUART), jnp.bfloat16),
             pltpu.SemaphoreType.DMA((2, 4)),
         ],
-        compiler_params=pltpu.CompilerParams(vmem_limit_bytes=52 << 20),
+        compiler_params=pltpu.CompilerParams(vmem_limit_bytes=room << 20),
         cost_estimate=pl.CostEstimate(
             flops=flops, bytes_accessed=3 * NE * n * 2 + (2 << 20), transcendentals=0
         ),
@@ -165,11 +166,30 @@
     return jnp.where((row % 16) * 16 + row // 16 == col, 1.0, 0.0).astype(jnp.bfloat16)
 
 
-def prepare_kernel(cut, turn_ref, less_ref, great_ref, *refs):
+def place_of(pattern_ref, row, slot):
+    def plain(t):
+        offset = pattern_ref[row, t] - row
+        return jnp.logical_and(offset != 0, offset != 6)
+
+    rank = jnp.int32(0)
+    for t in range(slot):
+        rank = rank + jnp.where(plain(t), 1, 0)
+    other = jnp.where(rank == 0, 1, rank + 2)
+    return jnp.where(plain(slot), other, jnp.where(pattern_ref[row, slot] == row, 0, 2))
+
+
+def prepare_kernel(cut, turn_ref, row_ref, pattern_ref, less_ref, great_ref, *refs):
     early_ref, late_refs, turn, held, sem = refs[0], refs[1:5], refs[5], refs[6], refs[7]
     slots = less_ref.shape[1]
+    places = [place_of(pattern_ref, row_ref[0], t) for t in range(slots)]
+    source = []
+    for s in range(slots):
+        at = jnp.int32(0)
+        for t in range(slots):
+            at = jnp.where(places[t] == s, t, at)
+        source.append(at)
     loads = [
-        [pltpu.make_async_copy(ref.at[:, s], held.at[s, k], sem.at[s, k]) for k, ref in enumerate((less_ref, great_ref))]
+        [pltpu.make_async_copy(ref.at[:, source[s]], held.at[s, k], sem.at[s, k]) for k, ref in enumerate((less_ref, great_ref))]
         for s in range(slots)
     ]
     order = [*range(cut, slots), *range(cut)]
@@ -193,7 +213,7 @@
                     late_refs[j][:, k, s - cut] = v
 
 
-def prepare(turn, less, great, cut):
+def prepare(turn, row, pattern, less, great, cut):
     el, slots, bi, wide = less.shape
     vmem = pl.BlockSpec(memory_space=pltpu.VMEM)
     hbm = pl.BlockSpec(memory_space=pltpu.HBM)
@@ -201,7 +221,7 @@
     early, *late = pl.pallas_call(
         functools.partial(prepare_kernel, cut),
         out_shape=[jax.ShapeDtypeStruct((NP, NZ, 2, cut, el, wide), jnp.bfloat16)] + [piece] * 4,
-        in_specs=[pl.BlockSpec(memory_space=pltpu.SMEM), hbm, hbm],
+        in_specs=[pl.BlockSpec(memory_space=pltpu.SMEM)] * 3 + [hbm, hbm],
         out_specs=[vmem] * 5,
         scratch_shapes=[
             pltpu.VMEM((256, 256), jnp.bfloat16),
@@ -211,33 +231,37 @@
         compiler_params=pltpu.CompilerParams(vmem_limit_bytes=60 << 20),
         cost_estimate=pl.CostEstimate(flops=0, bytes_accessed=4 * el * slots * bi * wide * 2, transcendentals=0),
         name="prepare",
-    )(turn, less, great)
+    )(turn, row, pattern, less, great)
     return early, late
 
 
 def settle_kernel(slots, pieces, *refs):
-    in_refs, out_ref, turn = refs[:pieces], refs[-2], refs[-1]
+    in_refs, out_refs, turn = refs[:pieces], refs[pieces:-1], refs[-1]
     turn[...] = turning()
     for k, j in enumerate(ORDER[::-1]):
         x = [(in_refs[k][:, s] if pieces == 4 else in_refs[0][:, j, s]).reshape(256, 128) for s in range(slots)]
         x = jnp.dot(turn[...], jnp.concatenate(x, 1), preferred_element_type=jnp.float32).astype(jnp.bfloat16)
         for s in range(slots):
-            out_ref[:, s, j * NP : (j + 1) * NP] = x[:, s * 128 : (s + 1) * 128].reshape(NL, NP, 128)
-
-
-def settle(inputs, flops):
+            v = x[:, s * 128 : (s + 1) * 128].reshape(NL, NP, 128)
+            for out_ref, first in zip(out_refs, (0, 1, 0)):
+                if 0 <= s - first < out_ref.shape[1]:
+                    out_ref[:, s - first, j * NP : (j + 1) * NP] = v
+
+
+def settle(inputs, parts, flops):
     slots = inputs[0].shape[-3]
     vmem = pl.BlockSpec(memory_space=pltpu.VMEM)
+    counts = [slots, slots - 1, slots - 1] if parts else [slots]
     return pl.pallas_call(
         functools.partial(settle_kernel, slots, len(inputs)),
-        out_shape=jax.ShapeDtypeStruct((NL, slots, 64, 128), jnp.bfloat16),
+        out_shape=[jax.ShapeDtypeStruct((NL, n, 64, 128), jnp.bfloat16) for n in counts],
         in_specs=[vmem] * len(inputs),
-        out_specs=vmem,
+        out_specs=[vmem] * len(counts),
         scratch_shapes=[pltpu.VMEM((256, 256), jnp.bfloat16)],
         cost_estimate=pl.CostEstimate(flops=flops, bytes_accessed=NL * slots * 64 * 128 * 4, transcendentals=0),
         compiler_params=pltpu.CompilerParams(vmem_limit_bytes=12 << 20),
         name="settle",
-    )(*(inputs[j] for j in ORDER[::-1]) if len(inputs) == 4 else inputs)
+    )(*((inputs[j] for j in ORDER[::-1]) if len(inputs) == 4 else inputs))
 
 
 def gather_kernel(*refs):
@@ -277,38 +301,36 @@
 
 
 def screen_kernel(row_ref, pattern_ref, w_ref, *refs):
-    pairs, out_ref = (refs[0:2], refs[2:4], refs[4:6]), refs[6]
+    pairs, out_ref, at_ref = (refs[0:2], refs[2:4], refs[4:6]), refs[6], refs[7]
     slots = out_ref.shape[1]
     rows = pattern_ref.shape[0]
-    row = row_ref[0]
-    found = {}
-    for d, step in ((0, -1), (2, 1)):
-        k = row + step
-        inside = jnp.logical_and(k >= 0, k < rows)
-        k = jnp.clip(k, 0, rows - 1)
-        for s in range(slots):
-            want = pattern_ref[row, s]
-            at, hit = jnp.int32(0), jnp.int32(0)
-            for t in range(slots):
-                same = jnp.logical_and(inside, pattern_ref[k, t] == want)
-                at = jnp.where(same, t, at)
-                hit = jnp.where(same, 1, hit)
-            found[d, s] = at, hit
+
+    @pl.when(pl.program_id(0) == 0)
+    def _():
+        row = row_ref[0]
+        for d in range(3):
+            k = row + d - 1
+            inside = jnp.logical_and(k >= 0, k < rows)
+            k = jnp.clip(k, 0, rows - 1)
+            places = [place_of(pattern_ref, k, t) for t in range(slots)]
+            for s in range(slots):
+                want = pattern_ref[row, s]
+                at = jnp.int32(-1)
+                for t in range(slots):
+                    at = jnp.where(jnp.logical_and(inside, pattern_ref[k, t] == want), places[t], at)
+                at_ref[d, s] = at
+
     w = w_ref[...]
     for l in range(out_ref.shape[0]):
         cols = []
         for s in range(slots):
             blocks = []
             for d, (low, high) in enumerate(pairs):
-                cut = low.shape[1]
-                if d == 1:
-                    blocks.append(low[l, s] if s < cut else high[l, s - cut])
-                else:
-                    at, hit = found[d, s]
-                    one = low[l, jnp.minimum(at, cut - 1)]
-                    two = high[l, jnp.maximum(at - cut, 0)]
-                    got = jnp.where(at < cut, one, two)
-                    blocks.append(jnp.where(hit > 0, got, jnp.zeros_like(got)))
+                at = at_ref[d, s]
+                one = low[l, jnp.clip(at - 1 if d == 0 else at, 0, low.shape[1] - 1)]
+                two = high[l, jnp.clip(at - CUT, 0, high.shape[1] - 1)]
+                got = jnp.where(at < CUT, one, two)
+                blocks.append(got if d == 1 else jnp.where(at >= 0, got, jnp.zeros_like(got)))
             cols.append(jnp.concatenate(blocks, 0))
         res = jnp.dot(w, jnp.concatenate(cols, 1), preferred_element_type=jnp.float32)
         for s in range(slots):
@@ -328,6 +350,7 @@
         out_shape=jax.ShapeDtypeStruct((el, slots, bi, wide), jnp.bfloat16),
         in_specs=[smem, smem, pl.BlockSpec(weights.shape, lambda i: (0, 0)), *blocks],
         out_specs=pl.BlockSpec((step, slots, bi, wide), lambda i: (i, 0, 0, 0)),
+        scratch_shapes=[pltpu.SMEM((3, 5), jnp.int32)],
         cost_estimate=pl.CostEstimate(
             flops=2 * el * slots * bi * 3 * bi * wide, bytes_accessed=8 * el * slots * bi * wide, transcendentals=0
         ),
@@ -362,7 +385,7 @@
 
     cut = CUT
     both = (g_less.reshape(el, slots, bi, wide), g_greater.reshape(el, slots, bi, wide))
-    early, late = prepare((turn % 4).reshape(1), *both, cut)
+    early, late = prepare((turn % 4).reshape(1), s_row.reshape(1), pattern, *both, cut)
     late = [hop(late[j], STEPS[j]) for j in range(4)]
     late[1], rot = lax.optimization_barrier([late[1], marker(rot, [late[0], late[3]], HEAVY)])
     late = gather(late, 0)
@@ -372,24 +395,19 @@
     late = lax.all_to_all(late, PLANE, split_axis=0, concat_axis=0, tiled=True)
 
     late, rot = lax.optimization_barrier([late, marker(rot, early[1:3], HEAVY)])
-    hi = correlate(rot, [late], fwd, inv, False, 0)
+    hi = correlate(rot, [late], fwd, inv, False, 0, ROOM_HI)
     early[0] = after(early[0], hi)
-    lo = correlate(rot, early, fwd, inv, True, HEAVY)
+    lo = correlate(rot, early, fwd, inv, True, HEAVY, ROOM_LO)
 
     hi = lax.all_to_all(hi, PLANE, split_axis=0, concat_axis=0, tiled=True)
     lo = gather([hop(p, STEPS[j]) for j, p in enumerate(lo)], 0)
-    hi = settle([hop(hi[:, j], STEPS[j]) for j in range(4)], HEAVY)
+    (hi,) = settle([hop(hi[:, j], STEPS[j]) for j in range(4)], False, HEAVY)
     lo = lax.all_to_all(lo, PLANE, split_axis=0, concat_axis=0, tiled=True)
-    lo = settle([after(lo, hi)], 0)
-
-    def halo(cells):
-        up = lax.ppermute(cells, "s", [(0, 1), (1, 2), (2, 3)])
-        down = lax.ppermute(cells, "s", [(1, 0), (2, 1), (3, 2)])
-        return up, down
-
-    up_hi, down_hi = halo(hi)
-    lo = lax.optimization_barrier([lo, up_hi, down_hi])[0]
-    up_lo, down_lo = halo(lo)
+    lo, lo_up, lo_down = settle([after(lo, hi)], True, 0)
+    upward, downward = [(0, 1), (1, 2), (2, 3)], [(1, 0), (2, 1), (3, 2)]
+    up_hi, down_hi = lax.ppermute(hi, "s", upward), lax.ppermute(hi, "s", downward)
+    lo_up, lo_down = lax.optimization_barrier([lo_up, lo_down, up_hi, down_hi])[:2]
+    up_lo, down_lo = lax.ppermute(lo_up, "s", upward), lax.ppermute(lo_down, "s", downward)
     return screen(s_row.reshape(1), pattern, weights, (up_lo, up_hi), (lo, hi), (down_lo, down_hi))[:, None]
 
 

time: 157 us -> 156 us (level)
  Pallas kernels: 24.5 us -> 27.4 us
  local copies, waits for them, and re-layouts: 5.19 us -> 2.67 us
    unnamed x13 -> x9, local copies, waits for them, and re-layouts: 1.96 us -> 0.13 us
  transfers between devices with their start and end apart: 24 -> 24, of which waited for: 16 -> 17; matrix products, arithmetic and copies ran while one was open for 1% -> 0% of each run, Pallas kernels for 11% -> 12%
where the time goes in v8:
time: 156 us; the launch traced here: 155 us
  waiting for transfers between devices  66.5 us (43%)
  starting transfers between devices  57.9 us (37%)
  Pallas kernels  27.4 us (18%)
  local copies, waits for them, and re-layouts  2.67 us (2%)
    ppermute x16, waiting for transfers between devices, hop(): return lax.ppermute(piece, ALL, perm)  38.2 us
    ppermute x16, starting transfers between devices, hop(): return lax.ppermute(piece, ALL, perm)  23.1 us
    pallas_call x2, Pallas kernels, correlate(): pl.pallas_call(functools.partial(correlate_kernel, slots, len(inputs), sp...  14.5 us
    all_to_all x1, waiting for transfers between devices, shards(): late = lax.all_to_all(late, PLANE, split_axis=0, concat_axis=0, tiled=True)  11.8 us
    all_to_all x1, starting transfers between devices, shards(): lax.all_to_all(early, PLANE, split_axis=0, concat_axis=0, tiled=True)  6.93 us
    all_to_all x1, starting transfers between devices, shards(): late = lax.all_to_all(late, PLANE, split_axis=0, concat_axis=0, tiled=True)  6.23 us
    all_to_all x1, starting transfers between devices, shards(): lo = lax.all_to_all(lo, PLANE, split_axis=0, concat_axis=0, tiled=True)  5.26 us
    pallas_call x1, Pallas kernels, prepare(): pl.pallas_call(functools.partial(prepare_kernel, cut), out_shape=[jax.Sha...  4.64 us
  transfers between devices with their start and end apart: 24, of which 17 were waited for; matrix products, arithmetic and copies ran while one was open for 0% of the time, Pallas kernels for 12%

profile of v8, /device:TPU:1, one launch (start us, length us, event | category | flops | bytes accessed | tf_op | source)
XLA Modules:
  0.0 155.2 jit_solution(17400582303546606982)
XLA Ops:
  0.0 4.6 %prepare.1 = (bf16[16,4,2,3,16,128]{5,4,3,2,1,0:T(8,128)(2,1)}, bf16[16,2,2,16,128]{4,3,2,1,0:T(8,128)(2,1)}, bf16[16,2,2,16,128]{4,3,2,1,0:T(8,128)(2,1)}, bf16...) custom-call(s32[1]{0:T(128)} %bitcast.6.turn_ref, s32[1]{0:T(128)} %bitcast.row_ref, s32[4,5]{1,0:T(4,128)} %pattern_ref.3, ...), custom_call_target="tpu_custom_call" | custom-call | bytes 5242880 | tf_op jit(solution)/shard_map/prepare/pallas_call | solution.py:221
  4.6 5.3 %collective-permute-start = (bf16[16,2,2,16,128]{4,3,2,1,0:T(8,128)(2,1)}, bf16[16,2,2,16,128]{4,3,2,1,0:T(8,128)(2,1)S(1)}, u32[]{:S(2)}, u32[]{:S(2)}) collective-permute-start(bf16[16,2,2,16,128]{4,3,2,1,0:T(8,128)(2,1)} %get-tuple-element.26), channel_id=1, source_target_pairs={{0,66},{1,67},{2,128},{3,129},{4,70},{5,71},{6,132},{7,133},{8,74}... | collective-permute-start | bytes 786440 | tf_op jit(solution)/shard_map/ppermute | solution.py:54
  9.9 2.2 %collective-permute-start.1 = (bf16[16,2,2,16,128]{4,3,2,1,0:T(8,128)(2,1)}, bf16[16,2,2,16,128]{4,3,2,1,0:T(8,128)(2,1)S(1)}, u32[]{:S(2)}, u32[]{:S(2)}) collective-permute-start(bf16[16,2,2,16,128]{4,3,2,1,0:T(8,128)(2,1)} %get-tuple-element.27), channel_id=1, source_target_pairs={{0,130},{1,131},{2,192},{3,193},{4,134},{5,135},{6,196},{7,197},{8... | collective-permute-start | bytes 786440 | tf_op jit(solution)/shard_map/ppermute | solution.py:54
  12.1 6.9 %all-to-all-start.1 = ((bf16[16,4,2,3,16,128]{5,4,3,2,1,0:T(8,128)(2,1)}), bf16[16,4,2,3,16,128]{5,4,3,2,1,0:T(8,128)(2,1)}, u32[]{:S(2)}, u32[]{:S(2)}) async-start(bf16[16,4,2,3,16,128]{5,4,3,2,1,0:T(8,128)(2,1)} %get-tuple-element.32), calls=%async_computation.1 | async-start | bytes 3145728 | tf_op jit(solution)/shard_map/all_to_all | solution.py:392
  19.1 0.8 collective-permute-start.2
  19.9 1.9 %collective-permute-start.3 = (bf16[16,2,2,16,128]{4,3,2,1,0:T(8,128)(2,1)S(1)}, bf16[16,2,2,16,128]{4,3,2,1,0:T(8,128)(2,1)S(1)}, u32[]{:S(2)}, u32[]{:S(2)}) collective-permute-start(bf16[16,2,2,16,128]{4,3,2,1,0:T(8,128)(2,1)S(1)} %copy-done.2), channel_id=1, source_target_pairs={{0,194},{1,195},{2,0},{3,1},{4,198},{5,199},{6,4},{7,5},{8,202},{9... | collective-permute-start | bytes 786440 | tf_op jit(solution)/shard_map/ppermute | solution.py:54
  21.8 0.1 pad_maximum_fusion.refs_0_
  21.9 4.3 %collective-permute-done.refs_1_.refs_0_ = bf16[16,2,2,16,128]{4,3,2,1,0:T(8,128)(2,1)S(1)} collective-permute-done((bf16[16,2,2,16,128]{4,3,2,1,0:T(8,128)(2,1)}, bf16[16,2,2,16,128]{4,3,2,1,0:T(8,128)(2,1)S(1)}, u32[]{:S(2)}, u32[]{:S(2)}) %collective-permute-start) | collective-permute-done | bytes 262176 | tf_op jit(solution)/shard_map/ppermute | solution.py:54
  26.2 0.0 collective-permute-done.1.refs_2_.refs_1_
  26.2 8.6 %collective-permute-done.2.refs_2_ = bf16[16,2,2,16,128]{4,3,2,1,0:T(8,128)(2,1)S(1)} collective-permute-done((bf16[16,2,2,16,128]{4,3,2,1,0:T(8,128)(2,1)S(1)}, bf16[16,2,2,16,128]{4,3,2,1,0:T(8,128)(2,1)S(1)}, u32[]{:S(2)}, u32[]{:S(2)}) %collective-permute-start.2) | collective-permute-done | bytes 262176 | tf_op jit(solution)/shard_map/ppermute | solution.py:54
  34.7 1.7 %collective-permute-done.3.refs_3_ = bf16[16,2,2,16,128]{4,3,2,1,0:T(8,128)(2,1)S(1)} collective-permute-done((bf16[16,2,2,16,128]{4,3,2,1,0:T(8,128)(2,1)S(1)}, bf16[16,2,2,16,128]{4,3,2,1,0:T(8,128)(2,1)S(1)}, u32[]{:S(2)}, u32[]{:S(2)}) %collective-permute-start.3) | collective-permute-done | bytes 262176 | tf_op jit(solution)/shard_map/ppermute | solution.py:54
  36.4 1.0 gather.2
  37.4 3.6 %all-to-all-done.1 = bf16[16,4,2,3,16,128]{5,4,3,2,1,0:T(8,128)(2,1)} async-done(((bf16[16,4,2,3,16,128]{5,4,3,2,1,0:T(8,128)(2,1)}), bf16[16,4,2,3,16,128]{5,4,3,2,1,0:T(8,128)(2,1)}, u32[]{:S(2)}, u32[]{:S(2)}) %all-to-all-start.1) | async-done | bytes 1572896 | tf_op jit(solution)/shard_map/all_to_all | solution.py:392
  41.0 2.4 %slice_bitcast_fusion = (bf16[16,2,3,16,128]{4,3,2,1,0:T(8,128)(2,1)S(1)}, bf16[16,2,3,16,128]{4,3,2,1,0:T(8,128)(2,1)}, bf16[16,2,3,16,128]{4,3,2,1,0:T(8,128)(2,1)S(1)}, bf16[16,2,3,16,128]{4,3,2,1,0:T(8,128)(2,1)S(1)}) fusion(bf16[16,4,2,3,16,128]{5,4,3,2,1,0:T(8,128)(2,1)} %all-to-all-done.1), kind=kLoop, calls=%fused_computation.2 | loop fusion | bytes 3145728 | tf_op jit(solution)/shard_map/squeeze | solution.py:394
  43.4 1.4 collective-permute-start.5
  44.8 0.0 collective-permute-start.4
  44.9 6.2 %all-to-all-start = ((bf16[16,4,2,2,16,128]{5,4,3,2,1,0:T(8,128)(2,1)}), bf16[16,4,2,2,16,128]{5,4,3,2,1,0:T(8,128)(2,1)S(1)}, u32[]{:S(2)}, u32[]{:S(2)}) async-start(bf16[16,4,2,2,16,128]{5,4,3,2,1,0:T(8,128)(2,1)} %gather.2), calls=%async_computation | async-start | bytes 2097152 | tf_op jit(solution)/shard_map/all_to_all | solution.py:395
  51.1 3.6 %collective-permute-start.7 = (bf16[16,2,3,16,128]{4,3,2,1,0:T(8,128)(2,1)S(1)}, bf16[16,2,3,16,128]{4,3,2,1,0:T(8,128)(2,1)}, u32[]{:S(2)}, u32[]{:S(2)}) collective-permute-start(bf16[16,2,3,16,128]{4,3,2,1,0:T(8,128)(2,1)S(1)} %get-tuple-element.47), channel_id=1, source_target_pairs={{0,130},{1,131},{2,192},{3,193},{4,134},{5,135},{6,196},{7,197},{8... | collective-permute-start | bytes 1179656 | tf_op jit(solution)/shard_map/ppermute | solution.py:54
  54.8 0.0 collective-permute-start.6
  54.8 0.0 collective-permute-done.5.refs_2_
  54.8 0.0 collective-permute-done.4.refs_1_
  54.8 11.8 %all-to-all-done.refs_0_ = bf16[16,4,2,2,16,128]{5,4,3,2,1,0:T(8,128)(2,1)S(1)} async-done(((bf16[16,4,2,2,16,128]{5,4,3,2,1,0:T(8,128)(2,1)}), bf16[16,4,2,2,16,128]{5,4,3,2,1,0:T(8,128)(2,1)S(1)}, u32[]{:S(2)}, u32[]{:S(2)}) %all-to-all-start) | async-done | bytes 1048608 | tf_op jit(solution)/shard_map/all_to_all | solution.py:395
  66.5 6.6 %correlate.2 = bf16[16,4,2,16,128]{4,3,2,1,0:T(8,128)(2,1)} custom-call(f32[3]{0:T(128)S(1)} %marker.3.rot_ref, bf16[16,4,2,2,16,128]{5,4,3,2,1,0:T(8,128)(2,1)S(1)} %all-to-all-done.refs_0_, bf16[4,512,256]{2,1,0:T(8,128)(2,1)} %constant.87.clone.refs_1_.refs_4_, bf16[4,512,256]{2,1,0:T(8,128)(2,1)} %constant.88.clone.refs_2_.refs_5_), custom_call_target="tpu_custom_call" | custom-call | bytes 3670016 | tf_op jit(solution)/shard_map/correlate/pallas_call | solution.py:140
  73.1 4.5 %all-to-all-start.3 = ((bf16[16,4,2,16,128]{4,3,2,1,0:T(8,128)(2,1)}), bf16[16,4,2,16,128]{4,3,2,1,0:T(8,128)(2,1)S(1)}, u32[]{:S(2)}, u32[]{:S(2)}) async-start(bf16[16,4,2,16,128]{4,3,2,1,0:T(8,128)(2,1)} %correlate.2), calls=%async_computation.3 | async-start | bytes 1048576 | tf_op jit(solution)/shard_map/all_to_all | solution.py:402
  77.7 6.3 %collective-permute-done.6.refs_0_ = bf16[16,2,3,16,128]{4,3,2,1,0:T(8,128)(2,1)S(1)} collective-permute-done((bf16[16,2,3,16,128]{4,3,2,1,0:T(8,128)(2,1)}, bf16[16,2,3,16,128]{4,3,2,1,0:T(8,128)(2,1)S(1)}, u32[]{:S(2)}, u32[]{:S(2)}) %collective-permute-start.6) | collective-permute-done | bytes 393248 | tf_op jit(solution)/shard_map/ppermute | solution.py:54
  84.0 0.0 collective-permute-done.7.refs_3_
  84.0 7.9 %correlate.3 = (bf16[16,3,16,128]{3,2,1,0:T(8,128)(2,1)S(1)}, bf16[16,3,16,128]{3,2,1,0:T(8,128)(2,1)S(1)}, bf16[16,3,16,128]{3,2,1,0:T(8,128)(2,1)S(1)}, bf16[16,3,16,128]{3,2,1,0:T(8,128)(2,1)S(1)}) custom-call(f32[3]{0:T(128)S(1)} %marker.3.rot_ref, bf16[16,2,3,16,128]{4,3,2,1,0:T(8,128)(2,1)S(1)} %collective-permute-done.6.refs_0_, ...), custom_call_target="tpu_custom_call" | custom-call | flops 99999997952 | bytes 4456448 | tf_op jit(solution)/shard_map/correlate/pallas_call | solution.py:140
  91.9 0.1 collective-permute-start.8
  91.9 4.5 %collective-permute-start.9 = (bf16[16,3,16,128]{3,2,1,0:T(8,128)(2,1)S(1)}, bf16[16,3,16,128]{3,2,1,0:T(8,128)(2,1)S(1)}, u32[]{:S(2)}, u32[]{:S(2)}) collective-permute-start(bf16[16,3,16,128]{3,2,1,0:T(8,128)(2,1)S(1)} %get-tuple-element.38), channel_id=1, source_target_pairs={{0,130},{1,131},{2,192},{3,193},{4,134},{5,135},{6,196},{7,197},{8... | collective-permute-start | bytes 589832 | tf_op jit(solution)/shard_map/ppermute | solution.py:54
  96.4 0.0 collective-permute-start.10
  96.4 2.7 %collective-permute-start.11 = (bf16[16,3,16,128]{3,2,1,0:T(8,128)(2,1)S(1)}, bf16[16,3,16,128]{3,2,1,0:T(8,128)(2,1)S(1)}, u32[]{:S(2)}, u32[]{:S(2)}) collective-permute-start(bf16[16,3,16,128]{3,2,1,0:T(8,128)(2,1)S(1)} %get-tuple-element.40), channel_id=1, source_target_pairs={{0,194},{1,195},{2,0},{3,1},{4,198},{5,199},{6,4},{7,5},{8,202},{9... | collective-permute-start | bytes 589832 | tf_op jit(solution)/shard_map/ppermute | solution.py:54
  99.1 0.0 all-to-all-done.3
  99.1 0.1 collective-permute-start.15
  99.2 6.1 %collective-permute-done.8.refs_0_ = bf16[16,3,16,128]{3,2,1,0:T(8,128)(2,1)S(1)} collective-permute-done((bf16[16,3,16,128]{3,2,1,0:T(8,128)(2,1)S(1)}, bf16[16,3,16,128]{3,2,1,0:T(8,128)(2,1)S(1)}, u32[]{:S(2)}, u32[]{:S(2)}) %collective-permute-start.8) | collective-permute-done | bytes 196640 | tf_op jit(solution)/shard_map/ppermute | solution.py:54
  105.4 0.4 collective-permute-start.14
  105.8 1.0 collective-permute-done.9.refs_1_
  106.8 0.0 collective-permute-start.13
  106.8 4.0 %collective-permute-done.10.refs_2_ = bf16[16,3,16,128]{3,2,1,0:T(8,128)(2,1)S(1)} collective-permute-done((bf16[16,3,16,128]{3,2,1,0:T(8,128)(2,1)S(1)}, bf16[16,3,16,128]{3,2,1,0:T(8,128)(2,1)S(1)}, u32[]{:S(2)}, u32[]{:S(2)}) %collective-permute-start.10) | collective-permute-done | bytes 196640 | tf_op jit(solution)/shard_map/ppermute | solution.py:54
  110.8 0.0 collective-permute-start.12
  110.8 2.1 %collective-permute-done.11.refs_3_ = bf16[16,3,16,128]{3,2,1,0:T(8,128)(2,1)S(1)} collective-permute-done((bf16[16,3,16,128]{3,2,1,0:T(8,128)(2,1)S(1)}, bf16[16,3,16,128]{3,2,1,0:T(8,128)(2,1)S(1)}, u32[]{:S(2)}, u32[]{:S(2)}) %collective-permute-start.11) | collective-permute-done | bytes 196640 | tf_op jit(solution)/shard_map/ppermute | solution.py:54
  112.9 0.9 gather.3
  113.8 5.3 %all-to-all-start.2 = ((bf16[16,4,3,16,128]{4,3,2,1,0:T(8,128)(2,1)}), bf16[16,4,3,16,128]{4,3,2,1,0:T(8,128)(2,1)S(1)}, u32[]{:S(2)}, u32[]{:S(2)}) async-start(bf16[16,4,3,16,128]{4,3,2,1,0:T(8,128)(2,1)} %gather.3), calls=%async_computation.2 | async-start | bytes 1572864 | tf_op jit(solution)/shard_map/all_to_all | solution.py:405
  119.1 0.0 copy-start.1
  119.1 0.0 copy-start
  119.1 0.0 collective-permute-done.15.refs_3_
  119.1 0.0 collective-permute-done.14.refs_2_
  119.1 2.2 %collective-permute-done.13.refs_1_ = bf16[16,2,16,128]{3,2,1,0:T(8,128)(2,1)S(1)} collective-permute-done((bf16[16,2,16,128]{3,2,1,0:T(8,128)(2,1)S(1)}, bf16[16,2,16,128]{3,2,1,0:T(8,128)(2,1)S(1)}, u32[]{:S(2)}, u32[]{:S(2)}) %collective-permute-start.13) | collective-permute-done | bytes 131104 | tf_op jit(solution)/shard_map/ppermute | solution.py:54
  121.3 2.0 %collective-permute-done.12.refs_0_ = bf16[16,2,16,128]{3,2,1,0:T(8,128)(2,1)S(1)} collective-permute-done((bf16[16,2,16,128]{3,2,1,0:T(8,128)(2,1)S(1)}, bf16[16,2,16,128]{3,2,1,0:T(8,128)(2,1)S(1)}, u32[]{:S(2)}, u32[]{:S(2)}) %collective-permute-start.12) | collective-permute-done | bytes 131104 | tf_op jit(solution)/shard_map/ppermute | solution.py:54
  123.3 0.3 settle.2.refs_3_
  123.6 3.1 %collective-permute-start.17 = (bf16[16,2,64,128]{3,2,1,0:T(8,128)(2,1)S(1)}, bf16[16,2,64,128]{3,2,1,0:T(8,128)(2,1)S(1)}, u32[]{:S(2)}, u32[]{:S(2)}) collective-permute-start(bf16[16,2,64,128]{3,2,1,0:T(8,128)(2,1)S(1)} %settle.2.refs_3_), channel_id=1, source_target_pairs={{1,0},{2,1},{3,2},{5,4},{6,5},{7,6},{9,8},{10,9},{11,10},{13,12},{... | collective-permute-start | bytes 1572872 | tf_op jit(solution)/shard_map/ppermute | solution.py:408
  126.8 2.4 %collective-permute-start.16 = (bf16[16,2,64,128]{3,2,1,0:T(8,128)(2,1)S(1)}, bf16[16,2,64,128]{3,2,1,0:T(8,128)(2,1)S(1)}, u32[]{:S(2)}, u32[]{:S(2)}) collective-permute-start(bf16[16,2,64,128]{3,2,1,0:T(8,128)(2,1)S(1)} %settle.2.refs_3_), channel_id=1, source_target_pairs={{0,1},{1,2},{2,3},{4,5},{5,6},{6,7},{8,9},{9,10},{10,11},{12,13},{... | collective-permute-start | bytes 1572872 | tf_op jit(solution)/shard_map/ppermute | solution.py:408
  129.2 0.1 copy.19
  129.3 0.3 all-to-all-done.2.refs_0_
  129.6 1.4 settle.3
  131.0 3.4 %collective-permute-done.17.refs_5_ = bf16[16,2,64,128]{3,2,1,0:T(8,128)(2,1)S(1)} collective-permute-done((bf16[16,2,64,128]{3,2,1,0:T(8,128)(2,1)S(1)}, bf16[16,2,64,128]{3,2,1,0:T(8,128)(2,1)S(1)}, u32[]{:S(2)}, u32[]{:S(2)}) %collective-permute-start.17) | collective-permute-done | bytes 524320 | tf_op jit(solution)/shard_map/ppermute | solution.py:408
  134.4 0.9 collective-permute-done.16.refs_1_
  135.3 4.4 %collective-permute-start.18 = (bf16[16,2,64,128]{3,2,1,0:T(8,128)(2,1)}, bf16[16,2,64,128]{3,2,1,0:T(8,128)(2,1)S(1)}, u32[]{:S(2)}, u32[]{:S(2)}) collective-permute-start(bf16[16,2,64,128]{3,2,1,0:T(8,128)(2,1)} %get-tuple-element.44), channel_id=1, source_target_pairs={{0,1},{1,2},{2,3},{4,5},{5,6},{6,7},{8,9},{9,10},{10,11},{12,13},{... | collective-permute-start | bytes 1572872 | tf_op jit(solution)/shard_map/ppermute | solution.py:410
  139.7 1.9 %collective-permute-start.19 = (bf16[16,2,64,128]{3,2,1,0:T(8,128)(2,1)}, bf16[16,2,64,128]{3,2,1,0:T(8,128)(2,1)}, u32[]{:S(2)}, u32[]{:S(2)}) collective-permute-start(bf16[16,2,64,128]{3,2,1,0:T(8,128)(2,1)} %get-tuple-element.46), channel_id=1, source_target_pairs={{1,0},{2,1},{3,2},{5,4},{6,5},{7,6},{9,8},{10,9},{11,10},{13,12},{... | collective-permute-start | bytes 1572872 | tf_op jit(solution)/shard_map/ppermute | solution.py:410
  141.7 0.1 add_select_fusion
  141.7 0.2 fusion
  142.0 0.1 copy.30.w_ref
  142.1 4.0 %collective-permute-done.18.refs_0_ = bf16[16,2,64,128]{3,2,1,0:T(8,128)(2,1)S(1)} collective-permute-done((bf16[16,2,64,128]{3,2,1,0:T(8,128)(2,1)}, bf16[16,2,64,128]{3,2,1,0:T(8,128)(2,1)S(1)}, u32[]{:S(2)}, u32[]{:S(2)}) %collective-permute-start.18) | collective-permute-done | bytes 524320 | tf_op jit(solution)/shard_map/ppermute | solution.py:410
  146.1 4.4 %collective-permute-done.19.refs_4_ = bf16[16,2,64,128]{3,2,1,0:T(8,128)(2,1)} collective-permute-done((bf16[16,2,64,128]{3,2,1,0:T(8,128)(2,1)}, bf16[16,2,64,128]{3,2,1,0:T(8,128)(2,1)}, u32[]{:S(2)}, u32[]{:S(2)}) %collective-permute-start.19) | collective-permute-done | bytes 524320 | tf_op jit(solution)/shard_map/ppermute | solution.py:410
  150.5 4.6 %screen.1 = bf16[16,5,64,128]{3,2,1,0:T(8,128)(2,1)} custom-call(s32[1]{0:T(128)} %bitcast.row_ref, s32[4,5]{1,0:T(4,128)S(1)} %copy-done, bf16[64,192]{1,0:T(8,128)(2,1)S(1)} %copy.30.w_ref, bf16[16,2,64,128]{3,2,1,0:T(8,128)(2,1)S(1)} %collective-permute-done.18.refs_0_, bf16[16,2,64,128]{3,2,1,0:T(8,128)(2,1)S(1)} %collective-permute-done.16.refs_1_, ...), custom_call_target="tpu_custom_call" | custom-call | flops 251658240 | bytes 5242880 | tf_op jit(solution)/shard_map/screen/pallas_call | solution.py:347
  (11 shorter events, 0.1 us)
Async XLA Ops:
  4.6 21.5 %collective-permute-start = (bf16[16,2,2,16,128]{4,3,2,1,0:T(8,128)(2,1)}, bf16[16,2,2,16,128]{4,3,2,1,0:T(8,128)(2,1)S(1)}, u32[]{:S(2)}, u32[]{:S(2)}) collective-permute-start(bf16[16,2,2,16,128]{4,3,2,1,0:T(8,128)(2,1)} %get-tuple-element.26), channel_id=1, source_target_pairs={{0,66},{1,67},{2,128},{3,129},{4,70},{5,71},{6,132},{7,133},{8,74}... | collective-permute-start | bytes 786440 | tf_op jit(solution)/shard_map/ppermute | solution.py:54
  9.9 16.3 %collective-permute-start.1 = (bf16[16,2,2,16,128]{4,3,2,1,0:T(8,128)(2,1)}, bf16[16,2,2,16,128]{4,3,2,1,0:T(8,128)(2,1)S(1)}, u32[]{:S(2)}, u32[]{:S(2)}) collective-permute-start(bf16[16,2,2,16,128]{4,3,2,1,0:T(8,128)(2,1)} %get-tuple-element.27), channel_id=1, source_target_pairs={{0,130},{1,131},{2,192},{3,193},{4,134},{5,135},{6,196},{7,197},{8... | collective-permute-start | bytes 786440 | tf_op jit(solution)/shard_map/ppermute | solution.py:54
  12.1 6.9 %copy-start.3 = (bf16[16,2,2,16,128]{4,3,2,1,0:T(8,128)(2,1)S(1)}, bf16[16,2,2,16,128]{4,3,2,1,0:T(8,128)(2,1)}, u32[]{:S(2)}) copy-start(bf16[16,2,2,16,128]{4,3,2,1,0:T(8,128)(2,1)} %get-tuple-element.28) | copy-start | bytes 786436
  12.1 7.8 %copy-start.2 = (bf16[16,2,2,16,128]{4,3,2,1,0:T(8,128)(2,1)S(1)}, bf16[16,2,2,16,128]{4,3,2,1,0:T(8,128)(2,1)}, u32[]{:S(2)}) copy-start(bf16[16,2,2,16,128]{4,3,2,1,0:T(8,128)(2,1)} %get-tuple-element.30) | copy-start | bytes 786436
  12.1 28.9 %all-to-all-start.1 = ((bf16[16,4,2,3,16,128]{5,4,3,2,1,0:T(8,128)(2,1)}), bf16[16,4,2,3,16,128]{5,4,3,2,1,0:T(8,128)(2,1)}, u32[]{:S(2)}, u32[]{:S(2)}) async-start(bf16[16,4,2,3,16,128]{5,4,3,2,1,0:T(8,128)(2,1)} %get-tuple-element.32), calls=%async_computation.1 | async-start | bytes 3145728 | tf_op jit(solution)/shard_map/all_to_all | solution.py:392
  19.1 15.7 %collective-permute-start.2 = (bf16[16,2,2,16,128]{4,3,2,1,0:T(8,128)(2,1)S(1)}, bf16[16,2,2,16,128]{4,3,2,1,0:T(8,128)(2,1)S(1)}, u32[]{:S(2)}, u32[]{:S(2)}) collective-permute-start(bf16[16,2,2,16,128]{4,3,2,1,0:T(8,128)(2,1)S(1)} %copy-done.3), channel_id=1, source_target_pairs={{0,2},{1,3},{2,64},{3,65},{4,6},{5,7},{6,68},{7,69},{8,10},{9,11},... | collective-permute-start | bytes 786440 | tf_op jit(solution)/shard_map/ppermute | solution.py:54
  19.9 16.5 %collective-permute-start.3 = (bf16[16,2,2,16,128]{4,3,2,1,0:T(8,128)(2,1)S(1)}, bf16[16,2,2,16,128]{4,3,2,1,0:T(8,128)(2,1)S(1)}, u32[]{:S(2)}, u32[]{:S(2)}) collective-permute-start(bf16[16,2,2,16,128]{4,3,2,1,0:T(8,128)(2,1)S(1)} %copy-done.2), channel_id=1, source_target_pairs={{0,194},{1,195},{2,0},{3,1},{4,198},{5,199},{6,4},{7,5},{8,202},{9... | collective-permute-start | bytes 786440 | tf_op jit(solution)/shard_map/ppermute | solution.py:54
  43.4 11.4 %collective-permute-start.5 = (bf16[16,2,3,16,128]{4,3,2,1,0:T(8,128)(2,1)S(1)}, bf16[16,2,3,16,128]{4,3,2,1,0:T(8,128)(2,1)S(1)}, u32[]{:S(2)}, u32[]{:S(2)}) collective-permute-start(bf16[16,2,3,16,128]{4,3,2,1,0:T(8,128)(2,1)S(1)} %get-tuple-element.49), channel_id=1, source_target_pairs={{0,194},{1,195},{2,0},{3,1},{4,198},{5,199},{6,4},{7,5},{8,202},{9... | collective-permute-start | bytes 1179656 | tf_op jit(solution)/shard_map/ppermute | solution.py:54
  44.8 9.9 %collective-permute-start.4 = (bf16[16,2,3,16,128]{4,3,2,1,0:T(8,128)(2,1)S(1)}, bf16[16,2,3,16,128]{4,3,2,1,0:T(8,128)(2,1)S(1)}, u32[]{:S(2)}, u32[]{:S(2)}) collective-permute-start(bf16[16,2,3,16,128]{4,3,2,1,0:T(8,128)(2,1)S(1)} %get-tuple-element.50), channel_id=1, source_target_pairs={{0,2},{1,3},{2,64},{3,65},{4,6},{5,7},{6,68},{7,69},{8,10},{9,11},... | collective-permute-start | bytes 1179656 | tf_op jit(solution)/shard_map/ppermute | solution.py:54
  44.9 21.7 %all-to-all-start = ((bf16[16,4,2,2,16,128]{5,4,3,2,1,0:T(8,128)(2,1)}), bf16[16,4,2,2,16,128]{5,4,3,2,1,0:T(8,128)(2,1)S(1)}, u32[]{:S(2)}, u32[]{:S(2)}) async-start(bf16[16,4,2,2,16,128]{5,4,3,2,1,0:T(8,128)(2,1)} %gather.2), calls=%async_computation | async-start | bytes 2097152 | tf_op jit(solution)/shard_map/all_to_all | solution.py:395
  51.1 32.9 %collective-permute-start.7 = (bf16[16,2,3,16,128]{4,3,2,1,0:T(8,128)(2,1)S(1)}, bf16[16,2,3,16,128]{4,3,2,1,0:T(8,128)(2,1)}, u32[]{:S(2)}, u32[]{:S(2)}) collective-permute-start(bf16[16,2,3,16,128]{4,3,2,1,0:T(8,128)(2,1)S(1)} %get-tuple-element.47), channel_id=1, source_target_pairs={{0,130},{1,131},{2,192},{3,193},{4,134},{5,135},{6,196},{7,197},{8... | collective-permute-start | bytes 1179656 | tf_op jit(solution)/shard_map/ppermute | solution.py:54
  54.8 29.2 %collective-permute-start.6 = (bf16[16,2,3,16,128]{4,3,2,1,0:T(8,128)(2,1)}, bf16[16,2,3,16,128]{4,3,2,1,0:T(8,128)(2,1)S(1)}, u32[]{:S(2)}, u32[]{:S(2)}) collective-permute-start(bf16[16,2,3,16,128]{4,3,2,1,0:T(8,128)(2,1)} %get-tuple-element.48), channel_id=1, source_target_pairs={{0,66},{1,67},{2,128},{3,129},{4,70},{5,71},{6,132},{7,133},{8,74}... | collective-permute-start | bytes 1179656 | tf_op jit(solution)/shard_map/ppermute | solution.py:54
  73.1 25.9 %all-to-all-start.3 = ((bf16[16,4,2,16,128]{4,3,2,1,0:T(8,128)(2,1)}), bf16[16,4,2,16,128]{4,3,2,1,0:T(8,128)(2,1)S(1)}, u32[]{:S(2)}, u32[]{:S(2)}) async-start(bf16[16,4,2,16,128]{4,3,2,1,0:T(8,128)(2,1)} %correlate.2), calls=%async_computation.3 | async-start | bytes 1048576 | tf_op jit(solution)/shard_map/all_to_all | solution.py:402
  91.9 13.5 %collective-permute-start.8 = (bf16[16,3,16,128]{3,2,1,0:T(8,128)(2,1)S(1)}, bf16[16,3,16,128]{3,2,1,0:T(8,128)(2,1)S(1)}, u32[]{:S(2)}, u32[]{:S(2)}) collective-permute-start(bf16[16,3,16,128]{3,2,1,0:T(8,128)(2,1)S(1)} %get-tuple-element.37), channel_id=1, source_target_pairs={{0,66},{1,67},{2,128},{3,129},{4,70},{5,71},{6,132},{7,133},{8,74}... | collective-permute-start | bytes 589832 | tf_op jit(solution)/shard_map/ppermute | solution.py:54
  91.9 14.8 %collective-permute-start.9 = (bf16[16,3,16,128]{3,2,1,0:T(8,128)(2,1)S(1)}, bf16[16,3,16,128]{3,2,1,0:T(8,128)(2,1)S(1)}, u32[]{:S(2)}, u32[]{:S(2)}) collective-permute-start(bf16[16,3,16,128]{3,2,1,0:T(8,128)(2,1)S(1)} %get-tuple-element.38), channel_id=1, source_target_pairs={{0,130},{1,131},{2,192},{3,193},{4,134},{5,135},{6,196},{7,197},{8... | collective-permute-start | bytes 589832 | tf_op jit(solution)/shard_map/ppermute | solution.py:54
  96.4 14.4 %collective-permute-start.10 = (bf16[16,3,16,128]{3,2,1,0:T(8,128)(2,1)S(1)}, bf16[16,3,16,128]{3,2,1,0:T(8,128)(2,1)S(1)}, u32[]{:S(2)}, u32[]{:S(2)}) collective-permute-start(bf16[16,3,16,128]{3,2,1,0:T(8,128)(2,1)S(1)} %get-tuple-element.39), channel_id=1, source_target_pairs={{0,2},{1,3},{2,64},{3,65},{4,6},{5,7},{6,68},{7,69},{8,10},{9,11},... | collective-permute-start | bytes 589832 | tf_op jit(solution)/shard_map/ppermute | solution.py:54
  96.4 16.5 %collective-permute-start.11 = (bf16[16,3,16,128]{3,2,1,0:T(8,128)(2,1)S(1)}, bf16[16,3,16,128]{3,2,1,0:T(8,128)(2,1)S(1)}, u32[]{:S(2)}, u32[]{:S(2)}) collective-permute-start(bf16[16,3,16,128]{3,2,1,0:T(8,128)(2,1)S(1)} %get-tuple-element.40), channel_id=1, source_target_pairs={{0,194},{1,195},{2,0},{3,1},{4,198},{5,199},{6,4},{7,5},{8,202},{9... | collective-permute-start | bytes 589832 | tf_op jit(solution)/shard_map/ppermute | solution.py:54
  99.1 20.0 %collective-permute-start.15 = (bf16[16,2,16,128]{3,2,1,0:T(8,128)(2,1)S(1)}, bf16[16,2,16,128]{3,2,1,0:T(8,128)(2,1)S(1)}, u32[]{:S(2)}, u32[]{:S(2)}) collective-permute-start(bf16[16,2,16,128]{3,2,1,0:T(8,128)(2,1)S(1)} %get-tuple-element.51), channel_id=1, source_target_pairs={{0,66},{1,67},{2,128},{3,129},{4,70},{5,71},{6,132},{7,133},{8,74}... | collective-permute-start | bytes 393224 | tf_op jit(solution)/shard_map/ppermute | solution.py:54
  105.4 13.7 %collective-permute-start.14 = (bf16[16,2,16,128]{3,2,1,0:T(8,128)(2,1)S(1)}, bf16[16,2,16,128]{3,2,1,0:T(8,128)(2,1)S(1)}, u32[]{:S(2)}, u32[]{:S(2)}) collective-permute-start(bf16[16,2,16,128]{3,2,1,0:T(8,128)(2,1)S(1)} %get-tuple-element.52), channel_id=1, source_target_pairs={{0,130},{1,131},{2,192},{3,193},{4,134},{5,135},{6,196},{7,197},{8... | collective-permute-start | bytes 393224 | tf_op jit(solution)/shard_map/ppermute | solution.py:54
  106.8 14.5 %collective-permute-start.13 = (bf16[16,2,16,128]{3,2,1,0:T(8,128)(2,1)S(1)}, bf16[16,2,16,128]{3,2,1,0:T(8,128)(2,1)S(1)}, u32[]{:S(2)}, u32[]{:S(2)}) collective-permute-start(bf16[16,2,16,128]{3,2,1,0:T(8,128)(2,1)S(1)} %get-tuple-element.53), channel_id=1, source_target_pairs={{0,2},{1,3},{2,64},{3,65},{4,6},{5,7},{6,68},{7,69},{8,10},{9,11},... | collective-permute-start | bytes 393224 | tf_op jit(solution)/shard_map/ppermute | solution.py:54
  110.8 12.5 %collective-permute-start.12 = (bf16[16,2,16,128]{3,2,1,0:T(8,128)(2,1)S(1)}, bf16[16,2,16,128]{3,2,1,0:T(8,128)(2,1)S(1)}, u32[]{:S(2)}, u32[]{:S(2)}) collective-permute-start(bf16[16,2,16,128]{3,2,1,0:T(8,128)(2,1)S(1)} %get-tuple-element.54), channel_id=1, source_target_pairs={{0,194},{1,195},{2,0},{3,1},{4,198},{5,199},{6,4},{7,5},{8,202},{9... | collective-permute-start | bytes 393224 | tf_op jit(solution)/shard_map/ppermute | solution.py:54
  113.8 15.8 %all-to-all-start.2 = ((bf16[16,4,3,16,128]{4,3,2,1,0:T(8,128)(2,1)}), bf16[16,4,3,16,128]{4,3,2,1,0:T(8,128)(2,1)S(1)}, u32[]{:S(2)}, u32[]{:S(2)}) async-start(bf16[16,4,3,16,128]{4,3,2,1,0:T(8,128)(2,1)} %gather.3), calls=%async_computation.2 | async-start | bytes 1572864 | tf_op jit(solution)/shard_map/all_to_all | solution.py:405
  119.1 10.2 %copy-start.1 = (bf16[1,64,192]{2,1,0:T(8,128)(2,1)S(1)}, bf16[1,64,192]{2,1,0:T(8,128)(2,1)}, u32[]{:S(2)}) copy-start(bf16[1,64,192]{2,1,0:T(8,128)(2,1)} %param.8) | copy-start | bytes 73732
  119.1 31.4 %copy-start = (s32[4,5]{1,0:T(4,128)S(1)}, s32[4,5]{1,0:T(4,128)}, u32[]{:S(2)}) copy-start(s32[4,5]{1,0:T(4,128)} %pattern_ref.3) | copy-start | bytes 244
  123.6 10.8 %collective-permute-start.17 = (bf16[16,2,64,128]{3,2,1,0:T(8,128)(2,1)S(1)}, bf16[16,2,64,128]{3,2,1,0:T(8,128)(2,1)S(1)}, u32[]{:S(2)}, u32[]{:S(2)}) collective-permute-start(bf16[16,2,64,128]{3,2,1,0:T(8,128)(2,1)S(1)} %settle.2.refs_3_), channel_id=1, source_target_pairs={{1,0},{2,1},{3,2},{5,4},{6,5},{7,6},{9,8},{10,9},{11,10},{13,12},{... | collective-permute-start | bytes 1572872 | tf_op jit(solution)/shard_map/ppermute | solution.py:408
  126.8 8.6 %collective-permute-start.16 = (bf16[16,2,64,128]{3,2,1,0:T(8,128)(2,1)S(1)}, bf16[16,2,64,128]{3,2,1,0:T(8,128)(2,1)S(1)}, u32[]{:S(2)}, u32[]{:S(2)}) collective-permute-start(bf16[16,2,64,128]{3,2,1,0:T(8,128)(2,1)S(1)} %settle.2.refs_3_), channel_id=1, source_target_pairs={{0,1},{1,2},{2,3},{4,5},{5,6},{6,7},{8,9},{9,10},{10,11},{12,13},{... | collective-permute-start | bytes 1572872 | tf_op jit(solution)/shard_map/ppermute | solution.py:408
  135.3 10.8 %collective-permute-start.18 = (bf16[16,2,64,128]{3,2,1,0:T(8,128)(2,1)}, bf16[16,2,64,128]{3,2,1,0:T(8,128)(2,1)S(1)}, u32[]{:S(2)}, u32[]{:S(2)}) collective-permute-start(bf16[16,2,64,128]{3,2,1,0:T(8,128)(2,1)} %get-tuple-element.44), channel_id=1, source_target_pairs={{0,1},{1,2},{2,3},{4,5},{5,6},{6,7},{8,9},{9,10},{10,11},{12,13},{... | collective-permute-start | bytes 1572872 | tf_op jit(solution)/shard_map/ppermute | solution.py:410
  139.7 10.8 %collective-permute-start.19 = (bf16[16,2,64,128]{3,2,1,0:T(8,128)(2,1)}, bf16[16,2,64,128]{3,2,1,0:T(8,128)(2,1)}, u32[]{:S(2)}, u32[]{:S(2)}) collective-permute-start(bf16[16,2,64,128]{3,2,1,0:T(8,128)(2,1)} %get-tuple-element.46), channel_id=1, source_target_pairs={{1,0},{2,1},{3,2},{5,4},{6,5},{7,6},{9,8},{10,9},{11,10},{13,12},{... | collective-permute-start | bytes 1572872 | tf_op jit(solution)/shard_map/ppermute | solution.py:410

commit v9 on v8

--- a/solution.py
+++ b/solution.py
@@ -283,6 +283,27 @@
     )(*(pieces[j] for j in ORDER))
 
 
+def split_kernel(in_ref, *out_refs):
+    for j in range(4):
+        out_refs[j][...] = in_ref[:, j]
+
+
+def split(value):
+    shape = value.shape
+    rest = shape[2:]
+    zeros = (0,) * len(rest)
+    return pl.pallas_call(
+        split_kernel,
+        grid=(4,),
+        out_shape=[jax.ShapeDtypeStruct((shape[0], *rest), value.dtype)] * 4,
+        in_specs=[pl.BlockSpec((shape[0] // 4, 4, *rest), lambda i: (i, 0, *zeros))],
+        out_specs=[pl.BlockSpec((shape[0] // 4, *rest), lambda i: (i, *zeros))] * 4,
+        cost_estimate=pl.CostEstimate(flops=0, bytes_accessed=value.size * 4, transcendentals=0),
+        compiler_params=pltpu.CompilerParams(vmem_limit_bytes=12 << 20),
+        name="split",
+    )(value)
+
+
 def marker(value, pieces, flops):
     hbm = pl.BlockSpec(memory_space=pl.ANY)
 
@@ -308,16 +329,19 @@
     @pl.when(pl.program_id(0) == 0)
     def _():
         row = row_ref[0]
-        for d in range(3):
+        for d in (1, 0, 2):
             k = row + d - 1
             inside = jnp.logical_and(k >= 0, k < rows)
             k = jnp.clip(k, 0, rows - 1)
             places = [place_of(pattern_ref, k, t) for t in range(slots)]
             for s in range(slots):
-                want = pattern_ref[row, s]
                 at = jnp.int32(-1)
                 for t in range(slots):
-                    at = jnp.where(jnp.logical_and(inside, pattern_ref[k, t] == want), places[t], at)
+                    if d == 1:
+                        at = jnp.where(places[t] == s, t, at)
+                    else:
+                        same = pattern_ref[k, t] == pattern_ref[row, at_ref[1, s]]
+                        at = jnp.where(jnp.logical_and(inside, same), places[t], at)
                 at_ref[d, s] = at
 
     w = w_ref[...]
@@ -326,15 +350,18 @@
         for s in range(slots):
             blocks = []
             for d, (low, high) in enumerate(pairs):
+                if d == 1:
+                    blocks.append(low[l, s] if s < CUT else high[l, s - CUT])
+                    continue
                 at = at_ref[d, s]
                 one = low[l, jnp.clip(at - 1 if d == 0 else at, 0, low.shape[1] - 1)]
                 two = high[l, jnp.clip(at - CUT, 0, high.shape[1] - 1)]
                 got = jnp.where(at < CUT, one, two)
-                blocks.append(got if d == 1 else jnp.where(at >= 0, got, jnp.zeros_like(got)))
+                blocks.append(jnp.where(at >= 0, got, jnp.zeros_like(got)))
             cols.append(jnp.concatenate(blocks, 0))
         res = jnp.dot(w, jnp.concatenate(cols, 1), preferred_element_type=jnp.float32)
         for s in range(slots):
-            out_ref[l, s] = res[:, s * 128 : (s + 1) * 128].astype(jnp.bfloat16)
+            out_ref[l, at_ref[1, s]] = res[:, s * 128 : (s + 1) * 128].astype(jnp.bfloat16)
 
 
 def screen(row, pattern, weights, up, own, down):
@@ -391,7 +418,7 @@
     late = gather(late, 0)
     early = lax.all_to_all(early, PLANE, split_axis=0, concat_axis=0, tiled=True)
     early = after(early, late)
-    early = [hop(early[:, j], STEPS[j]) for j in range(4)]
+    early = [hop(p, STEPS[j]) for j, p in enumerate(split(early))]
     late = lax.all_to_all(late, PLANE, split_axis=0, concat_axis=0, tiled=True)
 
     late, rot = lax.optimization_barrier([late, marker(rot, early[1:3], HEAVY)])

time: 156 us -> 158 us (1.013)
  starting transfers between devices: 57.9 us -> 70.3 us
  waiting for transfers between devices: 66.5 us -> 57.6 us
  local copies, waits for them, and re-layouts: 2.67 us -> 0.26 us
    ppermute x16, waiting for transfers between devices: 38.2 us -> 30.5 us  [hop(): return lax.ppermute(piece, ALL, perm)]
    ppermute x16, starting transfers between devices: 23.1 us -> 30.4 us  [hop(): return lax.ppermute(piece, ALL, perm)]
    ppermute x1, starting transfers between devices: 3.12 us -> 6.23 us  [shards(): lax.ppermute(hi, 's', downward)]
    squeeze x1 -> x0, local copies, waits for them, and re-layouts: 2.41 us -> none  [shards(): early = [hop(early[:, j], STEPS[j]) for j in range(4)]]
    all_to_all x1, starting transfers between devices: 5.26 us -> 6.85 us  [shards(): lo = lax.all_to_all(lo, PLANE, split_axis=0, concat_axis=0, tiled=True)]
  transfers between devices with their start and end apart: 24 -> 24, of which waited for: 17 -> 14; matrix products, arithmetic and copies ran while one was open for 0% -> 0% of each run, Pallas kernels for 12% -> 12%
where the time goes in v9:
time: 158 us; the launch traced here: 157 us
  starting transfers between devices  70.3 us (44%)
  waiting for transfers between devices  57.6 us (36%)
  Pallas kernels  28.5 us (18%)
    ppermute x16, waiting for transfers between devices, hop(): return lax.ppermute(piece, ALL, perm)  30.5 us
    ppermute x16, starting transfers between devices, hop(): return lax.ppermute(piece, ALL, perm)  30.4 us
    pallas_call x2, Pallas kernels, correlate(): pl.pallas_call(functools.partial(correlate_kernel, slots, len(inputs), sp...  14.5 us
    all_to_all x1, waiting for transfers between devices, shards(): late = lax.all_to_all(late, PLANE, split_axis=0, concat_axis=0, tiled=True)  10.5 us
    all_to_all x1, starting transfers between devices, shards(): lax.all_to_all(early, PLANE, split_axis=0, concat_axis=0, tiled=True)  6.88 us
    all_to_all x1, starting transfers between devices, shards(): lo = lax.all_to_all(lo, PLANE, split_axis=0, concat_axis=0, tiled=True)  6.85 us
    ppermute x1, starting transfers between devices, shards(): lax.ppermute(hi, 's', downward)  6.23 us
    all_to_all x1, starting transfers between devices, shards(): late = lax.all_to_all(late, PLANE, split_axis=0, concat_axis=0, tiled=True)  5.52 us
  transfers between devices with their start and end apart: 24, of which 14 were waited for; matrix products, arithmetic and copies ran while one was open for 0% of the time, Pallas kernels for 12%

profile of v9, /device:TPU:1, one launch (start us, length us, event | category | flops | bytes accessed | tf_op | source)
XLA Modules:
  0.0 157.4 jit_solution(6338911926230072295)
XLA Ops:
  0.0 4.7 %prepare.1 = (bf16[16,4,2,3,16,128]{5,4,3,2,1,0:T(8,128)(2,1)}, bf16[16,2,2,16,128]{4,3,2,1,0:T(8,128)(2,1)}, bf16[16,2,2,16,128]{4,3,2,1,0:T(8,128)(2,1)}, bf16...) custom-call(s32[1]{0:T(128)} %bitcast.6.turn_ref, s32[1]{0:T(128)} %bitcast.row_ref, s32[4,5]{1,0:T(4,128)} %pattern_ref.3, ...), custom_call_target="tpu_custom_call" | custom-call | bytes 5242880 | tf_op jit(solution)/shard_map/prepare/pallas_call | solution.py:221
  4.7 5.3 %collective-permute-start = (bf16[16,2,2,16,128]{4,3,2,1,0:T(8,128)(2,1)}, bf16[16,2,2,16,128]{4,3,2,1,0:T(8,128)(2,1)S(1)}, u32[]{:S(2)}, u32[]{:S(2)}) collective-permute-start(bf16[16,2,2,16,128]{4,3,2,1,0:T(8,128)(2,1)} %get-tuple-element.30), channel_id=1, source_target_pairs={{0,66},{1,67},{2,128},{3,129},{4,70},{5,71},{6,132},{7,133},{8,74}... | collective-permute-start | bytes 786440 | tf_op jit(solution)/shard_map/ppermute | solution.py:54
  9.9 2.2 %collective-permute-start.1 = (bf16[16,2,2,16,128]{4,3,2,1,0:T(8,128)(2,1)}, bf16[16,2,2,16,128]{4,3,2,1,0:T(8,128)(2,1)S(1)}, u32[]{:S(2)}, u32[]{:S(2)}) collective-permute-start(bf16[16,2,2,16,128]{4,3,2,1,0:T(8,128)(2,1)} %get-tuple-element.31), channel_id=1, source_target_pairs={{0,130},{1,131},{2,192},{3,193},{4,134},{5,135},{6,196},{7,197},{8... | collective-permute-start | bytes 786440 | tf_op jit(solution)/shard_map/ppermute | solution.py:54
  12.1 6.9 %all-to-all-start.1 = ((bf16[16,4,2,3,16,128]{5,4,3,2,1,0:T(8,128)(2,1)}), bf16[16,4,2,3,16,128]{5,4,3,2,1,0:T(8,128)(2,1)S(1)}, u32[]{:S(2)}, u32[]{:S(2)}) async-start(bf16[16,4,2,3,16,128]{5,4,3,2,1,0:T(8,128)(2,1)} %get-tuple-element.36), calls=%async_computation.1 | async-start | bytes 3145728 | tf_op jit(solution)/shard_map/all_to_all | solution.py:419
  19.0 0.8 collective-permute-start.2
  19.9 1.9 %collective-permute-start.3 = (bf16[16,2,2,16,128]{4,3,2,1,0:T(8,128)(2,1)S(1)}, bf16[16,2,2,16,128]{4,3,2,1,0:T(8,128)(2,1)S(1)}, u32[]{:S(2)}, u32[]{:S(2)}) collective-permute-start(bf16[16,2,2,16,128]{4,3,2,1,0:T(8,128)(2,1)S(1)} %copy-done.2), channel_id=1, source_target_pairs={{0,194},{1,195},{2,0},{3,1},{4,198},{5,199},{6,4},{7,5},{8,202},{9... | collective-permute-start | bytes 786440 | tf_op jit(solution)/shard_map/ppermute | solution.py:54
  21.8 0.1 pad_maximum_fusion.refs_0_
  21.9 4.3 %collective-permute-done.refs_1_.refs_0_ = bf16[16,2,2,16,128]{4,3,2,1,0:T(8,128)(2,1)S(1)} collective-permute-done((bf16[16,2,2,16,128]{4,3,2,1,0:T(8,128)(2,1)}, bf16[16,2,2,16,128]{4,3,2,1,0:T(8,128)(2,1)S(1)}, u32[]{:S(2)}, u32[]{:S(2)}) %collective-permute-start) | collective-permute-done | bytes 262176 | tf_op jit(solution)/shard_map/ppermute | solution.py:54
  26.2 0.0 collective-permute-done.1.refs_2_.refs_1_
  26.2 8.5 %collective-permute-done.2.refs_2_ = bf16[16,2,2,16,128]{4,3,2,1,0:T(8,128)(2,1)S(1)} collective-permute-done((bf16[16,2,2,16,128]{4,3,2,1,0:T(8,128)(2,1)S(1)}, bf16[16,2,2,16,128]{4,3,2,1,0:T(8,128)(2,1)S(1)}, u32[]{:S(2)}, u32[]{:S(2)}) %collective-permute-start.2) | collective-permute-done | bytes 262176 | tf_op jit(solution)/shard_map/ppermute | solution.py:54
  34.7 1.7 %collective-permute-done.3.refs_3_ = bf16[16,2,2,16,128]{4,3,2,1,0:T(8,128)(2,1)S(1)} collective-permute-done((bf16[16,2,2,16,128]{4,3,2,1,0:T(8,128)(2,1)S(1)}, bf16[16,2,2,16,128]{4,3,2,1,0:T(8,128)(2,1)S(1)}, u32[]{:S(2)}, u32[]{:S(2)}) %collective-permute-start.3) | collective-permute-done | bytes 262176 | tf_op jit(solution)/shard_map/ppermute | solution.py:54
  36.3 1.0 gather.2
  37.4 3.6 %all-to-all-done.1.in_ref = bf16[16,4,2,3,16,128]{5,4,3,2,1,0:T(8,128)(2,1)S(1)} async-done(((bf16[16,4,2,3,16,128]{5,4,3,2,1,0:T(8,128)(2,1)}), bf16[16,4,2,3,16,128]{5,4,3,2,1,0:T(8,128)(2,1)S(1)}, u32[]{:S(2)}, u32[]{:S(2)}) %all-to-all-start.1) | async-done | bytes 1572896 | tf_op jit(solution)/shard_map/all_to_all | solution.py:419
  40.9 1.4 split.1
  42.3 0.7 collective-permute-start.4
  43.0 1.9 %collective-permute-start.5 = (bf16[16,2,3,16,128]{4,3,2,1,0:T(8,128)(2,1)S(1)}, bf16[16,2,3,16,128]{4,3,2,1,0:T(8,128)(2,1)S(1)}, u32[]{:S(2)}, u32[]{:S(2)}) collective-permute-start(bf16[16,2,3,16,128]{4,3,2,1,0:T(8,128)(2,1)S(1)} %get-tuple-element.39), channel_id=1, source_target_pairs={{0,194},{1,195},{2,0},{3,1},{4,198},{5,199},{6,4},{7,5},{8,202},{9... | collective-permute-start | bytes 1179656 | tf_op jit(solution)/shard_map/ppermute | solution.py:54
  45.0 5.5 %all-to-all-start = ((bf16[16,4,2,2,16,128]{5,4,3,2,1,0:T(8,128)(2,1)}), bf16[16,4,2,2,16,128]{5,4,3,2,1,0:T(8,128)(2,1)S(1)}, u32[]{:S(2)}, u32[]{:S(2)}) async-start(bf16[16,4,2,2,16,128]{5,4,3,2,1,0:T(8,128)(2,1)} %gather.2), calls=%async_computation | async-start | bytes 2097152 | tf_op jit(solution)/shard_map/all_to_all | solution.py:422
  50.5 2.4 %collective-permute-start.6 = (bf16[16,2,3,16,128]{4,3,2,1,0:T(8,128)(2,1)S(1)}, bf16[16,2,3,16,128]{4,3,2,1,0:T(8,128)(2,1)S(1)}, u32[]{:S(2)}, u32[]{:S(2)}) collective-permute-start(bf16[16,2,3,16,128]{4,3,2,1,0:T(8,128)(2,1)S(1)} %get-tuple-element.41), channel_id=1, source_target_pairs={{0,66},{1,67},{2,128},{3,129},{4,70},{5,71},{6,132},{7,133},{8,74}... | collective-permute-start | bytes 1179656 | tf_op jit(solution)/shard_map/ppermute | solution.py:54
  52.9 2.1 %collective-permute-start.7 = (bf16[16,2,3,16,128]{4,3,2,1,0:T(8,128)(2,1)S(1)}, bf16[16,2,3,16,128]{4,3,2,1,0:T(8,128)(2,1)}, u32[]{:S(2)}, u32[]{:S(2)}) collective-permute-start(bf16[16,2,3,16,128]{4,3,2,1,0:T(8,128)(2,1)S(1)} %get-tuple-element.44), channel_id=1, source_target_pairs={{0,130},{1,131},{2,192},{3,193},{4,134},{5,135},{6,196},{7,197},{8... | collective-permute-start | bytes 1179656 | tf_op jit(solution)/shard_map/ppermute | solution.py:54
  55.0 0.0 collective-permute-done.4.refs_1_
  55.0 0.0 collective-permute-done.5.refs_2_
  55.1 10.5 %all-to-all-done.refs_0_ = bf16[16,4,2,2,16,128]{5,4,3,2,1,0:T(8,128)(2,1)S(1)} async-done(((bf16[16,4,2,2,16,128]{5,4,3,2,1,0:T(8,128)(2,1)}), bf16[16,4,2,2,16,128]{5,4,3,2,1,0:T(8,128)(2,1)S(1)}, u32[]{:S(2)}, u32[]{:S(2)}) %all-to-all-start) | async-done | bytes 1048608 | tf_op jit(solution)/shard_map/all_to_all | solution.py:422
  65.6 6.6 %correlate.2 = bf16[16,4,2,16,128]{4,3,2,1,0:T(8,128)(2,1)} custom-call(f32[3]{0:T(128)S(1)} %marker.3.rot_ref, bf16[16,4,2,2,16,128]{5,4,3,2,1,0:T(8,128)(2,1)S(1)} %all-to-all-done.refs_0_, bf16[4,512,256]{2,1,0:T(8,128)(2,1)} %constant.87.clone.refs_1_.refs_4_, bf16[4,512,256]{2,1,0:T(8,128)(2,1)} %constant.88.clone.refs_2_.refs_5_), custom_call_target="tpu_custom_call" | custom-call | bytes 3670016 | tf_op jit(solution)/shard_map/correlate/pallas_call | solution.py:140
  72.2 4.9 %all-to-all-start.3 = ((bf16[16,4,2,16,128]{4,3,2,1,0:T(8,128)(2,1)}), bf16[16,4,2,16,128]{4,3,2,1,0:T(8,128)(2,1)S(1)}, u32[]{:S(2)}, u32[]{:S(2)}) async-start(bf16[16,4,2,16,128]{4,3,2,1,0:T(8,128)(2,1)} %correlate.2), calls=%async_computation.3 | async-start | bytes 1048576 | tf_op jit(solution)/shard_map/all_to_all | solution.py:429
  77.1 0.8 collective-permute-done.6.refs_0_
  77.9 0.0 collective-permute-done.7.refs_3_
  77.9 7.9 %correlate.3 = (bf16[16,3,16,128]{3,2,1,0:T(8,128)(2,1)S(1)}, bf16[16,3,16,128]{3,2,1,0:T(8,128)(2,1)S(1)}, bf16[16,3,16,128]{3,2,1,0:T(8,128)(2,1)S(1)}, bf16[16,3,16,128]{3,2,1,0:T(8,128)(2,1)S(1)}) custom-call(f32[3]{0:T(128)S(1)} %marker.3.rot_ref, bf16[16,2,3,16,128]{4,3,2,1,0:T(8,128)(2,1)S(1)} %collective-permute-done.6.refs_0_, ...), custom_call_target="tpu_custom_call" | custom-call | flops 99999997952 | bytes 4456448 | tf_op jit(solution)/shard_map/correlate/pallas_call | solution.py:140
  85.8 7.3 %collective-permute-start.8 = (bf16[16,3,16,128]{3,2,1,0:T(8,128)(2,1)S(1)}, bf16[16,3,16,128]{3,2,1,0:T(8,128)(2,1)S(1)}, u32[]{:S(2)}, u32[]{:S(2)}) collective-permute-start(bf16[16,3,16,128]{3,2,1,0:T(8,128)(2,1)S(1)} %get-tuple-element.45), channel_id=1, source_target_pairs={{0,66},{1,67},{2,128},{3,129},{4,70},{5,71},{6,132},{7,133},{8,74}... | collective-permute-start | bytes 589832 | tf_op jit(solution)/shard_map/ppermute | solution.py:54
  93.1 0.0 collective-permute-start.9
  93.1 2.5 %collective-permute-start.10 = (bf16[16,3,16,128]{3,2,1,0:T(8,128)(2,1)S(1)}, bf16[16,3,16,128]{3,2,1,0:T(8,128)(2,1)S(1)}, u32[]{:S(2)}, u32[]{:S(2)}) collective-permute-start(bf16[16,3,16,128]{3,2,1,0:T(8,128)(2,1)S(1)} %get-tuple-element.47), channel_id=1, source_target_pairs={{0,2},{1,3},{2,64},{3,65},{4,6},{5,7},{6,68},{7,69},{8,10},{9,11},... | collective-permute-start | bytes 589832 | tf_op jit(solution)/shard_map/ppermute | solution.py:54
  95.6 0.2 collective-permute-start.11
  95.8 0.0 all-to-all-done.3
  95.9 2.1 %collective-permute-start.15 = (bf16[16,2,16,128]{3,2,1,0:T(8,128)(2,1)S(1)}, bf16[16,2,16,128]{3,2,1,0:T(8,128)(2,1)S(1)}, u32[]{:S(2)}, u32[]{:S(2)}) collective-permute-start(bf16[16,2,16,128]{3,2,1,0:T(8,128)(2,1)S(1)} %get-tuple-element.55), channel_id=1, source_target_pairs={{0,66},{1,67},{2,128},{3,129},{4,70},{5,71},{6,132},{7,133},{8,74}... | collective-permute-start | bytes 393224 | tf_op jit(solution)/shard_map/ppermute | solution.py:54
  98.0 6.4 %collective-permute-done.8.refs_0_ = bf16[16,3,16,128]{3,2,1,0:T(8,128)(2,1)S(1)} collective-permute-done((bf16[16,3,16,128]{3,2,1,0:T(8,128)(2,1)S(1)}, bf16[16,3,16,128]{3,2,1,0:T(8,128)(2,1)S(1)}, u32[]{:S(2)}, u32[]{:S(2)}) %collective-permute-start.8) | collective-permute-done | bytes 196640 | tf_op jit(solution)/shard_map/ppermute | solution.py:54
  104.4 0.0 collective-permute-start.14
  104.4 0.0 collective-permute-done.9.refs_1_
  104.4 0.8 collective-permute-start.13
  105.2 7.4 %collective-permute-done.10.refs_2_ = bf16[16,3,16,128]{3,2,1,0:T(8,128)(2,1)S(1)} collective-permute-done((bf16[16,3,16,128]{3,2,1,0:T(8,128)(2,1)S(1)}, bf16[16,3,16,128]{3,2,1,0:T(8,128)(2,1)S(1)}, u32[]{:S(2)}, u32[]{:S(2)}) %collective-permute-start.10) | collective-permute-done | bytes 196640 | tf_op jit(solution)/shard_map/ppermute | solution.py:54
  112.7 0.0 collective-permute-start.12
  112.7 1.4 collective-permute-done.11.refs_3_
  114.0 0.9 gather.3
  115.0 6.8 %all-to-all-start.2 = ((bf16[16,4,3,16,128]{4,3,2,1,0:T(8,128)(2,1)}), bf16[16,4,3,16,128]{4,3,2,1,0:T(8,128)(2,1)S(1)}, u32[]{:S(2)}, u32[]{:S(2)}) async-start(bf16[16,4,3,16,128]{4,3,2,1,0:T(8,128)(2,1)} %gather.3), calls=%async_computation.2 | async-start | bytes 1572864 | tf_op jit(solution)/shard_map/all_to_all | solution.py:432
  121.8 0.0 copy-start.1
  121.8 0.0 copy-start
  121.8 0.0 collective-permute-done.15.refs_3_
  121.9 0.0 collective-permute-done.14.refs_2_
  121.9 0.0 collective-permute-done.13.refs_1_
  121.9 0.0 collective-permute-done.12.refs_0_
  121.9 0.3 settle.2.refs_3_
  122.2 6.2 %collective-permute-start.17 = (bf16[16,2,64,128]{3,2,1,0:T(8,128)(2,1)S(1)}, bf16[16,2,64,128]{3,2,1,0:T(8,128)(2,1)S(1)}, u32[]{:S(2)}, u32[]{:S(2)}) collective-permute-start(bf16[16,2,64,128]{3,2,1,0:T(8,128)(2,1)S(1)} %settle.2.refs_3_), channel_id=1, source_target_pairs={{1,0},{2,1},{3,2},{5,4},{6,5},{7,6},{9,8},{10,9},{11,10},{13,12},{... | collective-permute-start | bytes 1572872 | tf_op jit(solution)/shard_map/ppermute | solution.py:435
  128.4 3.1 %collective-permute-start.16 = (bf16[16,2,64,128]{3,2,1,0:T(8,128)(2,1)S(1)}, bf16[16,2,64,128]{3,2,1,0:T(8,128)(2,1)S(1)}, u32[]{:S(2)}, u32[]{:S(2)}) collective-permute-start(bf16[16,2,64,128]{3,2,1,0:T(8,128)(2,1)S(1)} %settle.2.refs_3_), channel_id=1, source_target_pairs={{0,1},{1,2},{2,3},{4,5},{5,6},{6,7},{8,9},{9,10},{10,11},{12,13},{... | collective-permute-start | bytes 1572872 | tf_op jit(solution)/shard_map/ppermute | solution.py:435
  131.5 0.1 copy.17
  131.7 0.6 all-to-all-done.2.refs_0_
  132.3 1.4 settle.3
  133.7 3.1 %collective-permute-done.17.refs_5_ = bf16[16,2,64,128]{3,2,1,0:T(8,128)(2,1)S(1)} collective-permute-done((bf16[16,2,64,128]{3,2,1,0:T(8,128)(2,1)S(1)}, bf16[16,2,64,128]{3,2,1,0:T(8,128)(2,1)S(1)}, u32[]{:S(2)}, u32[]{:S(2)}) %collective-permute-start.17) | collective-permute-done | bytes 524320 | tf_op jit(solution)/shard_map/ppermute | solution.py:435
  136.8 0.9 collective-permute-done.16.refs_1_
  137.6 4.6 %collective-permute-start.18 = (bf16[16,2,64,128]{3,2,1,0:T(8,128)(2,1)}, bf16[16,2,64,128]{3,2,1,0:T(8,128)(2,1)S(1)}, u32[]{:S(2)}, u32[]{:S(2)}) collective-permute-start(bf16[16,2,64,128]{3,2,1,0:T(8,128)(2,1)} %get-tuple-element.52), channel_id=1, source_target_pairs={{0,1},{1,2},{2,3},{4,5},{5,6},{6,7},{8,9},{9,10},{10,11},{12,13},{... | collective-permute-start | bytes 1572872 | tf_op jit(solution)/shard_map/ppermute | solution.py:437
  142.2 1.9 %collective-permute-start.19 = (bf16[16,2,64,128]{3,2,1,0:T(8,128)(2,1)}, bf16[16,2,64,128]{3,2,1,0:T(8,128)(2,1)}, u32[]{:S(2)}, u32[]{:S(2)}) collective-permute-start(bf16[16,2,64,128]{3,2,1,0:T(8,128)(2,1)} %get-tuple-element.54), channel_id=1, source_target_pairs={{1,0},{2,1},{3,2},{5,4},{6,5},{7,6},{9,8},{10,9},{11,10},{13,12},{... | collective-permute-start | bytes 1572872 | tf_op jit(solution)/shard_map/ppermute | solution.py:437
  144.2 0.1 add_select_fusion
  144.3 0.2 fusion
  144.5 0.1 copy.24.w_ref
  144.6 4.0 %collective-permute-done.18.refs_0_ = bf16[16,2,64,128]{3,2,1,0:T(8,128)(2,1)S(1)} collective-permute-done((bf16[16,2,64,128]{3,2,1,0:T(8,128)(2,1)}, bf16[16,2,64,128]{3,2,1,0:T(8,128)(2,1)S(1)}, u32[]{:S(2)}, u32[]{:S(2)}) %collective-permute-start.18) | collective-permute-done | bytes 524320 | tf_op jit(solution)/shard_map/ppermute | solution.py:437
  148.6 4.4 %collective-permute-done.19.refs_4_ = bf16[16,2,64,128]{3,2,1,0:T(8,128)(2,1)} collective-permute-done((bf16[16,2,64,128]{3,2,1,0:T(8,128)(2,1)}, bf16[16,2,64,128]{3,2,1,0:T(8,128)(2,1)}, u32[]{:S(2)}, u32[]{:S(2)}) %collective-permute-start.19) | collective-permute-done | bytes 524320 | tf_op jit(solution)/shard_map/ppermute | solution.py:437
  153.0 4.3 %screen.1 = bf16[16,5,64,128]{3,2,1,0:T(8,128)(2,1)} custom-call(s32[1]{0:T(128)} %bitcast.row_ref, s32[4,5]{1,0:T(4,128)S(1)} %copy-done, bf16[64,192]{1,0:T(8,128)(2,1)S(1)} %copy.24.w_ref, bf16[16,2,64,128]{3,2,1,0:T(8,128)(2,1)S(1)} %collective-permute-done.18.refs_0_, bf16[16,2,64,128]{3,2,1,0:T(8,128)(2,1)S(1)} %collective-permute-done.16.refs_1_, ...), custom_call_target="tpu_custom_call" | custom-call | flops 251658240 | bytes 5242880 | tf_op jit(solution)/shard_map/screen/pallas_call | solution.py:374
  (11 shorter events, 0.1 us)
Async XLA Ops:
  4.7 21.5 %collective-permute-start = (bf16[16,2,2,16,128]{4,3,2,1,0:T(8,128)(2,1)}, bf16[16,2,2,16,128]{4,3,2,1,0:T(8,128)(2,1)S(1)}, u32[]{:S(2)}, u32[]{:S(2)}) collective-permute-start(bf16[16,2,2,16,128]{4,3,2,1,0:T(8,128)(2,1)} %get-tuple-element.30), channel_id=1, source_target_pairs={{0,66},{1,67},{2,128},{3,129},{4,70},{5,71},{6,132},{7,133},{8,74}... | collective-permute-start | bytes 786440 | tf_op jit(solution)/shard_map/ppermute | solution.py:54
  9.9 16.3 %collective-permute-start.1 = (bf16[16,2,2,16,128]{4,3,2,1,0:T(8,128)(2,1)}, bf16[16,2,2,16,128]{4,3,2,1,0:T(8,128)(2,1)S(1)}, u32[]{:S(2)}, u32[]{:S(2)}) collective-permute-start(bf16[16,2,2,16,128]{4,3,2,1,0:T(8,128)(2,1)} %get-tuple-element.31), channel_id=1, source_target_pairs={{0,130},{1,131},{2,192},{3,193},{4,134},{5,135},{6,196},{7,197},{8... | collective-permute-start | bytes 786440 | tf_op jit(solution)/shard_map/ppermute | solution.py:54
  12.1 6.9 %copy-start.3 = (bf16[16,2,2,16,128]{4,3,2,1,0:T(8,128)(2,1)S(1)}, bf16[16,2,2,16,128]{4,3,2,1,0:T(8,128)(2,1)}, u32[]{:S(2)}) copy-start(bf16[16,2,2,16,128]{4,3,2,1,0:T(8,128)(2,1)} %get-tuple-element.32) | copy-start | bytes 786436
  12.1 7.7 %copy-start.2 = (bf16[16,2,2,16,128]{4,3,2,1,0:T(8,128)(2,1)S(1)}, bf16[16,2,2,16,128]{4,3,2,1,0:T(8,128)(2,1)}, u32[]{:S(2)}) copy-start(bf16[16,2,2,16,128]{4,3,2,1,0:T(8,128)(2,1)} %get-tuple-element.34) | copy-start | bytes 786436
  12.1 28.8 %all-to-all-start.1 = ((bf16[16,4,2,3,16,128]{5,4,3,2,1,0:T(8,128)(2,1)}), bf16[16,4,2,3,16,128]{5,4,3,2,1,0:T(8,128)(2,1)S(1)}, u32[]{:S(2)}, u32[]{:S(2)}) async-start(bf16[16,4,2,3,16,128]{5,4,3,2,1,0:T(8,128)(2,1)} %get-tuple-element.36), calls=%async_computation.1 | async-start | bytes 3145728 | tf_op jit(solution)/shard_map/all_to_all | solution.py:419
  19.0 15.6 %collective-permute-start.2 = (bf16[16,2,2,16,128]{4,3,2,1,0:T(8,128)(2,1)S(1)}, bf16[16,2,2,16,128]{4,3,2,1,0:T(8,128)(2,1)S(1)}, u32[]{:S(2)}, u32[]{:S(2)}) collective-permute-start(bf16[16,2,2,16,128]{4,3,2,1,0:T(8,128)(2,1)S(1)} %copy-done.3), channel_id=1, source_target_pairs={{0,2},{1,3},{2,64},{3,65},{4,6},{5,7},{6,68},{7,69},{8,10},{9,11},... | collective-permute-start | bytes 786440 | tf_op jit(solution)/shard_map/ppermute | solution.py:54
  19.9 16.5 %collective-permute-start.3 = (bf16[16,2,2,16,128]{4,3,2,1,0:T(8,128)(2,1)S(1)}, bf16[16,2,2,16,128]{4,3,2,1,0:T(8,128)(2,1)S(1)}, u32[]{:S(2)}, u32[]{:S(2)}) collective-permute-start(bf16[16,2,2,16,128]{4,3,2,1,0:T(8,128)(2,1)S(1)} %copy-done.2), channel_id=1, source_target_pairs={{0,194},{1,195},{2,0},{3,1},{4,198},{5,199},{6,4},{7,5},{8,202},{9... | collective-permute-start | bytes 786440 | tf_op jit(solution)/shard_map/ppermute | solution.py:54
  42.3 12.8 %collective-permute-start.4 = (bf16[16,2,3,16,128]{4,3,2,1,0:T(8,128)(2,1)}, bf16[16,2,3,16,128]{4,3,2,1,0:T(8,128)(2,1)S(1)}, u32[]{:S(2)}, u32[]{:S(2)}) collective-permute-start(bf16[16,2,3,16,128]{4,3,2,1,0:T(8,128)(2,1)} %get-tuple-element.38), channel_id=1, source_target_pairs={{0,2},{1,3},{2,64},{3,65},{4,6},{5,7},{6,68},{7,69},{8,10},{9,11},... | collective-permute-start | bytes 1179656 | tf_op jit(solution)/shard_map/ppermute | solution.py:54
  43.0 12.0 %collective-permute-start.5 = (bf16[16,2,3,16,128]{4,3,2,1,0:T(8,128)(2,1)S(1)}, bf16[16,2,3,16,128]{4,3,2,1,0:T(8,128)(2,1)S(1)}, u32[]{:S(2)}, u32[]{:S(2)}) collective-permute-start(bf16[16,2,3,16,128]{4,3,2,1,0:T(8,128)(2,1)S(1)} %get-tuple-element.39), channel_id=1, source_target_pairs={{0,194},{1,195},{2,0},{3,1},{4,198},{5,199},{6,4},{7,5},{8,202},{9... | collective-permute-start | bytes 1179656 | tf_op jit(solution)/shard_map/ppermute | solution.py:54
  45.0 20.6 %all-to-all-start = ((bf16[16,4,2,2,16,128]{5,4,3,2,1,0:T(8,128)(2,1)}), bf16[16,4,2,2,16,128]{5,4,3,2,1,0:T(8,128)(2,1)S(1)}, u32[]{:S(2)}, u32[]{:S(2)}) async-start(bf16[16,4,2,2,16,128]{5,4,3,2,1,0:T(8,128)(2,1)} %gather.2), calls=%async_computation | async-start | bytes 2097152 | tf_op jit(solution)/shard_map/all_to_all | solution.py:422
  50.5 27.4 %collective-permute-start.6 = (bf16[16,2,3,16,128]{4,3,2,1,0:T(8,128)(2,1)S(1)}, bf16[16,2,3,16,128]{4,3,2,1,0:T(8,128)(2,1)S(1)}, u32[]{:S(2)}, u32[]{:S(2)}) collective-permute-start(bf16[16,2,3,16,128]{4,3,2,1,0:T(8,128)(2,1)S(1)} %get-tuple-element.41), channel_id=1, source_target_pairs={{0,66},{1,67},{2,128},{3,129},{4,70},{5,71},{6,132},{7,133},{8,74}... | collective-permute-start | bytes 1179656 | tf_op jit(solution)/shard_map/ppermute | solution.py:54
  52.9 25.0 %collective-permute-start.7 = (bf16[16,2,3,16,128]{4,3,2,1,0:T(8,128)(2,1)S(1)}, bf16[16,2,3,16,128]{4,3,2,1,0:T(8,128)(2,1)}, u32[]{:S(2)}, u32[]{:S(2)}) collective-permute-start(bf16[16,2,3,16,128]{4,3,2,1,0:T(8,128)(2,1)S(1)} %get-tuple-element.44), channel_id=1, source_target_pairs={{0,130},{1,131},{2,192},{3,193},{4,134},{5,135},{6,196},{7,197},{8... | collective-permute-start | bytes 1179656 | tf_op jit(solution)/shard_map/ppermute | solution.py:54
  72.2 23.6 %all-to-all-start.3 = ((bf16[16,4,2,16,128]{4,3,2,1,0:T(8,128)(2,1)}), bf16[16,4,2,16,128]{4,3,2,1,0:T(8,128)(2,1)S(1)}, u32[]{:S(2)}, u32[]{:S(2)}) async-start(bf16[16,4,2,16,128]{4,3,2,1,0:T(8,128)(2,1)} %correlate.2), calls=%async_computation.3 | async-start | bytes 1048576 | tf_op jit(solution)/shard_map/all_to_all | solution.py:429
  85.8 18.6 %collective-permute-start.8 = (bf16[16,3,16,128]{3,2,1,0:T(8,128)(2,1)S(1)}, bf16[16,3,16,128]{3,2,1,0:T(8,128)(2,1)S(1)}, u32[]{:S(2)}, u32[]{:S(2)}) collective-permute-start(bf16[16,3,16,128]{3,2,1,0:T(8,128)(2,1)S(1)} %get-tuple-element.45), channel_id=1, source_target_pairs={{0,66},{1,67},{2,128},{3,129},{4,70},{5,71},{6,132},{7,133},{8,74}... | collective-permute-start | bytes 589832 | tf_op jit(solution)/shard_map/ppermute | solution.py:54
  93.1 11.3 %collective-permute-start.9 = (bf16[16,3,16,128]{3,2,1,0:T(8,128)(2,1)S(1)}, bf16[16,3,16,128]{3,2,1,0:T(8,128)(2,1)S(1)}, u32[]{:S(2)}, u32[]{:S(2)}) collective-permute-start(bf16[16,3,16,128]{3,2,1,0:T(8,128)(2,1)S(1)} %get-tuple-element.46), channel_id=1, source_target_pairs={{0,130},{1,131},{2,192},{3,193},{4,134},{5,135},{6,196},{7,197},{8... | collective-permute-start | bytes 589832 | tf_op jit(solution)/shard_map/ppermute | solution.py:54
  93.1 19.5 %collective-permute-start.10 = (bf16[16,3,16,128]{3,2,1,0:T(8,128)(2,1)S(1)}, bf16[16,3,16,128]{3,2,1,0:T(8,128)(2,1)S(1)}, u32[]{:S(2)}, u32[]{:S(2)}) collective-permute-start(bf16[16,3,16,128]{3,2,1,0:T(8,128)(2,1)S(1)} %get-tuple-element.47), channel_id=1, source_target_pairs={{0,2},{1,3},{2,64},{3,65},{4,6},{5,7},{6,68},{7,69},{8,10},{9,11},... | collective-permute-start | bytes 589832 | tf_op jit(solution)/shard_map/ppermute | solution.py:54
  95.6 18.4 %collective-permute-start.11 = (bf16[16,3,16,128]{3,2,1,0:T(8,128)(2,1)S(1)}, bf16[16,3,16,128]{3,2,1,0:T(8,128)(2,1)S(1)}, u32[]{:S(2)}, u32[]{:S(2)}) collective-permute-start(bf16[16,3,16,128]{3,2,1,0:T(8,128)(2,1)S(1)} %get-tuple-element.48), channel_id=1, source_target_pairs={{0,194},{1,195},{2,0},{3,1},{4,198},{5,199},{6,4},{7,5},{8,202},{9... | collective-permute-start | bytes 589832 | tf_op jit(solution)/shard_map/ppermute | solution.py:54
  95.9 26.0 %collective-permute-start.15 = (bf16[16,2,16,128]{3,2,1,0:T(8,128)(2,1)S(1)}, bf16[16,2,16,128]{3,2,1,0:T(8,128)(2,1)S(1)}, u32[]{:S(2)}, u32[]{:S(2)}) collective-permute-start(bf16[16,2,16,128]{3,2,1,0:T(8,128)(2,1)S(1)} %get-tuple-element.55), channel_id=1, source_target_pairs={{0,66},{1,67},{2,128},{3,129},{4,70},{5,71},{6,132},{7,133},{8,74}... | collective-permute-start | bytes 393224 | tf_op jit(solution)/shard_map/ppermute | solution.py:54
  104.4 17.4 %collective-permute-start.14 = (bf16[16,2,16,128]{3,2,1,0:T(8,128)(2,1)S(1)}, bf16[16,2,16,128]{3,2,1,0:T(8,128)(2,1)S(1)}, u32[]{:S(2)}, u32[]{:S(2)}) collective-permute-start(bf16[16,2,16,128]{3,2,1,0:T(8,128)(2,1)S(1)} %get-tuple-element.56), channel_id=1, source_target_pairs={{0,130},{1,131},{2,192},{3,193},{4,134},{5,135},{6,196},{7,197},{8... | collective-permute-start | bytes 393224 | tf_op jit(solution)/shard_map/ppermute | solution.py:54
  104.4 17.4 %collective-permute-start.13 = (bf16[16,2,16,128]{3,2,1,0:T(8,128)(2,1)S(1)}, bf16[16,2,16,128]{3,2,1,0:T(8,128)(2,1)S(1)}, u32[]{:S(2)}, u32[]{:S(2)}) collective-permute-start(bf16[16,2,16,128]{3,2,1,0:T(8,128)(2,1)S(1)} %get-tuple-element.57), channel_id=1, source_target_pairs={{0,2},{1,3},{2,64},{3,65},{4,6},{5,7},{6,68},{7,69},{8,10},{9,11},... | collective-permute-start | bytes 393224 | tf_op jit(solution)/shard_map/ppermute | solution.py:54
  112.7 9.2 %collective-permute-start.12 = (bf16[16,2,16,128]{3,2,1,0:T(8,128)(2,1)S(1)}, bf16[16,2,16,128]{3,2,1,0:T(8,128)(2,1)S(1)}, u32[]{:S(2)}, u32[]{:S(2)}) collective-permute-start(bf16[16,2,16,128]{3,2,1,0:T(8,128)(2,1)S(1)} %get-tuple-element.58), channel_id=1, source_target_pairs={{0,194},{1,195},{2,0},{3,1},{4,198},{5,199},{6,4},{7,5},{8,202},{9... | collective-permute-start | bytes 393224 | tf_op jit(solution)/shard_map/ppermute | solution.py:54
  115.0 17.3 %all-to-all-start.2 = ((bf16[16,4,3,16,128]{4,3,2,1,0:T(8,128)(2,1)}), bf16[16,4,3,16,128]{4,3,2,1,0:T(8,128)(2,1)S(1)}, u32[]{:S(2)}, u32[]{:S(2)}) async-start(bf16[16,4,3,16,128]{4,3,2,1,0:T(8,128)(2,1)} %gather.3), calls=%async_computation.2 | async-start | bytes 1572864 | tf_op jit(solution)/shard_map/all_to_all | solution.py:432
  121.8 9.7 %copy-start.1 = (bf16[1,64,192]{2,1,0:T(8,128)(2,1)S(1)}, bf16[1,64,192]{2,1,0:T(8,128)(2,1)}, u32[]{:S(2)}) copy-start(bf16[1,64,192]{2,1,0:T(8,128)(2,1)} %param.8) | copy-start | bytes 73732
  121.8 31.2 %copy-start = (s32[4,5]{1,0:T(4,128)S(1)}, s32[4,5]{1,0:T(4,128)}, u32[]{:S(2)}) copy-start(s32[4,5]{1,0:T(4,128)} %pattern_ref.3) | copy-start | bytes 244
  122.2 14.6 %collective-permute-start.17 = (bf16[16,2,64,128]{3,2,1,0:T(8,128)(2,1)S(1)}, bf16[16,2,64,128]{3,2,1,0:T(8,128)(2,1)S(1)}, u32[]{:S(2)}, u32[]{:S(2)}) collective-permute-start(bf16[16,2,64,128]{3,2,1,0:T(8,128)(2,1)S(1)} %settle.2.refs_3_), channel_id=1, source_target_pairs={{1,0},{2,1},{3,2},{5,4},{6,5},{7,6},{9,8},{10,9},{11,10},{13,12},{... | collective-permute-start | bytes 1572872 | tf_op jit(solution)/shard_map/ppermute | solution.py:435
  128.4 9.2 %collective-permute-start.16 = (bf16[16,2,64,128]{3,2,1,0:T(8,128)(2,1)S(1)}, bf16[16,2,64,128]{3,2,1,0:T(8,128)(2,1)S(1)}, u32[]{:S(2)}, u32[]{:S(2)}) collective-permute-start(bf16[16,2,64,128]{3,2,1,0:T(8,128)(2,1)S(1)} %settle.2.refs_3_), channel_id=1, source_target_pairs={{0,1},{1,2},{2,3},{4,5},{5,6},{6,7},{8,9},{9,10},{10,11},{12,13},{... | collective-permute-start | bytes 1572872 | tf_op jit(solution)/shard_map/ppermute | solution.py:435
  137.6 11.0 %collective-permute-start.18 = (bf16[16,2,64,128]{3,2,1,0:T(8,128)(2,1)}, bf16[16,2,64,128]{3,2,1,0:T(8,128)(2,1)S(1)}, u32[]{:S(2)}, u32[]{:S(2)}) collective-permute-start(bf16[16,2,64,128]{3,2,1,0:T(8,128)(2,1)} %get-tuple-element.52), channel_id=1, source_target_pairs={{0,1},{1,2},{2,3},{4,5},{5,6},{6,7},{8,9},{9,10},{10,11},{12,13},{... | collective-permute-start | bytes 1572872 | tf_op jit(solution)/shard_map/ppermute | solution.py:437
  142.2 10.8 %collective-permute-start.19 = (bf16[16,2,64,128]{3,2,1,0:T(8,128)(2,1)}, bf16[16,2,64,128]{3,2,1,0:T(8,128)(2,1)}, u32[]{:S(2)}, u32[]{:S(2)}) collective-permute-start(bf16[16,2,64,128]{3,2,1,0:T(8,128)(2,1)} %get-tuple-element.54), channel_id=1, source_target_pairs={{1,0},{2,1},{3,2},{5,4},{6,5},{7,6},{9,8},{10,9},{11,10},{13,12},{... | collective-permute-start | bytes 1572872 | tf_op jit(solution)/shard_map/ppermute | solution.py:437

commit v10 on v8

--- a/solution.py
+++ b/solution.py
@@ -308,16 +308,19 @@
     @pl.when(pl.program_id(0) == 0)
     def _():
         row = row_ref[0]
-        for d in range(3):
+        for d in (1, 0, 2):
             k = row + d - 1
             inside = jnp.logical_and(k >= 0, k < rows)
             k = jnp.clip(k, 0, rows - 1)
             places = [place_of(pattern_ref, k, t) for t in range(slots)]
             for s in range(slots):
-                want = pattern_ref[row, s]
                 at = jnp.int32(-1)
                 for t in range(slots):
-                    at = jnp.where(jnp.logical_and(inside, pattern_ref[k, t] == want), places[t], at)
+                    if d == 1:
+                        at = jnp.where(places[t] == s, t, at)
+                    else:
+                        same = pattern_ref[k, t] == pattern_ref[row, at_ref[1, s]]
+                        at = jnp.where(jnp.logical_and(inside, same), places[t], at)
                 at_ref[d, s] = at
 
     w = w_ref[...]
@@ -326,15 +329,18 @@
         for s in range(slots):
             blocks = []
             for d, (low, high) in enumerate(pairs):
+                if d == 1:
+                    blocks.append(low[l, s] if s < CUT else high[l, s - CUT])
+                    continue
                 at = at_ref[d, s]
                 one = low[l, jnp.clip(at - 1 if d == 0 else at, 0, low.shape[1] - 1)]
                 two = high[l, jnp.clip(at - CUT, 0, high.shape[1] - 1)]
                 got = jnp.where(at < CUT, one, two)
-                blocks.append(got if d == 1 else jnp.where(at >= 0, got, jnp.zeros_like(got)))
+                blocks.append(jnp.where(at >= 0, got, jnp.zeros_like(got)))
             cols.append(jnp.concatenate(blocks, 0))
         res = jnp.dot(w, jnp.concatenate(cols, 1), preferred_element_type=jnp.float32)
         for s in range(slots):
-            out_ref[l, s] = res[:, s * 128 : (s + 1) * 128].astype(jnp.bfloat16)
+            out_ref[l, at_ref[1, s]] = res[:, s * 128 : (s + 1) * 128].astype(jnp.bfloat16)
 
 
 def screen(row, pattern, weights, up, own, down):

time: 156 us -> 156 us (level)
  no operation moved by 1% of the time
where the time goes in v10:
time: 156 us; the launch traced here: 155 us
  waiting for transfers between devices  66.5 us (43%)
  starting transfers between devices  57.9 us (37%)
  Pallas kernels  27.1 us (17%)
  local copies, waits for them, and re-layouts  2.67 us (2%)
    ppermute x16, waiting for transfers between devices, hop(): return lax.ppermute(piece, ALL, perm)  38.2 us
    ppermute x16, starting transfers between devices, hop(): return lax.ppermute(piece, ALL, perm)  23.1 us
    pallas_call x2, Pallas kernels, correlate(): pl.pallas_call(functools.partial(correlate_kernel, slots, len(inputs), sp...  14.5 us
    all_to_all x1, waiting for transfers between devices, shards(): late = lax.all_to_all(late, PLANE, split_axis=0, concat_axis=0, tiled=True)  11.8 us
    all_to_all x1, starting transfers between devices, shards(): lax.all_to_all(early, PLANE, split_axis=0, concat_axis=0, tiled=True)  6.93 us
    all_to_all x1, starting transfers between devices, shards(): late = lax.all_to_all(late, PLANE, split_axis=0, concat_axis=0, tiled=True)  6.23 us
    all_to_all x1, starting transfers between devices, shards(): lo = lax.all_to_all(lo, PLANE, split_axis=0, concat_axis=0, tiled=True)  5.26 us
    pallas_call x1, Pallas kernels, prepare(): pl.pallas_call(functools.partial(prepare_kernel, cut), out_shape=[jax.Sha...  4.64 us
  transfers between devices with their start and end apart: 24, of which 17 were waited for; matrix products, arithmetic and copies ran while one was open for 0% of the time, Pallas kernels for 12%

profile of v10, /device:TPU:1, one launch (start us, length us, event | category | flops | bytes accessed | tf_op | source)
XLA Modules:
  0.0 154.8 jit_solution(9312434703162656288)
XLA Ops:
  0.0 4.6 %prepare.1 = (bf16[16,4,2,3,16,128]{5,4,3,2,1,0:T(8,128)(2,1)}, bf16[16,2,2,16,128]{4,3,2,1,0:T(8,128)(2,1)}, bf16[16,2,2,16,128]{4,3,2,1,0:T(8,128)(2,1)}, bf16...) custom-call(s32[1]{0:T(128)} %bitcast.6.turn_ref, s32[1]{0:T(128)} %bitcast.row_ref, s32[4,5]{1,0:T(4,128)} %pattern_ref.3, ...), custom_call_target="tpu_custom_call" | custom-call | bytes 5242880 | tf_op jit(solution)/shard_map/prepare/pallas_call | solution.py:221
  4.6 5.3 %collective-permute-start = (bf16[16,2,2,16,128]{4,3,2,1,0:T(8,128)(2,1)}, bf16[16,2,2,16,128]{4,3,2,1,0:T(8,128)(2,1)S(1)}, u32[]{:S(2)}, u32[]{:S(2)}) collective-permute-start(bf16[16,2,2,16,128]{4,3,2,1,0:T(8,128)(2,1)} %get-tuple-element.26), channel_id=1, source_target_pairs={{0,66},{1,67},{2,128},{3,129},{4,70},{5,71},{6,132},{7,133},{8,74}... | collective-permute-start | bytes 786440 | tf_op jit(solution)/shard_map/ppermute | solution.py:54
  9.9 2.2 %collective-permute-start.1 = (bf16[16,2,2,16,128]{4,3,2,1,0:T(8,128)(2,1)}, bf16[16,2,2,16,128]{4,3,2,1,0:T(8,128)(2,1)S(1)}, u32[]{:S(2)}, u32[]{:S(2)}) collective-permute-start(bf16[16,2,2,16,128]{4,3,2,1,0:T(8,128)(2,1)} %get-tuple-element.27), channel_id=1, source_target_pairs={{0,130},{1,131},{2,192},{3,193},{4,134},{5,135},{6,196},{7,197},{8... | collective-permute-start | bytes 786440 | tf_op jit(solution)/shard_map/ppermute | solution.py:54
  12.1 6.9 %all-to-all-start.1 = ((bf16[16,4,2,3,16,128]{5,4,3,2,1,0:T(8,128)(2,1)}), bf16[16,4,2,3,16,128]{5,4,3,2,1,0:T(8,128)(2,1)}, u32[]{:S(2)}, u32[]{:S(2)}) async-start(bf16[16,4,2,3,16,128]{5,4,3,2,1,0:T(8,128)(2,1)} %get-tuple-element.32), calls=%async_computation.1 | async-start | bytes 3145728 | tf_op jit(solution)/shard_map/all_to_all | solution.py:398
  19.1 0.8 collective-permute-start.2
  19.9 1.9 %collective-permute-start.3 = (bf16[16,2,2,16,128]{4,3,2,1,0:T(8,128)(2,1)S(1)}, bf16[16,2,2,16,128]{4,3,2,1,0:T(8,128)(2,1)S(1)}, u32[]{:S(2)}, u32[]{:S(2)}) collective-permute-start(bf16[16,2,2,16,128]{4,3,2,1,0:T(8,128)(2,1)S(1)} %copy-done.2), channel_id=1, source_target_pairs={{0,194},{1,195},{2,0},{3,1},{4,198},{5,199},{6,4},{7,5},{8,202},{9... | collective-permute-start | bytes 786440 | tf_op jit(solution)/shard_map/ppermute | solution.py:54
  21.8 0.1 pad_maximum_fusion.refs_0_
  21.9 4.3 %collective-permute-done.refs_1_.refs_0_ = bf16[16,2,2,16,128]{4,3,2,1,0:T(8,128)(2,1)S(1)} collective-permute-done((bf16[16,2,2,16,128]{4,3,2,1,0:T(8,128)(2,1)}, bf16[16,2,2,16,128]{4,3,2,1,0:T(8,128)(2,1)S(1)}, u32[]{:S(2)}, u32[]{:S(2)}) %collective-permute-start) | collective-permute-done | bytes 262176 | tf_op jit(solution)/shard_map/ppermute | solution.py:54
  26.2 0.0 collective-permute-done.1.refs_2_.refs_1_
  26.2 8.6 %collective-permute-done.2.refs_2_ = bf16[16,2,2,16,128]{4,3,2,1,0:T(8,128)(2,1)S(1)} collective-permute-done((bf16[16,2,2,16,128]{4,3,2,1,0:T(8,128)(2,1)S(1)}, bf16[16,2,2,16,128]{4,3,2,1,0:T(8,128)(2,1)S(1)}, u32[]{:S(2)}, u32[]{:S(2)}) %collective-permute-start.2) | collective-permute-done | bytes 262176 | tf_op jit(solution)/shard_map/ppermute | solution.py:54
  34.7 1.7 %collective-permute-done.3.refs_3_ = bf16[16,2,2,16,128]{4,3,2,1,0:T(8,128)(2,1)S(1)} collective-permute-done((bf16[16,2,2,16,128]{4,3,2,1,0:T(8,128)(2,1)S(1)}, bf16[16,2,2,16,128]{4,3,2,1,0:T(8,128)(2,1)S(1)}, u32[]{:S(2)}, u32[]{:S(2)}) %collective-permute-start.3) | collective-permute-done | bytes 262176 | tf_op jit(solution)/shard_map/ppermute | solution.py:54
  36.4 1.0 gather.2
  37.4 3.6 %all-to-all-done.1 = bf16[16,4,2,3,16,128]{5,4,3,2,1,0:T(8,128)(2,1)} async-done(((bf16[16,4,2,3,16,128]{5,4,3,2,1,0:T(8,128)(2,1)}), bf16[16,4,2,3,16,128]{5,4,3,2,1,0:T(8,128)(2,1)}, u32[]{:S(2)}, u32[]{:S(2)}) %all-to-all-start.1) | async-done | bytes 1572896 | tf_op jit(solution)/shard_map/all_to_all | solution.py:398
  41.0 2.4 %slice_bitcast_fusion = (bf16[16,2,3,16,128]{4,3,2,1,0:T(8,128)(2,1)S(1)}, bf16[16,2,3,16,128]{4,3,2,1,0:T(8,128)(2,1)}, bf16[16,2,3,16,128]{4,3,2,1,0:T(8,128)(2,1)S(1)}, bf16[16,2,3,16,128]{4,3,2,1,0:T(8,128)(2,1)S(1)}) fusion(bf16[16,4,2,3,16,128]{5,4,3,2,1,0:T(8,128)(2,1)} %all-to-all-done.1), kind=kLoop, calls=%fused_computation.2 | loop fusion | bytes 3145728 | tf_op jit(solution)/shard_map/squeeze | solution.py:400
  43.4 1.4 collective-permute-start.5
  44.8 0.0 collective-permute-start.4
  44.9 6.2 %all-to-all-start = ((bf16[16,4,2,2,16,128]{5,4,3,2,1,0:T(8,128)(2,1)}), bf16[16,4,2,2,16,128]{5,4,3,2,1,0:T(8,128)(2,1)S(1)}, u32[]{:S(2)}, u32[]{:S(2)}) async-start(bf16[16,4,2,2,16,128]{5,4,3,2,1,0:T(8,128)(2,1)} %gather.2), calls=%async_computation | async-start | bytes 2097152 | tf_op jit(solution)/shard_map/all_to_all | solution.py:401
  51.1 3.6 %collective-permute-start.7 = (bf16[16,2,3,16,128]{4,3,2,1,0:T(8,128)(2,1)S(1)}, bf16[16,2,3,16,128]{4,3,2,1,0:T(8,128)(2,1)}, u32[]{:S(2)}, u32[]{:S(2)}) collective-permute-start(bf16[16,2,3,16,128]{4,3,2,1,0:T(8,128)(2,1)S(1)} %get-tuple-element.47), channel_id=1, source_target_pairs={{0,130},{1,131},{2,192},{3,193},{4,134},{5,135},{6,196},{7,197},{8... | collective-permute-start | bytes 1179656 | tf_op jit(solution)/shard_map/ppermute | solution.py:54
  54.8 0.0 collective-permute-start.6
  54.8 0.0 collective-permute-done.5.refs_2_
  54.8 0.0 collective-permute-done.4.refs_1_
  54.8 11.8 %all-to-all-done.refs_0_ = bf16[16,4,2,2,16,128]{5,4,3,2,1,0:T(8,128)(2,1)S(1)} async-done(((bf16[16,4,2,2,16,128]{5,4,3,2,1,0:T(8,128)(2,1)}), bf16[16,4,2,2,16,128]{5,4,3,2,1,0:T(8,128)(2,1)S(1)}, u32[]{:S(2)}, u32[]{:S(2)}) %all-to-all-start) | async-done | bytes 1048608 | tf_op jit(solution)/shard_map/all_to_all | solution.py:401
  66.5 6.6 %correlate.2 = bf16[16,4,2,16,128]{4,3,2,1,0:T(8,128)(2,1)} custom-call(f32[3]{0:T(128)S(1)} %marker.3.rot_ref, bf16[16,4,2,2,16,128]{5,4,3,2,1,0:T(8,128)(2,1)S(1)} %all-to-all-done.refs_0_, bf16[4,512,256]{2,1,0:T(8,128)(2,1)} %constant.87.clone.refs_1_.refs_4_, bf16[4,512,256]{2,1,0:T(8,128)(2,1)} %constant.88.clone.refs_2_.refs_5_), custom_call_target="tpu_custom_call" | custom-call | bytes 3670016 | tf_op jit(solution)/shard_map/correlate/pallas_call | solution.py:140
  73.1 4.5 %all-to-all-start.3 = ((bf16[16,4,2,16,128]{4,3,2,1,0:T(8,128)(2,1)}), bf16[16,4,2,16,128]{4,3,2,1,0:T(8,128)(2,1)S(1)}, u32[]{:S(2)}, u32[]{:S(2)}) async-start(bf16[16,4,2,16,128]{4,3,2,1,0:T(8,128)(2,1)} %correlate.2), calls=%async_computation.3 | async-start | bytes 1048576 | tf_op jit(solution)/shard_map/all_to_all | solution.py:408
  77.7 6.3 %collective-permute-done.6.refs_0_ = bf16[16,2,3,16,128]{4,3,2,1,0:T(8,128)(2,1)S(1)} collective-permute-done((bf16[16,2,3,16,128]{4,3,2,1,0:T(8,128)(2,1)}, bf16[16,2,3,16,128]{4,3,2,1,0:T(8,128)(2,1)S(1)}, u32[]{:S(2)}, u32[]{:S(2)}) %collective-permute-start.6) | collective-permute-done | bytes 393248 | tf_op jit(solution)/shard_map/ppermute | solution.py:54
  84.0 0.0 collective-permute-done.7.refs_3_
  84.0 7.9 %correlate.3 = (bf16[16,3,16,128]{3,2,1,0:T(8,128)(2,1)S(1)}, bf16[16,3,16,128]{3,2,1,0:T(8,128)(2,1)S(1)}, bf16[16,3,16,128]{3,2,1,0:T(8,128)(2,1)S(1)}, bf16[16,3,16,128]{3,2,1,0:T(8,128)(2,1)S(1)}) custom-call(f32[3]{0:T(128)S(1)} %marker.3.rot_ref, bf16[16,2,3,16,128]{4,3,2,1,0:T(8,128)(2,1)S(1)} %collective-permute-done.6.refs_0_, ...), custom_call_target="tpu_custom_call" | custom-call | flops 99999997952 | bytes 4456448 | tf_op jit(solution)/shard_map/correlate/pallas_call | solution.py:140
  91.9 0.1 collective-permute-start.8
  91.9 4.5 %collective-permute-start.9 = (bf16[16,3,16,128]{3,2,1,0:T(8,128)(2,1)S(1)}, bf16[16,3,16,128]{3,2,1,0:T(8,128)(2,1)S(1)}, u32[]{:S(2)}, u32[]{:S(2)}) collective-permute-start(bf16[16,3,16,128]{3,2,1,0:T(8,128)(2,1)S(1)} %get-tuple-element.38), channel_id=1, source_target_pairs={{0,130},{1,131},{2,192},{3,193},{4,134},{5,135},{6,196},{7,197},{8... | collective-permute-start | bytes 589832 | tf_op jit(solution)/shard_map/ppermute | solution.py:54
  96.4 0.0 collective-permute-start.10
  96.4 2.7 %collective-permute-start.11 = (bf16[16,3,16,128]{3,2,1,0:T(8,128)(2,1)S(1)}, bf16[16,3,16,128]{3,2,1,0:T(8,128)(2,1)S(1)}, u32[]{:S(2)}, u32[]{:S(2)}) collective-permute-start(bf16[16,3,16,128]{3,2,1,0:T(8,128)(2,1)S(1)} %get-tuple-element.40), channel_id=1, source_target_pairs={{0,194},{1,195},{2,0},{3,1},{4,198},{5,199},{6,4},{7,5},{8,202},{9... | collective-permute-start | bytes 589832 | tf_op jit(solution)/shard_map/ppermute | solution.py:54
  99.1 0.0 all-to-all-done.3
  99.1 0.1 collective-permute-start.15
  99.2 6.1 %collective-permute-done.8.refs_0_ = bf16[16,3,16,128]{3,2,1,0:T(8,128)(2,1)S(1)} collective-permute-done((bf16[16,3,16,128]{3,2,1,0:T(8,128)(2,1)S(1)}, bf16[16,3,16,128]{3,2,1,0:T(8,128)(2,1)S(1)}, u32[]{:S(2)}, u32[]{:S(2)}) %collective-permute-start.8) | collective-permute-done | bytes 196640 | tf_op jit(solution)/shard_map/ppermute | solution.py:54
  105.4 0.4 collective-permute-start.14
  105.8 1.0 collective-permute-done.9.refs_1_
  106.8 0.0 collective-permute-start.13
  106.8 4.0 %collective-permute-done.10.refs_2_ = bf16[16,3,16,128]{3,2,1,0:T(8,128)(2,1)S(1)} collective-permute-done((bf16[16,3,16,128]{3,2,1,0:T(8,128)(2,1)S(1)}, bf16[16,3,16,128]{3,2,1,0:T(8,128)(2,1)S(1)}, u32[]{:S(2)}, u32[]{:S(2)}) %collective-permute-start.10) | collective-permute-done | bytes 196640 | tf_op jit(solution)/shard_map/ppermute | solution.py:54
  110.8 0.0 collective-permute-start.12
  110.8 2.1 %collective-permute-done.11.refs_3_ = bf16[16,3,16,128]{3,2,1,0:T(8,128)(2,1)S(1)} collective-permute-done((bf16[16,3,16,128]{3,2,1,0:T(8,128)(2,1)S(1)}, bf16[16,3,16,128]{3,2,1,0:T(8,128)(2,1)S(1)}, u32[]{:S(2)}, u32[]{:S(2)}) %collective-permute-start.11) | collective-permute-done | bytes 196640 | tf_op jit(solution)/shard_map/ppermute | solution.py:54
  112.9 0.9 gather.3
  113.8 5.3 %all-to-all-start.2 = ((bf16[16,4,3,16,128]{4,3,2,1,0:T(8,128)(2,1)}), bf16[16,4,3,16,128]{4,3,2,1,0:T(8,128)(2,1)S(1)}, u32[]{:S(2)}, u32[]{:S(2)}) async-start(bf16[16,4,3,16,128]{4,3,2,1,0:T(8,128)(2,1)} %gather.3), calls=%async_computation.2 | async-start | bytes 1572864 | tf_op jit(solution)/shard_map/all_to_all | solution.py:411
  119.1 0.0 copy-start.1
  119.1 0.0 copy-start
  119.1 0.0 collective-permute-done.15.refs_3_
  119.1 0.0 collective-permute-done.14.refs_2_
  119.1 2.2 %collective-permute-done.13.refs_1_ = bf16[16,2,16,128]{3,2,1,0:T(8,128)(2,1)S(1)} collective-permute-done((bf16[16,2,16,128]{3,2,1,0:T(8,128)(2,1)S(1)}, bf16[16,2,16,128]{3,2,1,0:T(8,128)(2,1)S(1)}, u32[]{:S(2)}, u32[]{:S(2)}) %collective-permute-start.13) | collective-permute-done | bytes 131104 | tf_op jit(solution)/shard_map/ppermute | solution.py:54
  121.3 2.0 %collective-permute-done.12.refs_0_ = bf16[16,2,16,128]{3,2,1,0:T(8,128)(2,1)S(1)} collective-permute-done((bf16[16,2,16,128]{3,2,1,0:T(8,128)(2,1)S(1)}, bf16[16,2,16,128]{3,2,1,0:T(8,128)(2,1)S(1)}, u32[]{:S(2)}, u32[]{:S(2)}) %collective-permute-start.12) | collective-permute-done | bytes 131104 | tf_op jit(solution)/shard_map/ppermute | solution.py:54
  123.3 0.3 settle.2.refs_3_
  123.6 3.1 %collective-permute-start.17 = (bf16[16,2,64,128]{3,2,1,0:T(8,128)(2,1)S(1)}, bf16[16,2,64,128]{3,2,1,0:T(8,128)(2,1)S(1)}, u32[]{:S(2)}, u32[]{:S(2)}) collective-permute-start(bf16[16,2,64,128]{3,2,1,0:T(8,128)(2,1)S(1)} %settle.2.refs_3_), channel_id=1, source_target_pairs={{1,0},{2,1},{3,2},{5,4},{6,5},{7,6},{9,8},{10,9},{11,10},{13,12},{... | collective-permute-start | bytes 1572872 | tf_op jit(solution)/shard_map/ppermute | solution.py:414
  126.8 2.4 %collective-permute-start.16 = (bf16[16,2,64,128]{3,2,1,0:T(8,128)(2,1)S(1)}, bf16[16,2,64,128]{3,2,1,0:T(8,128)(2,1)S(1)}, u32[]{:S(2)}, u32[]{:S(2)}) collective-permute-start(bf16[16,2,64,128]{3,2,1,0:T(8,128)(2,1)S(1)} %settle.2.refs_3_), channel_id=1, source_target_pairs={{0,1},{1,2},{2,3},{4,5},{5,6},{6,7},{8,9},{9,10},{10,11},{12,13},{... | collective-permute-start | bytes 1572872 | tf_op jit(solution)/shard_map/ppermute | solution.py:414
  129.2 0.1 copy.19
  129.3 0.3 all-to-all-done.2.refs_0_
  129.6 1.4 settle.3
  131.0 3.4 %collective-permute-done.17.refs_5_ = bf16[16,2,64,128]{3,2,1,0:T(8,128)(2,1)S(1)} collective-permute-done((bf16[16,2,64,128]{3,2,1,0:T(8,128)(2,1)S(1)}, bf16[16,2,64,128]{3,2,1,0:T(8,128)(2,1)S(1)}, u32[]{:S(2)}, u32[]{:S(2)}) %collective-permute-start.17) | collective-permute-done | bytes 524320 | tf_op jit(solution)/shard_map/ppermute | solution.py:414
  134.4 0.9 collective-permute-done.16.refs_1_
  135.3 4.4 %collective-permute-start.18 = (bf16[16,2,64,128]{3,2,1,0:T(8,128)(2,1)}, bf16[16,2,64,128]{3,2,1,0:T(8,128)(2,1)S(1)}, u32[]{:S(2)}, u32[]{:S(2)}) collective-permute-start(bf16[16,2,64,128]{3,2,1,0:T(8,128)(2,1)} %get-tuple-element.44), channel_id=1, source_target_pairs={{0,1},{1,2},{2,3},{4,5},{5,6},{6,7},{8,9},{9,10},{10,11},{12,13},{... | collective-permute-start | bytes 1572872 | tf_op jit(solution)/shard_map/ppermute | solution.py:416
  139.7 1.9 %collective-permute-start.19 = (bf16[16,2,64,128]{3,2,1,0:T(8,128)(2,1)}, bf16[16,2,64,128]{3,2,1,0:T(8,128)(2,1)}, u32[]{:S(2)}, u32[]{:S(2)}) collective-permute-start(bf16[16,2,64,128]{3,2,1,0:T(8,128)(2,1)} %get-tuple-element.46), channel_id=1, source_target_pairs={{1,0},{2,1},{3,2},{5,4},{6,5},{7,6},{9,8},{10,9},{11,10},{13,12},{... | collective-permute-start | bytes 1572872 | tf_op jit(solution)/shard_map/ppermute | solution.py:416
  141.7 0.1 add_select_fusion
  141.7 0.2 fusion
  142.0 0.1 copy.30.w_ref
  142.1 4.0 %collective-permute-done.18.refs_0_ = bf16[16,2,64,128]{3,2,1,0:T(8,128)(2,1)S(1)} collective-permute-done((bf16[16,2,64,128]{3,2,1,0:T(8,128)(2,1)}, bf16[16,2,64,128]{3,2,1,0:T(8,128)(2,1)S(1)}, u32[]{:S(2)}, u32[]{:S(2)}) %collective-permute-start.18) | collective-permute-done | bytes 524320 | tf_op jit(solution)/shard_map/ppermute | solution.py:416
  146.1 4.4 %collective-permute-done.19.refs_4_ = bf16[16,2,64,128]{3,2,1,0:T(8,128)(2,1)} collective-permute-done((bf16[16,2,64,128]{3,2,1,0:T(8,128)(2,1)}, bf16[16,2,64,128]{3,2,1,0:T(8,128)(2,1)}, u32[]{:S(2)}, u32[]{:S(2)}) %collective-permute-start.19) | collective-permute-done | bytes 524320 | tf_op jit(solution)/shard_map/ppermute | solution.py:416
  150.5 4.3 %screen.1 = bf16[16,5,64,128]{3,2,1,0:T(8,128)(2,1)} custom-call(s32[1]{0:T(128)} %bitcast.row_ref, s32[4,5]{1,0:T(4,128)S(1)} %copy-done, bf16[64,192]{1,0:T(8,128)(2,1)S(1)} %copy.30.w_ref, bf16[16,2,64,128]{3,2,1,0:T(8,128)(2,1)S(1)} %collective-permute-done.18.refs_0_, bf16[16,2,64,128]{3,2,1,0:T(8,128)(2,1)S(1)} %collective-permute-done.16.refs_1_, ...), custom_call_target="tpu_custom_call" | custom-call | flops 251658240 | bytes 5242880 | tf_op jit(solution)/shard_map/screen/pallas_call | solution.py:353
  (11 shorter events, 0.1 us)
Async XLA Ops:
  4.6 21.5 %collective-permute-start = (bf16[16,2,2,16,128]{4,3,2,1,0:T(8,128)(2,1)}, bf16[16,2,2,16,128]{4,3,2,1,0:T(8,128)(2,1)S(1)}, u32[]{:S(2)}, u32[]{:S(2)}) collective-permute-start(bf16[16,2,2,16,128]{4,3,2,1,0:T(8,128)(2,1)} %get-tuple-element.26), channel_id=1, source_target_pairs={{0,66},{1,67},{2,128},{3,129},{4,70},{5,71},{6,132},{7,133},{8,74}... | collective-permute-start | bytes 786440 | tf_op jit(solution)/shard_map/ppermute | solution.py:54
  9.9 16.3 %collective-permute-start.1 = (bf16[16,2,2,16,128]{4,3,2,1,0:T(8,128)(2,1)}, bf16[16,2,2,16,128]{4,3,2,1,0:T(8,128)(2,1)S(1)}, u32[]{:S(2)}, u32[]{:S(2)}) collective-permute-start(bf16[16,2,2,16,128]{4,3,2,1,0:T(8,128)(2,1)} %get-tuple-element.27), channel_id=1, source_target_pairs={{0,130},{1,131},{2,192},{3,193},{4,134},{5,135},{6,196},{7,197},{8... | collective-permute-start | bytes 786440 | tf_op jit(solution)/shard_map/ppermute | solution.py:54
  12.1 6.9 %copy-start.3 = (bf16[16,2,2,16,128]{4,3,2,1,0:T(8,128)(2,1)S(1)}, bf16[16,2,2,16,128]{4,3,2,1,0:T(8,128)(2,1)}, u32[]{:S(2)}) copy-start(bf16[16,2,2,16,128]{4,3,2,1,0:T(8,128)(2,1)} %get-tuple-element.28) | copy-start | bytes 786436
  12.1 7.8 %copy-start.2 = (bf16[16,2,2,16,128]{4,3,2,1,0:T(8,128)(2,1)S(1)}, bf16[16,2,2,16,128]{4,3,2,1,0:T(8,128)(2,1)}, u32[]{:S(2)}) copy-start(bf16[16,2,2,16,128]{4,3,2,1,0:T(8,128)(2,1)} %get-tuple-element.30) | copy-start | bytes 786436
  12.1 28.9 %all-to-all-start.1 = ((bf16[16,4,2,3,16,128]{5,4,3,2,1,0:T(8,128)(2,1)}), bf16[16,4,2,3,16,128]{5,4,3,2,1,0:T(8,128)(2,1)}, u32[]{:S(2)}, u32[]{:S(2)}) async-start(bf16[16,4,2,3,16,128]{5,4,3,2,1,0:T(8,128)(2,1)} %get-tuple-element.32), calls=%async_computation.1 | async-start | bytes 3145728 | tf_op jit(solution)/shard_map/all_to_all | solution.py:398
  19.1 15.7 %collective-permute-start.2 = (bf16[16,2,2,16,128]{4,3,2,1,0:T(8,128)(2,1)S(1)}, bf16[16,2,2,16,128]{4,3,2,1,0:T(8,128)(2,1)S(1)}, u32[]{:S(2)}, u32[]{:S(2)}) collective-permute-start(bf16[16,2,2,16,128]{4,3,2,1,0:T(8,128)(2,1)S(1)} %copy-done.3), channel_id=1, source_target_pairs={{0,2},{1,3},{2,64},{3,65},{4,6},{5,7},{6,68},{7,69},{8,10},{9,11},... | collective-permute-start | bytes 786440 | tf_op jit(solution)/shard_map/ppermute | solution.py:54
  19.9 16.5 %collective-permute-start.3 = (bf16[16,2,2,16,128]{4,3,2,1,0:T(8,128)(2,1)S(1)}, bf16[16,2,2,16,128]{4,3,2,1,0:T(8,128)(2,1)S(1)}, u32[]{:S(2)}, u32[]{:S(2)}) collective-permute-start(bf16[16,2,2,16,128]{4,3,2,1,0:T(8,128)(2,1)S(1)} %copy-done.2), channel_id=1, source_target_pairs={{0,194},{1,195},{2,0},{3,1},{4,198},{5,199},{6,4},{7,5},{8,202},{9... | collective-permute-start | bytes 786440 | tf_op jit(solution)/shard_map/ppermute | solution.py:54
  43.4 11.4 %collective-permute-start.5 = (bf16[16,2,3,16,128]{4,3,2,1,0:T(8,128)(2,1)S(1)}, bf16[16,2,3,16,128]{4,3,2,1,0:T(8,128)(2,1)S(1)}, u32[]{:S(2)}, u32[]{:S(2)}) collective-permute-start(bf16[16,2,3,16,128]{4,3,2,1,0:T(8,128)(2,1)S(1)} %get-tuple-element.49), channel_id=1, source_target_pairs={{0,194},{1,195},{2,0},{3,1},{4,198},{5,199},{6,4},{7,5},{8,202},{9... | collective-permute-start | bytes 1179656 | tf_op jit(solution)/shard_map/ppermute | solution.py:54
  44.8 9.9 %collective-permute-start.4 = (bf16[16,2,3,16,128]{4,3,2,1,0:T(8,128)(2,1)S(1)}, bf16[16,2,3,16,128]{4,3,2,1,0:T(8,128)(2,1)S(1)}, u32[]{:S(2)}, u32[]{:S(2)}) collective-permute-start(bf16[16,2,3,16,128]{4,3,2,1,0:T(8,128)(2,1)S(1)} %get-tuple-element.50), channel_id=1, source_target_pairs={{0,2},{1,3},{2,64},{3,65},{4,6},{5,7},{6,68},{7,69},{8,10},{9,11},... | collective-permute-start | bytes 1179656 | tf_op jit(solution)/shard_map/ppermute | solution.py:54
  44.9 21.7 %all-to-all-start = ((bf16[16,4,2,2,16,128]{5,4,3,2,1,0:T(8,128)(2,1)}), bf16[16,4,2,2,16,128]{5,4,3,2,1,0:T(8,128)(2,1)S(1)}, u32[]{:S(2)}, u32[]{:S(2)}) async-start(bf16[16,4,2,2,16,128]{5,4,3,2,1,0:T(8,128)(2,1)} %gather.2), calls=%async_computation | async-start | bytes 2097152 | tf_op jit(solution)/shard_map/all_to_all | solution.py:401
  51.1 32.9 %collective-permute-start.7 = (bf16[16,2,3,16,128]{4,3,2,1,0:T(8,128)(2,1)S(1)}, bf16[16,2,3,16,128]{4,3,2,1,0:T(8,128)(2,1)}, u32[]{:S(2)}, u32[]{:S(2)}) collective-permute-start(bf16[16,2,3,16,128]{4,3,2,1,0:T(8,128)(2,1)S(1)} %get-tuple-element.47), channel_id=1, source_target_pairs={{0,130},{1,131},{2,192},{3,193},{4,134},{5,135},{6,196},{7,197},{8... | collective-permute-start | bytes 1179656 | tf_op jit(solution)/shard_map/ppermute | solution.py:54
  54.8 29.2 %collective-permute-start.6 = (bf16[16,2,3,16,128]{4,3,2,1,0:T(8,128)(2,1)}, bf16[16,2,3,16,128]{4,3,2,1,0:T(8,128)(2,1)S(1)}, u32[]{:S(2)}, u32[]{:S(2)}) collective-permute-start(bf16[16,2,3,16,128]{4,3,2,1,0:T(8,128)(2,1)} %get-tuple-element.48), channel_id=1, source_target_pairs={{0,66},{1,67},{2,128},{3,129},{4,70},{5,71},{6,132},{7,133},{8,74}... | collective-permute-start | bytes 1179656 | tf_op jit(solution)/shard_map/ppermute | solution.py:54
  73.1 25.9 %all-to-all-start.3 = ((bf16[16,4,2,16,128]{4,3,2,1,0:T(8,128)(2,1)}), bf16[16,4,2,16,128]{4,3,2,1,0:T(8,128)(2,1)S(1)}, u32[]{:S(2)}, u32[]{:S(2)}) async-start(bf16[16,4,2,16,128]{4,3,2,1,0:T(8,128)(2,1)} %correlate.2), calls=%async_computation.3 | async-start | bytes 1048576 | tf_op jit(solution)/shard_map/all_to_all | solution.py:408
  91.9 13.5 %collective-permute-start.8 = (bf16[16,3,16,128]{3,2,1,0:T(8,128)(2,1)S(1)}, bf16[16,3,16,128]{3,2,1,0:T(8,128)(2,1)S(1)}, u32[]{:S(2)}, u32[]{:S(2)}) collective-permute-start(bf16[16,3,16,128]{3,2,1,0:T(8,128)(2,1)S(1)} %get-tuple-element.37), channel_id=1, source_target_pairs={{0,66},{1,67},{2,128},{3,129},{4,70},{5,71},{6,132},{7,133},{8,74}... | collective-permute-start | bytes 589832 | tf_op jit(solution)/shard_map/ppermute | solution.py:54
  91.9 14.8 %collective-permute-start.9 = (bf16[16,3,16,128]{3,2,1,0:T(8,128)(2,1)S(1)}, bf16[16,3,16,128]{3,2,1,0:T(8,128)(2,1)S(1)}, u32[]{:S(2)}, u32[]{:S(2)}) collective-permute-start(bf16[16,3,16,128]{3,2,1,0:T(8,128)(2,1)S(1)} %get-tuple-element.38), channel_id=1, source_target_pairs={{0,130},{1,131},{2,192},{3,193},{4,134},{5,135},{6,196},{7,197},{8... | collective-permute-start | bytes 589832 | tf_op jit(solution)/shard_map/ppermute | solution.py:54
  96.4 14.4 %collective-permute-start.10 = (bf16[16,3,16,128]{3,2,1,0:T(8,128)(2,1)S(1)}, bf16[16,3,16,128]{3,2,1,0:T(8,128)(2,1)S(1)}, u32[]{:S(2)}, u32[]{:S(2)}) collective-permute-start(bf16[16,3,16,128]{3,2,1,0:T(8,128)(2,1)S(1)} %get-tuple-element.39), channel_id=1, source_target_pairs={{0,2},{1,3},{2,64},{3,65},{4,6},{5,7},{6,68},{7,69},{8,10},{9,11},... | collective-permute-start | bytes 589832 | tf_op jit(solution)/shard_map/ppermute | solution.py:54
  96.4 16.5 %collective-permute-start.11 = (bf16[16,3,16,128]{3,2,1,0:T(8,128)(2,1)S(1)}, bf16[16,3,16,128]{3,2,1,0:T(8,128)(2,1)S(1)}, u32[]{:S(2)}, u32[]{:S(2)}) collective-permute-start(bf16[16,3,16,128]{3,2,1,0:T(8,128)(2,1)S(1)} %get-tuple-element.40), channel_id=1, source_target_pairs={{0,194},{1,195},{2,0},{3,1},{4,198},{5,199},{6,4},{7,5},{8,202},{9... | collective-permute-start | bytes 589832 | tf_op jit(solution)/shard_map/ppermute | solution.py:54
  99.1 20.0 %collective-permute-start.15 = (bf16[16,2,16,128]{3,2,1,0:T(8,128)(2,1)S(1)}, bf16[16,2,16,128]{3,2,1,0:T(8,128)(2,1)S(1)}, u32[]{:S(2)}, u32[]{:S(2)}) collective-permute-start(bf16[16,2,16,128]{3,2,1,0:T(8,128)(2,1)S(1)} %get-tuple-element.51), channel_id=1, source_target_pairs={{0,66},{1,67},{2,128},{3,129},{4,70},{5,71},{6,132},{7,133},{8,74}... | collective-permute-start | bytes 393224 | tf_op jit(solution)/shard_map/ppermute | solution.py:54
  105.4 13.7 %collective-permute-start.14 = (bf16[16,2,16,128]{3,2,1,0:T(8,128)(2,1)S(1)}, bf16[16,2,16,128]{3,2,1,0:T(8,128)(2,1)S(1)}, u32[]{:S(2)}, u32[]{:S(2)}) collective-permute-start(bf16[16,2,16,128]{3,2,1,0:T(8,128)(2,1)S(1)} %get-tuple-element.52), channel_id=1, source_target_pairs={{0,130},{1,131},{2,192},{3,193},{4,134},{5,135},{6,196},{7,197},{8... | collective-permute-start | bytes 393224 | tf_op jit(solution)/shard_map/ppermute | solution.py:54
  106.8 14.5 %collective-permute-start.13 = (bf16[16,2,16,128]{3,2,1,0:T(8,128)(2,1)S(1)}, bf16[16,2,16,128]{3,2,1,0:T(8,128)(2,1)S(1)}, u32[]{:S(2)}, u32[]{:S(2)}) collective-permute-start(bf16[16,2,16,128]{3,2,1,0:T(8,128)(2,1)S(1)} %get-tuple-element.53), channel_id=1, source_target_pairs={{0,2},{1,3},{2,64},{3,65},{4,6},{5,7},{6,68},{7,69},{8,10},{9,11},... | collective-permute-start | bytes 393224 | tf_op jit(solution)/shard_map/ppermute | solution.py:54
  110.8 12.5 %collective-permute-start.12 = (bf16[16,2,16,128]{3,2,1,0:T(8,128)(2,1)S(1)}, bf16[16,2,16,128]{3,2,1,0:T(8,128)(2,1)S(1)}, u32[]{:S(2)}, u32[]{:S(2)}) collective-permute-start(bf16[16,2,16,128]{3,2,1,0:T(8,128)(2,1)S(1)} %get-tuple-element.54), channel_id=1, source_target_pairs={{0,194},{1,195},{2,0},{3,1},{4,198},{5,199},{6,4},{7,5},{8,202},{9... | collective-permute-start | bytes 393224 | tf_op jit(solution)/shard_map/ppermute | solution.py:54
  113.8 15.8 %all-to-all-start.2 = ((bf16[16,4,3,16,128]{4,3,2,1,0:T(8,128)(2,1)}), bf16[16,4,3,16,128]{4,3,2,1,0:T(8,128)(2,1)S(1)}, u32[]{:S(2)}, u32[]{:S(2)}) async-start(bf16[16,4,3,16,128]{4,3,2,1,0:T(8,128)(2,1)} %gather.3), calls=%async_computation.2 | async-start | bytes 1572864 | tf_op jit(solution)/shard_map/all_to_all | solution.py:411
  119.1 10.2 %copy-start.1 = (bf16[1,64,192]{2,1,0:T(8,128)(2,1)S(1)}, bf16[1,64,192]{2,1,0:T(8,128)(2,1)}, u32[]{:S(2)}) copy-start(bf16[1,64,192]{2,1,0:T(8,128)(2,1)} %param.8) | copy-start | bytes 73732
  119.1 31.4 %copy-start = (s32[4,5]{1,0:T(4,128)S(1)}, s32[4,5]{1,0:T(4,128)}, u32[]{:S(2)}) copy-start(s32[4,5]{1,0:T(4,128)} %pattern_ref.3) | copy-start | bytes 244
  123.6 10.8 %collective-permute-start.17 = (bf16[16,2,64,128]{3,2,1,0:T(8,128)(2,1)S(1)}, bf16[16,2,64,128]{3,2,1,0:T(8,128)(2,1)S(1)}, u32[]{:S(2)}, u32[]{:S(2)}) collective-permute-start(bf16[16,2,64,128]{3,2,1,0:T(8,128)(2,1)S(1)} %settle.2.refs_3_), channel_id=1, source_target_pairs={{1,0},{2,1},{3,2},{5,4},{6,5},{7,6},{9,8},{10,9},{11,10},{13,12},{... | collective-permute-start | bytes 1572872 | tf_op jit(solution)/shard_map/ppermute | solution.py:414
  126.8 8.6 %collective-permute-start.16 = (bf16[16,2,64,128]{3,2,1,0:T(8,128)(2,1)S(1)}, bf16[16,2,64,128]{3,2,1,0:T(8,128)(2,1)S(1)}, u32[]{:S(2)}, u32[]{:S(2)}) collective-permute-start(bf16[16,2,64,128]{3,2,1,0:T(8,128)(2,1)S(1)} %settle.2.refs_3_), channel_id=1, source_target_pairs={{0,1},{1,2},{2,3},{4,5},{5,6},{6,7},{8,9},{9,10},{10,11},{12,13},{... | collective-permute-start | bytes 1572872 | tf_op jit(solution)/shard_map/ppermute | solution.py:414
  135.3 10.8 %collective-permute-start.18 = (bf16[16,2,64,128]{3,2,1,0:T(8,128)(2,1)}, bf16[16,2,64,128]{3,2,1,0:T(8,128)(2,1)S(1)}, u32[]{:S(2)}, u32[]{:S(2)}) collective-permute-start(bf16[16,2,64,128]{3,2,1,0:T(8,128)(2,1)} %get-tuple-element.44), channel_id=1, source_target_pairs={{0,1},{1,2},{2,3},{4,5},{5,6},{6,7},{8,9},{9,10},{10,11},{12,13},{... | collective-permute-start | bytes 1572872 | tf_op jit(solution)/shard_map/ppermute | solution.py:416
  139.7 10.8 %collective-permute-start.19 = (bf16[16,2,64,128]{3,2,1,0:T(8,128)(2,1)}, bf16[16,2,64,128]{3,2,1,0:T(8,128)(2,1)}, u32[]{:S(2)}, u32[]{:S(2)}) collective-permute-start(bf16[16,2,64,128]{3,2,1,0:T(8,128)(2,1)} %get-tuple-element.46), channel_id=1, source_target_pairs={{1,0},{2,1},{3,2},{5,4},{6,5},{7,6},{9,8},{10,9},{11,10},{13,12},{... | collective-permute-start | bytes 1572872 | tf_op jit(solution)/shard_map/ppermute | solution.py:416
